TPU v7x, 32 devices: a whole 2x2x4 slice. The times are simulated.
32 devices in a mesh: gossip: 16 (over z, y, core), group: 2 (over x).
Axes of the slice: x: 2, y: 2, z: 4, core: 2. Of those that a mesh axis runs over, the one named last changes fastest.
Arguments:
- weights: bfloat16 [32, 1024, 512], P(('gossip', 'group')), may hold values from -6 to 6
- inputs: bfloat16 [24576, 1024], P(('gossip', 'group')), may hold values from -6 to 6
- targets: bfloat16 [24576, 512], P(('gossip', 'group')), may hold values from -6 to 6
- peer_plan: int32 [3, 2], replicated, may hold values from 1 to 4
- shard_order: int32 [32, 3], P(('gossip', 'group')), may hold values from 0 to 2, each once within a row
Outputs:
- replica_weights: bfloat16 [32, 1024, 512], P(('gossip', 'group'))
- mean_weights: float32 [1024, 512], P(('gossip', 'group'))
All inputs are finite; a program needn't handle non-finite values.
Results may differ from a plain program's by a relative error of at most 0.0054.
Values may be sent and summed in bfloat16 or wider, within the bound.
No kernel may reach another device: no remote copies, remote signals or barrier semaphores. Data moves between devices by JAX's collectives and lax.ppermute only.
A program may use at most 64 MiB of HBM per device.

v0:
```python
import math

import jax
import jax.numpy as jnp
from jax import lax
from jax.sharding import PartitionSpec as P

STEPS = 3


learning_rate = 0.3
momentum_decay = 0.9


def shifted(value, axis, steps):
    count = lax.axis_size(axis)
    pairs = [(source, (source + steps) % count) for source in range(count)]
    return lax.ppermute(value, axis, pairs)


def local_gradient(batch_in, batch_out, rounded):
    fan_scale = 1.0 / math.sqrt(batch_in.shape[1])
    preact = jnp.dot(batch_in, rounded, preferred_element_type=jnp.float32) * fan_scale
    normal_cdf = 0.5 * (1.0 + lax.erf(preact * (1.0 / math.sqrt(2.0))))
    normal_pdf = jnp.exp(-0.5 * preact * preact) * (1.0 / math.sqrt(2.0 * math.pi))
    residual = preact * normal_cdf - batch_out.astype(jnp.float32)
    derivative = normal_cdf + preact * normal_pdf
    delta = (residual * derivative).astype(jnp.bfloat16)
    product = lax.dot_general(
        batch_in, delta, (((0,), (0,)), ((), ())), preferred_element_type=jnp.float32
    )
    return product * fan_scale


def body(weights, inputs, targets, peer_plan, shard_order):
    master = weights[0].astype(jnp.float32)
    velocity = jnp.zeros_like(master)
    row_count = inputs.shape[0] // STEPS
    for step_index in range(STEPS):
        rounded = master.astype(jnp.bfloat16)
        neighbour = shifted(rounded, "gossip", 2**step_index)
        shard_pick = shard_order[0, step_index]
        batch_in = lax.dynamic_slice_in_dim(inputs, shard_pick * row_count, row_count, 0)
        batch_out = lax.dynamic_slice_in_dim(targets, shard_pick * row_count, row_count, 0)
        gradient = local_gradient(batch_in, batch_out, rounded)
        velocity = momentum_decay * velocity + gradient
        self_weight = peer_plan[step_index, 0].astype(jnp.float32)
        peer_weight = peer_plan[step_index, 1].astype(jnp.float32)
        master = (self_weight * master + peer_weight * neighbour.astype(jnp.float32)) / (
            self_weight + peer_weight
        ) - learning_rate * velocity
    replica_weights = master.astype(jnp.bfloat16)[None]
    replicas_all = lax.axis_size("gossip") * lax.axis_size("group")
    cycle_sums = lax.psum_scatter(master, "gossip", scatter_dimension=0, tiled=True)
    summed = lax.psum_scatter(cycle_sums, "group", scatter_dimension=0, tiled=True)
    mean_weights = summed / replicas_all
    return (replica_weights, mean_weights)


def solution(mesh):
    return jax.shard_map(
        body,
        mesh=mesh,
        in_specs=(
            P(("gossip", "group"), None, None),
            P(("gossip", "group"), None),
            P(("gossip", "group"), None),
            P(),
            P(("gossip", "group"), None),
        ),
        out_specs=(P(("gossip", "group"), None, None), P(("gossip", "group"), None)),
        check_vma=False,
    )
```

profile of v0, /device:TPU:0, one launch (start us, length us, event | category | flops | bytes accessed | tf_op | source)
XLA Modules:
  0.0 172.1 jit_solution(3791902536899616857)
XLA Ops:
  7.2 0.0 copy-start
  7.2 0.0 reduce-scatter.3.cloned.1.call-start
  7.2 0.5 collective-permute-start
  7.8 1.4 fusion.79
  9.8 1.6 fusion.78
  12.6 0.0 copy-start.1
  12.6 12.8 %collective-permute-done = bf16[1024,512]{1,0:T(8,128)(2,1)S(1)} collective-permute-done((bf16[1024,512]{1,0:T(8,128)(2,1)}, bf16[1024,512]{1,0:T(8,128)(2,1)S(1)}, u32[]{:S(2)}, u32[]{:S(2)}) %collective-permute-start) | collective-permute-done | bytes 1048608 | tf_op jit(solution)/shard_map/ppermute | solution.py:18
  25.4 0.0 copy-done
  25.4 5.3 %fusion.77 = (bf16[1024,512]{1,0:T(8,128)(2,1)}, f32[1024,512]{1,0:T(8,128)}, f32[1024,512]{1,0:T(8,128)}) fusion(f32[]{:T(128)S(6)} %add.59, bf16[1024,512]{1,0:T(8,128)(2,1)S(1)} %collective-permute-done, f32[]{:T(128)} %bitcast.4, bf16[1,1024,512]{2,1,0:T(8,128)(2,1)} %param.5, f32[]{:T(128)} %bitcast.2, bf16[768,1024]{1,0:T(8,128)(2,1)S(1)} %copy-done, ...), kind=kOutput, calls=%fused_computation.64 | convolution fusion | flops 543424512 | bytes 9702400 | tf_op jit(solution)/shard_map/dot_general | solution.py:29
  30.7 0.0 collective-permute-start.1
  32.6 23.1 %collective-permute-done.1 = bf16[1024,512]{1,0:T(8,128)(2,1)S(1)} collective-permute-done((bf16[1024,512]{1,0:T(8,128)(2,1)}, bf16[1024,512]{1,0:T(8,128)(2,1)S(1)}, u32[]{:S(2)}, u32[]{:S(2)}) %collective-permute-start.1) | collective-permute-done | bytes 1048608 | tf_op jit(solution)/shard_map/ppermute | solution.py:18
  55.7 0.0 copy-done.1
  55.7 5.7 %fusion.74 = (bf16[1024,512]{1,0:T(8,128)(2,1)}, f32[1024,512]{1,0:T(8,128)}) fusion(f32[]{:T(128)S(6)} %add.64, bf16[1024,512]{1,0:T(8,128)(2,1)S(1)} %collective-permute-done.1, f32[]{:T(128)} %bitcast.6, f32[1024,512]{1,0:T(8,128)} %get-tuple-element.3, f32[]{:T(128)} %bitcast.1, bf16[1024,512]{1,0:T(8,128)(2,1)} %get-tuple-element.2, ...), kind=kOutput, calls=%fused_computation.63 | convolution fusion | flops 544473088 | bytes 10749960 | tf_op jit(solution)/shard_map/dot_general | solution.py:29
  61.5 0.0 collective-permute-start.2
  63.4 21.4 %collective-permute-done.2 = bf16[1024,512]{1,0:T(8,128)(2,1)} collective-permute-done((bf16[1024,512]{1,0:T(8,128)(2,1)}, bf16[1024,512]{1,0:T(8,128)(2,1)}, u32[]{:S(2)}, u32[]{:S(2)}) %collective-permute-start.2) | collective-permute-done | bytes 1048608 | tf_op jit(solution)/shard_map/ppermute | solution.py:18
  84.8 7.3 %multiply_subtract_fusion = f32[1024,512]{1,0:T(8,128)} fusion(f32[1024,512]{1,0:T(8,128)} %get-tuple-element.15, bf16[1024,512]{1,0:T(8,128)(2,1)} %collective-permute-done.2, f32[]{:T(128)S(6)} %add.70, f32[]{:T(128)} %bitcast.8, f32[]{:T(128)} %bitcast, bf16[768,1024]{1,0:T(8,128)(2,1)S(1)} %copy-done, s32[]{:T(128)S(6)} %select_n.14, ...), kind=kOutput, calls=%fused_computation | convolution fusion | flops 551813120 | bytes 14948352 | tf_op jit(solution)/shard_map/dot_general | solution.py:29
  92.1 0.0 reduce-scatter.3.cloned.1.call-update
  92.1 0.0 reduce-scatter.5.cloned.1.call-start
  92.1 60.1 %reduce-scatter.3.cloned.1.call-done = f32[64,512]{1,0:T(8,128)} async-done(((f32[1024,512]{1,0:T(8,128)}), f32[64,512]{1,0:T(8,128)}) %reduce-scatter.3.cloned.1.call-update) | async-done | bytes 131088 | tf_op jit(solution)/shard_map/reduce_scatter | solution.py:54
  152.2 0.0 reduce-scatter.5.cloned.1.call-update
  152.3 2.7 %convert_bitcast_fusion = bf16[1,1024,512]{2,1,0:T(8,128)(2,1)} fusion(f32[1024,512]{1,0:T(8,128)} %multiply_subtract_fusion), kind=kLoop, calls=%fused_computation.4 | loop fusion | flops 524288 | bytes 3145728 | tf_op jit(solution)/shard_map/broadcast_in_dim | solution.py:52
  155.0 8.8 %reduce-scatter.5.cloned.1.call-done = f32[32,512]{1,0:T(8,128)} async-done(((f32[64,512]{1,0:T(8,128)}), f32[32,512]{1,0:T(8,128)}) %reduce-scatter.5.cloned.1.call-update) | async-done | bytes 65552 | tf_op jit(solution)/shard_map/reduce_scatter | solution.py:55
  163.8 1.5 broadcast_multiply_fusion
Async XLA Ops:
  7.2 18.3 %copy-start = (bf16[768,1024]{1,0:T(8,128)(2,1)S(1)}, bf16[768,1024]{1,0:T(8,128)(2,1)}, u32[]{:S(2)}) copy-start(bf16[768,1024]{1,0:T(8,128)(2,1)} %param.6) | copy-start | bytes 4718596
  7.2 145.1 %reduce-scatter.3.cloned.1.call-start = ((), (), s32[]{:S(2)}) async-start(), calls=%async_computation.2 | async-start | bytes 2228224 | tf_op jit(solution)/shard_map/reduce_scatter | solution.py:54
  7.2 18.2 %collective-permute-start = (bf16[1024,512]{1,0:T(8,128)(2,1)}, bf16[1024,512]{1,0:T(8,128)(2,1)S(1)}, u32[]{:S(2)}, u32[]{:S(2)}) collective-permute-start(bf16[1024,512]{1,0:T(8,128)(2,1)} %bitcast.20), channel_id=1, source_target_pairs={{0,2},{2,4},{4,6},{6,8},{8,10},{10,12},{12,14},{14,16},{16,18},{18... | collective-permute-start | bytes 3145736 | tf_op jit(solution)/shard_map/ppermute | solution.py:18
  12.6 43.1 %copy-start.1 = (bf16[768,512]{1,0:T(8,128)(2,1)S(1)}, bf16[768,512]{1,0:T(8,128)(2,1)}, u32[]{:S(2)}) copy-start(bf16[768,512]{1,0:T(8,128)(2,1)} %param.7) | copy-start | bytes 2359300
  30.7 25.0 %collective-permute-start.1 = (bf16[1024,512]{1,0:T(8,128)(2,1)}, bf16[1024,512]{1,0:T(8,128)(2,1)S(1)}, u32[]{:S(2)}, u32[]{:S(2)}) collective-permute-start(bf16[1024,512]{1,0:T(8,128)(2,1)} %get-tuple-element.2), channel_id=1, source_target_pairs={{0,4},{2,6},{4,8},{6,10},{8,12},{10,14},{12,16},{14,18},{16,20},{1... | collective-permute-start | bytes 3145736 | tf_op jit(solution)/shard_map/ppermute | solution.py:18
  61.5 23.3 %collective-permute-start.2 = (bf16[1024,512]{1,0:T(8,128)(2,1)}, bf16[1024,512]{1,0:T(8,128)(2,1)}, u32[]{:S(2)}, u32[]{:S(2)}) collective-permute-start(bf16[1024,512]{1,0:T(8,128)(2,1)} %get-tuple-element.14), channel_id=1, source_target_pairs={{0,8},{2,10},{4,12},{6,14},{8,16},{10,18},{12,20},{14,22},{16,24},... | collective-permute-start | bytes 3145736 | tf_op jit(solution)/shard_map/ppermute | solution.py:18
  92.1 71.7 %reduce-scatter.5.cloned.1.call-start = ((), (), s32[]{:S(2)}) async-start(), calls=%async_computation.3 | async-start | bytes 196608 | tf_op jit(solution)/shard_map/reduce_scatter | solution.py:55
Sparse Core Ops, SparseCore 0:
  92.2 59.9 reduce-scatter.2
  154.4 9.2 reduce-scatter.4
where the time goes:
time: 172 us
  waiting for transfers between devices  126 us (73%)
  between operations  19.7 us (11%)
  matrix products  18.3 us (11%)
  other arithmetic  4.17 us (2%)
  local copies, waits for them, and re-layouts  2.99 us (2%)
    reduce_scatter x1, waiting for transfers between devices, body(): lax.psum_scatter(master, 'gossip', scatter_dimension=0, tiled=True)  60.1 us
    ppermute x3, waiting for transfers between devices, shifted(): return lax.ppermute(value, axis, pairs)  57.3 us
    dot_general x3, matrix products, local_gradient(): lax.dot_general(batch_in, delta, (((0,), (0,)), ((), ())), preferred_elem...  18.3 us
    reduce_scatter x1, waiting for transfers between devices, body(): lax.psum_scatter(cycle_sums, 'group', scatter_dimension=0, tiled=True)  8.82 us
  transfers between devices with their start and end apart: 5, of which 5 were waited for; matrix products, arithmetic and copies ran while one was open for 3% of the time, Pallas kernels for 0%

commit v1 on v0

v1 whole, which is shorter than its diff:
```python
import math

import jax
import jax.numpy as jnp
from jax import lax
from jax.sharding import PartitionSpec as P


STEPS = 3

learning_rate = 0.3
momentum_decay = 0.9


def shifted(value, axis, steps):
    count = lax.axis_size(axis)
    pairs = [(source, (source + steps) % count) for source in range(count)]
    return lax.ppermute(value, axis, pairs)


def flipped(value, axis, bit):
    count = lax.axis_size(axis)
    return lax.ppermute(value, axis, [(source, source ^ bit) for source in range(count)])


def local_gradient(batch_in, batch_out, rounded):
    fan_scale = 1.0 / math.sqrt(batch_in.shape[1])
    preact = jnp.dot(batch_in, rounded, preferred_element_type=jnp.float32) * fan_scale
    normal_cdf = 0.5 * (1.0 + lax.erf(preact * (1.0 / math.sqrt(2.0))))
    normal_pdf = jnp.exp(-0.5 * preact * preact) * (1.0 / math.sqrt(2.0 * math.pi))
    residual = preact * normal_cdf - batch_out.astype(jnp.float32)
    derivative = normal_cdf + preact * normal_pdf
    delta = (residual * derivative).astype(jnp.bfloat16)
    product = lax.dot_general(
        batch_in, delta, (((0,), (0,)), ((), ())), preferred_element_type=jnp.float32
    )
    return product * fan_scale


def scattered_sum(value):
    n_gossip, n_group = lax.axis_size("gossip"), lax.axis_size("group")
    gossip_bits, group_bits = n_gossip.bit_length() - 1, n_group.bit_length() - 1
    rows = value.shape[0]
    value = value.reshape((2,) * (gossip_bits + group_bits) + (rows // (n_gossip * n_group), value.shape[1]))
    left = [("gossip", bit) for bit in reversed(range(gossip_bits))]
    left += [("group", bit) for bit in reversed(range(group_bits))]
    order = [("gossip", 0)] + [("group", bit) for bit in range(group_bits)]
    order += [("gossip", bit) for bit in range(1, gossip_bits)]
    for axis, bit in order:
        place = left.index((axis, bit))
        mine = (lax.axis_index(axis) >> bit) & 1
        keep = lax.dynamic_index_in_dim(value, mine, place, keepdims=False)
        give = lax.dynamic_index_in_dim(value, 1 - mine, place, keepdims=False)
        arrived = flipped(give, axis, 1 << bit)
        value = keep + arrived
        left.pop(place)
    return value


def steps(weights, inputs, targets, peer_plan, shard_order):
    rounded = weights[0]
    master = rounded.astype(jnp.float32)
    velocity = None
    row_count = inputs.shape[0] // STEPS
    for step_index in range(STEPS):
        neighbour = shifted(rounded, "gossip", 2**step_index)
        shard_pick = shard_order[0, step_index]
        batch_in = lax.dynamic_slice_in_dim(inputs, shard_pick * row_count, row_count, 0)
        batch_out = lax.dynamic_slice_in_dim(targets, shard_pick * row_count, row_count, 0)
        gradient = local_gradient(batch_in, batch_out, rounded)
        velocity = gradient if velocity is None else momentum_decay * velocity + gradient
        plan = peer_plan[step_index].astype(jnp.float32)
        total = plan[0] + plan[1]
        own_share, peer_share = plan[0] / total, plan[1] / total
        base = lax.optimization_barrier(own_share * master - learning_rate * velocity)
        if step_index == STEPS - 1:
            part = lax.optimization_barrier(base + peer_share * rounded.astype(jnp.float32))
            replicas_all = lax.axis_size("gossip") * lax.axis_size("group")
            mean_weights = scattered_sum(part) / replicas_all
            mean_weights, neighbour = lax.optimization_barrier((mean_weights, neighbour))
        master = base + peer_share * neighbour.astype(jnp.float32)
        rounded = master.astype(jnp.bfloat16)
    return (rounded[None], mean_weights)


def solution(mesh):
    return jax.shard_map(
        steps,
        mesh=mesh,
        in_specs=(
            P(("gossip", "group"), None, None),
            P(("gossip", "group"), None),
            P(("gossip", "group"), None),
            P(),
            P(("gossip", "group"), None),
        ),
        out_specs=(P(("gossip", "group"), None, None), P(("gossip", "group"), None)),
        check_vma=False,
    )
```

time: 172 us -> 119 us (0.69)
  waiting for transfers between devices: 126 us -> 67.1 us
  other arithmetic: 4.17 us -> 15.8 us
  between operations: 19.7 us -> 10.5 us
  local copies, waits for them, and re-layouts: 2.99 us -> 5.77 us
  starting transfers between devices: 0.63 us -> 3.25 us
  matrix products: 18.3 us -> 16 us
    reduce_scatter x2 -> x0, waiting for transfers between devices: 68.9 us -> none  [the longest x1 60.1 us: body(): lax.psum_scatter(master, 'gossip', scatter_dimension=0, tiled=True)]
    ppermute x0 -> x5, waiting for transfers between devices: none -> 48.1 us  [flipped(): lax.ppermute(value, axis, [(source, source ^ bit) for source in range(cou...]
    ppermute x3, waiting for transfers between devices: 57.3 us -> 19 us  [shifted(): return lax.ppermute(value, axis, pairs)]
    add x0 -> x5, other arithmetic: none -> 5.98 us  [the longest x4 4.06 us: scattered_sum(): value = keep + arrived]
    convert_element_type x0 -> x3, other arithmetic: none -> 5.98 us  [the longest x2 5.12 us: steps(): rounded = master.astype(jnp.bfloat16)]
    dot_general x3, matrix products: 18.3 us -> 16 us  [local_gradient(): lax.dot_general(batch_in, delta, (((0,), (0,)), ((), ())), preferred_elem...]
    ppermute x0 -> x5, starting transfers between devices: none -> 2.33 us  [flipped(): lax.ppermute(value, axis, [(source, source ^ bit) for source in range(cou...]
    dynamic_slice x0 -> x2, local copies, waits for them, and re-layouts: none -> 2.22 us  [the longest x1 1.16 us: scattered_sum(): keep = lax.dynamic_index_in_dim(value, mine, place, keepdims=False)]
  transfers between devices with their start and end apart: 5 -> 8, of which waited for: 5 -> 7; matrix products, arithmetic and copies ran while one was open for 3% -> 13% of each run, Pallas kernels for 0% -> 0%
where the time goes in v1:
time: 119 us; the launch traced here: 118 us
  waiting for transfers between devices  67.1 us (56%)
  matrix products  16 us (13%)
  other arithmetic  15.8 us (13%)
  between operations  10.5 us (9%)
  local copies, waits for them, and re-layouts  5.77 us (5%)
  starting transfers between devices  3.25 us (3%)
    ppermute x5, waiting for transfers between devices, flipped(): lax.ppermute(value, axis, [(source, source ^ bit) for source in range(cou...  48.1 us
    ppermute x3, waiting for transfers between devices, shifted(): return lax.ppermute(value, axis, pairs)  19 us
    dot_general x3, matrix products, local_gradient(): lax.dot_general(batch_in, delta, (((0,), (0,)), ((), ())), preferred_elem...  16 us
    convert_element_type x2, other arithmetic, steps(): rounded = master.astype(jnp.bfloat16)  5.12 us
    add x4, other arithmetic, scattered_sum(): value = keep + arrived  4.06 us
    broadcast_in_dim x1, other arithmetic, steps(): return (rounded[None], mean_weights)  3.18 us
  transfers between devices with their start and end apart: 8, of which 7 were waited for; matrix products, arithmetic and copies ran while one was open for 13% of the time, Pallas kernels for 0%

profile of v1, /device:TPU:0, one launch (start us, length us, event | category | flops | bytes accessed | tf_op | source)
XLA Modules:
  0.0 118.3 jit_solution(16198716668365969145)
XLA Ops:
  0.6 0.0 copy-start
  0.6 0.5 collective-permute-start
  1.2 0.9 slice_convert_fusion.2
  2.1 0.5 fusion.75
  5.2 1.4 %fusion.76 = (s32[1,1]{1,0:T(1,128)}, s32[1,1]{1,0:T(1,128)}, s32[1,1]{1,0:T(1,128)}) fusion(s32[1,3]{1,0:T(1,128)} %param.9), kind=kLoop, calls=%fused_computation.86 | loop fusion | bytes 24 | tf_op jit(solution)/shard_map/slice | solution.py:67
  7.2 0.0 copy-done
  7.2 4.7 %multiply_subtract_fusion.2 = (f32[1024,512]{1,0:T(8,128)}, f32[1024,512]{1,0:T(8,128)}) fusion(f32[]{:T(128)S(6)} %div.26, bf16[1,1024,512]{2,1,0:T(8,128)(2,1)} %param.5, bf16[768,1024]{1,0:T(8,128)(2,1)S(1)} %copy-done, s32[]{:T(128)S(6)} %select_n.47, bf16[768,512]{1,0:T(8,128)(2,1)} %param.7), kind=kOutput, calls=%fused_computation.7 | convolution fusion | flops 540803072 | bytes 7604224 | tf_op jit(solution)/shard_map/dot_general | solution.py:34
  11.9 0.0 copy-start.2
  11.9 7.0 %collective-permute-done = bf16[1024,512]{1,0:T(8,128)(2,1)S(1)} collective-permute-done((bf16[1024,512]{1,0:T(8,128)(2,1)}, bf16[1024,512]{1,0:T(8,128)(2,1)S(1)}, u32[]{:S(2)}, u32[]{:S(2)}) %collective-permute-start) | collective-permute-done | bytes 1048608 | tf_op jit(solution)/shard_map/ppermute | solution.py:18
  18.9 2.9 %fusion = bf16[1024,512]{1,0:T(8,128)(2,1)} fusion(f32[1024,512]{1,0:T(8,128)} %get-tuple-element.20, bf16[1024,512]{1,0:T(8,128)(2,1)S(1)} %collective-permute-done, f32[]{:T(128)S(6)} %div.27), kind=kLoop, calls=%fused_computation.8 | loop fusion | flops 2097152 | bytes 4194308 | tf_op jit(solution)/shard_map/convert_element_type | solution.py:82
  21.8 0.0 collective-permute-start.1
  22.4 0.6 fusion.73
  28.8 0.0 copy-done.2
  28.8 6.0 %multiply_subtract_fusion.1 = (f32[1024,512]{1,0:T(8,128)}, f32[1024,512]{1,0:T(8,128)}) fusion(f32[1024,512]{1,0:T(8,128)} %get-tuple-element.20, bf16[1024,512]{1,0:T(8,128)(2,1)S(1)} %collective-permute-done, f32[]{:T(128)S(6)} %div.27, f32[]{:T(128)S(6)} %div.25, bf16[1024,512]{1,0:T(8,128)(2,1)} %fusion, bf16[768,1024]{1,0:T(8,128)(2,1)S(1)} %copy-done, ...), kind=kOutput, calls=%fused_computation.4 | convolution fusion | flops 543424512 | bytes 11799040 | tf_op jit(solution)/shard_map/dot_general | solution.py:34
  34.8 12.0 %collective-permute-done.1 = bf16[1024,512]{1,0:T(8,128)(2,1)} collective-permute-done((bf16[1024,512]{1,0:T(8,128)(2,1)}, bf16[1024,512]{1,0:T(8,128)(2,1)}, u32[]{:S(2)}, u32[]{:S(2)}) %collective-permute-start.1) | collective-permute-done | bytes 1048608 | tf_op jit(solution)/shard_map/ppermute | solution.py:18
  46.9 2.2 %fusion.1 = bf16[1024,512]{1,0:T(8,128)(2,1)S(1)} fusion(f32[1024,512]{1,0:T(8,128)} %get-tuple-element.22, bf16[1024,512]{1,0:T(8,128)(2,1)} %collective-permute-done.1, f32[]{:T(128)S(6)} %div.28), kind=kLoop, calls=%fused_computation.9 | loop fusion | flops 2097152 | bytes 4194308 | tf_op jit(solution)/shard_map/convert_element_type | solution.py:82
  49.1 5.3 %multiply_subtract_fusion = f32[1024,512]{1,0:T(8,128)} fusion(f32[1024,512]{1,0:T(8,128)} %get-tuple-element.23, f32[1024,512]{1,0:T(8,128)} %get-tuple-element.22, bf16[1024,512]{1,0:T(8,128)(2,1)} %collective-permute-done.1, f32[]{:T(128)S(6)} %div.28, f32[]{:T(128)S(6)} %div.24, bf16[768,1024]{1,0:T(8,128)(2,1)S(1)} %copy-done, s32[]{:T(128)S(6)} %select_n.49, ...), kind=kOutput, calls=%fused_computation.2 | convolution fusion | flops 543424512 | bytes 9701888 | tf_op jit(solution)/shard_map/dot_general | solution.py:34
  54.3 1.9 %multiply_add_fusion = f32[1024,512]{1,0:T(8,128)S(1)} fusion(f32[1024,512]{1,0:T(8,128)} %multiply_subtract_fusion, bf16[1024,512]{1,0:T(8,128)(2,1)S(1)} %fusion.1, f32[]{:T(128)S(6)} %div.29), kind=kLoop, calls=%fused_computation.1 | loop fusion | flops 1572864 | bytes 5242884 | tf_op jit(solution)/shard_map/add | solution.py:77
  56.3 1.2 constant_dynamic-slice_fusion.1
  57.4 1.1 copy.11
  58.5 0.0 collective-permute-start.2
  58.5 3.0 %collective-permute-done.2 = f32[2,2,2,2,32,512]{5,4,2,1,0,3:T(8,128)} collective-permute-done((f32[2,2,2,2,32,512]{5,4,2,1,0,3:T(8,128)}, f32[2,2,2,2,32,512]{5,4,2,1,0,3:T(8,128)}, u32[]{:S(2)}, u32[]{:S(2)}) %collective-permute-start.2) | collective-permute-done | bytes 1048608 | tf_op jit(solution)/shard_map/ppermute | solution.py:23
  61.5 1.8 %bitcast_add_fusion = f32[2,2,2,2,32,512]{5,4,2,1,0,3:T(8,128)S(1)} fusion(f32[2,2,2,2,32,512]{5,4,2,1,0,3:T(8,128)} %collective-permute-done.2, f32[2,2,2,1,2,32,512]{6,5,4,3,2,1,0:T(8,128)} %get-tuple-element.6), kind=kLoop, calls=%fused_computation.11 | loop fusion | flops 262144 | bytes 3145728 | tf_op jit(solution)/shard_map/add | solution.py:55
  63.3 0.0 copy-start.1
  63.3 1.0 copy-done.1
  64.3 1.6 %collective-permute-start.3 = (f32[2,2,2,32,512]{4,3,2,1,0:T(8,128)S(1)}, f32[2,2,2,32,512]{4,3,2,1,0:T(8,128)}, u32[]{:S(2)}, u32[]{:S(2)}) collective-permute-start(f32[2,2,2,32,512]{4,3,2,1,0:T(8,128)S(1)} %dynamic-slice_bitcast_fusion), channel_id=1, source_target_pairs={{0,1},{1,0},{2,3},{3,2},{4,5},{5,4},{6,7},{7,6},{8,9},{9,8},{10,11... | collective-permute-start | bytes 1572872 | tf_op jit(solution)/shard_map/ppermute | solution.py:23
  65.8 12.6 %collective-permute-done.3 = f32[2,2,2,32,512]{4,3,2,1,0:T(8,128)} collective-permute-done((f32[2,2,2,32,512]{4,3,2,1,0:T(8,128)S(1)}, f32[2,2,2,32,512]{4,3,2,1,0:T(8,128)}, u32[]{:S(2)}, u32[]{:S(2)}) %collective-permute-start.3) | collective-permute-done | bytes 524320 | tf_op jit(solution)/shard_map/ppermute | solution.py:23
  78.4 1.3 %bitcast_add_fusion.1 = f32[2,2,2,32,512]{4,3,2,1,0:T(8,128)S(1)} fusion(f32[2,2,2,32,512]{4,3,2,1,0:T(8,128)} %collective-permute-done.3, f32[2,2,2,2,32,512]{5,4,2,1,0,3:T(8,128)} %copy-done.1, s32[]{:T(128)S(6)} %select_n.52), kind=kLoop, calls=%fused_computation.13 | loop fusion | flops 131072 | bytes 1572868 | tf_op jit(solution)/shard_map/add | solution.py:55
  79.7 0.1 collective-permute-start.4
  79.8 0.4 collective-permute-start.7
  80.2 7.2 %collective-permute-done.4 = f32[2,2,32,512]{3,2,1,0:T(8,128)} collective-permute-done((f32[2,2,32,512]{3,2,1,0:T(8,128)S(1)}, f32[2,2,32,512]{3,2,1,0:T(8,128)}, u32[]{:S(2)}, u32[]{:S(2)}) %collective-permute-start.4) | collective-permute-done | bytes 262176 | tf_op jit(solution)/shard_map/ppermute | solution.py:23
  87.4 1.0 bitcast_add_fusion.2
  88.4 0.1 collective-permute-start.5
  88.5 20.3 %collective-permute-done.5 = f32[2,32,512]{2,1,0:T(8,128)S(1)} collective-permute-done((f32[2,32,512]{2,1,0:T(8,128)S(1)}, f32[2,32,512]{2,1,0:T(8,128)S(1)}, u32[]{:S(2)}, u32[]{:S(2)}) %collective-permute-start.5) | collective-permute-done | bytes 131104 | tf_op jit(solution)/shard_map/ppermute | solution.py:23
  108.9 0.6 collective-permute-start.6
  109.5 5.0 %collective-permute-done.6 = f32[32,512]{1,0:T(8,128)S(1)} collective-permute-done((f32[32,512]{1,0:T(8,128)S(1)}, f32[32,512]{1,0:T(8,128)S(1)}, u32[]{:S(2)}, u32[]{:S(2)}) %collective-permute-start.6) | collective-permute-done | bytes 65568 | tf_op jit(solution)/shard_map/ppermute | solution.py:23
  114.5 0.6 fusion.46
  115.1 0.0 collective-permute-done.7
  115.1 3.2 %fusion.2 = bf16[1,1024,512]{2,1,0:T(8,128)(2,1)} fusion(f32[1024,512]{1,0:T(8,128)} %multiply_subtract_fusion, bf16[1024,512]{1,0:T(8,128)(2,1)} %collective-permute-done.7, f32[]{:T(128)S(6)} %div.29), kind=kLoop, calls=%fused_computation.10 | loop fusion | flops 2097152 | bytes 4194308 | tf_op jit(solution)/shard_map/broadcast_in_dim | solution.py:83
  (5 shorter events, 0.1 us)
Async XLA Ops:
  0.6 6.6 %copy-start = (bf16[768,1024]{1,0:T(8,128)(2,1)S(1)}, bf16[768,1024]{1,0:T(8,128)(2,1)}, u32[]{:S(2)}) copy-start(bf16[768,1024]{1,0:T(8,128)(2,1)} %param.6) | copy-start | bytes 4718596
  0.6 18.2 %collective-permute-start = (bf16[1024,512]{1,0:T(8,128)(2,1)}, bf16[1024,512]{1,0:T(8,128)(2,1)S(1)}, u32[]{:S(2)}, u32[]{:S(2)}) collective-permute-start(bf16[1024,512]{1,0:T(8,128)(2,1)} %bitcast.45), channel_id=1, source_target_pairs={{0,2},{2,4},{4,6},{6,8},{8,10},{10,12},{12,14},{14,16},{16,18},{18... | collective-permute-start | bytes 3145736 | tf_op jit(solution)/shard_map/ppermute | solution.py:18
  11.9 16.9 %copy-start.2 = (bf16[768,512]{1,0:T(8,128)(2,1)S(1)}, bf16[768,512]{1,0:T(8,128)(2,1)}, u32[]{:S(2)}) copy-start(bf16[768,512]{1,0:T(8,128)(2,1)} %param.7) | copy-start | bytes 2359300
  21.8 25.1 %collective-permute-start.1 = (bf16[1024,512]{1,0:T(8,128)(2,1)}, bf16[1024,512]{1,0:T(8,128)(2,1)}, u32[]{:S(2)}, u32[]{:S(2)}) collective-permute-start(bf16[1024,512]{1,0:T(8,128)(2,1)} %fusion), channel_id=1, source_target_pairs={{0,4},{2,6},{4,8},{6,10},{8,12},{10,14},{12,16},{14,18},{16,20},{1... | collective-permute-start | bytes 3145736 | tf_op jit(solution)/shard_map/ppermute | solution.py:18
  58.5 3.0 %collective-permute-start.2 = (f32[2,2,2,2,32,512]{5,4,2,1,0,3:T(8,128)}, f32[2,2,2,2,32,512]{5,4,2,1,0,3:T(8,128)}, u32[]{:S(2)}, u32[]{:S(2)}) collective-permute-start(f32[2,2,2,2,32,512]{5,4,2,1,0,3:T(8,128)} %bitcast.43), channel_id=1, source_target_pairs={{0,2},{2,0},{4,6},{6,4},{8,10},{10,8},{12,14},{14,12},{16,18},{18,... | collective-permute-start | bytes 3145736 | tf_op jit(solution)/shard_map/ppermute | solution.py:23
  63.3 1.0 copy-start.1
  64.3 14.1 %collective-permute-start.3 = (f32[2,2,2,32,512]{4,3,2,1,0:T(8,128)S(1)}, f32[2,2,2,32,512]{4,3,2,1,0:T(8,128)}, u32[]{:S(2)}, u32[]{:S(2)}) collective-permute-start(f32[2,2,2,32,512]{4,3,2,1,0:T(8,128)S(1)} %dynamic-slice_bitcast_fusion), channel_id=1, source_target_pairs={{0,1},{1,0},{2,3},{3,2},{4,5},{5,4},{6,7},{7,6},{8,9},{9,8},{10,11... | collective-permute-start | bytes 1572872 | tf_op jit(solution)/shard_map/ppermute | solution.py:23
  79.7 7.7 %collective-permute-start.4 = (f32[2,2,32,512]{3,2,1,0:T(8,128)S(1)}, f32[2,2,32,512]{3,2,1,0:T(8,128)}, u32[]{:S(2)}, u32[]{:S(2)}) collective-permute-start(f32[2,2,32,512]{3,2,1,0:T(8,128)S(1)} %dynamic-slice_bitcast_fusion.1), channel_id=1, source_target_pairs={{0,4},{2,6},{4,0},{6,2},{8,12},{10,14},{12,8},{14,10},{16,20},{18,... | collective-permute-start | bytes 786440 | tf_op jit(solution)/shard_map/ppermute | solution.py:23
  79.8 35.3 %collective-permute-start.7 = (bf16[1024,512]{1,0:T(8,128)(2,1)S(1)}, bf16[1024,512]{1,0:T(8,128)(2,1)}, u32[]{:S(2)}, u32[]{:S(2)}) collective-permute-start(bf16[1024,512]{1,0:T(8,128)(2,1)S(1)} %fusion.1), channel_id=1, source_target_pairs={{0,8},{2,10},{4,12},{6,14},{8,16},{10,18},{12,20},{14,22},{16,24},... | collective-permute-start | bytes 3145736 | tf_op jit(solution)/shard_map/ppermute | solution.py:18
  88.4 20.4 %collective-permute-start.5 = (f32[2,32,512]{2,1,0:T(8,128)S(1)}, f32[2,32,512]{2,1,0:T(8,128)S(1)}, u32[]{:S(2)}, u32[]{:S(2)}) collective-permute-start(f32[2,32,512]{2,1,0:T(8,128)S(1)} %dynamic-slice_bitcast_fusion.2), channel_id=1, source_target_pairs={{0,8},{2,10},{4,12},{6,14},{8,0},{10,2},{12,4},{14,6},{16,24},{18,... | collective-permute-start | bytes 393224 | tf_op jit(solution)/shard_map/ppermute | solution.py:23
  108.9 5.6 %collective-permute-start.6 = (f32[32,512]{1,0:T(8,128)S(1)}, f32[32,512]{1,0:T(8,128)S(1)}, u32[]{:S(2)}, u32[]{:S(2)}) collective-permute-start(f32[32,512]{1,0:T(8,128)S(1)} %dynamic-slice_bitcast_fusion.3), channel_id=1, source_target_pairs={{0,16},{2,18},{4,20},{6,22},{8,24},{10,26},{12,28},{14,30},{16,0},... | collective-permute-start | bytes 196616 | tf_op jit(solution)/shard_map/ppermute | solution.py:23

commit v2 on v1

v2 whole, which is shorter than its diff:
```python
import functools
import math

import jax
import jax.numpy as jnp
from jax import lax
from jax.experimental import pallas as pl
from jax.experimental.pallas import tpu as pltpu
from jax.sharding import PartitionSpec as P


STEPS = 3
HALVES = 2
KERNEL_VMEM = 20 << 20

learning_rate = 0.3
momentum_decay = 0.9


def shifted(value, axis, steps):
    count = lax.axis_size(axis)
    pairs = [(source, (source + steps) % count) for source in range(count)]
    return lax.ppermute(value, axis, pairs)


def flipped(value, axis, bit):
    count = lax.axis_size(axis)
    return lax.ppermute(value, axis, [(source, source ^ bit) for source in range(count)])


def shares(plan_ref, step):
    own = plan_ref[step, 0].astype(jnp.float32)
    peer = plan_ref[step, 1].astype(jnp.float32)
    own, peer = jnp.full((1, 1), own), jnp.full((1, 1), peer)
    return own / (own + peer), peer / (own + peer)


def gradient_of(batch_in, batch_out, rounded):
    fan_scale = 1.0 / math.sqrt(batch_in.shape[1])
    preact = jnp.dot(batch_in, rounded, preferred_element_type=jnp.float32) * fan_scale
    normal_cdf = 0.5 * (1.0 + lax.erf(preact * (1.0 / math.sqrt(2.0))))
    normal_pdf = jnp.exp(-0.5 * preact * preact) * (1.0 / math.sqrt(2.0 * math.pi))
    residual = preact * normal_cdf - batch_out.astype(jnp.float32)
    derivative = normal_cdf + preact * normal_pdf
    delta = (residual * derivative).astype(jnp.bfloat16)
    product = lax.dot_general(
        batch_in, delta, (((0,), (0,)), ((), ())), preferred_element_type=jnp.float32
    )
    return product * fan_scale


def shard_of(order, x, t, step, columns):
    batch = x.shape[0] // STEPS
    rows = pl.ds(pl.multiple_of(order[0, step] * batch, batch), batch)
    return x[rows, :], t[rows, columns]


def first_kernel(order, plan, x, t, w, base, velocity):
    own, _ = shares(plan, 0)
    width = w.shape[1] // HALVES
    for half in range(HALVES):
        columns = slice(half * width, (half + 1) * width)
        gradient = gradient_of(*shard_of(order, x, t, 0, columns), w[:, columns])
        velocity[:, columns] = gradient
        base[:, columns] = own * w[:, columns].astype(jnp.float32) - learning_rate * gradient


def middle_kernel(columns, order, plan, x, t, rounded, base_in, arrived, velocity_in, base, velocity):
    _, peer = shares(plan, 0)
    own, _ = shares(plan, 1)
    v = momentum_decay * velocity_in[:, columns] + gradient_of(*shard_of(order, x, t, 1, columns), rounded[...])
    velocity[...] = v
    master = base_in[:, columns] + peer * arrived[:, columns].astype(jnp.float32)
    base[...] = own * master - learning_rate * v


def last_kernel(columns, split, order, plan, x, t, rounded, base_in, arrived, velocity_in, base, *outs):
    _, peer = shares(plan, STEPS - 2)
    own, last_peer = shares(plan, STEPS - 1)
    r = rounded[...]
    v = momentum_decay * velocity_in[...] + gradient_of(*shard_of(order, x, t, STEPS - 1, columns), r)
    master = base_in[...] + peer * arrived[...].astype(jnp.float32)
    b = own * master - learning_rate * v
    base[...] = b
    part = b + last_peer * r.astype(jnp.float32)
    if not split:
        outs[0][...] = part
        return
    keep, give, held = outs
    held[...] = part.reshape(held.shape)
    mine = lax.axis_index("gossip") & 1
    keep[...] = held[:, pl.ds(mine, 1)].reshape(keep.shape)
    give[...] = held[:, pl.ds(1 - mine, 1)].reshape(give.shape)


def round_kernel(step, plan, base, arrived, *rounded):
    _, peer = shares(plan, step)
    width = base.shape[1] // len(rounded)
    for i, r in enumerate(rounded):
        columns = slice(i * width, (i + 1) * width)
        r[...] = (base[:, columns] + peer * arrived[:, columns].astype(jnp.float32)).astype(jnp.bfloat16)


def finish_kernel(plan, *refs):
    _, peer = shares(plan, STEPS - 1)
    out = refs[-1]
    width = out.shape[1] // HALVES
    for i in range(HALVES):
        base, arrived = refs[2 * i], refs[2 * i + 1]
        out[:, i * width:(i + 1) * width] = (base[...] + peer * arrived[...].astype(jnp.float32)).astype(jnp.bfloat16)


def leg_kernel(axis, bit, *refs):
    keep, give = refs[-2:]
    pairs = refs[:-2]
    width = 2 * keep.shape[-1] // len(pairs)
    mine = (lax.axis_index(axis) >> bit) & 1
    for i in range(len(pairs) // 2):
        kept, arrived = pairs[2 * i], pairs[2 * i + 1]
        columns = slice(i * width, (i + 1) * width)
        for out, side in ((keep, mine), (give, 1 - mine)):
            at = pl.ds(side, 1)
            total = kept[:, at] + arrived[:, at].astype(jnp.float32)
            out[:, :, columns] = total.reshape(out.shape[:-1] + (width,)).astype(out.dtype)


def spread_kernel(kept, arrived, keep, *gives):
    mine = lax.axis_index("gossip") >> 2
    for other, out in enumerate((keep,) + gives):
        at = pl.ds(mine ^ other, 1)
        total = kept[at] + arrived[at].astype(jnp.float32)
        out[...] = total.reshape(out.shape).astype(out.dtype)


def mean_kernel(replicas, keep, *refs):
    total = keep[...]
    for arrived in refs[:-1]:
        total = total + arrived[...].astype(jnp.float32)
    refs[-1][...] = total / replicas


def call(kernel, ins, outs, scratch=()):
    in_vmem, in_smem = pl.BlockSpec(memory_space=pltpu.VMEM), pl.BlockSpec(memory_space=pltpu.SMEM)
    return pl.pallas_call(
        kernel,
        in_specs=[in_smem if array.dtype == jnp.int32 else in_vmem for array in ins],
        out_specs=[in_vmem] * len(outs),
        out_shape=[jax.ShapeDtypeStruct(shape, dtype) for shape, dtype in outs],
        scratch_shapes=list(scratch),
        compiler_params=pltpu.CompilerParams(vmem_limit_bytes=KERNEL_VMEM),
    )(*ins)


def scattered_sum(value):
    n_gossip, n_group = lax.axis_size("gossip"), lax.axis_size("group")
    gossip_bits, group_bits = n_gossip.bit_length() - 1, n_group.bit_length() - 1
    rows = value.shape[0]
    value = value.reshape((2,) * (gossip_bits + group_bits) + (rows // (n_gossip * n_group), value.shape[1]))
    left = [("gossip", bit) for bit in reversed(range(gossip_bits))]
    left += [("group", bit) for bit in reversed(range(group_bits))]
    order = [("gossip", 0)] + [("group", bit) for bit in range(group_bits)]
    order += [("gossip", bit) for bit in range(1, gossip_bits)]
    for axis, bit in order:
        place = left.index((axis, bit))
        mine = (lax.axis_index(axis) >> bit) & 1
        keep = lax.dynamic_index_in_dim(value, mine, place, keepdims=False)
        give = lax.dynamic_index_in_dim(value, 1 - mine, place, keepdims=False)
        value = keep + flipped(give, axis, 1 << bit)
        left.pop(place)
    return value


def leg(pairs, axis, bit):
    lead, _, rows, width = pairs[0][0].shape
    shape = (lead, rows, width * len(pairs))
    ins = [array for pair in pairs for array in pair]
    return call(functools.partial(leg_kernel, axis, bit), ins, [(shape, jnp.float32), (shape, jnp.bfloat16)])


def steps(weights, inputs, targets, plan, order):
    n_gossip, n_group = lax.axis_size("gossip"), lax.axis_size("group")
    replicas = n_gossip * n_group
    weights = weights[0]
    din, dout = weights.shape
    width = dout // HALVES
    own_rows = din // replicas
    split = own_rows % 16 == 0 and n_group == 2 and n_gossip % 4 == 0
    columns = [slice(half * width, (half + 1) * width) for half in range(HALVES)]
    half_f32, half_bf16 = ((din, width), jnp.float32), ((din, width), jnp.bfloat16)

    arrived0 = shifted(weights, "gossip", 1)
    base0, velocity0 = call(
        first_kernel, [order, plan, inputs, targets, weights], [((din, dout), jnp.float32)] * 2
    )
    rounded1 = call(functools.partial(round_kernel, 0), [plan, base0, arrived0], [half_bf16] * HALVES)
    arrived1, middles = [], []
    for half in range(HALVES):
        arrived1.append(shifted(rounded1[half], "gossip", 2))
    for half in range(HALVES):
        middles.append(
            call(
                functools.partial(middle_kernel, columns[half]),
                [order, plan, inputs, targets, rounded1[half], base0, arrived0, velocity0],
                [half_f32] * 2,
            )
        )
    parts, last = [], []
    for half in range(HALVES):
        base1, velocity1 = middles[half]
        (rounded2,) = call(functools.partial(round_kernel, 1), [plan, base1, arrived1[half]], [half_bf16])
        arrived2 = shifted(rounded2, "gossip", 4)
        outs, scratch = [half_f32] * 2, ()
        if split:
            pair = (n_gossip // 2, n_group * own_rows, width)
            outs = [half_f32, (pair, jnp.float32), (pair, jnp.float32)]
            scratch = (pltpu.VMEM((pair[0], 2) + pair[1:], jnp.float32),)
        base2, *part = call(
            functools.partial(last_kernel, columns[half], split),
            [order, plan, inputs, targets, rounded2, base1, arrived1[half], velocity1],
            outs,
            scratch,
        )
        last += [base2, arrived2]
        if not split:
            parts.append(part[0])
            continue
        keep, give = part
        got = flipped(give, "gossip", 1)
        view = (n_gossip // 2, n_group, own_rows, width)
        keep, give = leg([(keep.reshape(view), got.reshape(view))], "group", 0)
        got = flipped(give, "group", 1)
        parts.append((keep, got))
    if split:
        view = (n_gossip // 4, 2, own_rows, width)
        keep, give = leg([(keep.reshape(view), got.reshape(view)) for keep, got in parts], "gossip", 1)
        got = flipped(give, "gossip", 2)
        shape = (own_rows, dout)
        others = [(shape, jnp.bfloat16)] * (n_gossip // 4 - 1)
        keep, *gives = call(spread_kernel, [keep, got], [(shape, jnp.float32)] + others)
        gots = []
        for other, give in enumerate(gives, 1):
            gots.append(flipped(give, "gossip", 4 * other))
        (mean_weights,) = call(functools.partial(mean_kernel, replicas), [keep] + gots, [(shape, jnp.float32)])
    else:
        mean_weights = scattered_sum(jnp.concatenate(parts, axis=1)) / replicas
    (replica_weights,) = call(finish_kernel, [plan] + last, [((din, dout), jnp.bfloat16)])
    return (replica_weights[None], mean_weights)


def solution(mesh):
    return jax.shard_map(
        steps,
        mesh=mesh,
        in_specs=(
            P(("gossip", "group"), None, None),
            P(("gossip", "group"), None),
            P(("gossip", "group"), None),
            P(),
            P(("gossip", "group"), None),
        ),
        out_specs=(P(("gossip", "group"), None, None), P(("gossip", "group"), None)),
        check_vma=False,
    )
```

time: 119 us -> 77.8 us (0.65)
  waiting for transfers between devices: 67.1 us -> 46.9 us
  matrix products: 16 us -> 0 us
  other arithmetic: 15.8 us -> 0 us
  Pallas kernels: 0 us -> 13.4 us
  between operations: 10.5 us -> 0.75 us
  starting transfers between devices: 3.25 us -> 11.2 us
    ppermute x5 -> x8, waiting for transfers between devices: 48.1 us -> 10.3 us  [flipped(): lax.ppermute(value, axis, [(source, source ^ bit) for source in range(cou...]
    ppermute x3 -> x5, waiting for transfers between devices: 19 us -> 36.6 us  [shifted(): return lax.ppermute(value, axis, pairs)]
    dot_general x3 -> x0, matrix products: 16 us -> none  [local_gradient(): lax.dot_general(batch_in, delta, (((0,), (0,)), ((), ())), preferred_elem...]
    pallas_call x0 -> x14, Pallas kernels: none -> 13.4 us  [call(): pl.pallas_call(kernel, in_specs=[in_smem if array.dtype == jnp.int32 else...]
    add x5 -> x0, other arithmetic: 5.98 us -> none  [the longest x4 4.06 us: scattered_sum(): value = keep + arrived]
    convert_element_type x3 -> x0, other arithmetic: 5.98 us -> none  [the longest x2 5.12 us: steps(): rounded = master.astype(jnp.bfloat16)]
    ppermute x5 -> x8, starting transfers between devices: 2.33 us -> 7.54 us  [flipped(): lax.ppermute(value, axis, [(source, source ^ bit) for source in range(cou...]
    unnamed x6 -> x13, local copies, waits for them, and re-layouts: 0.98 us -> 5.2 us
  transfers between devices with their start and end apart: 8 -> 13, of which waited for: 7 -> 7; matrix products, arithmetic and copies ran while one was open for 13% -> 1% of each run, Pallas kernels for 0% -> 15%
where the time goes in v2:
time: 77.8 us; the launch traced here: 77.5 us
  waiting for transfers between devices  46.9 us (60%)
  Pallas kernels  13.4 us (17%)
  starting transfers between devices  11.2 us (14%)
  local copies, waits for them, and re-layouts  5.2 us (7%)
    ppermute x5, waiting for transfers between devices, shifted(): return lax.ppermute(value, axis, pairs)  36.6 us
    pallas_call x14, Pallas kernels, call(): pl.pallas_call(kernel, in_specs=[in_smem if array.dtype == jnp.int32 else...  13.4 us
    ppermute x8, waiting for transfers between devices, flipped(): lax.ppermute(value, axis, [(source, source ^ bit) for source in range(cou...  10.3 us
    ppermute x8, starting transfers between devices, flipped(): lax.ppermute(value, axis, [(source, source ^ bit) for source in range(cou...  7.54 us
    unnamed x13, local copies, waits for them, and re-layouts  5.2 us
    ppermute x5, starting transfers between devices, shifted(): return lax.ppermute(value, axis, pairs)  3.67 us
  transfers between devices with their start and end apart: 13, of which 7 were waited for; matrix products, arithmetic and copies ran while one was open for 1% of the time, Pallas kernels for 15%

profile of v2, /device:TPU:0, one launch (start us, length us, event | category | flops | bytes accessed | tf_op | source)
XLA Modules:
  0.0 77.5 jit_solution(15398617018915315733)
XLA Ops:
  0.6 0.5 collective-permute-start
  1.2 0.8 copy.15.plan
  1.9 1.4 %copy-done = bf16[768,1024]{1,0:T(8,128)(2,1)S(1)} copy-done((bf16[768,1024]{1,0:T(8,128)(2,1)S(1)}, bf16[768,1024]{1,0:T(8,128)(2,1)}, u32[]{:S(2)}) %copy-start) | copy-done | bytes 1572888
  3.3 1.1 %copy-done.2 = bf16[768,512]{1,0:T(8,128)(2,1)S(1)} copy-done((bf16[768,512]{1,0:T(8,128)(2,1)S(1)}, bf16[768,512]{1,0:T(8,128)(2,1)}, u32[]{:S(2)}) %copy-start.2) | copy-done | bytes 786456
  4.5 1.2 %copy-done.4 = bf16[1,1024,512]{2,1,0:T(8,128)(2,1)S(1)} copy-done((bf16[1,1024,512]{2,1,0:T(8,128)(2,1)S(1)}, bf16[1,1024,512]{2,1,0:T(8,128)(2,1)}, u32[]{:S(2)}) %copy-start.4) | copy-done | bytes 1048600
  5.7 0.7 copy-done.5
  6.4 1.9 %shard_map.68 = (f32[1024,512]{1,0:T(8,128)S(1)}, f32[1024,512]{1,0:T(8,128)S(1)}) custom-call(s32[1,3]{1,0:T(1,128)S(1)} %copy-done.5, s32[3,2]{1,0:T(4,128)S(1)} %copy.15.plan, bf16[768,1024]{1,0:T(8,128)(2,1)S(1)} %copy-done, bf16[768,512]{1,0:T(8,128)(2,1)S(1)} %copy-done.2, bf16[1024,512]{1,0:T(8,128)(2,1)S(1)} %bitcast.11), custom_call_target="tpu_custom_call" | custom-call | tf_op jit(solution)/shard_map/pallas_call | solution.py:144
  8.2 0.0 copy-start.1
  8.2 0.0 copy-start.3
  8.3 10.6 %collective-permute-done.arrived = bf16[1024,512]{1,0:T(8,128)(2,1)S(1)} collective-permute-done((bf16[1024,512]{1,0:T(8,128)(2,1)}, bf16[1024,512]{1,0:T(8,128)(2,1)S(1)}, u32[]{:S(2)}, u32[]{:S(2)}) %collective-permute-start) | collective-permute-done | bytes 1048608 | tf_op jit(solution)/shard_map/ppermute | solution.py:23
  18.9 0.8 %shard_map.69 = (bf16[1024,256]{1,0:T(8,128)(2,1)S(1)}, bf16[1024,256]{1,0:T(8,128)(2,1)S(1)}) custom-call(s32[3,2]{1,0:T(4,128)S(1)} %copy.15.plan, f32[1024,512]{1,0:T(8,128)S(1)} %get-tuple-element.26.base.base_in, bf16[1024,512]{1,0:T(8,128)(2,1)S(1)} %collective-permute-done.arrived), custom_call_target="tpu_custom_call" | custom-call | tf_op jit(solution)/shard_map/pallas_call | solution.py:144
  19.7 0.1 collective-permute-start.3
  19.8 1.7 %collective-permute-start.1 = (bf16[1024,256]{1,0:T(8,128)(2,1)S(1)}, bf16[1024,256]{1,0:T(8,128)(2,1)S(1)}, u32[]{:S(2)}, u32[]{:S(2)}) collective-permute-start(bf16[1024,256]{1,0:T(8,128)(2,1)S(1)} %get-tuple-element.27.rounded), channel_id=1, source_target_pairs={{0,4},{2,6},{4,8},{6,10},{8,12},{10,14},{12,16},{14,18},{16,20},{1... | collective-permute-start | bytes 1572872 | tf_op jit(solution)/shard_map/ppermute | solution.py:23
  21.4 0.0 copy-done.1
  21.4 0.0 copy-done.3
  21.4 1.5 %shard_map.70 = (f32[1024,256]{1,0:T(8,128)S(1)}, f32[1024,256]{1,0:T(8,128)S(1)}) custom-call(s32[1,3]{1,0:T(1,128)S(1)} %copy-done.5, s32[3,2]{1,0:T(4,128)S(1)} %copy.15.plan, bf16[768,1024]{1,0:T(8,128)(2,1)S(1)} %copy-done.1, bf16[768,512]{1,0:T(8,128)(2,1)S(1)} %copy-done.3, bf16[1024,256]{1,0:T(8,128)(2,1)S(1)} %get-tuple-element.27.rounded, ...), custom_call_target="tpu_custom_call" | custom-call | tf_op jit(solution)/shard_map/pallas_call | solution.py:144
  23.0 1.5 %shard_map.73 = (f32[1024,256]{1,0:T(8,128)S(1)}, f32[1024,256]{1,0:T(8,128)S(1)}) custom-call(s32[1,3]{1,0:T(1,128)S(1)} %copy-done.5, s32[3,2]{1,0:T(4,128)S(1)} %copy.15.plan, bf16[768,1024]{1,0:T(8,128)(2,1)S(1)} %copy-done.1, bf16[768,512]{1,0:T(8,128)(2,1)S(1)} %copy-done.3, bf16[1024,256]{1,0:T(8,128)(2,1)S(1)} %get-tuple-element.32.rounded, ...), custom_call_target="tpu_custom_call" | custom-call | tf_op jit(solution)/shard_map/pallas_call | solution.py:144
  24.5 12.7 %collective-permute-done.3.arrived = bf16[1024,256]{1,0:T(8,128)(2,1)S(1)} collective-permute-done((bf16[1024,256]{1,0:T(8,128)(2,1)S(1)}, bf16[1024,256]{1,0:T(8,128)(2,1)S(1)}, u32[]{:S(2)}, u32[]{:S(2)}) %collective-permute-start.3) | collective-permute-done | bytes 524320 | tf_op jit(solution)/shard_map/ppermute | solution.py:23
  37.2 0.7 shard_map.74.rounded
  37.9 1.8 %shard_map.75 = (f32[1024,256]{1,0:T(8,128)S(1)}, f32[8,64,256]{2,1,0:T(8,128)S(1)}, f32[8,64,256]{2,1,0:T(8,128)S(1)}) custom-call(s32[1,3]{1,0:T(1,128)S(1)} %copy-done.5, s32[3,2]{1,0:T(4,128)S(1)} %copy.15.plan, bf16[768,1024]{1,0:T(8,128)(2,1)S(1)} %copy-done.1, bf16[768,512]{1,0:T(8,128)(2,1)S(1)} %copy-done.3, ...), custom_call_target="tpu_custom_call" | custom-call | tf_op jit(solution)/shard_map/pallas_call | solution.py:144
  39.8 0.1 collective-permute-start.7
  39.8 4.7 %collective-permute-done.1.arrived = bf16[1024,256]{1,0:T(8,128)(2,1)S(1)} collective-permute-done((bf16[1024,256]{1,0:T(8,128)(2,1)S(1)}, bf16[1024,256]{1,0:T(8,128)(2,1)S(1)}, u32[]{:S(2)}, u32[]{:S(2)}) %collective-permute-start.1) | collective-permute-done | bytes 524320 | tf_op jit(solution)/shard_map/ppermute | solution.py:23
  44.5 0.7 shard_map.71.rounded
  45.2 1.8 %shard_map.72 = (f32[1024,256]{1,0:T(8,128)S(1)}, f32[8,64,256]{2,1,0:T(8,128)S(1)}, f32[8,64,256]{2,1,0:T(8,128)S(1)}) custom-call(s32[1,3]{1,0:T(1,128)S(1)} %copy-done.5, s32[3,2]{1,0:T(4,128)S(1)} %copy.15.plan, bf16[768,1024]{1,0:T(8,128)(2,1)S(1)} %copy-done.1, bf16[768,512]{1,0:T(8,128)(2,1)S(1)} %copy-done.3, ...), custom_call_target="tpu_custom_call" | custom-call | tf_op jit(solution)/shard_map/pallas_call | solution.py:144
  47.0 0.1 collective-permute-start.5
  47.1 0.1 collective-permute-start.4
  47.2 1.3 %collective-permute-start.2 = (bf16[1024,256]{1,0:T(8,128)(2,1)S(1)}, bf16[1024,256]{1,0:T(8,128)(2,1)S(1)}, u32[]{:S(2)}, u32[]{:S(2)}) collective-permute-start(bf16[1024,256]{1,0:T(8,128)(2,1)S(1)} %shard_map.71.rounded), channel_id=1, source_target_pairs={{0,8},{2,10},{4,12},{6,14},{8,16},{10,18},{12,20},{14,22},{16,24},... | collective-permute-start | bytes 1572872 | tf_op jit(solution)/shard_map/ppermute | solution.py:23
  48.5 0.0 collective-permute-done.7
  48.5 0.1 shard_map.78
  48.6 1.6 %collective-permute-start.8 = (bf16[8,32,256]{2,1,0:T(8,128)(2,1)S(1)}, bf16[8,32,256]{2,1,0:T(8,128)(2,1)S(1)}, u32[]{:S(2)}, u32[]{:S(2)}) collective-permute-start(bf16[8,32,256]{2,1,0:T(8,128)(2,1)S(1)} %get-tuple-element.43), channel_id=1, source_target_pairs={{0,1},{1,0},{2,3},{3,2},{4,5},{5,4},{6,7},{7,6},{8,9},{9,8},{10,11... | collective-permute-start | bytes 393224 | tf_op jit(solution)/shard_map/ppermute | solution.py:28
  50.1 0.0 collective-permute-done.5
  50.1 0.1 shard_map.77
  50.2 0.6 collective-permute-start.6
  50.8 4.2 %collective-permute-done.8 = bf16[8,32,256]{2,1,0:T(8,128)(2,1)S(1)} collective-permute-done((bf16[8,32,256]{2,1,0:T(8,128)(2,1)S(1)}, bf16[8,32,256]{2,1,0:T(8,128)(2,1)S(1)}, u32[]{:S(2)}, u32[]{:S(2)}) %collective-permute-start.8) | collective-permute-done | bytes 131104 | tf_op jit(solution)/shard_map/ppermute | solution.py:28
  55.0 1.7 %collective-permute-done.6 = bf16[8,32,256]{2,1,0:T(8,128)(2,1)S(1)} collective-permute-done((bf16[8,32,256]{2,1,0:T(8,128)(2,1)S(1)}, bf16[8,32,256]{2,1,0:T(8,128)(2,1)S(1)}, u32[]{:S(2)}, u32[]{:S(2)}) %collective-permute-start.6) | collective-permute-done | bytes 131104 | tf_op jit(solution)/shard_map/ppermute | solution.py:28
  56.7 0.1 shard_map.79
  56.8 0.7 collective-permute-start.9
  57.5 4.3 %collective-permute-done.9.arrived = bf16[4,32,512]{2,1,0:T(8,128)(2,1)S(1)} collective-permute-done((bf16[4,32,512]{2,1,0:T(8,128)(2,1)S(1)}, bf16[4,32,512]{2,1,0:T(8,128)(2,1)S(1)}, u32[]{:S(2)}, u32[]{:S(2)}) %collective-permute-start.9) | collective-permute-done | bytes 131104 | tf_op jit(solution)/shard_map/ppermute | solution.py:28
  61.9 1.6 %collective-permute-start.10 = (bf16[32,512]{1,0:T(8,128)(2,1)S(1)}, bf16[32,512]{1,0:T(8,128)(2,1)S(1)}, u32[]{:S(2)}, u32[]{:S(2)}) collective-permute-start(bf16[32,512]{1,0:T(8,128)(2,1)S(1)} %get-tuple-element.47), channel_id=1, source_target_pairs={{0,8},{2,10},{4,12},{6,14},{8,0},{10,2},{12,4},{14,6},{16,24},{18,... | collective-permute-start | bytes 98312 | tf_op jit(solution)/shard_map/ppermute | solution.py:28
  63.5 1.8 %collective-permute-start.11 = (bf16[32,512]{1,0:T(8,128)(2,1)S(1)}, bf16[32,512]{1,0:T(8,128)(2,1)S(1)}, u32[]{:S(2)}, u32[]{:S(2)}) collective-permute-start(bf16[32,512]{1,0:T(8,128)(2,1)S(1)} %get-tuple-element.48), channel_id=1, source_target_pairs={{0,16},{2,18},{4,20},{6,22},{8,24},{10,26},{12,28},{14,30},{16,0},... | collective-permute-start | bytes 98312 | tf_op jit(solution)/shard_map/ppermute | solution.py:28
  65.3 1.2 %collective-permute-start.12 = (bf16[32,512]{1,0:T(8,128)(2,1)S(1)}, bf16[32,512]{1,0:T(8,128)(2,1)S(1)}, u32[]{:S(2)}, u32[]{:S(2)}) collective-permute-start(bf16[32,512]{1,0:T(8,128)(2,1)S(1)} %get-tuple-element.49), channel_id=1, source_target_pairs={{0,24},{2,26},{4,28},{6,30},{8,16},{10,18},{12,20},{14,22},{16,8},... | collective-permute-start | bytes 98312 | tf_op jit(solution)/shard_map/ppermute | solution.py:28
  66.4 0.0 collective-permute-done.4.refs_3_
  66.4 8.6 %collective-permute-done.2.refs_1_ = bf16[1024,256]{1,0:T(8,128)(2,1)S(1)} collective-permute-done((bf16[1024,256]{1,0:T(8,128)(2,1)S(1)}, bf16[1024,256]{1,0:T(8,128)(2,1)S(1)}, u32[]{:S(2)}, u32[]{:S(2)}) %collective-permute-start.2) | collective-permute-done | bytes 524320 | tf_op jit(solution)/shard_map/ppermute | solution.py:23
  75.1 1.8 %shard_map.76 = bf16[1024,512]{1,0:T(8,128)(2,1)} custom-call(s32[3,2]{1,0:T(4,128)S(1)} %copy.15.plan, f32[1024,256]{1,0:T(8,128)S(1)} %get-tuple-element.31.refs_0_, bf16[1024,256]{1,0:T(8,128)(2,1)S(1)} %collective-permute-done.2.refs_1_, f32[1024,256]{1,0:T(8,128)S(1)} %get-tuple-element.35.refs_2_, bf16[1024,256]{1,0:T(8,128)(2,1)S(1)} %collective-permute-done.4.refs_3_), custom_call_target="tpu_custom_call" | custom-call | tf_op jit(solution)/shard_map/pallas_call | solution.py:144
  76.9 0.0 collective-permute-done.10.refs_0_
  76.9 0.0 collective-permute-done.11.refs_1_
  76.9 0.0 collective-permute-done.12.refs_2_
  76.9 0.7 shard_map.81
  (5 shorter events, 0.0 us)
Async XLA Ops:
  0.6 18.2 %collective-permute-start = (bf16[1024,512]{1,0:T(8,128)(2,1)}, bf16[1024,512]{1,0:T(8,128)(2,1)S(1)}, u32[]{:S(2)}, u32[]{:S(2)}) collective-permute-start(bf16[1024,512]{1,0:T(8,128)(2,1)} %bitcast.10), channel_id=1, source_target_pairs={{0,2},{2,4},{4,6},{6,8},{8,10},{10,12},{12,14},{14,16},{16,18},{18... | collective-permute-start | bytes 3145736 | tf_op jit(solution)/shard_map/ppermute | solution.py:23
  1.9 1.4 %copy-start = (bf16[768,1024]{1,0:T(8,128)(2,1)S(1)}, bf16[768,1024]{1,0:T(8,128)(2,1)}, u32[]{:S(2)}) copy-start(bf16[768,1024]{1,0:T(8,128)(2,1)} %x.9) | copy-start | bytes 4718596
  3.3 1.1 %copy-start.2 = (bf16[768,512]{1,0:T(8,128)(2,1)S(1)}, bf16[768,512]{1,0:T(8,128)(2,1)}, u32[]{:S(2)}) copy-start(bf16[768,512]{1,0:T(8,128)(2,1)} %t.9) | copy-start | bytes 2359300
  4.5 1.2 %copy-start.4 = (bf16[1,1024,512]{2,1,0:T(8,128)(2,1)S(1)}, bf16[1,1024,512]{2,1,0:T(8,128)(2,1)}, u32[]{:S(2)}) copy-start(bf16[1,1024,512]{2,1,0:T(8,128)(2,1)} %param.5) | copy-start | bytes 3145732
  5.7 0.7 copy-start.5
  8.2 13.2 %copy-start.1 = (bf16[768,1024]{1,0:T(8,128)(2,1)S(1)}, bf16[768,1024]{1,0:T(8,128)(2,1)}, u32[]{:S(2)}) copy-start(bf16[768,1024]{1,0:T(8,128)(2,1)} %x.9) | copy-start | bytes 4718596
  8.2 13.2 %copy-start.3 = (bf16[768,512]{1,0:T(8,128)(2,1)S(1)}, bf16[768,512]{1,0:T(8,128)(2,1)}, u32[]{:S(2)}) copy-start(bf16[768,512]{1,0:T(8,128)(2,1)} %t.9) | copy-start | bytes 2359300
  19.7 17.5 %collective-permute-start.3 = (bf16[1024,256]{1,0:T(8,128)(2,1)S(1)}, bf16[1024,256]{1,0:T(8,128)(2,1)S(1)}, u32[]{:S(2)}, u32[]{:S(2)}) collective-permute-start(bf16[1024,256]{1,0:T(8,128)(2,1)S(1)} %get-tuple-element.32.rounded), channel_id=1, source_target_pairs={{0,4},{2,6},{4,8},{6,10},{8,12},{10,14},{12,16},{14,18},{16,20},{1... | collective-permute-start | bytes 1572872 | tf_op jit(solution)/shard_map/ppermute | solution.py:23
  19.8 24.7 %collective-permute-start.1 = (bf16[1024,256]{1,0:T(8,128)(2,1)S(1)}, bf16[1024,256]{1,0:T(8,128)(2,1)S(1)}, u32[]{:S(2)}, u32[]{:S(2)}) collective-permute-start(bf16[1024,256]{1,0:T(8,128)(2,1)S(1)} %get-tuple-element.27.rounded), channel_id=1, source_target_pairs={{0,4},{2,6},{4,8},{6,10},{8,12},{10,14},{12,16},{14,18},{16,20},{1... | collective-permute-start | bytes 1572872 | tf_op jit(solution)/shard_map/ppermute | solution.py:23
  39.8 8.8 %collective-permute-start.7 = (f32[8,64,256]{2,1,0:T(8,128)S(1)}, f32[8,64,256]{2,1,0:T(8,128)S(1)}, u32[]{:S(2)}, u32[]{:S(2)}) collective-permute-start(f32[8,64,256]{2,1,0:T(8,128)S(1)} %get-tuple-element.41), channel_id=1, source_target_pairs={{0,2},{2,0},{4,6},{6,4},{8,10},{10,8},{12,14},{14,12},{16,18},{18,... | collective-permute-start | bytes 1572872 | tf_op jit(solution)/shard_map/ppermute | solution.py:28
  47.0 3.1 %collective-permute-start.5 = (f32[8,64,256]{2,1,0:T(8,128)S(1)}, f32[8,64,256]{2,1,0:T(8,128)S(1)}, u32[]{:S(2)}, u32[]{:S(2)}) collective-permute-start(f32[8,64,256]{2,1,0:T(8,128)S(1)} %get-tuple-element.37), channel_id=1, source_target_pairs={{0,2},{2,0},{4,6},{6,4},{8,10},{10,8},{12,14},{14,12},{16,18},{18,... | collective-permute-start | bytes 1572872 | tf_op jit(solution)/shard_map/ppermute | solution.py:28
  47.1 19.3 %collective-permute-start.4 = (bf16[1024,256]{1,0:T(8,128)(2,1)S(1)}, bf16[1024,256]{1,0:T(8,128)(2,1)S(1)}, u32[]{:S(2)}, u32[]{:S(2)}) collective-permute-start(bf16[1024,256]{1,0:T(8,128)(2,1)S(1)} %shard_map.74.rounded), channel_id=1, source_target_pairs={{0,8},{2,10},{4,12},{6,14},{8,16},{10,18},{12,20},{14,22},{16,24},... | collective-permute-start | bytes 1572872 | tf_op jit(solution)/shard_map/ppermute | solution.py:23
  47.2 27.9 %collective-permute-start.2 = (bf16[1024,256]{1,0:T(8,128)(2,1)S(1)}, bf16[1024,256]{1,0:T(8,128)(2,1)S(1)}, u32[]{:S(2)}, u32[]{:S(2)}) collective-permute-start(bf16[1024,256]{1,0:T(8,128)(2,1)S(1)} %shard_map.71.rounded), channel_id=1, source_target_pairs={{0,8},{2,10},{4,12},{6,14},{8,16},{10,18},{12,20},{14,22},{16,24},... | collective-permute-start | bytes 1572872 | tf_op jit(solution)/shard_map/ppermute | solution.py:23
  48.6 6.4 %collective-permute-start.8 = (bf16[8,32,256]{2,1,0:T(8,128)(2,1)S(1)}, bf16[8,32,256]{2,1,0:T(8,128)(2,1)S(1)}, u32[]{:S(2)}, u32[]{:S(2)}) collective-permute-start(bf16[8,32,256]{2,1,0:T(8,128)(2,1)S(1)} %get-tuple-element.43), channel_id=1, source_target_pairs={{0,1},{1,0},{2,3},{3,2},{4,5},{5,4},{6,7},{7,6},{8,9},{9,8},{10,11... | collective-permute-start | bytes 393224 | tf_op jit(solution)/shard_map/ppermute | solution.py:28
  50.2 6.5 %collective-permute-start.6 = (bf16[8,32,256]{2,1,0:T(8,128)(2,1)S(1)}, bf16[8,32,256]{2,1,0:T(8,128)(2,1)S(1)}, u32[]{:S(2)}, u32[]{:S(2)}) collective-permute-start(bf16[8,32,256]{2,1,0:T(8,128)(2,1)S(1)} %get-tuple-element.39), channel_id=1, source_target_pairs={{0,1},{1,0},{2,3},{3,2},{4,5},{5,4},{6,7},{7,6},{8,9},{9,8},{10,11... | collective-permute-start | bytes 393224 | tf_op jit(solution)/shard_map/ppermute | solution.py:28
  56.8 5.0 %collective-permute-start.9 = (bf16[4,32,512]{2,1,0:T(8,128)(2,1)S(1)}, bf16[4,32,512]{2,1,0:T(8,128)(2,1)S(1)}, u32[]{:S(2)}, u32[]{:S(2)}) collective-permute-start(bf16[4,32,512]{2,1,0:T(8,128)(2,1)S(1)} %get-tuple-element.45), channel_id=1, source_target_pairs={{0,4},{2,6},{4,0},{6,2},{8,12},{10,14},{12,8},{14,10},{16,20},{18,... | collective-permute-start | bytes 393224 | tf_op jit(solution)/shard_map/ppermute | solution.py:28
  61.9 15.0 %collective-permute-start.10 = (bf16[32,512]{1,0:T(8,128)(2,1)S(1)}, bf16[32,512]{1,0:T(8,128)(2,1)S(1)}, u32[]{:S(2)}, u32[]{:S(2)}) collective-permute-start(bf16[32,512]{1,0:T(8,128)(2,1)S(1)} %get-tuple-element.47), channel_id=1, source_target_pairs={{0,8},{2,10},{4,12},{6,14},{8,0},{10,2},{12,4},{14,6},{16,24},{18,... | collective-permute-start | bytes 98312 | tf_op jit(solution)/shard_map/ppermute | solution.py:28
  63.5 13.3 %collective-permute-start.11 = (bf16[32,512]{1,0:T(8,128)(2,1)S(1)}, bf16[32,512]{1,0:T(8,128)(2,1)S(1)}, u32[]{:S(2)}, u32[]{:S(2)}) collective-permute-start(bf16[32,512]{1,0:T(8,128)(2,1)S(1)} %get-tuple-element.48), channel_id=1, source_target_pairs={{0,16},{2,18},{4,20},{6,22},{8,24},{10,26},{12,28},{14,30},{16,0},... | collective-permute-start | bytes 98312 | tf_op jit(solution)/shard_map/ppermute | solution.py:28
  65.3 11.6 %collective-permute-start.12 = (bf16[32,512]{1,0:T(8,128)(2,1)S(1)}, bf16[32,512]{1,0:T(8,128)(2,1)S(1)}, u32[]{:S(2)}, u32[]{:S(2)}) collective-permute-start(bf16[32,512]{1,0:T(8,128)(2,1)S(1)} %get-tuple-element.49), channel_id=1, source_target_pairs={{0,24},{2,26},{4,28},{6,30},{8,16},{10,18},{12,20},{14,22},{16,8},... | collective-permute-start | bytes 98312 | tf_op jit(solution)/shard_map/ppermute | solution.py:28

commit v3 on v2

--- a/solution.py
+++ b/solution.py
@@ -110,26 +110,38 @@
         out[:, i * width:(i + 1) * width] = (base[...] + peer * arrived[...].astype(jnp.float32)).astype(jnp.bfloat16)
 
 
-def leg_kernel(axis, bit, *refs):
-    keep, give = refs[-2:]
-    pairs = refs[:-2]
-    width = 2 * keep.shape[-1] // len(pairs)
+def leg_kernel(axis, bit, kept, arrived, keep, give):
     mine = (lax.axis_index(axis) >> bit) & 1
-    for i in range(len(pairs) // 2):
-        kept, arrived = pairs[2 * i], pairs[2 * i + 1]
-        columns = slice(i * width, (i + 1) * width)
-        for out, side in ((keep, mine), (give, 1 - mine)):
-            at = pl.ds(side, 1)
-            total = kept[:, at] + arrived[:, at].astype(jnp.float32)
-            out[:, :, columns] = total.reshape(out.shape[:-1] + (width,)).astype(out.dtype)
-
-
-def spread_kernel(kept, arrived, keep, *gives):
+    for out, side in ((keep, mine), (give, 1 - mine)):
+        at = pl.ds(side, 1)
+        total = kept[:, at] + arrived[:, at].astype(jnp.float32)
+        out[...] = total.reshape(out.shape).astype(out.dtype)
+
+
+def corner_kernel(first, first_arrived, second, second_arrived, keep, give_y, give_x, give_xy):
+    y, x = (lax.axis_index("gossip") >> 1) & 1, lax.axis_index("group") & 1
+    width = first.shape[-1]
+    for out, row in ((keep, y), (give_y, 1 - y)):
+        at, column = pl.ds(row, 1), pl.ds(x, 1)
+        total = first[:, at] + first_arrived[:, at].astype(jnp.float32)
+        out[:, :, :width] = total.reshape(out.shape[:-1] + (width,)).astype(out.dtype)
+        total = second[:, at, column] + second_arrived[:, at, column]
+        out[:, :, width:] = total.reshape(out.shape[:-1] + (width,)).astype(out.dtype)
+    for out, row in ((give_x, y), (give_xy, 1 - y)):
+        at, column = pl.ds(row, 1), pl.ds(1 - x, 1)
+        total = second[:, at, column] + second_arrived[:, at, column]
+        out[...] = total.reshape(out.shape).astype(out.dtype)
+
+
+def spread_kernel(kept, from_y, from_x, from_xy, keep, *gives):
     mine = lax.axis_index("gossip") >> 2
+    width = from_x.shape[-1]
     for other, out in enumerate((keep,) + gives):
         at = pl.ds(mine ^ other, 1)
-        total = kept[at] + arrived[at].astype(jnp.float32)
-        out[...] = total.reshape(out.shape).astype(out.dtype)
+        rows = kept[at] + from_y[at].astype(jnp.float32)
+        late = from_x[at].astype(jnp.float32) + from_xy[at].astype(jnp.float32)
+        out[:, :width] = rows[:, :, :width].reshape(out.shape[0], width).astype(out.dtype)
+        out[:, width:] = (rows[:, :, width:] + late).reshape(out.shape[0], width).astype(out.dtype)
 
 
 def mean_kernel(replicas, keep, *refs):
@@ -168,13 +180,6 @@
         value = keep + flipped(give, axis, 1 << bit)
         left.pop(place)
     return value
-
-
-def leg(pairs, axis, bit):
-    lead, _, rows, width = pairs[0][0].shape
-    shape = (lead, rows, width * len(pairs))
-    ins = [array for pair in pairs for array in pair]
-    return call(functools.partial(leg_kernel, axis, bit), ins, [(shape, jnp.float32), (shape, jnp.bfloat16)])
 
 
 def steps(weights, inputs, targets, plan, order):
@@ -226,17 +231,33 @@
             continue
         keep, give = part
         got = flipped(give, "gossip", 1)
-        view = (n_gossip // 2, n_group, own_rows, width)
-        keep, give = leg([(keep.reshape(view), got.reshape(view))], "group", 0)
-        got = flipped(give, "group", 1)
-        parts.append((keep, got))
+        if half < HALVES - 1:
+            view = (n_gossip // 2, n_group, own_rows, width)
+            shape = (n_gossip // 2, own_rows, width)
+            keep, give = call(
+                functools.partial(leg_kernel, "group", 0),
+                [keep.reshape(view), got.reshape(view)],
+                [(shape, jnp.float32), (shape, jnp.bfloat16)],
+            )
+            got = flipped(give, "group", 1)
+        parts += [keep, got]
     if split:
-        view = (n_gossip // 4, 2, own_rows, width)
-        keep, give = leg([(keep.reshape(view), got.reshape(view)) for keep, got in parts], "gossip", 1)
-        got = flipped(give, "gossip", 2)
+        lead = n_gossip // 4
+        view = (lead, 2, own_rows, width)
+        deep = (lead, 2, n_group, own_rows, width)
+        wide, narrow = (lead, own_rows, dout), (lead, own_rows, width)
+        keep, give_y, give_x, give_xy = call(
+            corner_kernel,
+            [parts[0].reshape(view), parts[1].reshape(view), parts[2].reshape(deep), parts[3].reshape(deep)],
+            [(wide, jnp.float32), (wide, jnp.bfloat16), (narrow, jnp.bfloat16), (narrow, jnp.bfloat16)],
+        )
+        from_x = flipped(give_x, "group", 1)
+        from_y = flipped(give_y, "gossip", 2)
+        pairs = [(source, source ^ (2 * n_group + 1)) for source in range(replicas)]
+        from_xy = lax.ppermute(give_xy, ("gossip", "group"), pairs)
         shape = (own_rows, dout)
-        others = [(shape, jnp.bfloat16)] * (n_gossip // 4 - 1)
-        keep, *gives = call(spread_kernel, [keep, got], [(shape, jnp.float32)] + others)
+        others = [(shape, jnp.bfloat16)] * (lead - 1)
+        keep, *gives = call(spread_kernel, [keep, from_y, from_x, from_xy], [(shape, jnp.float32)] + others)
         gots = []
         for other, give in enumerate(gives, 1):
             gots.append(flipped(give, "gossip", 4 * other))

time: 77.8 us -> 77.8 us (level)
  starting transfers between devices: 11.2 us -> 13.4 us
  waiting for transfers between devices: 46.9 us -> 44.8 us
    ppermute x8, waiting for transfers between devices: 10.3 us -> 5.74 us  [flipped(): lax.ppermute(value, axis, [(source, source ^ bit) for source in range(cou...]
    ppermute x0 -> x1, waiting for transfers between devices: none -> 1.85 us  [steps(): from_xy = lax.ppermute(give_xy, ('gossip', 'group'), pairs)]
    ppermute x0 -> x1, starting transfers between devices: none -> 1.37 us  [steps(): from_xy = lax.ppermute(give_xy, ('gossip', 'group'), pairs)]
    ppermute x8, starting transfers between devices: 7.54 us -> 8.33 us  [flipped(): lax.ppermute(value, axis, [(source, source ^ bit) for source in range(cou...]
    pallas_call x14 -> x13, Pallas kernels: 13.4 us -> 13.4 us  [call(): pl.pallas_call(kernel, in_specs=[in_smem if array.dtype == jnp.int32 else...]
  transfers between devices with their start and end apart: 13 -> 14, of which waited for: 7 -> 7; matrix products, arithmetic and copies ran while one was open for 1% -> 1% of each run, Pallas kernels for 15% -> 15%
where the time goes in v3:
time: 77.8 us; the launch traced here: 77.6 us
  waiting for transfers between devices  44.8 us (58%)
  starting transfers between devices  13.4 us (17%)
  Pallas kernels  13.4 us (17%)
  local copies, waits for them, and re-layouts  5.2 us (7%)
    ppermute x5, waiting for transfers between devices, shifted(): return lax.ppermute(value, axis, pairs)  37.2 us
    pallas_call x13, Pallas kernels, call(): pl.pallas_call(kernel, in_specs=[in_smem if array.dtype == jnp.int32 else...  13.4 us
    ppermute x8, starting transfers between devices, flipped(): lax.ppermute(value, axis, [(source, source ^ bit) for source in range(cou...  8.33 us
    ppermute x8, waiting for transfers between devices, flipped(): lax.ppermute(value, axis, [(source, source ^ bit) for source in range(cou...  5.74 us
    unnamed x13, local copies, waits for them, and re-layouts  5.2 us
    ppermute x5, starting transfers between devices, shifted(): return lax.ppermute(value, axis, pairs)  3.67 us
    ppermute x1, waiting for transfers between devices, steps(): from_xy = lax.ppermute(give_xy, ('gossip', 'group'), pairs)  1.85 us
  transfers between devices with their start and end apart: 14, of which 7 were waited for; matrix products, arithmetic and copies ran while one was open for 1% of the time, Pallas kernels for 15%

profile of v3, /device:TPU:0, one launch (start us, length us, event | category | flops | bytes accessed | tf_op | source)
XLA Modules:
  0.0 77.6 jit_solution(5110330097813248065)
XLA Ops:
  0.6 0.5 collective-permute-start
  1.2 0.8 copy.15.plan
  1.9 1.4 %copy-done = bf16[768,1024]{1,0:T(8,128)(2,1)S(1)} copy-done((bf16[768,1024]{1,0:T(8,128)(2,1)S(1)}, bf16[768,1024]{1,0:T(8,128)(2,1)}, u32[]{:S(2)}) %copy-start) | copy-done | bytes 1572888
  3.3 1.1 %copy-done.2 = bf16[768,512]{1,0:T(8,128)(2,1)S(1)} copy-done((bf16[768,512]{1,0:T(8,128)(2,1)S(1)}, bf16[768,512]{1,0:T(8,128)(2,1)}, u32[]{:S(2)}) %copy-start.2) | copy-done | bytes 786456
  4.5 1.2 %copy-done.4 = bf16[1,1024,512]{2,1,0:T(8,128)(2,1)S(1)} copy-done((bf16[1,1024,512]{2,1,0:T(8,128)(2,1)S(1)}, bf16[1,1024,512]{2,1,0:T(8,128)(2,1)}, u32[]{:S(2)}) %copy-start.4) | copy-done | bytes 1048600
  5.7 0.7 copy-done.5
  6.4 1.9 %shard_map.68 = (f32[1024,512]{1,0:T(8,128)S(1)}, f32[1024,512]{1,0:T(8,128)S(1)}) custom-call(s32[1,3]{1,0:T(1,128)S(1)} %copy-done.5, s32[3,2]{1,0:T(4,128)S(1)} %copy.15.plan, bf16[768,1024]{1,0:T(8,128)(2,1)S(1)} %copy-done, bf16[768,512]{1,0:T(8,128)(2,1)S(1)} %copy-done.2, bf16[1024,512]{1,0:T(8,128)(2,1)S(1)} %bitcast.9), custom_call_target="tpu_custom_call" | custom-call | tf_op jit(solution)/shard_map/pallas_call | solution.py:156
  8.2 0.0 copy-start.1
  8.2 0.0 copy-start.3
  8.3 10.6 %collective-permute-done.arrived = bf16[1024,512]{1,0:T(8,128)(2,1)S(1)} collective-permute-done((bf16[1024,512]{1,0:T(8,128)(2,1)}, bf16[1024,512]{1,0:T(8,128)(2,1)S(1)}, u32[]{:S(2)}, u32[]{:S(2)}) %collective-permute-start) | collective-permute-done | bytes 1048608 | tf_op jit(solution)/shard_map/ppermute | solution.py:23
  18.9 0.8 %shard_map.69 = (bf16[1024,256]{1,0:T(8,128)(2,1)S(1)}, bf16[1024,256]{1,0:T(8,128)(2,1)S(1)}) custom-call(s32[3,2]{1,0:T(4,128)S(1)} %copy.15.plan, f32[1024,512]{1,0:T(8,128)S(1)} %get-tuple-element.26.base.base_in, bf16[1024,512]{1,0:T(8,128)(2,1)S(1)} %collective-permute-done.arrived), custom_call_target="tpu_custom_call" | custom-call | tf_op jit(solution)/shard_map/pallas_call | solution.py:156
  19.7 0.1 collective-permute-start.1
  19.8 1.7 %collective-permute-start.3 = (bf16[1024,256]{1,0:T(8,128)(2,1)S(1)}, bf16[1024,256]{1,0:T(8,128)(2,1)S(1)}, u32[]{:S(2)}, u32[]{:S(2)}) collective-permute-start(bf16[1024,256]{1,0:T(8,128)(2,1)S(1)} %get-tuple-element.32.rounded), channel_id=1, source_target_pairs={{0,4},{2,6},{4,8},{6,10},{8,12},{10,14},{12,16},{14,18},{16,20},{1... | collective-permute-start | bytes 1572872 | tf_op jit(solution)/shard_map/ppermute | solution.py:23
  21.4 0.0 copy-done.1
  21.4 1.5 %shard_map.70 = (f32[1024,256]{1,0:T(8,128)S(1)}, f32[1024,256]{1,0:T(8,128)S(1)}) custom-call(s32[1,3]{1,0:T(1,128)S(1)} %copy-done.5, s32[3,2]{1,0:T(4,128)S(1)} %copy.15.plan, bf16[768,1024]{1,0:T(8,128)(2,1)S(1)} %copy-done.1, bf16[768,512]{1,0:T(8,128)(2,1)S(1)} %copy-done.3, bf16[1024,256]{1,0:T(8,128)(2,1)S(1)} %get-tuple-element.27.rounded, ...), custom_call_target="tpu_custom_call" | custom-call | tf_op jit(solution)/shard_map/pallas_call | solution.py:156
  23.0 14.3 %collective-permute-done.1.arrived = bf16[1024,256]{1,0:T(8,128)(2,1)S(1)} collective-permute-done((bf16[1024,256]{1,0:T(8,128)(2,1)S(1)}, bf16[1024,256]{1,0:T(8,128)(2,1)S(1)}, u32[]{:S(2)}, u32[]{:S(2)}) %collective-permute-start.1) | collective-permute-done | bytes 524320 | tf_op jit(solution)/shard_map/ppermute | solution.py:23
  37.2 0.7 shard_map.71.rounded
  37.9 1.8 %shard_map.72 = (f32[1024,256]{1,0:T(8,128)S(1)}, f32[8,64,256]{2,1,0:T(8,128)S(1)}, f32[8,64,256]{2,1,0:T(8,128)S(1)}) custom-call(s32[1,3]{1,0:T(1,128)S(1)} %copy-done.5, s32[3,2]{1,0:T(4,128)S(1)} %copy.15.plan, bf16[768,1024]{1,0:T(8,128)(2,1)S(1)} %copy-done.1, bf16[768,512]{1,0:T(8,128)(2,1)S(1)} %copy-done.3, ...), custom_call_target="tpu_custom_call" | custom-call | tf_op jit(solution)/shard_map/pallas_call | solution.py:156
  39.8 0.1 collective-permute-start.5
  39.8 1.5 %shard_map.73 = (f32[1024,256]{1,0:T(8,128)S(1)}, f32[1024,256]{1,0:T(8,128)S(1)}) custom-call(s32[1,3]{1,0:T(1,128)S(1)} %copy-done.5, s32[3,2]{1,0:T(4,128)S(1)} %copy.15.plan, bf16[768,1024]{1,0:T(8,128)(2,1)S(1)} %copy-done.1, bf16[768,512]{1,0:T(8,128)(2,1)S(1)} %copy-done.3, bf16[1024,256]{1,0:T(8,128)(2,1)S(1)} %get-tuple-element.32.rounded, ...), custom_call_target="tpu_custom_call" | custom-call | tf_op jit(solution)/shard_map/pallas_call | solution.py:156
  41.4 3.1 %collective-permute-done.3.arrived = bf16[1024,256]{1,0:T(8,128)(2,1)S(1)} collective-permute-done((bf16[1024,256]{1,0:T(8,128)(2,1)S(1)}, bf16[1024,256]{1,0:T(8,128)(2,1)S(1)}, u32[]{:S(2)}, u32[]{:S(2)}) %collective-permute-start.3) | collective-permute-done | bytes 524320 | tf_op jit(solution)/shard_map/ppermute | solution.py:23
  44.5 0.7 shard_map.74.rounded
  45.2 1.8 %shard_map.75 = (f32[1024,256]{1,0:T(8,128)S(1)}, f32[8,64,256]{2,1,0:T(8,128)S(1)}, f32[8,64,256]{2,1,0:T(8,128)S(1)}) custom-call(s32[1,3]{1,0:T(1,128)S(1)} %copy-done.5, s32[3,2]{1,0:T(4,128)S(1)} %copy.15.plan, bf16[768,1024]{1,0:T(8,128)(2,1)S(1)} %copy-done.1, bf16[768,512]{1,0:T(8,128)(2,1)S(1)} %copy-done.3, ...), custom_call_target="tpu_custom_call" | custom-call | tf_op jit(solution)/shard_map/pallas_call | solution.py:156
  47.1 0.1 collective-permute-start.7
  47.1 0.1 collective-permute-start.4
  47.2 1.3 %collective-permute-start.2 = (bf16[1024,256]{1,0:T(8,128)(2,1)S(1)}, bf16[1024,256]{1,0:T(8,128)(2,1)S(1)}, u32[]{:S(2)}, u32[]{:S(2)}) collective-permute-start(bf16[1024,256]{1,0:T(8,128)(2,1)S(1)} %shard_map.71.rounded), channel_id=1, source_target_pairs={{0,8},{2,10},{4,12},{6,14},{8,16},{10,18},{12,20},{14,22},{16,24},... | collective-permute-start | bytes 1572872 | tf_op jit(solution)/shard_map/ppermute | solution.py:23
  48.5 0.0 collective-permute-done.5
  48.5 0.1 shard_map.77
  48.6 1.6 %collective-permute-start.6 = (bf16[8,32,256]{2,1,0:T(8,128)(2,1)S(1)}, bf16[8,32,256]{2,1,0:T(8,128)(2,1)S(1)}, u32[]{:S(2)}, u32[]{:S(2)}) collective-permute-start(bf16[8,32,256]{2,1,0:T(8,128)(2,1)S(1)} %get-tuple-element.39), channel_id=1, source_target_pairs={{0,1},{1,0},{2,3},{3,2},{4,5},{5,4},{6,7},{7,6},{8,9},{9,8},{10,11... | collective-permute-start | bytes 393224 | tf_op jit(solution)/shard_map/ppermute | solution.py:28
  50.2 0.0 collective-permute-done.7
  50.2 3.8 %collective-permute-done.6 = bf16[8,32,256]{2,1,0:T(8,128)(2,1)S(1)} collective-permute-done((bf16[8,32,256]{2,1,0:T(8,128)(2,1)S(1)}, bf16[8,32,256]{2,1,0:T(8,128)(2,1)S(1)}, u32[]{:S(2)}, u32[]{:S(2)}) %collective-permute-start.6) | collective-permute-done | bytes 131104 | tf_op jit(solution)/shard_map/ppermute | solution.py:28
  54.0 0.1 shard_map.78
  54.0 0.7 collective-permute-start.8
  54.7 1.5 %collective-permute-start.9 = (bf16[4,32,256]{2,1,0:T(8,128)(2,1)S(1)}, bf16[4,32,256]{2,1,0:T(8,128)(2,1)S(1)}, u32[]{:S(2)}, u32[]{:S(2)}) collective-permute-start(bf16[4,32,256]{2,1,0:T(8,128)(2,1)S(1)} %get-tuple-element.44), channel_id=1, source_target_pairs={{0,1},{1,0},{2,3},{3,2},{4,5},{5,4},{6,7},{7,6},{8,9},{9,8},{10,11... | collective-permute-start | bytes 196616 | tf_op jit(solution)/shard_map/ppermute | solution.py:28
  56.2 1.4 %collective-permute-start.10 = (bf16[4,32,256]{2,1,0:T(8,128)(2,1)S(1)}, bf16[4,32,256]{2,1,0:T(8,128)(2,1)S(1)}, u32[]{:S(2)}, u32[]{:S(2)}) collective-permute-start(bf16[4,32,256]{2,1,0:T(8,128)(2,1)S(1)} %get-tuple-element.45), channel_id=1, source_target_pairs={{0,5},{1,4},{2,7},{3,6},{4,1},{5,0},{6,3},{7,2},{8,13},{9,12},{10,... | collective-permute-start | bytes 196616 | tf_op jit(solution)/shard_map/ppermute | solution.py:257
  57.6 1.9 %collective-permute-done.9.from_x = bf16[4,32,256]{2,1,0:T(8,128)(2,1)S(1)} collective-permute-done((bf16[4,32,256]{2,1,0:T(8,128)(2,1)S(1)}, bf16[4,32,256]{2,1,0:T(8,128)(2,1)S(1)}, u32[]{:S(2)}, u32[]{:S(2)}) %collective-permute-start.9) | collective-permute-done | bytes 65568 | tf_op jit(solution)/shard_map/ppermute | solution.py:28
  59.5 1.9 %collective-permute-done.10.from_xy = bf16[4,32,256]{2,1,0:T(8,128)(2,1)S(1)} collective-permute-done((bf16[4,32,256]{2,1,0:T(8,128)(2,1)S(1)}, bf16[4,32,256]{2,1,0:T(8,128)(2,1)S(1)}, u32[]{:S(2)}, u32[]{:S(2)}) %collective-permute-start.10) | collective-permute-done | bytes 65568 | tf_op jit(solution)/shard_map/ppermute | solution.py:257
  61.4 0.0 collective-permute-done.8.from_y
  61.4 1.1 %collective-permute-start.11 = (bf16[32,512]{1,0:T(8,128)(2,1)S(1)}, bf16[32,512]{1,0:T(8,128)(2,1)S(1)}, u32[]{:S(2)}, u32[]{:S(2)}) collective-permute-start(bf16[32,512]{1,0:T(8,128)(2,1)S(1)} %get-tuple-element.47), channel_id=1, source_target_pairs={{0,8},{2,10},{4,12},{6,14},{8,0},{10,2},{12,4},{14,6},{16,24},{18,... | collective-permute-start | bytes 98312 | tf_op jit(solution)/shard_map/ppermute | solution.py:28
  62.5 1.8 %collective-permute-start.12 = (bf16[32,512]{1,0:T(8,128)(2,1)S(1)}, bf16[32,512]{1,0:T(8,128)(2,1)S(1)}, u32[]{:S(2)}, u32[]{:S(2)}) collective-permute-start(bf16[32,512]{1,0:T(8,128)(2,1)S(1)} %get-tuple-element.48), channel_id=1, source_target_pairs={{0,16},{2,18},{4,20},{6,22},{8,24},{10,26},{12,28},{14,30},{16,0},... | collective-permute-start | bytes 98312 | tf_op jit(solution)/shard_map/ppermute | solution.py:28
  64.3 1.6 %collective-permute-start.13 = (bf16[32,512]{1,0:T(8,128)(2,1)S(1)}, bf16[32,512]{1,0:T(8,128)(2,1)S(1)}, u32[]{:S(2)}, u32[]{:S(2)}) collective-permute-start(bf16[32,512]{1,0:T(8,128)(2,1)S(1)} %get-tuple-element.49), channel_id=1, source_target_pairs={{0,24},{2,26},{4,28},{6,30},{8,16},{10,18},{12,20},{14,22},{16,8},... | collective-permute-start | bytes 98312 | tf_op jit(solution)/shard_map/ppermute | solution.py:28
  65.9 0.0 collective-permute-done.4.refs_3_
  65.9 9.2 %collective-permute-done.2.refs_1_ = bf16[1024,256]{1,0:T(8,128)(2,1)S(1)} collective-permute-done((bf16[1024,256]{1,0:T(8,128)(2,1)S(1)}, bf16[1024,256]{1,0:T(8,128)(2,1)S(1)}, u32[]{:S(2)}, u32[]{:S(2)}) %collective-permute-start.2) | collective-permute-done | bytes 524320 | tf_op jit(solution)/shard_map/ppermute | solution.py:23
  75.1 1.8 %shard_map.76 = bf16[1024,512]{1,0:T(8,128)(2,1)} custom-call(s32[3,2]{1,0:T(4,128)S(1)} %copy.15.plan, f32[1024,256]{1,0:T(8,128)S(1)} %get-tuple-element.31.refs_0_, bf16[1024,256]{1,0:T(8,128)(2,1)S(1)} %collective-permute-done.2.refs_1_, f32[1024,256]{1,0:T(8,128)S(1)} %get-tuple-element.35.refs_2_, bf16[1024,256]{1,0:T(8,128)(2,1)S(1)} %collective-permute-done.4.refs_3_), custom_call_target="tpu_custom_call" | custom-call | tf_op jit(solution)/shard_map/pallas_call | solution.py:156
  76.9 0.0 collective-permute-done.11.refs_0_
  76.9 0.0 collective-permute-done.12.refs_1_
  76.9 0.0 collective-permute-done.13.refs_2_
  76.9 0.7 shard_map.80
  (6 shorter events, 0.1 us)
Async XLA Ops:
  0.6 18.2 %collective-permute-start = (bf16[1024,512]{1,0:T(8,128)(2,1)}, bf16[1024,512]{1,0:T(8,128)(2,1)S(1)}, u32[]{:S(2)}, u32[]{:S(2)}) collective-permute-start(bf16[1024,512]{1,0:T(8,128)(2,1)} %bitcast.8), channel_id=1, source_target_pairs={{0,2},{2,4},{4,6},{6,8},{8,10},{10,12},{12,14},{14,16},{16,18},{18... | collective-permute-start | bytes 3145736 | tf_op jit(solution)/shard_map/ppermute | solution.py:23
  1.9 1.4 %copy-start = (bf16[768,1024]{1,0:T(8,128)(2,1)S(1)}, bf16[768,1024]{1,0:T(8,128)(2,1)}, u32[]{:S(2)}) copy-start(bf16[768,1024]{1,0:T(8,128)(2,1)} %x.9) | copy-start | bytes 4718596
  3.3 1.1 %copy-start.2 = (bf16[768,512]{1,0:T(8,128)(2,1)S(1)}, bf16[768,512]{1,0:T(8,128)(2,1)}, u32[]{:S(2)}) copy-start(bf16[768,512]{1,0:T(8,128)(2,1)} %t.9) | copy-start | bytes 2359300
  4.5 1.2 %copy-start.4 = (bf16[1,1024,512]{2,1,0:T(8,128)(2,1)S(1)}, bf16[1,1024,512]{2,1,0:T(8,128)(2,1)}, u32[]{:S(2)}) copy-start(bf16[1,1024,512]{2,1,0:T(8,128)(2,1)} %param.5) | copy-start | bytes 3145732
  5.7 0.7 copy-start.5
  8.2 13.2 %copy-start.1 = (bf16[768,1024]{1,0:T(8,128)(2,1)S(1)}, bf16[768,1024]{1,0:T(8,128)(2,1)}, u32[]{:S(2)}) copy-start(bf16[768,1024]{1,0:T(8,128)(2,1)} %x.9) | copy-start | bytes 4718596
  8.2 13.2 %copy-start.3 = (bf16[768,512]{1,0:T(8,128)(2,1)S(1)}, bf16[768,512]{1,0:T(8,128)(2,1)}, u32[]{:S(2)}) copy-start(bf16[768,512]{1,0:T(8,128)(2,1)} %t.9) | copy-start | bytes 2359300
  19.7 17.5 %collective-permute-start.1 = (bf16[1024,256]{1,0:T(8,128)(2,1)S(1)}, bf16[1024,256]{1,0:T(8,128)(2,1)S(1)}, u32[]{:S(2)}, u32[]{:S(2)}) collective-permute-start(bf16[1024,256]{1,0:T(8,128)(2,1)S(1)} %get-tuple-element.27.rounded), channel_id=1, source_target_pairs={{0,4},{2,6},{4,8},{6,10},{8,12},{10,14},{12,16},{14,18},{16,20},{1... | collective-permute-start | bytes 1572872 | tf_op jit(solution)/shard_map/ppermute | solution.py:23
  19.8 24.7 %collective-permute-start.3 = (bf16[1024,256]{1,0:T(8,128)(2,1)S(1)}, bf16[1024,256]{1,0:T(8,128)(2,1)S(1)}, u32[]{:S(2)}, u32[]{:S(2)}) collective-permute-start(bf16[1024,256]{1,0:T(8,128)(2,1)S(1)} %get-tuple-element.32.rounded), channel_id=1, source_target_pairs={{0,4},{2,6},{4,8},{6,10},{8,12},{10,14},{12,16},{14,18},{16,20},{1... | collective-permute-start | bytes 1572872 | tf_op jit(solution)/shard_map/ppermute | solution.py:23
  39.8 8.8 %collective-permute-start.5 = (f32[8,64,256]{2,1,0:T(8,128)S(1)}, f32[8,64,256]{2,1,0:T(8,128)S(1)}, u32[]{:S(2)}, u32[]{:S(2)}) collective-permute-start(f32[8,64,256]{2,1,0:T(8,128)S(1)} %get-tuple-element.37), channel_id=1, source_target_pairs={{0,2},{2,0},{4,6},{6,4},{8,10},{10,8},{12,14},{14,12},{16,18},{18,... | collective-permute-start | bytes 1572872 | tf_op jit(solution)/shard_map/ppermute | solution.py:28
  47.1 3.1 %collective-permute-start.7 = (f32[8,64,256]{2,1,0:T(8,128)S(1)}, f32[8,64,256]{2,1,0:T(8,128)S(1)}, u32[]{:S(2)}, u32[]{:S(2)}) collective-permute-start(f32[8,64,256]{2,1,0:T(8,128)S(1)} %get-tuple-element.41), channel_id=1, source_target_pairs={{0,2},{2,0},{4,6},{6,4},{8,10},{10,8},{12,14},{14,12},{16,18},{18,... | collective-permute-start | bytes 1572872 | tf_op jit(solution)/shard_map/ppermute | solution.py:28
  47.1 18.7 %collective-permute-start.4 = (bf16[1024,256]{1,0:T(8,128)(2,1)S(1)}, bf16[1024,256]{1,0:T(8,128)(2,1)S(1)}, u32[]{:S(2)}, u32[]{:S(2)}) collective-permute-start(bf16[1024,256]{1,0:T(8,128)(2,1)S(1)} %shard_map.74.rounded), channel_id=1, source_target_pairs={{0,8},{2,10},{4,12},{6,14},{8,16},{10,18},{12,20},{14,22},{16,24},... | collective-permute-start | bytes 1572872 | tf_op jit(solution)/shard_map/ppermute | solution.py:23
  47.2 27.9 %collective-permute-start.2 = (bf16[1024,256]{1,0:T(8,128)(2,1)S(1)}, bf16[1024,256]{1,0:T(8,128)(2,1)S(1)}, u32[]{:S(2)}, u32[]{:S(2)}) collective-permute-start(bf16[1024,256]{1,0:T(8,128)(2,1)S(1)} %shard_map.71.rounded), channel_id=1, source_target_pairs={{0,8},{2,10},{4,12},{6,14},{8,16},{10,18},{12,20},{14,22},{16,24},... | collective-permute-start | bytes 1572872 | tf_op jit(solution)/shard_map/ppermute | solution.py:23
  48.6 5.4 %collective-permute-start.6 = (bf16[8,32,256]{2,1,0:T(8,128)(2,1)S(1)}, bf16[8,32,256]{2,1,0:T(8,128)(2,1)S(1)}, u32[]{:S(2)}, u32[]{:S(2)}) collective-permute-start(bf16[8,32,256]{2,1,0:T(8,128)(2,1)S(1)} %get-tuple-element.39), channel_id=1, source_target_pairs={{0,1},{1,0},{2,3},{3,2},{4,5},{5,4},{6,7},{7,6},{8,9},{9,8},{10,11... | collective-permute-start | bytes 393224 | tf_op jit(solution)/shard_map/ppermute | solution.py:28
  54.0 7.3 %collective-permute-start.8 = (bf16[4,32,512]{2,1,0:T(8,128)(2,1)S(1)}, bf16[4,32,512]{2,1,0:T(8,128)(2,1)S(1)}, u32[]{:S(2)}, u32[]{:S(2)}) collective-permute-start(bf16[4,32,512]{2,1,0:T(8,128)(2,1)S(1)} %get-tuple-element.43), channel_id=1, source_target_pairs={{0,4},{2,6},{4,0},{6,2},{8,12},{10,14},{12,8},{14,10},{16,20},{18,... | collective-permute-start | bytes 393224 | tf_op jit(solution)/shard_map/ppermute | solution.py:28
  54.7 4.8 %collective-permute-start.9 = (bf16[4,32,256]{2,1,0:T(8,128)(2,1)S(1)}, bf16[4,32,256]{2,1,0:T(8,128)(2,1)S(1)}, u32[]{:S(2)}, u32[]{:S(2)}) collective-permute-start(bf16[4,32,256]{2,1,0:T(8,128)(2,1)S(1)} %get-tuple-element.44), channel_id=1, source_target_pairs={{0,1},{1,0},{2,3},{3,2},{4,5},{5,4},{6,7},{7,6},{8,9},{9,8},{10,11... | collective-permute-start | bytes 196616 | tf_op jit(solution)/shard_map/ppermute | solution.py:28
  56.2 5.2 %collective-permute-start.10 = (bf16[4,32,256]{2,1,0:T(8,128)(2,1)S(1)}, bf16[4,32,256]{2,1,0:T(8,128)(2,1)S(1)}, u32[]{:S(2)}, u32[]{:S(2)}) collective-permute-start(bf16[4,32,256]{2,1,0:T(8,128)(2,1)S(1)} %get-tuple-element.45), channel_id=1, source_target_pairs={{0,5},{1,4},{2,7},{3,6},{4,1},{5,0},{6,3},{7,2},{8,13},{9,12},{10,... | collective-permute-start | bytes 196616 | tf_op jit(solution)/shard_map/ppermute | solution.py:257
  61.4 15.5 %collective-permute-start.11 = (bf16[32,512]{1,0:T(8,128)(2,1)S(1)}, bf16[32,512]{1,0:T(8,128)(2,1)S(1)}, u32[]{:S(2)}, u32[]{:S(2)}) collective-permute-start(bf16[32,512]{1,0:T(8,128)(2,1)S(1)} %get-tuple-element.47), channel_id=1, source_target_pairs={{0,8},{2,10},{4,12},{6,14},{8,0},{10,2},{12,4},{14,6},{16,24},{18,... | collective-permute-start | bytes 98312 | tf_op jit(solution)/shard_map/ppermute | solution.py:28
  62.5 14.4 %collective-permute-start.12 = (bf16[32,512]{1,0:T(8,128)(2,1)S(1)}, bf16[32,512]{1,0:T(8,128)(2,1)S(1)}, u32[]{:S(2)}, u32[]{:S(2)}) collective-permute-start(bf16[32,512]{1,0:T(8,128)(2,1)S(1)} %get-tuple-element.48), channel_id=1, source_target_pairs={{0,16},{2,18},{4,20},{6,22},{8,24},{10,26},{12,28},{14,30},{16,0},... | collective-permute-start | bytes 98312 | tf_op jit(solution)/shard_map/ppermute | solution.py:28
  64.3 12.6 %collective-permute-start.13 = (bf16[32,512]{1,0:T(8,128)(2,1)S(1)}, bf16[32,512]{1,0:T(8,128)(2,1)S(1)}, u32[]{:S(2)}, u32[]{:S(2)}) collective-permute-start(bf16[32,512]{1,0:T(8,128)(2,1)S(1)} %get-tuple-element.49), channel_id=1, source_target_pairs={{0,24},{2,26},{4,28},{6,30},{8,16},{10,18},{12,20},{14,22},{16,8},... | collective-permute-start | bytes 98312 | tf_op jit(solution)/shard_map/ppermute | solution.py:28

commit v4 on v3

--- a/solution.py
+++ b/solution.py
@@ -21,6 +21,12 @@
     count = lax.axis_size(axis)
     pairs = [(source, (source + steps) % count) for source in range(count)]
     return lax.ppermute(value, axis, pairs)
+
+
+def moved(value, target):
+    count = lax.axis_size("gossip")
+    pairs = [(source, target(source) % count) for source in range(count) if target(source) is not None]
+    return lax.ppermute(value, "gossip", pairs)
 
 
 def flipped(value, axis, bit):
@@ -65,22 +71,18 @@
         base[:, columns] = own * w[:, columns].astype(jnp.float32) - learning_rate * gradient
 
 
-def middle_kernel(columns, order, plan, x, t, rounded, base_in, arrived, velocity_in, base, velocity):
-    _, peer = shares(plan, 0)
+def middle_kernel(columns, order, plan, x, t, rounded, master, velocity_in, base, velocity):
     own, _ = shares(plan, 1)
     v = momentum_decay * velocity_in[:, columns] + gradient_of(*shard_of(order, x, t, 1, columns), rounded[...])
     velocity[...] = v
-    master = base_in[:, columns] + peer * arrived[:, columns].astype(jnp.float32)
-    base[...] = own * master - learning_rate * v
-
-
-def last_kernel(columns, split, order, plan, x, t, rounded, base_in, arrived, velocity_in, base, *outs):
-    _, peer = shares(plan, STEPS - 2)
+    base[...] = own * master[...] - learning_rate * v
+
+
+def last_kernel(columns, split, order, plan, x, t, rounded, master, velocity_in, base, *outs):
     own, last_peer = shares(plan, STEPS - 1)
     r = rounded[...]
     v = momentum_decay * velocity_in[...] + gradient_of(*shard_of(order, x, t, STEPS - 1, columns), r)
-    master = base_in[...] + peer * arrived[...].astype(jnp.float32)
-    b = own * master - learning_rate * v
+    b = own * master[...] - learning_rate * v
     base[...] = b
     part = b + last_peer * r.astype(jnp.float32)
     if not split:
@@ -93,12 +95,31 @@
     give[...] = held[:, pl.ds(1 - mine, 1)].reshape(give.shape)
 
 
-def round_kernel(step, plan, base, arrived, *rounded):
-    _, peer = shares(plan, step)
+def early_kernel(plan, base, arrived, *rounded):
+    _, peer = shares(plan, 0)
     width = base.shape[1] // len(rounded)
     for i, r in enumerate(rounded):
         columns = slice(i * width, (i + 1) * width)
         r[...] = (base[:, columns] + peer * arrived[:, columns].astype(jnp.float32)).astype(jnp.bfloat16)
+
+
+def round_kernel(step, halves, plan, base, *refs):
+    _, peer = shares(plan, step)
+    at = lax.axis_index("gossip")
+    core, chip = at & 1, (at >> 1) & 1
+    arrays, outs = refs[:-2 * halves], refs[-2 * halves:]
+    width = base.shape[1] // halves
+    for i in range(halves):
+        columns = slice(i * width, (i + 1) * width)
+        direct, *others = [array[:, columns].astype(jnp.float32) for array in arrays]
+        arrived = direct
+        if len(others) == 1:
+            arrived = jnp.where(core == 1, others[0], direct)
+        elif others:
+            arrived = jnp.where(core == 1, jnp.where(chip == 1, others[0], others[1]), direct)
+        master = base[:, columns] + peer * arrived
+        outs[2 * i][...] = master.astype(jnp.bfloat16)
+        outs[2 * i + 1][...] = master
 
 
 def finish_kernel(plan, *refs):
@@ -193,26 +214,37 @@
     columns = [slice(half * width, (half + 1) * width) for half in range(HALVES)]
     half_f32, half_bf16 = ((din, width), jnp.float32), ((din, width), jnp.bfloat16)
 
-    arrived0 = shifted(weights, "gossip", 1)
+    ship = moved(weights, lambda at: at + 1 if at & 1 else None)
+    chip = moved(weights, lambda at: None if at & 1 else at + 1)
     base0, velocity0 = call(
         first_kernel, [order, plan, inputs, targets, weights], [((din, dout), jnp.float32)] * 2
     )
-    rounded1 = call(functools.partial(round_kernel, 0), [plan, base0, arrived0], [half_bf16] * HALVES)
-    arrived1, middles = [], []
-    for half in range(HALVES):
-        arrived1.append(shifted(rounded1[half], "gossip", 2))
+    early = call(early_kernel, [plan, base0, chip], [half_bf16] * HALVES)
+    hops, sends, relays = [], [], []
+    for half in range(HALVES):
+        hops.append(moved(early[half], lambda at: at ^ 2 if at & 1 else None))
+    firsts = call(functools.partial(round_kernel, 0, HALVES), [plan, base0, ship, chip], [half_bf16, half_f32] * HALVES)
+    for half in range(HALVES):
+        sends.append(moved(firsts[2 * half], lambda at: None if at & 1 else at + 2))
+    middles = []
     for half in range(HALVES):
         middles.append(
             call(
                 functools.partial(middle_kernel, columns[half]),
-                [order, plan, inputs, targets, rounded1[half], base0, arrived0, velocity0],
+                [order, plan, inputs, targets] + list(firsts[2 * half:2 * half + 2]) + [velocity0],
                 [half_f32] * 2,
             )
         )
+    for half in range(HALVES):
+        relays.append(moved(hops[half], lambda at: at + 4 if at & 3 == 1 else None))
     parts, last = [], []
     for half in range(HALVES):
         base1, velocity1 = middles[half]
-        (rounded2,) = call(functools.partial(round_kernel, 1), [plan, base1, arrived1[half]], [half_bf16])
+        rounded2, master2 = call(
+            functools.partial(round_kernel, 1, 1),
+            [plan, base1, sends[half], hops[half], relays[half]],
+            [half_bf16, half_f32],
+        )
         arrived2 = shifted(rounded2, "gossip", 4)
         outs, scratch = [half_f32] * 2, ()
         if split:
@@ -221,7 +253,7 @@
             scratch = (pltpu.VMEM((pair[0], 2) + pair[1:], jnp.float32),)
         base2, *part = call(
             functools.partial(last_kernel, columns[half], split),
-            [order, plan, inputs, targets, rounded2, base1, arrived1[half], velocity1],
+            [order, plan, inputs, targets, rounded2, master2, velocity1],
             outs,
             scratch,
         )

time: 77.8 us -> 89.6 us (1.15)
  starting transfers between devices: 13.4 us -> 38.8 us
  waiting for transfers between devices: 44.8 us -> 29.8 us
  Pallas kernels: 13.4 us -> 14.6 us
    ppermute x5 -> x2, waiting for transfers between devices: 37.2 us -> 9.11 us  [shifted(): return lax.ppermute(value, axis, pairs)]
    ppermute x8, starting transfers between devices: 8.33 us -> 24.2 us  [flipped(): lax.ppermute(value, axis, [(source, source ^ bit) for source in range(cou...]
    ppermute x0 -> x8, waiting for transfers between devices: none -> 13.4 us  [moved(): return lax.ppermute(value, 'gossip', pairs)]
    ppermute x0 -> x8, starting transfers between devices: none -> 12.5 us  [moved(): return lax.ppermute(value, 'gossip', pairs)]
    ppermute x5 -> x2, starting transfers between devices: 3.67 us -> 0.37 us  [shifted(): return lax.ppermute(value, axis, pairs)]
    pallas_call x13 -> x14, Pallas kernels: 13.4 us -> 14.6 us  [call(): pl.pallas_call(kernel, in_specs=[in_smem if array.dtype == jnp.int32 else...]
    ppermute x8, waiting for transfers between devices: 5.74 us -> 4.67 us  [flipped(): lax.ppermute(value, axis, [(source, source ^ bit) for source in range(cou...]
  transfers between devices with their start and end apart: 14 -> 19, of which waited for: 7 -> 6; matrix products, arithmetic and copies ran while one was open for 1% -> 1% of each run, Pallas kernels for 15% -> 16%
where the time goes in v4:
time: 89.6 us; the launch traced here: 89.2 us
  starting transfers between devices  38.8 us (43%)
  waiting for transfers between devices  29.8 us (33%)
  Pallas kernels  14.6 us (16%)
  local copies, waits for them, and re-layouts  5.2 us (6%)
    ppermute x8, starting transfers between devices, flipped(): lax.ppermute(value, axis, [(source, source ^ bit) for source in range(cou...  24.2 us
    pallas_call x14, Pallas kernels, call(): pl.pallas_call(kernel, in_specs=[in_smem if array.dtype == jnp.int32 else...  14.6 us
    ppermute x8, waiting for transfers between devices, moved(): return lax.ppermute(value, 'gossip', pairs)  13.4 us
    ppermute x8, starting transfers between devices, moved(): return lax.ppermute(value, 'gossip', pairs)  12.5 us
    ppermute x2, waiting for transfers between devices, shifted(): return lax.ppermute(value, axis, pairs)  9.11 us
    unnamed x13, local copies, waits for them, and re-layouts  5.2 us
    ppermute x8, waiting for transfers between devices, flipped(): lax.ppermute(value, axis, [(source, source ^ bit) for source in range(cou...  4.67 us
    ppermute x1, waiting for transfers between devices, steps(): from_xy = lax.ppermute(give_xy, ('gossip', 'group'), pairs)  2.64 us
  transfers between devices with their start and end apart: 19, of which 6 were waited for; matrix products, arithmetic and copies ran while one was open for 1% of the time, Pallas kernels for 16%

profile of v4, /device:TPU:0, one launch (start us, length us, event | category | flops | bytes accessed | tf_op | source)
XLA Modules:
  0.0 89.2 jit_solution(11201689206323829176)
XLA Ops:
  0.6 2.5 %collective-permute-start.1 = (bf16[1024,512]{1,0:T(8,128)(2,1)}, bf16[1024,512]{1,0:T(8,128)(2,1)S(1)}, u32[]{:S(2)}, u32[]{:S(2)}) collective-permute-start(bf16[1024,512]{1,0:T(8,128)(2,1)} %bitcast.8), channel_id=1, source_target_pairs={{0,2},{4,6},{8,10},{12,14},{16,18},{20,22},{24,26},{28,30},{1,3},{... | collective-permute-start | bytes 3145736 | tf_op jit(solution)/shard_map/ppermute | solution.py:29
  3.1 1.3 %collective-permute-start = (bf16[1024,512]{1,0:T(8,128)(2,1)}, bf16[1024,512]{1,0:T(8,128)(2,1)S(1)}, u32[]{:S(2)}, u32[]{:S(2)}) collective-permute-start(bf16[1024,512]{1,0:T(8,128)(2,1)} %bitcast.9), channel_id=1, source_target_pairs={{2,4},{6,8},{10,12},{14,16},{18,20},{22,24},{26,28},{30,0},{3,5},{... | collective-permute-start | bytes 3145736 | tf_op jit(solution)/shard_map/ppermute | solution.py:29
  4.4 0.8 copy.16.plan
  5.2 1.4 %copy-done = bf16[768,1024]{1,0:T(8,128)(2,1)S(1)} copy-done((bf16[768,1024]{1,0:T(8,128)(2,1)S(1)}, bf16[768,1024]{1,0:T(8,128)(2,1)}, u32[]{:S(2)}) %copy-start) | copy-done | bytes 1572888
  6.6 1.1 %copy-done.2 = bf16[768,512]{1,0:T(8,128)(2,1)S(1)} copy-done((bf16[768,512]{1,0:T(8,128)(2,1)S(1)}, bf16[768,512]{1,0:T(8,128)(2,1)}, u32[]{:S(2)}) %copy-start.2) | copy-done | bytes 786456
  7.7 1.2 %copy-done.4 = bf16[1,1024,512]{2,1,0:T(8,128)(2,1)S(1)} copy-done((bf16[1,1024,512]{2,1,0:T(8,128)(2,1)S(1)}, bf16[1,1024,512]{2,1,0:T(8,128)(2,1)}, u32[]{:S(2)}) %copy-start.4) | copy-done | bytes 1048600
  8.9 0.7 copy-done.5
  9.6 1.9 %shard_map.68 = (f32[1024,512]{1,0:T(8,128)S(1)}, f32[1024,512]{1,0:T(8,128)S(1)}) custom-call(s32[1,3]{1,0:T(1,128)S(1)} %copy-done.5, s32[3,2]{1,0:T(4,128)S(1)} %copy.16.plan, bf16[768,1024]{1,0:T(8,128)(2,1)S(1)} %copy-done, bf16[768,512]{1,0:T(8,128)(2,1)S(1)} %copy-done.2, bf16[1024,512]{1,0:T(8,128)(2,1)S(1)} %bitcast.10), custom_call_target="tpu_custom_call" | custom-call | tf_op jit(solution)/shard_map/pallas_call | solution.py:177
  11.5 0.8 shard_map.71
  12.3 0.7 collective-permute-start.3
  13.0 0.0 copy-start.1
  13.0 0.0 copy-start.3
  13.1 0.8 collective-permute-start.7
  13.9 8.3 %collective-permute-done.refs_0_ = bf16[1024,512]{1,0:T(8,128)(2,1)S(1)} collective-permute-done((bf16[1024,512]{1,0:T(8,128)(2,1)}, bf16[1024,512]{1,0:T(8,128)(2,1)S(1)}, u32[]{:S(2)}, u32[]{:S(2)}) %collective-permute-start) | collective-permute-done | bytes 1048608 | tf_op jit(solution)/shard_map/ppermute | solution.py:29
  22.2 1.0 %shard_map.69 = (bf16[1024,256]{1,0:T(8,128)(2,1)S(1)}, f32[1024,256]{1,0:T(8,128)S(1)}, bf16[1024,256]{1,0:T(8,128)(2,1)S(1)}, f32[1024,256]{1,0:T(8,128)S(1)}) custom-call(s32[3,2]{1,0:T(4,128)S(1)} %copy.16.plan, f32[1024,512]{1,0:T(8,128)S(1)} %get-tuple-element.34.base, bf16[1024,512]{1,0:T(8,128)(2,1)S(1)} %collective-permute-done.refs_0_, ...), custom_call_target="tpu_custom_call" | custom-call | tf_op jit(solution)/shard_map/pallas_call | solution.py:177
  23.2 1.9 %collective-permute-start.2 = (bf16[1024,256]{1,0:T(8,128)(2,1)S(1)}, bf16[1024,256]{1,0:T(8,128)(2,1)S(1)}, u32[]{:S(2)}, u32[]{:S(2)}) collective-permute-start(bf16[1024,256]{1,0:T(8,128)(2,1)S(1)} %get-tuple-element.35.rounded), channel_id=1, source_target_pairs={{0,4},{4,8},{8,12},{12,16},{16,20},{20,24},{24,28},{28,0},{1,5},{5... | collective-permute-start | bytes 1572872 | tf_op jit(solution)/shard_map/ppermute | solution.py:29
  25.2 0.7 collective-permute-start.4
  25.9 4.0 %collective-permute-start.6 = (bf16[1024,256]{1,0:T(8,128)(2,1)S(1)}, bf16[1024,256]{1,0:T(8,128)(2,1)S(1)}, u32[]{:S(2)}, u32[]{:S(2)}) collective-permute-start(bf16[1024,256]{1,0:T(8,128)(2,1)S(1)} %get-tuple-element.44.rounded), channel_id=1, source_target_pairs={{0,4},{4,8},{8,12},{12,16},{16,20},{20,24},{24,28},{28,0},{1,5},{5... | collective-permute-start | bytes 1572872 | tf_op jit(solution)/shard_map/ppermute | solution.py:29
  29.8 0.0 collective-permute-done.7.refs_1_
  29.8 0.7 collective-permute-start.8
  30.6 1.5 %shard_map.70 = (f32[1024,256]{1,0:T(8,128)S(1)}, f32[1024,256]{1,0:T(8,128)S(1)}) custom-call(s32[1,3]{1,0:T(1,128)S(1)} %copy-done.5, s32[3,2]{1,0:T(4,128)S(1)} %copy.16.plan, bf16[768,1024]{1,0:T(8,128)(2,1)S(1)} %copy-done.1, bf16[768,512]{1,0:T(8,128)(2,1)S(1)} %copy-done.3, bf16[1024,256]{1,0:T(8,128)(2,1)S(1)} %get-tuple-element.35.rounded, ...), custom_call_target="tpu_custom_call" | custom-call | tf_op jit(solution)/shard_map/pallas_call | solution.py:177
  32.1 5.0 %collective-permute-done.2.refs_0_ = bf16[1024,256]{1,0:T(8,128)(2,1)S(1)} collective-permute-done((bf16[1024,256]{1,0:T(8,128)(2,1)S(1)}, bf16[1024,256]{1,0:T(8,128)(2,1)S(1)}, u32[]{:S(2)}, u32[]{:S(2)}) %collective-permute-start.2) | collective-permute-done | bytes 524320 | tf_op jit(solution)/shard_map/ppermute | solution.py:29
  37.1 0.8 shard_map.72
  37.9 1.8 %shard_map.73 = (f32[1024,256]{1,0:T(8,128)S(1)}, f32[8,64,256]{2,1,0:T(8,128)S(1)}, f32[8,64,256]{2,1,0:T(8,128)S(1)}) custom-call(s32[1,3]{1,0:T(1,128)S(1)} %copy-done.5, s32[3,2]{1,0:T(4,128)S(1)} %copy.16.plan, bf16[768,1024]{1,0:T(8,128)(2,1)S(1)} %copy-done.1, bf16[768,512]{1,0:T(8,128)(2,1)S(1)} %copy-done.3, ...), custom_call_target="tpu_custom_call" | custom-call | tf_op jit(solution)/shard_map/pallas_call | solution.py:177
  39.7 11.1 %collective-permute-start.10 = (f32[8,64,256]{2,1,0:T(8,128)S(1)}, f32[8,64,256]{2,1,0:T(8,128)S(1)}, u32[]{:S(2)}, u32[]{:S(2)}) collective-permute-start(f32[8,64,256]{2,1,0:T(8,128)S(1)} %get-tuple-element.53), channel_id=1, source_target_pairs={{0,2},{2,0},{4,6},{6,4},{8,10},{10,8},{12,14},{14,12},{16,18},{18,... | collective-permute-start | bytes 1572872 | tf_op jit(solution)/shard_map/ppermute | solution.py:34
  50.9 1.5 %shard_map.74 = (f32[1024,256]{1,0:T(8,128)S(1)}, f32[1024,256]{1,0:T(8,128)S(1)}) custom-call(s32[1,3]{1,0:T(1,128)S(1)} %copy-done.5, s32[3,2]{1,0:T(4,128)S(1)} %copy.16.plan, bf16[768,1024]{1,0:T(8,128)(2,1)S(1)} %copy-done.1, bf16[768,512]{1,0:T(8,128)(2,1)S(1)} %copy-done.3, bf16[1024,256]{1,0:T(8,128)(2,1)S(1)} %get-tuple-element.44.rounded, ...), custom_call_target="tpu_custom_call" | custom-call | tf_op jit(solution)/shard_map/pallas_call | solution.py:177
  52.4 0.8 shard_map.75
  53.2 1.8 %shard_map.76 = (f32[1024,256]{1,0:T(8,128)S(1)}, f32[8,64,256]{2,1,0:T(8,128)S(1)}, f32[8,64,256]{2,1,0:T(8,128)S(1)}) custom-call(s32[1,3]{1,0:T(1,128)S(1)} %copy-done.5, s32[3,2]{1,0:T(4,128)S(1)} %copy.16.plan, bf16[768,1024]{1,0:T(8,128)(2,1)S(1)} %copy-done.1, bf16[768,512]{1,0:T(8,128)(2,1)S(1)} %copy-done.3, ...), custom_call_target="tpu_custom_call" | custom-call | tf_op jit(solution)/shard_map/pallas_call | solution.py:177
  55.0 3.8 %collective-permute-start.12 = (f32[8,64,256]{2,1,0:T(8,128)S(1)}, f32[8,64,256]{2,1,0:T(8,128)S(1)}, u32[]{:S(2)}, u32[]{:S(2)}) collective-permute-start(f32[8,64,256]{2,1,0:T(8,128)S(1)} %get-tuple-element.57), channel_id=1, source_target_pairs={{0,2},{2,0},{4,6},{6,4},{8,10},{10,8},{12,14},{14,12},{16,18},{18,... | collective-permute-start | bytes 1572872 | tf_op jit(solution)/shard_map/ppermute | solution.py:34
  58.8 0.0 collective-permute-start.9
  58.8 0.4 collective-permute-start.5
  59.2 0.0 collective-permute-done.10
  59.2 0.1 shard_map.78
  59.3 2.0 %collective-permute-start.11 = (bf16[8,32,256]{2,1,0:T(8,128)(2,1)S(1)}, bf16[8,32,256]{2,1,0:T(8,128)(2,1)S(1)}, u32[]{:S(2)}, u32[]{:S(2)}) collective-permute-start(bf16[8,32,256]{2,1,0:T(8,128)(2,1)S(1)} %get-tuple-element.55), channel_id=1, source_target_pairs={{0,1},{1,0},{2,3},{3,2},{4,5},{5,4},{6,7},{7,6},{8,9},{9,8},{10,11... | collective-permute-start | bytes 393224 | tf_op jit(solution)/shard_map/ppermute | solution.py:34
  61.3 3.8 %collective-permute-done.11 = bf16[8,32,256]{2,1,0:T(8,128)(2,1)S(1)} collective-permute-done((bf16[8,32,256]{2,1,0:T(8,128)(2,1)S(1)}, bf16[8,32,256]{2,1,0:T(8,128)(2,1)S(1)}, u32[]{:S(2)}, u32[]{:S(2)}) %collective-permute-start.11) | collective-permute-done | bytes 131104 | tf_op jit(solution)/shard_map/ppermute | solution.py:34
  65.1 0.1 shard_map.79
  65.2 0.1 collective-permute-start.13
  65.3 1.8 %collective-permute-start.14 = (bf16[4,32,256]{2,1,0:T(8,128)(2,1)S(1)}, bf16[4,32,256]{2,1,0:T(8,128)(2,1)S(1)}, u32[]{:S(2)}, u32[]{:S(2)}) collective-permute-start(bf16[4,32,256]{2,1,0:T(8,128)(2,1)S(1)} %get-tuple-element.60), channel_id=1, source_target_pairs={{0,1},{1,0},{2,3},{3,2},{4,5},{5,4},{6,7},{7,6},{8,9},{9,8},{10,11... | collective-permute-start | bytes 196616 | tf_op jit(solution)/shard_map/ppermute | solution.py:34
  67.1 1.7 %collective-permute-start.15 = (bf16[4,32,256]{2,1,0:T(8,128)(2,1)S(1)}, bf16[4,32,256]{2,1,0:T(8,128)(2,1)S(1)}, u32[]{:S(2)}, u32[]{:S(2)}) collective-permute-start(bf16[4,32,256]{2,1,0:T(8,128)(2,1)S(1)} %get-tuple-element.61), channel_id=1, source_target_pairs={{0,5},{1,4},{2,7},{3,6},{4,1},{5,0},{6,3},{7,2},{8,13},{9,12},{10,... | collective-permute-start | bytes 196616 | tf_op jit(solution)/shard_map/ppermute | solution.py:289
  68.8 0.9 collective-permute-done.14.from_x
  69.6 2.6 %collective-permute-done.15.from_xy = bf16[4,32,256]{2,1,0:T(8,128)(2,1)S(1)} collective-permute-done((bf16[4,32,256]{2,1,0:T(8,128)(2,1)S(1)}, bf16[4,32,256]{2,1,0:T(8,128)(2,1)S(1)}, u32[]{:S(2)}, u32[]{:S(2)}) %collective-permute-start.15) | collective-permute-done | bytes 65568 | tf_op jit(solution)/shard_map/ppermute | solution.py:289
  72.3 0.1 shard_map.80
  72.3 0.6 collective-permute-start.16
  72.9 3.5 %collective-permute-start.17 = (bf16[32,512]{1,0:T(8,128)(2,1)S(1)}, bf16[32,512]{1,0:T(8,128)(2,1)S(1)}, u32[]{:S(2)}, u32[]{:S(2)}) collective-permute-start(bf16[32,512]{1,0:T(8,128)(2,1)S(1)} %get-tuple-element.64), channel_id=1, source_target_pairs={{0,16},{2,18},{4,20},{6,22},{8,24},{10,26},{12,28},{14,30},{16,0},... | collective-permute-start | bytes 98312 | tf_op jit(solution)/shard_map/ppermute | solution.py:34
  76.5 1.2 %collective-permute-start.18 = (bf16[32,512]{1,0:T(8,128)(2,1)S(1)}, bf16[32,512]{1,0:T(8,128)(2,1)S(1)}, u32[]{:S(2)}, u32[]{:S(2)}) collective-permute-start(bf16[32,512]{1,0:T(8,128)(2,1)S(1)} %get-tuple-element.65), channel_id=1, source_target_pairs={{0,24},{2,26},{4,28},{6,30},{8,16},{10,18},{12,20},{14,22},{16,8},... | collective-permute-start | bytes 98312 | tf_op jit(solution)/shard_map/ppermute | solution.py:34
  77.6 9.1 %collective-permute-done.5.refs_1_ = bf16[1024,256]{1,0:T(8,128)(2,1)S(1)} collective-permute-done((bf16[1024,256]{1,0:T(8,128)(2,1)S(1)}, bf16[1024,256]{1,0:T(8,128)(2,1)S(1)}, u32[]{:S(2)}, u32[]{:S(2)}) %collective-permute-start.5) | collective-permute-done | bytes 524320 | tf_op jit(solution)/shard_map/ppermute | solution.py:23
  86.8 1.8 %shard_map.77 = bf16[1024,512]{1,0:T(8,128)(2,1)} custom-call(s32[3,2]{1,0:T(4,128)S(1)} %copy.16.plan, f32[1024,256]{1,0:T(8,128)S(1)} %get-tuple-element.43.refs_0_, bf16[1024,256]{1,0:T(8,128)(2,1)S(1)} %collective-permute-done.5.refs_1_, f32[1024,256]{1,0:T(8,128)S(1)} %get-tuple-element.51.refs_2_, bf16[1024,256]{1,0:T(8,128)(2,1)S(1)} %collective-permute-done.9.refs_3_), custom_call_target="tpu_custom_call" | custom-call | tf_op jit(solution)/shard_map/pallas_call | solution.py:177
  88.6 0.7 shard_map.81
  (17 shorter events, 0.0 us)
Async XLA Ops:
  0.6 10.8 %collective-permute-start.1 = (bf16[1024,512]{1,0:T(8,128)(2,1)}, bf16[1024,512]{1,0:T(8,128)(2,1)S(1)}, u32[]{:S(2)}, u32[]{:S(2)}) collective-permute-start(bf16[1024,512]{1,0:T(8,128)(2,1)} %bitcast.8), channel_id=1, source_target_pairs={{0,2},{4,6},{8,10},{12,14},{16,18},{20,22},{24,26},{28,30},{1,3},{... | collective-permute-start | bytes 3145736 | tf_op jit(solution)/shard_map/ppermute | solution.py:29
  3.1 19.1 %collective-permute-start = (bf16[1024,512]{1,0:T(8,128)(2,1)}, bf16[1024,512]{1,0:T(8,128)(2,1)S(1)}, u32[]{:S(2)}, u32[]{:S(2)}) collective-permute-start(bf16[1024,512]{1,0:T(8,128)(2,1)} %bitcast.9), channel_id=1, source_target_pairs={{2,4},{6,8},{10,12},{14,16},{18,20},{22,24},{26,28},{30,0},{3,5},{... | collective-permute-start | bytes 3145736 | tf_op jit(solution)/shard_map/ppermute | solution.py:29
  5.2 1.4 %copy-start = (bf16[768,1024]{1,0:T(8,128)(2,1)S(1)}, bf16[768,1024]{1,0:T(8,128)(2,1)}, u32[]{:S(2)}) copy-start(bf16[768,1024]{1,0:T(8,128)(2,1)} %x.9) | copy-start | bytes 4718596
  6.6 1.1 %copy-start.2 = (bf16[768,512]{1,0:T(8,128)(2,1)S(1)}, bf16[768,512]{1,0:T(8,128)(2,1)}, u32[]{:S(2)}) copy-start(bf16[768,512]{1,0:T(8,128)(2,1)} %t.9) | copy-start | bytes 2359300
  7.7 1.2 %copy-start.4 = (bf16[1,1024,512]{2,1,0:T(8,128)(2,1)S(1)}, bf16[1,1024,512]{2,1,0:T(8,128)(2,1)}, u32[]{:S(2)}) copy-start(bf16[1,1024,512]{2,1,0:T(8,128)(2,1)} %param.5) | copy-start | bytes 3145732
  8.9 0.7 copy-start.5
  12.3 12.8 %collective-permute-start.3 = (bf16[1024,256]{1,0:T(8,128)(2,1)S(1)}, bf16[1024,256]{1,0:T(8,128)(2,1)S(1)}, u32[]{:S(2)}, u32[]{:S(2)}) collective-permute-start(bf16[1024,256]{1,0:T(8,128)(2,1)S(1)} %get-tuple-element.39), channel_id=1, source_target_pairs={{2,6},{6,2},{10,14},{14,10},{18,22},{22,18},{26,30},{30,26},{3,7},... | collective-permute-start | bytes 1572872 | tf_op jit(solution)/shard_map/ppermute | solution.py:29
  13.0 17.5 %copy-start.1 = (bf16[768,1024]{1,0:T(8,128)(2,1)S(1)}, bf16[768,1024]{1,0:T(8,128)(2,1)}, u32[]{:S(2)}) copy-start(bf16[768,1024]{1,0:T(8,128)(2,1)} %x.9) | copy-start | bytes 4718596
  13.0 17.5 %copy-start.3 = (bf16[768,512]{1,0:T(8,128)(2,1)S(1)}, bf16[768,512]{1,0:T(8,128)(2,1)}, u32[]{:S(2)}) copy-start(bf16[768,512]{1,0:T(8,128)(2,1)} %t.9) | copy-start | bytes 2359300
  13.1 16.8 %collective-permute-start.7 = (bf16[1024,256]{1,0:T(8,128)(2,1)S(1)}, bf16[1024,256]{1,0:T(8,128)(2,1)S(1)}, u32[]{:S(2)}, u32[]{:S(2)}) collective-permute-start(bf16[1024,256]{1,0:T(8,128)(2,1)S(1)} %get-tuple-element.47), channel_id=1, source_target_pairs={{2,6},{6,2},{10,14},{14,10},{18,22},{22,18},{26,30},{30,26},{3,7},... | collective-permute-start | bytes 1572872 | tf_op jit(solution)/shard_map/ppermute | solution.py:29
  23.2 13.9 %collective-permute-start.2 = (bf16[1024,256]{1,0:T(8,128)(2,1)S(1)}, bf16[1024,256]{1,0:T(8,128)(2,1)S(1)}, u32[]{:S(2)}, u32[]{:S(2)}) collective-permute-start(bf16[1024,256]{1,0:T(8,128)(2,1)S(1)} %get-tuple-element.35.rounded), channel_id=1, source_target_pairs={{0,4},{4,8},{8,12},{12,16},{16,20},{20,24},{24,28},{28,0},{1,5},{5... | collective-permute-start | bytes 1572872 | tf_op jit(solution)/shard_map/ppermute | solution.py:29
  25.2 11.9 %collective-permute-start.4 = (bf16[1024,256]{1,0:T(8,128)(2,1)S(1)}, bf16[1024,256]{1,0:T(8,128)(2,1)S(1)}, u32[]{:S(2)}, u32[]{:S(2)}) collective-permute-start(bf16[1024,256]{1,0:T(8,128)(2,1)S(1)} %collective-permute-done.3.refs_1_), channel_id=1, source_target_pairs={{2,10},{10,18},{18,26},{26,2},{3,11},{11,19},{19,27},{27,3}} | collective-permute-start | bytes 1572872 | tf_op jit(solution)/shard_map/ppermute | solution.py:29
  25.9 26.5 %collective-permute-start.6 = (bf16[1024,256]{1,0:T(8,128)(2,1)S(1)}, bf16[1024,256]{1,0:T(8,128)(2,1)S(1)}, u32[]{:S(2)}, u32[]{:S(2)}) collective-permute-start(bf16[1024,256]{1,0:T(8,128)(2,1)S(1)} %get-tuple-element.44.rounded), channel_id=1, source_target_pairs={{0,4},{4,8},{8,12},{12,16},{16,20},{20,24},{24,28},{28,0},{1,5},{5... | collective-permute-start | bytes 1572872 | tf_op jit(solution)/shard_map/ppermute | solution.py:29
  29.8 22.5 %collective-permute-start.8 = (bf16[1024,256]{1,0:T(8,128)(2,1)S(1)}, bf16[1024,256]{1,0:T(8,128)(2,1)S(1)}, u32[]{:S(2)}, u32[]{:S(2)}) collective-permute-start(bf16[1024,256]{1,0:T(8,128)(2,1)S(1)} %collective-permute-done.7.refs_1_), channel_id=1, source_target_pairs={{2,10},{10,18},{18,26},{26,2},{3,11},{11,19},{19,27},{27,3}} | collective-permute-start | bytes 1572872 | tf_op jit(solution)/shard_map/ppermute | solution.py:29
  39.7 19.5 %collective-permute-start.10 = (f32[8,64,256]{2,1,0:T(8,128)S(1)}, f32[8,64,256]{2,1,0:T(8,128)S(1)}, u32[]{:S(2)}, u32[]{:S(2)}) collective-permute-start(f32[8,64,256]{2,1,0:T(8,128)S(1)} %get-tuple-element.53), channel_id=1, source_target_pairs={{0,2},{2,0},{4,6},{6,4},{8,10},{10,8},{12,14},{14,12},{16,18},{18,... | collective-permute-start | bytes 1572872 | tf_op jit(solution)/shard_map/ppermute | solution.py:34
  55.0 6.3 %collective-permute-start.12 = (f32[8,64,256]{2,1,0:T(8,128)S(1)}, f32[8,64,256]{2,1,0:T(8,128)S(1)}, u32[]{:S(2)}, u32[]{:S(2)}) collective-permute-start(f32[8,64,256]{2,1,0:T(8,128)S(1)} %get-tuple-element.57), channel_id=1, source_target_pairs={{0,2},{2,0},{4,6},{6,4},{8,10},{10,8},{12,14},{14,12},{16,18},{18,... | collective-permute-start | bytes 1572872 | tf_op jit(solution)/shard_map/ppermute | solution.py:34
  58.8 18.8 %collective-permute-start.9 = (bf16[1024,256]{1,0:T(8,128)(2,1)S(1)}, bf16[1024,256]{1,0:T(8,128)(2,1)S(1)}, u32[]{:S(2)}, u32[]{:S(2)}) collective-permute-start(bf16[1024,256]{1,0:T(8,128)(2,1)S(1)} %get-tuple-element.48.rounded), channel_id=1, source_target_pairs={{0,8},{2,10},{4,12},{6,14},{8,16},{10,18},{12,20},{14,22},{16,24},... | collective-permute-start | bytes 1572872 | tf_op jit(solution)/shard_map/ppermute | solution.py:23
  58.8 27.9 %collective-permute-start.5 = (bf16[1024,256]{1,0:T(8,128)(2,1)S(1)}, bf16[1024,256]{1,0:T(8,128)(2,1)S(1)}, u32[]{:S(2)}, u32[]{:S(2)}) collective-permute-start(bf16[1024,256]{1,0:T(8,128)(2,1)S(1)} %get-tuple-element.40.rounded), channel_id=1, source_target_pairs={{0,8},{2,10},{4,12},{6,14},{8,16},{10,18},{12,20},{14,22},{16,24},... | collective-permute-start | bytes 1572872 | tf_op jit(solution)/shard_map/ppermute | solution.py:23
  59.3 5.8 %collective-permute-start.11 = (bf16[8,32,256]{2,1,0:T(8,128)(2,1)S(1)}, bf16[8,32,256]{2,1,0:T(8,128)(2,1)S(1)}, u32[]{:S(2)}, u32[]{:S(2)}) collective-permute-start(bf16[8,32,256]{2,1,0:T(8,128)(2,1)S(1)} %get-tuple-element.55), channel_id=1, source_target_pairs={{0,1},{1,0},{2,3},{3,2},{4,5},{5,4},{6,7},{7,6},{8,9},{9,8},{10,11... | collective-permute-start | bytes 393224 | tf_op jit(solution)/shard_map/ppermute | solution.py:34
  65.2 7.0 %collective-permute-start.13 = (bf16[4,32,512]{2,1,0:T(8,128)(2,1)S(1)}, bf16[4,32,512]{2,1,0:T(8,128)(2,1)S(1)}, u32[]{:S(2)}, u32[]{:S(2)}) collective-permute-start(bf16[4,32,512]{2,1,0:T(8,128)(2,1)S(1)} %get-tuple-element.59), channel_id=1, source_target_pairs={{0,4},{2,6},{4,0},{6,2},{8,12},{10,14},{12,8},{14,10},{16,20},{18,... | collective-permute-start | bytes 393224 | tf_op jit(solution)/shard_map/ppermute | solution.py:34
  65.3 4.3 %collective-permute-start.14 = (bf16[4,32,256]{2,1,0:T(8,128)(2,1)S(1)}, bf16[4,32,256]{2,1,0:T(8,128)(2,1)S(1)}, u32[]{:S(2)}, u32[]{:S(2)}) collective-permute-start(bf16[4,32,256]{2,1,0:T(8,128)(2,1)S(1)} %get-tuple-element.60), channel_id=1, source_target_pairs={{0,1},{1,0},{2,3},{3,2},{4,5},{5,4},{6,7},{7,6},{8,9},{9,8},{10,11... | collective-permute-start | bytes 196616 | tf_op jit(solution)/shard_map/ppermute | solution.py:34
  67.1 5.2 %collective-permute-start.15 = (bf16[4,32,256]{2,1,0:T(8,128)(2,1)S(1)}, bf16[4,32,256]{2,1,0:T(8,128)(2,1)S(1)}, u32[]{:S(2)}, u32[]{:S(2)}) collective-permute-start(bf16[4,32,256]{2,1,0:T(8,128)(2,1)S(1)} %get-tuple-element.61), channel_id=1, source_target_pairs={{0,5},{1,4},{2,7},{3,6},{4,1},{5,0},{6,3},{7,2},{8,13},{9,12},{10,... | collective-permute-start | bytes 196616 | tf_op jit(solution)/shard_map/ppermute | solution.py:289
  72.3 16.3 %collective-permute-start.16 = (bf16[32,512]{1,0:T(8,128)(2,1)S(1)}, bf16[32,512]{1,0:T(8,128)(2,1)S(1)}, u32[]{:S(2)}, u32[]{:S(2)}) collective-permute-start(bf16[32,512]{1,0:T(8,128)(2,1)S(1)} %get-tuple-element.63), channel_id=1, source_target_pairs={{0,8},{2,10},{4,12},{6,14},{8,0},{10,2},{12,4},{14,6},{16,24},{18,... | collective-permute-start | bytes 98312 | tf_op jit(solution)/shard_map/ppermute | solution.py:34
  72.9 15.7 %collective-permute-start.17 = (bf16[32,512]{1,0:T(8,128)(2,1)S(1)}, bf16[32,512]{1,0:T(8,128)(2,1)S(1)}, u32[]{:S(2)}, u32[]{:S(2)}) collective-permute-start(bf16[32,512]{1,0:T(8,128)(2,1)S(1)} %get-tuple-element.64), channel_id=1, source_target_pairs={{0,16},{2,18},{4,20},{6,22},{8,24},{10,26},{12,28},{14,30},{16,0},... | collective-permute-start | bytes 98312 | tf_op jit(solution)/shard_map/ppermute | solution.py:34
  76.5 12.1 %collective-permute-start.18 = (bf16[32,512]{1,0:T(8,128)(2,1)S(1)}, bf16[32,512]{1,0:T(8,128)(2,1)S(1)}, u32[]{:S(2)}, u32[]{:S(2)}) collective-permute-start(bf16[32,512]{1,0:T(8,128)(2,1)S(1)} %get-tuple-element.65), channel_id=1, source_target_pairs={{0,24},{2,26},{4,28},{6,30},{8,16},{10,18},{12,20},{14,22},{16,8},... | collective-permute-start | bytes 98312 | tf_op jit(solution)/shard_map/ppermute | solution.py:34

commit v5 on v3

--- a/solution.py
+++ b/solution.py
@@ -55,32 +55,30 @@
     return x[rows, :], t[rows, columns]
 
 
-def first_kernel(order, plan, x, t, w, base, velocity):
+def first_kernel(order, plan, x, t, *refs):
     own, _ = shares(plan, 0)
-    width = w.shape[1] // HALVES
-    for half in range(HALVES):
+    weights, outs = refs[:HALVES], refs[HALVES:]
+    width = weights[0].shape[1]
+    for half, w in enumerate(weights):
+        base, velocity = outs[2 * half:2 * half + 2]
         columns = slice(half * width, (half + 1) * width)
-        gradient = gradient_of(*shard_of(order, x, t, 0, columns), w[:, columns])
-        velocity[:, columns] = gradient
-        base[:, columns] = own * w[:, columns].astype(jnp.float32) - learning_rate * gradient
-
-
-def middle_kernel(columns, order, plan, x, t, rounded, base_in, arrived, velocity_in, base, velocity):
-    _, peer = shares(plan, 0)
+        gradient = gradient_of(*shard_of(order, x, t, 0, columns), w[...])
+        velocity[...] = gradient
+        base[...] = own * w[...].astype(jnp.float32) - learning_rate * gradient
+
+
+def middle_kernel(columns, order, plan, x, t, rounded, master, velocity_in, base, velocity):
     own, _ = shares(plan, 1)
-    v = momentum_decay * velocity_in[:, columns] + gradient_of(*shard_of(order, x, t, 1, columns), rounded[...])
+    v = momentum_decay * velocity_in[...] + gradient_of(*shard_of(order, x, t, 1, columns), rounded[...])
     velocity[...] = v
-    master = base_in[:, columns] + peer * arrived[:, columns].astype(jnp.float32)
-    base[...] = own * master - learning_rate * v
-
-
-def last_kernel(columns, split, order, plan, x, t, rounded, base_in, arrived, velocity_in, base, *outs):
-    _, peer = shares(plan, STEPS - 2)
+    base[...] = own * master[...] - learning_rate * v
+
+
+def last_kernel(columns, split, order, plan, x, t, rounded, master, velocity_in, base, *outs):
     own, last_peer = shares(plan, STEPS - 1)
     r = rounded[...]
     v = momentum_decay * velocity_in[...] + gradient_of(*shard_of(order, x, t, STEPS - 1, columns), r)
-    master = base_in[...] + peer * arrived[...].astype(jnp.float32)
-    b = own * master - learning_rate * v
+    b = own * master[...] - learning_rate * v
     base[...] = b
     part = b + last_peer * r.astype(jnp.float32)
     if not split:
@@ -93,12 +91,11 @@
     give[...] = held[:, pl.ds(1 - mine, 1)].reshape(give.shape)
 
 
-def round_kernel(step, plan, base, arrived, *rounded):
+def round_kernel(step, plan, base, arrived, rounded, master):
     _, peer = shares(plan, step)
-    width = base.shape[1] // len(rounded)
-    for i, r in enumerate(rounded):
-        columns = slice(i * width, (i + 1) * width)
-        r[...] = (base[:, columns] + peer * arrived[:, columns].astype(jnp.float32)).astype(jnp.bfloat16)
+    total = base[...] + peer * arrived[...].astype(jnp.float32)
+    rounded[...] = total.astype(jnp.bfloat16)
+    master[...] = total
 
 
 def finish_kernel(plan, *refs):
@@ -193,26 +190,30 @@
     columns = [slice(half * width, (half + 1) * width) for half in range(HALVES)]
     half_f32, half_bf16 = ((din, width), jnp.float32), ((din, width), jnp.bfloat16)
 
-    arrived0 = shifted(weights, "gossip", 1)
-    base0, velocity0 = call(
-        first_kernel, [order, plan, inputs, targets, weights], [((din, dout), jnp.float32)] * 2
-    )
-    rounded1 = call(functools.partial(round_kernel, 0), [plan, base0, arrived0], [half_bf16] * HALVES)
-    arrived1, middles = [], []
-    for half in range(HALVES):
-        arrived1.append(shifted(rounded1[half], "gossip", 2))
+    pieces, arrived0, rounds0, arrived1, middles = [], [], [], [], []
+    for half in range(HALVES):
+        pieces.append(weights[:, columns[half]])
+        arrived0.append(shifted(pieces[half], "gossip", 1))
+    firsts = call(first_kernel, [order, plan, inputs, targets] + pieces, [half_f32] * (2 * HALVES))
+    for half in range(HALVES):
+        rounds0.append(
+            call(functools.partial(round_kernel, 0), [plan, firsts[2 * half], arrived0[half]], [half_bf16, half_f32])
+        )
+        arrived1.append(shifted(rounds0[half][0], "gossip", 2))
     for half in range(HALVES):
         middles.append(
             call(
                 functools.partial(middle_kernel, columns[half]),
-                [order, plan, inputs, targets, rounded1[half], base0, arrived0, velocity0],
+                [order, plan, inputs, targets] + list(rounds0[half]) + [firsts[2 * half + 1]],
                 [half_f32] * 2,
             )
         )
     parts, last = [], []
     for half in range(HALVES):
         base1, velocity1 = middles[half]
-        (rounded2,) = call(functools.partial(round_kernel, 1), [plan, base1, arrived1[half]], [half_bf16])
+        rounded2, master2 = call(
+            functools.partial(round_kernel, 1), [plan, base1, arrived1[half]], [half_bf16, half_f32]
+        )
         arrived2 = shifted(rounded2, "gossip", 4)
         outs, scratch = [half_f32] * 2, ()
         if split:
@@ -221,7 +222,7 @@
             scratch = (pltpu.VMEM((pair[0], 2) + pair[1:], jnp.float32),)
         base2, *part = call(
             functools.partial(last_kernel, columns[half], split),
-            [order, plan, inputs, targets, rounded2, base1, arrived1[half], velocity1],
+            [order, plan, inputs, targets, rounded2, master2, velocity1],
             outs,
             scratch,
         )

time: 77.8 us -> 75.8 us (0.974)
  local copies, waits for them, and re-layouts: 5.2 us -> 2.63 us
  waiting for transfers between devices: 44.8 us -> 42.7 us
  starting transfers between devices: 13.4 us -> 14.9 us
  Pallas kernels: 13.4 us -> 14.5 us
    unnamed x13 -> x11, local copies, waits for them, and re-layouts: 5.2 us -> 1.24 us
    ppermute x5 -> x6, waiting for transfers between devices: 37.2 us -> 35.7 us  [shifted(): return lax.ppermute(value, axis, pairs)]
    ppermute x5 -> x6, starting transfers between devices: 3.67 us -> 5.13 us  [shifted(): return lax.ppermute(value, axis, pairs)]
    slice x0 -> x1, local copies, waits for them, and re-layouts: none -> 1.39 us  [steps(): pieces.append(weights[:, columns[half]])]
    pallas_call x13 -> x14, Pallas kernels: 13.4 us -> 14.5 us  [call(): pl.pallas_call(kernel, in_specs=[in_smem if array.dtype == jnp.int32 else...]
  transfers between devices with their start and end apart: 14 -> 15, of which waited for: 7 -> 8; matrix products, arithmetic and copies ran while one was open for 1% -> 0% of each run, Pallas kernels for 15% -> 18%
where the time goes in v5:
time: 75.8 us; the launch traced here: 75.5 us
  waiting for transfers between devices  42.7 us (56%)
  starting transfers between devices  14.9 us (20%)
  Pallas kernels  14.5 us (19%)
  local copies, waits for them, and re-layouts  2.63 us (3%)
  between operations  0.79 us (1%)
    ppermute x6, waiting for transfers between devices, shifted(): return lax.ppermute(value, axis, pairs)  35.7 us
    pallas_call x14, Pallas kernels, call(): pl.pallas_call(kernel, in_specs=[in_smem if array.dtype == jnp.int32 else...  14.5 us
    ppermute x8, starting transfers between devices, flipped(): lax.ppermute(value, axis, [(source, source ^ bit) for source in range(cou...  7.89 us
    ppermute x6, starting transfers between devices, shifted(): return lax.ppermute(value, axis, pairs)  5.13 us
    ppermute x8, waiting for transfers between devices, flipped(): lax.ppermute(value, axis, [(source, source ^ bit) for source in range(cou...  4.99 us
    ppermute x1, waiting for transfers between devices, steps(): from_xy = lax.ppermute(give_xy, ('gossip', 'group'), pairs)  2.07 us
    ppermute x1, starting transfers between devices, steps(): from_xy = lax.ppermute(give_xy, ('gossip', 'group'), pairs)  1.92 us
  transfers between devices with their start and end apart: 15, of which 8 were waited for; matrix products, arithmetic and copies ran while one was open for 0% of the time, Pallas kernels for 18%

profile of v5, /device:TPU:0, one launch (start us, length us, event | category | flops | bytes accessed | tf_op | source)
XLA Modules:
  0.0 75.5 jit_solution(194643830456335657)
XLA Ops:
  0.6 0.0 copy-start.4
  0.7 1.4 %fusion = (bf16[1024,256]{1,0:T(8,128)(2,1)S(1)}, bf16[1024,256]{1,0:T(8,128)(2,1)S(1)}) fusion(bf16[1024,512]{1,0:T(8,128)(2,1)} %bitcast.14), kind=kLoop, calls=%fused_computation | loop fusion | bytes 2097152 | tf_op jit(solution)/shard_map/slice | solution.py:195
  2.1 0.5 collective-permute-start
  2.6 2.6 %collective-permute-start.3 = (bf16[1024,256]{1,0:T(8,128)(2,1)S(1)}, bf16[1024,256]{1,0:T(8,128)(2,1)S(1)}, u32[]{:S(2)}, u32[]{:S(2)}) collective-permute-start(bf16[1024,256]{1,0:T(8,128)(2,1)S(1)} %get-tuple-element.66.refs_1_), channel_id=1, source_target_pairs={{0,2},{2,4},{4,6},{6,8},{8,10},{10,12},{12,14},{14,16},{16,18},{18... | collective-permute-start | bytes 1572872 | tf_op jit(solution)/shard_map/ppermute | solution.py:23
  5.2 0.1 copy.16.plan
  5.3 1.1 %copy-done.1 = bf16[768,512]{1,0:T(8,128)(2,1)S(1)} copy-done((bf16[768,512]{1,0:T(8,128)(2,1)S(1)}, bf16[768,512]{1,0:T(8,128)(2,1)}, u32[]{:S(2)}) %copy-start.1) | copy-done | bytes 786456
  6.5 1.9 %shard_map.68 = (f32[1024,256]{1,0:T(8,128)S(1)}, f32[1024,256]{1,0:T(8,128)S(1)}, f32[1024,256]{1,0:T(8,128)S(1)}, f32[1024,256]{1,0:T(8,128)S(1)}) custom-call(s32[1,3]{1,0:T(1,128)S(1)} %copy-done.3, s32[3,2]{1,0:T(4,128)S(1)} %copy.16.plan, bf16[768,1024]{1,0:T(8,128)(2,1)S(1)} %copy-done, bf16[768,512]{1,0:T(8,128)(2,1)S(1)} %copy-done.1, ...), custom_call_target="tpu_custom_call" | custom-call | tf_op jit(solution)/shard_map/pallas_call | solution.py:153
  8.3 6.2 %collective-permute-done.arrived = bf16[1024,256]{1,0:T(8,128)(2,1)} collective-permute-done((bf16[1024,256]{1,0:T(8,128)(2,1)S(1)}, bf16[1024,256]{1,0:T(8,128)(2,1)}, u32[]{:S(2)}, u32[]{:S(2)}) %collective-permute-start) | collective-permute-done | bytes 524320 | tf_op jit(solution)/shard_map/ppermute | solution.py:23
  14.6 1.3 %shard_map.69 = (bf16[1024,256]{1,0:T(8,128)(2,1)S(1)}, f32[1024,256]{1,0:T(8,128)S(1)}) custom-call(s32[3,2]{1,0:T(4,128)S(1)} %copy.16.plan, f32[1024,256]{1,0:T(8,128)S(1)} %get-tuple-element.34.base, bf16[1024,256]{1,0:T(8,128)(2,1)} %collective-permute-done.arrived), custom_call_target="tpu_custom_call" | custom-call | tf_op jit(solution)/shard_map/pallas_call | solution.py:153
  15.8 0.1 collective-permute-start.1
  15.9 4.2 %collective-permute-done.3.arrived = bf16[1024,256]{1,0:T(8,128)(2,1)S(1)} collective-permute-done((bf16[1024,256]{1,0:T(8,128)(2,1)S(1)}, bf16[1024,256]{1,0:T(8,128)(2,1)S(1)}, u32[]{:S(2)}, u32[]{:S(2)}) %collective-permute-start.3) | collective-permute-done | bytes 524320 | tf_op jit(solution)/shard_map/ppermute | solution.py:23
  20.1 0.7 shard_map.73
  20.8 0.1 collective-permute-start.4
  20.9 0.0 copy-done.2
  20.9 1.5 %shard_map.70 = (f32[1024,256]{1,0:T(8,128)S(1)}, f32[1024,256]{1,0:T(8,128)S(1)}) custom-call(s32[1,3]{1,0:T(1,128)S(1)} %copy-done.3, s32[3,2]{1,0:T(4,128)S(1)} %copy.16.plan, bf16[768,1024]{1,0:T(8,128)(2,1)S(1)} %copy-done, bf16[768,512]{1,0:T(8,128)(2,1)S(1)} %copy-done.2, bf16[1024,256]{1,0:T(8,128)(2,1)S(1)} %get-tuple-element.35.rounded, ...), custom_call_target="tpu_custom_call" | custom-call | tf_op jit(solution)/shard_map/pallas_call | solution.py:153
  22.4 11.0 %collective-permute-done.1.arrived = bf16[1024,256]{1,0:T(8,128)(2,1)S(1)} collective-permute-done((bf16[1024,256]{1,0:T(8,128)(2,1)S(1)}, bf16[1024,256]{1,0:T(8,128)(2,1)S(1)}, u32[]{:S(2)}, u32[]{:S(2)}) %collective-permute-start.1) | collective-permute-done | bytes 524320 | tf_op jit(solution)/shard_map/ppermute | solution.py:23
  33.4 0.7 shard_map.71
  34.1 1.8 %shard_map.72 = (f32[1024,256]{1,0:T(8,128)S(1)}, f32[8,64,256]{2,1,0:T(8,128)S(1)}, f32[8,64,256]{2,1,0:T(8,128)S(1)}) custom-call(s32[1,3]{1,0:T(1,128)S(1)} %copy-done.3, s32[3,2]{1,0:T(4,128)S(1)} %copy.16.plan, bf16[768,1024]{1,0:T(8,128)(2,1)S(1)} %copy-done, bf16[768,512]{1,0:T(8,128)(2,1)S(1)} %copy-done.2, ...), custom_call_target="tpu_custom_call" | custom-call | tf_op jit(solution)/shard_map/pallas_call | solution.py:153
  35.9 0.1 collective-permute-start.6
  36.0 1.5 %shard_map.74 = (f32[1024,256]{1,0:T(8,128)S(1)}, f32[1024,256]{1,0:T(8,128)S(1)}) custom-call(s32[1,3]{1,0:T(1,128)S(1)} %copy-done.3, s32[3,2]{1,0:T(4,128)S(1)} %copy.16.plan, bf16[768,1024]{1,0:T(8,128)(2,1)S(1)} %copy-done, bf16[768,512]{1,0:T(8,128)(2,1)S(1)} %copy-done.2, bf16[1024,256]{1,0:T(8,128)(2,1)S(1)} %get-tuple-element.44.rounded, ...), custom_call_target="tpu_custom_call" | custom-call | tf_op jit(solution)/shard_map/pallas_call | solution.py:153
  37.5 5.1 %collective-permute-done.4.arrived = bf16[1024,256]{1,0:T(8,128)(2,1)S(1)} collective-permute-done((bf16[1024,256]{1,0:T(8,128)(2,1)S(1)}, bf16[1024,256]{1,0:T(8,128)(2,1)S(1)}, u32[]{:S(2)}, u32[]{:S(2)}) %collective-permute-start.4) | collective-permute-done | bytes 524320 | tf_op jit(solution)/shard_map/ppermute | solution.py:23
  42.5 0.7 shard_map.75
  43.2 1.8 %shard_map.76 = (f32[1024,256]{1,0:T(8,128)S(1)}, f32[8,64,256]{2,1,0:T(8,128)S(1)}, f32[8,64,256]{2,1,0:T(8,128)S(1)}) custom-call(s32[1,3]{1,0:T(1,128)S(1)} %copy-done.3, s32[3,2]{1,0:T(4,128)S(1)} %copy.16.plan, bf16[768,1024]{1,0:T(8,128)(2,1)S(1)} %copy-done, bf16[768,512]{1,0:T(8,128)(2,1)S(1)} %copy-done.2, ...), custom_call_target="tpu_custom_call" | custom-call | tf_op jit(solution)/shard_map/pallas_call | solution.py:153
  45.0 0.1 collective-permute-start.8
  45.1 0.3 collective-permute-start.2
  45.4 1.6 %collective-permute-start.5 = (bf16[1024,256]{1,0:T(8,128)(2,1)S(1)}, bf16[1024,256]{1,0:T(8,128)(2,1)S(1)}, u32[]{:S(2)}, u32[]{:S(2)}) collective-permute-start(bf16[1024,256]{1,0:T(8,128)(2,1)S(1)} %get-tuple-element.48.rounded), channel_id=1, source_target_pairs={{0,8},{2,10},{4,12},{6,14},{8,16},{10,18},{12,20},{14,22},{16,24},... | collective-permute-start | bytes 1572872 | tf_op jit(solution)/shard_map/ppermute | solution.py:23
  47.0 0.0 collective-permute-done.6
  47.0 0.1 shard_map.78
  47.0 1.6 %collective-permute-start.7 = (bf16[8,32,256]{2,1,0:T(8,128)(2,1)S(1)}, bf16[8,32,256]{2,1,0:T(8,128)(2,1)S(1)}, u32[]{:S(2)}, u32[]{:S(2)}) collective-permute-start(bf16[8,32,256]{2,1,0:T(8,128)(2,1)S(1)} %get-tuple-element.55), channel_id=1, source_target_pairs={{0,1},{1,0},{2,3},{3,2},{4,5},{5,4},{6,7},{7,6},{8,9},{9,8},{10,11... | collective-permute-start | bytes 393224 | tf_op jit(solution)/shard_map/ppermute | solution.py:28
  48.6 0.0 collective-permute-done.8
  48.6 3.8 %collective-permute-done.7 = bf16[8,32,256]{2,1,0:T(8,128)(2,1)S(1)} collective-permute-done((bf16[8,32,256]{2,1,0:T(8,128)(2,1)S(1)}, bf16[8,32,256]{2,1,0:T(8,128)(2,1)S(1)}, u32[]{:S(2)}, u32[]{:S(2)}) %collective-permute-start.7) | collective-permute-done | bytes 131104 | tf_op jit(solution)/shard_map/ppermute | solution.py:28
  52.4 0.1 shard_map.79
  52.5 0.1 collective-permute-start.9
  52.6 1.5 %collective-permute-start.10 = (bf16[4,32,256]{2,1,0:T(8,128)(2,1)S(1)}, bf16[4,32,256]{2,1,0:T(8,128)(2,1)S(1)}, u32[]{:S(2)}, u32[]{:S(2)}) collective-permute-start(bf16[4,32,256]{2,1,0:T(8,128)(2,1)S(1)} %get-tuple-element.60), channel_id=1, source_target_pairs={{0,1},{1,0},{2,3},{3,2},{4,5},{5,4},{6,7},{7,6},{8,9},{9,8},{10,11... | collective-permute-start | bytes 196616 | tf_op jit(solution)/shard_map/ppermute | solution.py:28
  54.1 1.9 %collective-permute-start.11 = (bf16[4,32,256]{2,1,0:T(8,128)(2,1)S(1)}, bf16[4,32,256]{2,1,0:T(8,128)(2,1)S(1)}, u32[]{:S(2)}, u32[]{:S(2)}) collective-permute-start(bf16[4,32,256]{2,1,0:T(8,128)(2,1)S(1)} %get-tuple-element.61), channel_id=1, source_target_pairs={{0,5},{1,4},{2,7},{3,6},{4,1},{5,0},{6,3},{7,2},{8,13},{9,12},{10,... | collective-permute-start | bytes 196616 | tf_op jit(solution)/shard_map/ppermute | solution.py:258
  56.0 1.2 %collective-permute-done.10.from_x = bf16[4,32,256]{2,1,0:T(8,128)(2,1)S(1)} collective-permute-done((bf16[4,32,256]{2,1,0:T(8,128)(2,1)S(1)}, bf16[4,32,256]{2,1,0:T(8,128)(2,1)S(1)}, u32[]{:S(2)}, u32[]{:S(2)}) %collective-permute-start.10) | collective-permute-done | bytes 65568 | tf_op jit(solution)/shard_map/ppermute | solution.py:28
  57.2 2.1 %collective-permute-done.11.from_xy = bf16[4,32,256]{2,1,0:T(8,128)(2,1)S(1)} collective-permute-done((bf16[4,32,256]{2,1,0:T(8,128)(2,1)S(1)}, bf16[4,32,256]{2,1,0:T(8,128)(2,1)S(1)}, u32[]{:S(2)}, u32[]{:S(2)}) %collective-permute-start.11) | collective-permute-done | bytes 65568 | tf_op jit(solution)/shard_map/ppermute | solution.py:258
  59.3 0.0 collective-permute-done.9.from_y
  59.3 1.6 %collective-permute-start.12 = (bf16[32,512]{1,0:T(8,128)(2,1)S(1)}, bf16[32,512]{1,0:T(8,128)(2,1)S(1)}, u32[]{:S(2)}, u32[]{:S(2)}) collective-permute-start(bf16[32,512]{1,0:T(8,128)(2,1)S(1)} %get-tuple-element.63), channel_id=1, source_target_pairs={{0,8},{2,10},{4,12},{6,14},{8,0},{10,2},{12,4},{14,6},{16,24},{18,... | collective-permute-start | bytes 98312 | tf_op jit(solution)/shard_map/ppermute | solution.py:28
  61.0 1.8 %collective-permute-start.13 = (bf16[32,512]{1,0:T(8,128)(2,1)S(1)}, bf16[32,512]{1,0:T(8,128)(2,1)S(1)}, u32[]{:S(2)}, u32[]{:S(2)}) collective-permute-start(bf16[32,512]{1,0:T(8,128)(2,1)S(1)} %get-tuple-element.64), channel_id=1, source_target_pairs={{0,16},{2,18},{4,20},{6,22},{8,24},{10,26},{12,28},{14,30},{16,0},... | collective-permute-start | bytes 98312 | tf_op jit(solution)/shard_map/ppermute | solution.py:28
  62.7 1.2 %collective-permute-start.14 = (bf16[32,512]{1,0:T(8,128)(2,1)S(1)}, bf16[32,512]{1,0:T(8,128)(2,1)S(1)}, u32[]{:S(2)}, u32[]{:S(2)}) collective-permute-start(bf16[32,512]{1,0:T(8,128)(2,1)S(1)} %get-tuple-element.65), channel_id=1, source_target_pairs={{0,24},{2,26},{4,28},{6,30},{8,16},{10,18},{12,20},{14,22},{16,8},... | collective-permute-start | bytes 98312 | tf_op jit(solution)/shard_map/ppermute | solution.py:28
  63.9 0.0 collective-permute-done.2.refs_1_
  63.9 9.2 %collective-permute-done.5.refs_3_ = bf16[1024,256]{1,0:T(8,128)(2,1)S(1)} collective-permute-done((bf16[1024,256]{1,0:T(8,128)(2,1)S(1)}, bf16[1024,256]{1,0:T(8,128)(2,1)S(1)}, u32[]{:S(2)}, u32[]{:S(2)}) %collective-permute-start.5) | collective-permute-done | bytes 524320 | tf_op jit(solution)/shard_map/ppermute | solution.py:23
  73.1 1.8 %shard_map.77 = bf16[1024,512]{1,0:T(8,128)(2,1)} custom-call(s32[3,2]{1,0:T(4,128)S(1)} %copy.16.plan, f32[1024,256]{1,0:T(8,128)S(1)} %get-tuple-element.42.refs_0_, bf16[1024,256]{1,0:T(8,128)(2,1)S(1)} %collective-permute-done.2.refs_1_, f32[1024,256]{1,0:T(8,128)S(1)} %get-tuple-element.51.refs_2_, bf16[1024,256]{1,0:T(8,128)(2,1)S(1)} %collective-permute-done.5.refs_3_), custom_call_target="tpu_custom_call" | custom-call | tf_op jit(solution)/shard_map/pallas_call | solution.py:153
  74.9 0.0 collective-permute-done.12.refs_0_
  74.9 0.0 collective-permute-done.13.refs_1_
  74.9 0.0 collective-permute-done.14.refs_2_
  74.9 0.7 shard_map.81
  (8 shorter events, 0.1 us)
Async XLA Ops:
  0.6 4.6 %copy-start.4 = (s32[3,2]{0,1:T(2,128)S(1)}, s32[3,2]{0,1:T(2,128)}, u32[]{:S(2)}) copy-start(s32[3,2]{0,1:T(2,128)} %param.8) | copy-start | bytes 76
  0.6 4.7 %copy-start.3 = (s32[1,3]{1,0:T(1,128)S(1)}, s32[1,3]{1,0:T(1,128)}, u32[]{:S(2)}) copy-start(s32[1,3]{1,0:T(1,128)} %order.9) | copy-start | bytes 40
  0.7 4.7 %copy-start = (bf16[768,1024]{1,0:T(8,128)(2,1)S(1)}, bf16[768,1024]{1,0:T(8,128)(2,1)}, u32[]{:S(2)}) copy-start(bf16[768,1024]{1,0:T(8,128)(2,1)} %x.9) | copy-start | bytes 4718596
  2.1 12.5 %collective-permute-start = (bf16[1024,256]{1,0:T(8,128)(2,1)S(1)}, bf16[1024,256]{1,0:T(8,128)(2,1)}, u32[]{:S(2)}, u32[]{:S(2)}) collective-permute-start(bf16[1024,256]{1,0:T(8,128)(2,1)S(1)} %get-tuple-element.67.refs_0_), channel_id=1, source_target_pairs={{0,2},{2,4},{4,6},{6,8},{8,10},{10,12},{12,14},{14,16},{16,18},{18... | collective-permute-start | bytes 1572872 | tf_op jit(solution)/shard_map/ppermute | solution.py:23
  2.6 17.5 %collective-permute-start.3 = (bf16[1024,256]{1,0:T(8,128)(2,1)S(1)}, bf16[1024,256]{1,0:T(8,128)(2,1)S(1)}, u32[]{:S(2)}, u32[]{:S(2)}) collective-permute-start(bf16[1024,256]{1,0:T(8,128)(2,1)S(1)} %get-tuple-element.66.refs_1_), channel_id=1, source_target_pairs={{0,2},{2,4},{4,6},{6,8},{8,10},{10,12},{12,14},{14,16},{16,18},{18... | collective-permute-start | bytes 1572872 | tf_op jit(solution)/shard_map/ppermute | solution.py:23
  5.3 1.1 %copy-start.1 = (bf16[768,512]{1,0:T(8,128)(2,1)S(1)}, bf16[768,512]{1,0:T(8,128)(2,1)}, u32[]{:S(2)}) copy-start(bf16[768,512]{1,0:T(8,128)(2,1)} %t.9) | copy-start | bytes 2359300
  14.6 6.3 %copy-start.2 = (bf16[768,512]{1,0:T(8,128)(2,1)S(1)}, bf16[768,512]{1,0:T(8,128)(2,1)}, u32[]{:S(2)}) copy-start(bf16[768,512]{1,0:T(8,128)(2,1)} %t.9) | copy-start | bytes 2359300
  15.8 17.5 %collective-permute-start.1 = (bf16[1024,256]{1,0:T(8,128)(2,1)S(1)}, bf16[1024,256]{1,0:T(8,128)(2,1)S(1)}, u32[]{:S(2)}, u32[]{:S(2)}) collective-permute-start(bf16[1024,256]{1,0:T(8,128)(2,1)S(1)} %get-tuple-element.35.rounded), channel_id=1, source_target_pairs={{0,4},{2,6},{4,8},{6,10},{8,12},{10,14},{12,16},{14,18},{16,20},{1... | collective-permute-start | bytes 1572872 | tf_op jit(solution)/shard_map/ppermute | solution.py:23
  20.8 21.7 %collective-permute-start.4 = (bf16[1024,256]{1,0:T(8,128)(2,1)S(1)}, bf16[1024,256]{1,0:T(8,128)(2,1)S(1)}, u32[]{:S(2)}, u32[]{:S(2)}) collective-permute-start(bf16[1024,256]{1,0:T(8,128)(2,1)S(1)} %get-tuple-element.44.rounded), channel_id=1, source_target_pairs={{0,4},{2,6},{4,8},{6,10},{8,12},{10,14},{12,16},{14,18},{16,20},{1... | collective-permute-start | bytes 1572872 | tf_op jit(solution)/shard_map/ppermute | solution.py:23
  35.9 11.1 %collective-permute-start.6 = (f32[8,64,256]{2,1,0:T(8,128)S(1)}, f32[8,64,256]{2,1,0:T(8,128)S(1)}, u32[]{:S(2)}, u32[]{:S(2)}) collective-permute-start(f32[8,64,256]{2,1,0:T(8,128)S(1)} %get-tuple-element.53), channel_id=1, source_target_pairs={{0,2},{2,0},{4,6},{6,4},{8,10},{10,8},{12,14},{14,12},{16,18},{18,... | collective-permute-start | bytes 1572872 | tf_op jit(solution)/shard_map/ppermute | solution.py:28
  45.0 3.5 %collective-permute-start.8 = (f32[8,64,256]{2,1,0:T(8,128)S(1)}, f32[8,64,256]{2,1,0:T(8,128)S(1)}, u32[]{:S(2)}, u32[]{:S(2)}) collective-permute-start(f32[8,64,256]{2,1,0:T(8,128)S(1)} %get-tuple-element.57), channel_id=1, source_target_pairs={{0,2},{2,0},{4,6},{6,4},{8,10},{10,8},{12,14},{14,12},{16,18},{18,... | collective-permute-start | bytes 1572872 | tf_op jit(solution)/shard_map/ppermute | solution.py:28
  45.1 18.8 %collective-permute-start.2 = (bf16[1024,256]{1,0:T(8,128)(2,1)S(1)}, bf16[1024,256]{1,0:T(8,128)(2,1)S(1)}, u32[]{:S(2)}, u32[]{:S(2)}) collective-permute-start(bf16[1024,256]{1,0:T(8,128)(2,1)S(1)} %get-tuple-element.39.rounded), channel_id=1, source_target_pairs={{0,8},{2,10},{4,12},{6,14},{8,16},{10,18},{12,20},{14,22},{16,24},... | collective-permute-start | bytes 1572872 | tf_op jit(solution)/shard_map/ppermute | solution.py:23
  45.4 27.7 %collective-permute-start.5 = (bf16[1024,256]{1,0:T(8,128)(2,1)S(1)}, bf16[1024,256]{1,0:T(8,128)(2,1)S(1)}, u32[]{:S(2)}, u32[]{:S(2)}) collective-permute-start(bf16[1024,256]{1,0:T(8,128)(2,1)S(1)} %get-tuple-element.48.rounded), channel_id=1, source_target_pairs={{0,8},{2,10},{4,12},{6,14},{8,16},{10,18},{12,20},{14,22},{16,24},... | collective-permute-start | bytes 1572872 | tf_op jit(solution)/shard_map/ppermute | solution.py:23
  47.0 5.4 %collective-permute-start.7 = (bf16[8,32,256]{2,1,0:T(8,128)(2,1)S(1)}, bf16[8,32,256]{2,1,0:T(8,128)(2,1)S(1)}, u32[]{:S(2)}, u32[]{:S(2)}) collective-permute-start(bf16[8,32,256]{2,1,0:T(8,128)(2,1)S(1)} %get-tuple-element.55), channel_id=1, source_target_pairs={{0,1},{1,0},{2,3},{3,2},{4,5},{5,4},{6,7},{7,6},{8,9},{9,8},{10,11... | collective-permute-start | bytes 393224 | tf_op jit(solution)/shard_map/ppermute | solution.py:28
  52.5 6.8 %collective-permute-start.9 = (bf16[4,32,512]{2,1,0:T(8,128)(2,1)S(1)}, bf16[4,32,512]{2,1,0:T(8,128)(2,1)S(1)}, u32[]{:S(2)}, u32[]{:S(2)}) collective-permute-start(bf16[4,32,512]{2,1,0:T(8,128)(2,1)S(1)} %get-tuple-element.59), channel_id=1, source_target_pairs={{0,4},{2,6},{4,0},{6,2},{8,12},{10,14},{12,8},{14,10},{16,20},{18,... | collective-permute-start | bytes 393224 | tf_op jit(solution)/shard_map/ppermute | solution.py:28
  52.6 4.6 %collective-permute-start.10 = (bf16[4,32,256]{2,1,0:T(8,128)(2,1)S(1)}, bf16[4,32,256]{2,1,0:T(8,128)(2,1)S(1)}, u32[]{:S(2)}, u32[]{:S(2)}) collective-permute-start(bf16[4,32,256]{2,1,0:T(8,128)(2,1)S(1)} %get-tuple-element.60), channel_id=1, source_target_pairs={{0,1},{1,0},{2,3},{3,2},{4,5},{5,4},{6,7},{7,6},{8,9},{9,8},{10,11... | collective-permute-start | bytes 196616 | tf_op jit(solution)/shard_map/ppermute | solution.py:28
  54.1 5.2 %collective-permute-start.11 = (bf16[4,32,256]{2,1,0:T(8,128)(2,1)S(1)}, bf16[4,32,256]{2,1,0:T(8,128)(2,1)S(1)}, u32[]{:S(2)}, u32[]{:S(2)}) collective-permute-start(bf16[4,32,256]{2,1,0:T(8,128)(2,1)S(1)} %get-tuple-element.61), channel_id=1, source_target_pairs={{0,5},{1,4},{2,7},{3,6},{4,1},{5,0},{6,3},{7,2},{8,13},{9,12},{10,... | collective-permute-start | bytes 196616 | tf_op jit(solution)/shard_map/ppermute | solution.py:258
  59.3 15.5 %collective-permute-start.12 = (bf16[32,512]{1,0:T(8,128)(2,1)S(1)}, bf16[32,512]{1,0:T(8,128)(2,1)S(1)}, u32[]{:S(2)}, u32[]{:S(2)}) collective-permute-start(bf16[32,512]{1,0:T(8,128)(2,1)S(1)} %get-tuple-element.63), channel_id=1, source_target_pairs={{0,8},{2,10},{4,12},{6,14},{8,0},{10,2},{12,4},{14,6},{16,24},{18,... | collective-permute-start | bytes 98312 | tf_op jit(solution)/shard_map/ppermute | solution.py:28
  61.0 13.9 %collective-permute-start.13 = (bf16[32,512]{1,0:T(8,128)(2,1)S(1)}, bf16[32,512]{1,0:T(8,128)(2,1)S(1)}, u32[]{:S(2)}, u32[]{:S(2)}) collective-permute-start(bf16[32,512]{1,0:T(8,128)(2,1)S(1)} %get-tuple-element.64), channel_id=1, source_target_pairs={{0,16},{2,18},{4,20},{6,22},{8,24},{10,26},{12,28},{14,30},{16,0},... | collective-permute-start | bytes 98312 | tf_op jit(solution)/shard_map/ppermute | solution.py:28
  62.7 12.2 %collective-permute-start.14 = (bf16[32,512]{1,0:T(8,128)(2,1)S(1)}, bf16[32,512]{1,0:T(8,128)(2,1)S(1)}, u32[]{:S(2)}, u32[]{:S(2)}) collective-permute-start(bf16[32,512]{1,0:T(8,128)(2,1)S(1)} %get-tuple-element.65), channel_id=1, source_target_pairs={{0,24},{2,26},{4,28},{6,30},{8,16},{10,18},{12,20},{14,22},{16,8},... | collective-permute-start | bytes 98312 | tf_op jit(solution)/shard_map/ppermute | solution.py:28

commit v6 on v5

--- a/solution.py
+++ b/solution.py
@@ -29,8 +29,8 @@
 
 
 def shares(plan_ref, step):
-    own = plan_ref[step, 0].astype(jnp.float32)
-    peer = plan_ref[step, 1].astype(jnp.float32)
+    own = plan_ref[0, step].astype(jnp.float32)
+    peer = plan_ref[1, step].astype(jnp.float32)
     own, peer = jnp.full((1, 1), own), jnp.full((1, 1), peer)
     return own / (own + peer), peer / (own + peer)
 
@@ -53,6 +53,13 @@
     batch = x.shape[0] // STEPS
     rows = pl.ds(pl.multiple_of(order[0, step] * batch, batch), batch)
     return x[rows, :], t[rows, columns]
+
+
+def piece_kernel(half, weights, piece, sem):
+    width = piece.shape[1]
+    copy = pltpu.make_async_copy(weights.at[:, half * width:(half + 1) * width], piece, sem)
+    copy.start()
+    copy.wait()
 
 
 def first_kernel(order, plan, x, t, *refs):
@@ -98,13 +105,24 @@
     master[...] = total
 
 
-def finish_kernel(plan, *refs):
+def final_weights(plan, base, arrived):
     _, peer = shares(plan, STEPS - 1)
-    out = refs[-1]
-    width = out.shape[1] // HALVES
-    for i in range(HALVES):
-        base, arrived = refs[2 * i], refs[2 * i + 1]
-        out[:, i * width:(i + 1) * width] = (base[...] + peer * arrived[...].astype(jnp.float32)).astype(jnp.bfloat16)
+    return (base[...] + peer * arrived[...].astype(jnp.float32)).astype(jnp.bfloat16)
+
+
+def finish_kernel(plan, base, arrived, out):
+    out[...] = final_weights(plan, base, arrived)
+
+
+def final_kernel(replicas, plan, base, arrived, whole, *refs):
+    del whole
+    out = refs[-2] if replicas else refs[-1]
+    out[...] = final_weights(plan, base, arrived)
+    if replicas:
+        total = refs[0][...]
+        for piece in refs[1:-2]:
+            total = total + piece[...].astype(jnp.float32)
+        refs[-1][...] = total / replicas
 
 
 def leg_kernel(axis, bit, kept, arrived, keep, give):
@@ -141,21 +159,24 @@
         out[:, width:] = (rows[:, :, width:] + late).reshape(out.shape[0], width).astype(out.dtype)
 
 
-def mean_kernel(replicas, keep, *refs):
-    total = keep[...]
-    for arrived in refs[:-1]:
-        total = total + arrived[...].astype(jnp.float32)
-    refs[-1][...] = total / replicas
-
-
-def call(kernel, ins, outs, scratch=()):
-    in_vmem, in_smem = pl.BlockSpec(memory_space=pltpu.VMEM), pl.BlockSpec(memory_space=pltpu.SMEM)
+IN_VMEM = pl.BlockSpec(memory_space=pltpu.VMEM)
+IN_SMEM = pl.BlockSpec(memory_space=pltpu.SMEM)
+
+
+def call(kernel, ins, outs, scratch=(), out_specs=None, in_place=None, in_specs=None):
+    in_specs = in_specs or [IN_SMEM if array.dtype == jnp.int32 else IN_VMEM for array in ins]
+    aliases = {}
+    if in_place is not None:
+        in_specs[in_place] = pl.BlockSpec(memory_space=pl.ANY)
+        aliases = {in_place: 0}
     return pl.pallas_call(
         kernel,
-        in_specs=[in_smem if array.dtype == jnp.int32 else in_vmem for array in ins],
-        out_specs=[in_vmem] * len(outs),
+        grid=(1,) if out_specs else (),
+        in_specs=in_specs,
+        out_specs=out_specs or [IN_VMEM] * len(outs),
         out_shape=[jax.ShapeDtypeStruct(shape, dtype) for shape, dtype in outs],
         scratch_shapes=list(scratch),
+        input_output_aliases=aliases,
         compiler_params=pltpu.CompilerParams(vmem_limit_bytes=KERNEL_VMEM),
     )(*ins)
 
@@ -190,9 +211,15 @@
     columns = [slice(half * width, (half + 1) * width) for half in range(HALVES)]
     half_f32, half_bf16 = ((din, width), jnp.float32), ((din, width), jnp.bfloat16)
 
+    in_hbm = pltpu.with_memory_space_constraint(weights, pltpu.HBM)
+    plan = plan.T
     pieces, arrived0, rounds0, arrived1, middles = [], [], [], [], []
     for half in range(HALVES):
-        pieces.append(weights[:, columns[half]])
+        (piece,) = call(
+            functools.partial(piece_kernel, half), [in_hbm], [half_bf16], (pltpu.SemaphoreType.DMA,),
+            in_specs=[pl.BlockSpec(memory_space=pltpu.HBM)],
+        )
+        pieces.append(piece)
         arrived0.append(shifted(pieces[half], "gossip", 1))
     firsts = call(first_kernel, [order, plan, inputs, targets] + pieces, [half_f32] * (2 * HALVES))
     for half in range(HALVES):
@@ -262,10 +289,21 @@
         gots = []
         for other, give in enumerate(gives, 1):
             gots.append(flipped(give, "gossip", 4 * other))
-        (mean_weights,) = call(functools.partial(mean_kernel, replicas), [keep] + gots, [(shape, jnp.float32)])
     else:
         mean_weights = scattered_sum(jnp.concatenate(parts, axis=1)) / replicas
-    (replica_weights,) = call(finish_kernel, [plan] + last, [((din, dout), jnp.bfloat16)])
+    result = ((din, dout), jnp.bfloat16)
+    blocks = [pl.BlockSpec((din, width), lambda i, half=half: (0, half)) for half in range(HALVES)]
+    (begun,) = call(finish_kernel, [plan] + last[:2], [result], out_specs=[blocks[0]])
+    ins = [plan] + last[2:] + [begun]
+    if split:
+        replica_weights, mean_weights = call(
+            functools.partial(final_kernel, replicas), ins + [keep] + gots, [result, (shape, jnp.float32)],
+            out_specs=[blocks[1], IN_VMEM], in_place=3,
+        )
+    else:
+        (replica_weights,) = call(
+            functools.partial(final_kernel, None), ins, [result], out_specs=[blocks[1]], in_place=3
+        )
     return (replica_weights[None], mean_weights)
 
 

time: 75.8 us -> 76.2 us (level)
  local copies, waits for them, and re-layouts: 2.63 us -> 0.02 us
  Pallas kernels: 14.5 us -> 16.4 us
  waiting for transfers between devices: 42.7 us -> 44 us
    ppermute x8, waiting for transfers between devices: 4.99 us -> 7.01 us  [flipped(): lax.ppermute(value, axis, [(source, source ^ bit) for source in range(cou...]
    pallas_call x14 -> x16, Pallas kernels: 14.5 us -> 16.4 us  [call(): pl.pallas_call(kernel, grid=(1,) if out_specs else (), in_specs=in_specs,...]
    slice x1 -> x0, local copies, waits for them, and re-layouts: 1.39 us -> none  [steps(): pieces.append(weights[:, columns[half]])]
    unnamed x11 -> x8, local copies, waits for them, and re-layouts: 1.24 us -> 0.02 us
  transfers between devices with their start and end apart: 15 -> 15, of which waited for: 8 -> 10; matrix products, arithmetic and copies ran while one was open for 0% -> 0% of each run, Pallas kernels for 18% -> 18%
where the time goes in v6:
time: 76.2 us; the launch traced here: 76 us
  waiting for transfers between devices  44 us (58%)
  Pallas kernels  16.4 us (22%)
  starting transfers between devices  14.8 us (19%)
  between operations  0.81 us (1%)
    ppermute x6, waiting for transfers between devices, shifted(): return lax.ppermute(value, axis, pairs)  35.1 us
    pallas_call x16, Pallas kernels, call(): pl.pallas_call(kernel, grid=(1,) if out_specs else (), in_specs=in_specs,...  16.4 us
    ppermute x8, starting transfers between devices, flipped(): lax.ppermute(value, axis, [(source, source ^ bit) for source in range(cou...  8.31 us
    ppermute x8, waiting for transfers between devices, flipped(): lax.ppermute(value, axis, [(source, source ^ bit) for source in range(cou...  7.01 us
    ppermute x6, starting transfers between devices, shifted(): return lax.ppermute(value, axis, pairs)  4.93 us
    ppermute x1, waiting for transfers between devices, steps(): from_xy = lax.ppermute(give_xy, ('gossip', 'group'), pairs)  1.9 us
  transfers between devices with their start and end apart: 15, of which 10 were waited for; matrix products, arithmetic and copies ran while one was open for 0% of the time, Pallas kernels for 18%

profile of v6, /device:TPU:0, one launch (start us, length us, event | category | flops | bytes accessed | tf_op | source)
XLA Modules:
  0.0 76.0 jit_solution(13820980621742128255)
XLA Ops:
  0.6 0.0 copy-start
  0.6 0.0 copy-start.1
  0.7 0.0 copy-start.2
  0.7 1.2 %shard_map.68.refs_0_ = bf16[1024,256]{1,0:T(8,128)(2,1)S(1)} custom-call(bf16[1024,512]{1,0:T(8,128)(2,1)} %bitcast.27), custom_call_target="tpu_custom_call" | custom-call | tf_op jit(solution)/shard_map/pallas_call | solution.py:172
  1.9 0.5 collective-permute-start.3
  2.4 1.0 %shard_map.69.refs_1_ = bf16[1024,256]{1,0:T(8,128)(2,1)S(1)} custom-call(bf16[1024,512]{1,0:T(8,128)(2,1)} %bitcast.28), custom_call_target="tpu_custom_call" | custom-call | tf_op jit(solution)/shard_map/pallas_call | solution.py:172
  3.5 2.7 %collective-permute-start = (bf16[1024,256]{1,0:T(8,128)(2,1)S(1)}, bf16[1024,256]{1,0:T(8,128)(2,1)S(1)}, u32[]{:S(2)}, u32[]{:S(2)}) collective-permute-start(bf16[1024,256]{1,0:T(8,128)(2,1)S(1)} %shard_map.69.refs_1_), channel_id=1, source_target_pairs={{0,2},{2,4},{4,6},{6,8},{8,10},{10,12},{12,14},{14,16},{16,18},{18... | collective-permute-start | bytes 1572872 | tf_op jit(solution)/shard_map/ppermute | solution.py:23
  6.2 1.9 %shard_map.70 = (f32[1024,256]{1,0:T(8,128)S(1)}, f32[1024,256]{1,0:T(8,128)S(1)}, f32[1024,256]{1,0:T(8,128)S(1)}, f32[1024,256]{1,0:T(8,128)S(1)}) custom-call(s32[1,3]{1,0:T(1,128)S(1)} %copy-done.3, s32[2,3]{1,0:T(2,128)S(1)} %bitcast.15, bf16[768,1024]{1,0:T(8,128)(2,1)S(1)} %copy-done, bf16[768,512]{1,0:T(8,128)(2,1)S(1)} %copy-done.1, ...), custom_call_target="tpu_custom_call" | custom-call | tf_op jit(solution)/shard_map/pallas_call | solution.py:172
  8.0 6.2 %collective-permute-done.3.arrived = bf16[1024,256]{1,0:T(8,128)(2,1)S(1)} collective-permute-done((bf16[1024,256]{1,0:T(8,128)(2,1)S(1)}, bf16[1024,256]{1,0:T(8,128)(2,1)S(1)}, u32[]{:S(2)}, u32[]{:S(2)}) %collective-permute-start.3) | collective-permute-done | bytes 524320 | tf_op jit(solution)/shard_map/ppermute | solution.py:23
  14.3 0.7 shard_map.75
  15.0 0.1 collective-permute-start.4
  15.0 4.9 %collective-permute-done.arrived = bf16[1024,256]{1,0:T(8,128)(2,1)S(1)} collective-permute-done((bf16[1024,256]{1,0:T(8,128)(2,1)S(1)}, bf16[1024,256]{1,0:T(8,128)(2,1)S(1)}, u32[]{:S(2)}, u32[]{:S(2)}) %collective-permute-start) | collective-permute-done | bytes 524320 | tf_op jit(solution)/shard_map/ppermute | solution.py:23
  19.9 0.7 shard_map.71
  20.6 0.1 collective-permute-start.1
  20.6 1.5 %shard_map.76 = (f32[1024,256]{1,0:T(8,128)S(1)}, f32[1024,256]{1,0:T(8,128)S(1)}) custom-call(s32[1,3]{1,0:T(1,128)S(1)} %copy-done.3, s32[2,3]{1,0:T(2,128)S(1)} %bitcast.18, bf16[768,1024]{1,0:T(8,128)(2,1)S(1)} %copy-done, bf16[768,512]{1,0:T(8,128)(2,1)S(1)} %copy-done.1, bf16[1024,256]{1,0:T(8,128)(2,1)S(1)} %get-tuple-element.46.rounded, ...), custom_call_target="tpu_custom_call" | custom-call | tf_op jit(solution)/shard_map/pallas_call | solution.py:172
  22.1 10.4 %collective-permute-done.4.arrived = bf16[1024,256]{1,0:T(8,128)(2,1)S(1)} collective-permute-done((bf16[1024,256]{1,0:T(8,128)(2,1)S(1)}, bf16[1024,256]{1,0:T(8,128)(2,1)S(1)}, u32[]{:S(2)}, u32[]{:S(2)}) %collective-permute-start.4) | collective-permute-done | bytes 524320 | tf_op jit(solution)/shard_map/ppermute | solution.py:23
  32.5 0.7 shard_map.77
  33.2 1.8 %shard_map.78 = (f32[1024,256]{1,0:T(8,128)S(1)}, f32[8,64,256]{2,1,0:T(8,128)S(1)}, f32[8,64,256]{2,1,0:T(8,128)S(1)}) custom-call(s32[1,3]{1,0:T(1,128)S(1)} %copy-done.3, s32[2,3]{1,0:T(2,128)S(1)} %bitcast.20, bf16[768,1024]{1,0:T(8,128)(2,1)S(1)} %copy-done, bf16[768,512]{1,0:T(8,128)(2,1)S(1)} %copy-done.1, ...), custom_call_target="tpu_custom_call" | custom-call | tf_op jit(solution)/shard_map/pallas_call | solution.py:172
  35.0 0.1 collective-permute-start.6
  35.0 1.5 %shard_map.72 = (f32[1024,256]{1,0:T(8,128)S(1)}, f32[1024,256]{1,0:T(8,128)S(1)}) custom-call(s32[1,3]{1,0:T(1,128)S(1)} %copy-done.3, s32[2,3]{1,0:T(2,128)S(1)} %bitcast.21, bf16[768,1024]{1,0:T(8,128)(2,1)S(1)} %copy-done, bf16[768,512]{1,0:T(8,128)(2,1)S(1)} %copy-done.1, bf16[1024,256]{1,0:T(8,128)(2,1)S(1)} %get-tuple-element.37.rounded, ...), custom_call_target="tpu_custom_call" | custom-call | tf_op jit(solution)/shard_map/pallas_call | solution.py:172
  36.5 5.8 %collective-permute-done.1.arrived = bf16[1024,256]{1,0:T(8,128)(2,1)S(1)} collective-permute-done((bf16[1024,256]{1,0:T(8,128)(2,1)S(1)}, bf16[1024,256]{1,0:T(8,128)(2,1)S(1)}, u32[]{:S(2)}, u32[]{:S(2)}) %collective-permute-start.1) | collective-permute-done | bytes 524320 | tf_op jit(solution)/shard_map/ppermute | solution.py:23
  42.4 0.7 shard_map.73
  43.0 1.8 %shard_map.74 = (f32[1024,256]{1,0:T(8,128)S(1)}, f32[8,64,256]{2,1,0:T(8,128)S(1)}, f32[8,64,256]{2,1,0:T(8,128)S(1)}) custom-call(s32[1,3]{1,0:T(1,128)S(1)} %copy-done.3, s32[2,3]{1,0:T(2,128)S(1)} %bitcast.23, bf16[768,1024]{1,0:T(8,128)(2,1)S(1)} %copy-done, bf16[768,512]{1,0:T(8,128)(2,1)S(1)} %copy-done.1, ...), custom_call_target="tpu_custom_call" | custom-call | tf_op jit(solution)/shard_map/pallas_call | solution.py:172
  44.8 0.1 collective-permute-start.8
  44.9 0.1 collective-permute-start.5
  45.0 1.5 %collective-permute-start.2 = (bf16[1024,256]{1,0:T(8,128)(2,1)S(1)}, bf16[1024,256]{1,0:T(8,128)(2,1)S(1)}, u32[]{:S(2)}, u32[]{:S(2)}) collective-permute-start(bf16[1024,256]{1,0:T(8,128)(2,1)S(1)} %get-tuple-element.41.rounded), channel_id=1, source_target_pairs={{0,8},{2,10},{4,12},{6,14},{8,16},{10,18},{12,20},{14,22},{16,24},... | collective-permute-start | bytes 1572872 | tf_op jit(solution)/shard_map/ppermute | solution.py:23
  46.5 0.0 collective-permute-done.6
  46.5 0.1 shard_map.80
  46.6 1.6 %collective-permute-start.7 = (bf16[8,32,256]{2,1,0:T(8,128)(2,1)S(1)}, bf16[8,32,256]{2,1,0:T(8,128)(2,1)S(1)}, u32[]{:S(2)}, u32[]{:S(2)}) collective-permute-start(bf16[8,32,256]{2,1,0:T(8,128)(2,1)S(1)} %get-tuple-element.57), channel_id=1, source_target_pairs={{0,1},{1,0},{2,3},{3,2},{4,5},{5,4},{6,7},{7,6},{8,9},{9,8},{10,11... | collective-permute-start | bytes 393224 | tf_op jit(solution)/shard_map/ppermute | solution.py:28
  48.1 0.0 collective-permute-done.8
  48.1 3.6 %collective-permute-done.7 = bf16[8,32,256]{2,1,0:T(8,128)(2,1)S(1)} collective-permute-done((bf16[8,32,256]{2,1,0:T(8,128)(2,1)S(1)}, bf16[8,32,256]{2,1,0:T(8,128)(2,1)S(1)}, u32[]{:S(2)}, u32[]{:S(2)}) %collective-permute-start.7) | collective-permute-done | bytes 131104 | tf_op jit(solution)/shard_map/ppermute | solution.py:28
  51.7 0.1 shard_map.81
  51.8 0.5 collective-permute-start.9
  52.4 1.5 %collective-permute-start.10 = (bf16[4,32,256]{2,1,0:T(8,128)(2,1)S(1)}, bf16[4,32,256]{2,1,0:T(8,128)(2,1)S(1)}, u32[]{:S(2)}, u32[]{:S(2)}) collective-permute-start(bf16[4,32,256]{2,1,0:T(8,128)(2,1)S(1)} %get-tuple-element.62), channel_id=1, source_target_pairs={{0,1},{1,0},{2,3},{3,2},{4,5},{5,4},{6,7},{7,6},{8,9},{9,8},{10,11... | collective-permute-start | bytes 196616 | tf_op jit(solution)/shard_map/ppermute | solution.py:28
  53.9 1.5 %collective-permute-start.11 = (bf16[4,32,256]{2,1,0:T(8,128)(2,1)S(1)}, bf16[4,32,256]{2,1,0:T(8,128)(2,1)S(1)}, u32[]{:S(2)}, u32[]{:S(2)}) collective-permute-start(bf16[4,32,256]{2,1,0:T(8,128)(2,1)S(1)} %get-tuple-element.63), channel_id=1, source_target_pairs={{0,5},{1,4},{2,7},{3,6},{4,1},{5,0},{6,3},{7,2},{8,13},{9,12},{10,... | collective-permute-start | bytes 196616 | tf_op jit(solution)/shard_map/ppermute | solution.py:285
  55.4 1.8 %collective-permute-done.10.from_x = bf16[4,32,256]{2,1,0:T(8,128)(2,1)S(1)} collective-permute-done((bf16[4,32,256]{2,1,0:T(8,128)(2,1)S(1)}, bf16[4,32,256]{2,1,0:T(8,128)(2,1)S(1)}, u32[]{:S(2)}, u32[]{:S(2)}) %collective-permute-start.10) | collective-permute-done | bytes 65568 | tf_op jit(solution)/shard_map/ppermute | solution.py:28
  57.2 1.9 %collective-permute-done.11.from_xy = bf16[4,32,256]{2,1,0:T(8,128)(2,1)S(1)} collective-permute-done((bf16[4,32,256]{2,1,0:T(8,128)(2,1)S(1)}, bf16[4,32,256]{2,1,0:T(8,128)(2,1)S(1)}, u32[]{:S(2)}, u32[]{:S(2)}) %collective-permute-start.11) | collective-permute-done | bytes 65568 | tf_op jit(solution)/shard_map/ppermute | solution.py:285
  59.1 0.0 collective-permute-done.9.from_y
  59.1 1.6 %collective-permute-start.12 = (bf16[32,512]{1,0:T(8,128)(2,1)S(1)}, bf16[32,512]{1,0:T(8,128)(2,1)S(1)}, u32[]{:S(2)}, u32[]{:S(2)}) collective-permute-start(bf16[32,512]{1,0:T(8,128)(2,1)S(1)} %get-tuple-element.65), channel_id=1, source_target_pairs={{0,8},{2,10},{4,12},{6,14},{8,0},{10,2},{12,4},{14,6},{16,24},{18,... | collective-permute-start | bytes 98312 | tf_op jit(solution)/shard_map/ppermute | solution.py:28
  60.7 1.8 %collective-permute-start.13 = (bf16[32,512]{1,0:T(8,128)(2,1)S(1)}, bf16[32,512]{1,0:T(8,128)(2,1)S(1)}, u32[]{:S(2)}, u32[]{:S(2)}) collective-permute-start(bf16[32,512]{1,0:T(8,128)(2,1)S(1)} %get-tuple-element.66), channel_id=1, source_target_pairs={{0,16},{2,18},{4,20},{6,22},{8,24},{10,26},{12,28},{14,30},{16,0},... | collective-permute-start | bytes 98312 | tf_op jit(solution)/shard_map/ppermute | solution.py:28
  62.5 1.2 %collective-permute-start.14 = (bf16[32,512]{1,0:T(8,128)(2,1)S(1)}, bf16[32,512]{1,0:T(8,128)(2,1)S(1)}, u32[]{:S(2)}, u32[]{:S(2)}) collective-permute-start(bf16[32,512]{1,0:T(8,128)(2,1)S(1)} %get-tuple-element.67), channel_id=1, source_target_pairs={{0,24},{2,26},{4,28},{6,30},{8,16},{10,18},{12,20},{14,22},{16,8},... | collective-permute-start | bytes 98312 | tf_op jit(solution)/shard_map/ppermute | solution.py:28
  63.7 0.0 collective-permute-done.5.arrived
  63.7 1.5 %shard_map.79.whole = bf16[1024,512]{1,0:T(8,128)(2,1)} custom-call(s32[2,3]{1,0:T(2,128)S(1)} %bitcast.24, f32[1024,256]{1,0:T(8,128)S(1)} %get-tuple-element.53.base, bf16[1024,256]{1,0:T(8,128)(2,1)S(1)} %collective-permute-done.5.arrived), custom_call_target="tpu_custom_call" | custom-call | tf_op jit(solution)/shard_map/pallas_call | solution.py:172
  65.2 7.7 %collective-permute-done.2.arrived = bf16[1024,256]{1,0:T(8,128)(2,1)S(1)} collective-permute-done((bf16[1024,256]{1,0:T(8,128)(2,1)S(1)}, bf16[1024,256]{1,0:T(8,128)(2,1)S(1)}, u32[]{:S(2)}, u32[]{:S(2)}) %collective-permute-start.2) | collective-permute-done | bytes 524320 | tf_op jit(solution)/shard_map/ppermute | solution.py:23
  72.9 1.1 %collective-permute-done.12.refs_1_ = bf16[32,512]{1,0:T(8,128)(2,1)S(1)} collective-permute-done((bf16[32,512]{1,0:T(8,128)(2,1)S(1)}, bf16[32,512]{1,0:T(8,128)(2,1)S(1)}, u32[]{:S(2)}, u32[]{:S(2)}) %collective-permute-start.12) | collective-permute-done | bytes 32800 | tf_op jit(solution)/shard_map/ppermute | solution.py:28
  74.0 0.5 collective-permute-done.13.refs_2_
  74.5 0.0 collective-permute-done.14.refs_3_
  74.5 1.5 %shard_map.83 = (bf16[1024,512]{1,0:T(8,128)(2,1)}, f32[32,512]{1,0:T(8,128)}) custom-call(s32[2,3]{1,0:T(2,128)S(1)} %bitcast.25, f32[1024,256]{1,0:T(8,128)S(1)} %get-tuple-element.44.base, bf16[1024,256]{1,0:T(8,128)(2,1)S(1)} %collective-permute-done.2.arrived, bf16[1024,512]{1,0:T(8,128)(2,1)} %shard_map.79.whole, ...), custom_call_target="tpu_custom_call", output_to_operand_aliasing={{0}: (3, {})} | custom-call | tf_op jit(solution)/shard_map/pallas_call | solution.py:172
  (6 shorter events, 0.1 us)
Async XLA Ops:
  0.6 5.5 %copy-start = (bf16[768,1024]{1,0:T(8,128)(2,1)S(1)}, bf16[768,1024]{1,0:T(8,128)(2,1)}, u32[]{:S(2)}) copy-start(bf16[768,1024]{1,0:T(8,128)(2,1)} %x.9) | copy-start | bytes 4718596
  0.6 5.5 %copy-start.1 = (bf16[768,512]{1,0:T(8,128)(2,1)S(1)}, bf16[768,512]{1,0:T(8,128)(2,1)}, u32[]{:S(2)}) copy-start(bf16[768,512]{1,0:T(8,128)(2,1)} %t.9) | copy-start | bytes 2359300
  0.7 5.5 %copy-start.2 = (s32[3,2]{0,1:T(2,128)S(1)}, s32[3,2]{0,1:T(2,128)}, u32[]{:S(2)}) copy-start(s32[3,2]{0,1:T(2,128)} %param.8) | copy-start | bytes 76
  0.7 5.5 %copy-start.3 = (s32[1,3]{1,0:T(1,128)S(1)}, s32[1,3]{1,0:T(1,128)}, u32[]{:S(2)}) copy-start(s32[1,3]{1,0:T(1,128)} %order.9) | copy-start | bytes 40
  1.9 12.4 %collective-permute-start.3 = (bf16[1024,256]{1,0:T(8,128)(2,1)S(1)}, bf16[1024,256]{1,0:T(8,128)(2,1)S(1)}, u32[]{:S(2)}, u32[]{:S(2)}) collective-permute-start(bf16[1024,256]{1,0:T(8,128)(2,1)S(1)} %shard_map.68.refs_0_), channel_id=1, source_target_pairs={{0,2},{2,4},{4,6},{6,8},{8,10},{10,12},{12,14},{14,16},{16,18},{18... | collective-permute-start | bytes 1572872 | tf_op jit(solution)/shard_map/ppermute | solution.py:23
  3.5 16.4 %collective-permute-start = (bf16[1024,256]{1,0:T(8,128)(2,1)S(1)}, bf16[1024,256]{1,0:T(8,128)(2,1)S(1)}, u32[]{:S(2)}, u32[]{:S(2)}) collective-permute-start(bf16[1024,256]{1,0:T(8,128)(2,1)S(1)} %shard_map.69.refs_1_), channel_id=1, source_target_pairs={{0,2},{2,4},{4,6},{6,8},{8,10},{10,12},{12,14},{14,16},{16,18},{18... | collective-permute-start | bytes 1572872 | tf_op jit(solution)/shard_map/ppermute | solution.py:23
  15.0 17.5 %collective-permute-start.4 = (bf16[1024,256]{1,0:T(8,128)(2,1)S(1)}, bf16[1024,256]{1,0:T(8,128)(2,1)S(1)}, u32[]{:S(2)}, u32[]{:S(2)}) collective-permute-start(bf16[1024,256]{1,0:T(8,128)(2,1)S(1)} %get-tuple-element.46.rounded), channel_id=1, source_target_pairs={{0,4},{2,6},{4,8},{6,10},{8,12},{10,14},{12,16},{14,18},{16,20},{1... | collective-permute-start | bytes 1572872 | tf_op jit(solution)/shard_map/ppermute | solution.py:23
  20.6 21.8 %collective-permute-start.1 = (bf16[1024,256]{1,0:T(8,128)(2,1)S(1)}, bf16[1024,256]{1,0:T(8,128)(2,1)S(1)}, u32[]{:S(2)}, u32[]{:S(2)}) collective-permute-start(bf16[1024,256]{1,0:T(8,128)(2,1)S(1)} %get-tuple-element.37.rounded), channel_id=1, source_target_pairs={{0,4},{2,6},{4,8},{6,10},{8,12},{10,14},{12,16},{14,18},{16,20},{1... | collective-permute-start | bytes 1572872 | tf_op jit(solution)/shard_map/ppermute | solution.py:23
  35.0 11.6 %collective-permute-start.6 = (f32[8,64,256]{2,1,0:T(8,128)S(1)}, f32[8,64,256]{2,1,0:T(8,128)S(1)}, u32[]{:S(2)}, u32[]{:S(2)}) collective-permute-start(f32[8,64,256]{2,1,0:T(8,128)S(1)} %get-tuple-element.55), channel_id=1, source_target_pairs={{0,2},{2,0},{4,6},{6,4},{8,10},{10,8},{12,14},{14,12},{16,18},{18,... | collective-permute-start | bytes 1572872 | tf_op jit(solution)/shard_map/ppermute | solution.py:28
  44.8 3.3 %collective-permute-start.8 = (f32[8,64,256]{2,1,0:T(8,128)S(1)}, f32[8,64,256]{2,1,0:T(8,128)S(1)}, u32[]{:S(2)}, u32[]{:S(2)}) collective-permute-start(f32[8,64,256]{2,1,0:T(8,128)S(1)} %get-tuple-element.59), channel_id=1, source_target_pairs={{0,2},{2,0},{4,6},{6,4},{8,10},{10,8},{12,14},{14,12},{16,18},{18,... | collective-permute-start | bytes 1572872 | tf_op jit(solution)/shard_map/ppermute | solution.py:28
  44.9 18.8 %collective-permute-start.5 = (bf16[1024,256]{1,0:T(8,128)(2,1)S(1)}, bf16[1024,256]{1,0:T(8,128)(2,1)S(1)}, u32[]{:S(2)}, u32[]{:S(2)}) collective-permute-start(bf16[1024,256]{1,0:T(8,128)(2,1)S(1)} %get-tuple-element.50.rounded), channel_id=1, source_target_pairs={{0,8},{2,10},{4,12},{6,14},{8,16},{10,18},{12,20},{14,22},{16,24},... | collective-permute-start | bytes 1572872 | tf_op jit(solution)/shard_map/ppermute | solution.py:23
  45.0 27.9 %collective-permute-start.2 = (bf16[1024,256]{1,0:T(8,128)(2,1)S(1)}, bf16[1024,256]{1,0:T(8,128)(2,1)S(1)}, u32[]{:S(2)}, u32[]{:S(2)}) collective-permute-start(bf16[1024,256]{1,0:T(8,128)(2,1)S(1)} %get-tuple-element.41.rounded), channel_id=1, source_target_pairs={{0,8},{2,10},{4,12},{6,14},{8,16},{10,18},{12,20},{14,22},{16,24},... | collective-permute-start | bytes 1572872 | tf_op jit(solution)/shard_map/ppermute | solution.py:23
  46.6 5.2 %collective-permute-start.7 = (bf16[8,32,256]{2,1,0:T(8,128)(2,1)S(1)}, bf16[8,32,256]{2,1,0:T(8,128)(2,1)S(1)}, u32[]{:S(2)}, u32[]{:S(2)}) collective-permute-start(bf16[8,32,256]{2,1,0:T(8,128)(2,1)S(1)} %get-tuple-element.57), channel_id=1, source_target_pairs={{0,1},{1,0},{2,3},{3,2},{4,5},{5,4},{6,7},{7,6},{8,9},{9,8},{10,11... | collective-permute-start | bytes 393224 | tf_op jit(solution)/shard_map/ppermute | solution.py:28
  51.8 7.2 %collective-permute-start.9 = (bf16[4,32,512]{2,1,0:T(8,128)(2,1)S(1)}, bf16[4,32,512]{2,1,0:T(8,128)(2,1)S(1)}, u32[]{:S(2)}, u32[]{:S(2)}) collective-permute-start(bf16[4,32,512]{2,1,0:T(8,128)(2,1)S(1)} %get-tuple-element.61), channel_id=1, source_target_pairs={{0,4},{2,6},{4,0},{6,2},{8,12},{10,14},{12,8},{14,10},{16,20},{18,... | collective-permute-start | bytes 393224 | tf_op jit(solution)/shard_map/ppermute | solution.py:28
  52.4 4.8 %collective-permute-start.10 = (bf16[4,32,256]{2,1,0:T(8,128)(2,1)S(1)}, bf16[4,32,256]{2,1,0:T(8,128)(2,1)S(1)}, u32[]{:S(2)}, u32[]{:S(2)}) collective-permute-start(bf16[4,32,256]{2,1,0:T(8,128)(2,1)S(1)} %get-tuple-element.62), channel_id=1, source_target_pairs={{0,1},{1,0},{2,3},{3,2},{4,5},{5,4},{6,7},{7,6},{8,9},{9,8},{10,11... | collective-permute-start | bytes 196616 | tf_op jit(solution)/shard_map/ppermute | solution.py:28
  53.9 5.2 %collective-permute-start.11 = (bf16[4,32,256]{2,1,0:T(8,128)(2,1)S(1)}, bf16[4,32,256]{2,1,0:T(8,128)(2,1)S(1)}, u32[]{:S(2)}, u32[]{:S(2)}) collective-permute-start(bf16[4,32,256]{2,1,0:T(8,128)(2,1)S(1)} %get-tuple-element.63), channel_id=1, source_target_pairs={{0,5},{1,4},{2,7},{3,6},{4,1},{5,0},{6,3},{7,2},{8,13},{9,12},{10,... | collective-permute-start | bytes 196616 | tf_op jit(solution)/shard_map/ppermute | solution.py:285
  59.1 14.9 %collective-permute-start.12 = (bf16[32,512]{1,0:T(8,128)(2,1)S(1)}, bf16[32,512]{1,0:T(8,128)(2,1)S(1)}, u32[]{:S(2)}, u32[]{:S(2)}) collective-permute-start(bf16[32,512]{1,0:T(8,128)(2,1)S(1)} %get-tuple-element.65), channel_id=1, source_target_pairs={{0,8},{2,10},{4,12},{6,14},{8,0},{10,2},{12,4},{14,6},{16,24},{18,... | collective-permute-start | bytes 98312 | tf_op jit(solution)/shard_map/ppermute | solution.py:28
  60.7 13.8 %collective-permute-start.13 = (bf16[32,512]{1,0:T(8,128)(2,1)S(1)}, bf16[32,512]{1,0:T(8,128)(2,1)S(1)}, u32[]{:S(2)}, u32[]{:S(2)}) collective-permute-start(bf16[32,512]{1,0:T(8,128)(2,1)S(1)} %get-tuple-element.66), channel_id=1, source_target_pairs={{0,16},{2,18},{4,20},{6,22},{8,24},{10,26},{12,28},{14,30},{16,0},... | collective-permute-start | bytes 98312 | tf_op jit(solution)/shard_map/ppermute | solution.py:28
  62.5 12.0 %collective-permute-start.14 = (bf16[32,512]{1,0:T(8,128)(2,1)S(1)}, bf16[32,512]{1,0:T(8,128)(2,1)S(1)}, u32[]{:S(2)}, u32[]{:S(2)}) collective-permute-start(bf16[32,512]{1,0:T(8,128)(2,1)S(1)} %get-tuple-element.67), channel_id=1, source_target_pairs={{0,24},{2,26},{4,28},{6,30},{8,16},{10,18},{12,20},{14,22},{16,8},... | collective-permute-start | bytes 98312 | tf_op jit(solution)/shard_map/ppermute | solution.py:28

commit v7 on v5

--- a/solution.py
+++ b/solution.py
@@ -29,8 +29,8 @@
 
 
 def shares(plan_ref, step):
-    own = plan_ref[step, 0].astype(jnp.float32)
-    peer = plan_ref[step, 1].astype(jnp.float32)
+    own = plan_ref[0, step].astype(jnp.float32)
+    peer = plan_ref[1, step].astype(jnp.float32)
     own, peer = jnp.full((1, 1), own), jnp.full((1, 1), peer)
     return own / (own + peer), peer / (own + peer)
 
@@ -98,13 +98,9 @@
     master[...] = total
 
 
-def finish_kernel(plan, *refs):
+def finish_kernel(plan, base, arrived, *refs):
     _, peer = shares(plan, STEPS - 1)
-    out = refs[-1]
-    width = out.shape[1] // HALVES
-    for i in range(HALVES):
-        base, arrived = refs[2 * i], refs[2 * i + 1]
-        out[:, i * width:(i + 1) * width] = (base[...] + peer * arrived[...].astype(jnp.float32)).astype(jnp.bfloat16)
+    refs[-1][...] = (base[...] + peer * arrived[...].astype(jnp.float32)).astype(jnp.bfloat16)
 
 
 def leg_kernel(axis, bit, kept, arrived, keep, give):
@@ -143,19 +139,29 @@
 
 def mean_kernel(replicas, keep, *refs):
     total = keep[...]
-    for arrived in refs[:-1]:
-        total = total + arrived[...].astype(jnp.float32)
+    for piece in refs[:-1]:
+        total = total + piece[...].astype(jnp.float32)
     refs[-1][...] = total / replicas
 
 
-def call(kernel, ins, outs, scratch=()):
-    in_vmem, in_smem = pl.BlockSpec(memory_space=pltpu.VMEM), pl.BlockSpec(memory_space=pltpu.SMEM)
+IN_VMEM = pl.BlockSpec(memory_space=pltpu.VMEM)
+IN_SMEM = pl.BlockSpec(memory_space=pltpu.SMEM)
+
+
+def call(kernel, ins, outs, scratch=(), out_specs=None, in_place=None):
+    in_specs = [IN_SMEM if array.dtype == jnp.int32 else IN_VMEM for array in ins]
+    aliases = {}
+    if in_place is not None:
+        in_specs[in_place] = pl.BlockSpec(memory_space=pl.ANY)
+        aliases = {in_place: 0}
     return pl.pallas_call(
         kernel,
-        in_specs=[in_smem if array.dtype == jnp.int32 else in_vmem for array in ins],
-        out_specs=[in_vmem] * len(outs),
+        grid=(1,) if out_specs else (),
+        in_specs=in_specs,
+        out_specs=out_specs or [IN_VMEM] * len(outs),
         out_shape=[jax.ShapeDtypeStruct(shape, dtype) for shape, dtype in outs],
         scratch_shapes=list(scratch),
+        input_output_aliases=aliases,
         compiler_params=pltpu.CompilerParams(vmem_limit_bytes=KERNEL_VMEM),
     )(*ins)
 
@@ -190,9 +196,11 @@
     columns = [slice(half * width, (half + 1) * width) for half in range(HALVES)]
     half_f32, half_bf16 = ((din, width), jnp.float32), ((din, width), jnp.bfloat16)
 
+    plan = plan.T
     pieces, arrived0, rounds0, arrived1, middles = [], [], [], [], []
     for half in range(HALVES):
         pieces.append(weights[:, columns[half]])
+        weights = lax.optimization_barrier(weights)
         arrived0.append(shifted(pieces[half], "gossip", 1))
     firsts = call(first_kernel, [order, plan, inputs, targets] + pieces, [half_f32] * (2 * HALVES))
     for half in range(HALVES):
@@ -262,11 +270,20 @@
         gots = []
         for other, give in enumerate(gives, 1):
             gots.append(flipped(give, "gossip", 4 * other))
-        (mean_weights,) = call(functools.partial(mean_kernel, replicas), [keep] + gots, [(shape, jnp.float32)])
     else:
         mean_weights = scattered_sum(jnp.concatenate(parts, axis=1)) / replicas
-    (replica_weights,) = call(finish_kernel, [plan] + last, [((din, dout), jnp.bfloat16)])
-    return (replica_weights[None], mean_weights)
+    result, replica_weights = ((din, dout), jnp.bfloat16), []
+    for half in range(HALVES):
+        replica_weights = call(
+            finish_kernel,
+            [plan, *last[2 * half:2 * half + 2], *replica_weights],
+            [result],
+            out_specs=[pl.BlockSpec((din, width), lambda i, half=half: (0, half))],
+            in_place=3 if half else None,
+        )
+    if split:
+        (mean_weights,) = call(functools.partial(mean_kernel, replicas), [keep] + gots, [(shape, jnp.float32)])
+    return (replica_weights[0][None], mean_weights)
 
 
 def solution(mesh):

time: 75.8 us -> 75.4 us (level)
  waiting for transfers between devices: 42.7 us -> 41.3 us
  local copies, waits for them, and re-layouts: 2.63 us -> 3.42 us
    ppermute x6, waiting for transfers between devices: 35.7 us -> 33.9 us  [shifted(): return lax.ppermute(value, axis, pairs)]
    slice x1 -> x2, local copies, waits for them, and re-layouts: 1.39 us -> 2.27 us  [steps(): pieces.append(weights[:, columns[half]])]
    pallas_call x14 -> x15, Pallas kernels: 14.5 us -> 14.9 us  [call(): pl.pallas_call(kernel, grid=(1,) if out_specs else (), in_specs=in_specs,...]
  transfers between devices with their start and end apart: 15 -> 15, of which waited for: 8 -> 9; matrix products, arithmetic and copies ran while one was open for 0% -> 1% of each run, Pallas kernels for 18% -> 19%
where the time goes in v7:
time: 75.4 us; the launch traced here: 75.1 us
  waiting for transfers between devices  41.3 us (55%)
  Pallas kernels  14.9 us (20%)
  starting transfers between devices  14.8 us (20%)
  local copies, waits for them, and re-layouts  3.42 us (5%)
  between operations  0.8 us (1%)
    ppermute x6, waiting for transfers between devices, shifted(): return lax.ppermute(value, axis, pairs)  33.9 us
    pallas_call x15, Pallas kernels, call(): pl.pallas_call(kernel, grid=(1,) if out_specs else (), in_specs=in_specs,...  14.9 us
    ppermute x8, starting transfers between devices, flipped(): lax.ppermute(value, axis, [(source, source ^ bit) for source in range(cou...  8.29 us
    ppermute x8, waiting for transfers between devices, flipped(): lax.ppermute(value, axis, [(source, source ^ bit) for source in range(cou...  5.57 us
    ppermute x6, starting transfers between devices, shifted(): return lax.ppermute(value, axis, pairs)  4.93 us
    slice x2, local copies, waits for them, and re-layouts, steps(): pieces.append(weights[:, columns[half]])  2.27 us
    ppermute x1, waiting for transfers between devices, steps(): from_xy = lax.ppermute(give_xy, ('gossip', 'group'), pairs)  1.86 us
    ppermute x1, starting transfers between devices, steps(): from_xy = lax.ppermute(give_xy, ('gossip', 'group'), pairs)  1.53 us
  transfers between devices with their start and end apart: 15, of which 9 were waited for; matrix products, arithmetic and copies ran while one was open for 1% of the time, Pallas kernels for 19%

profile of v7, /device:TPU:0, one launch (start us, length us, event | category | flops | bytes accessed | tf_op | source)
XLA Modules:
  0.0 75.1 jit_solution(7106483170147125758)
XLA Ops:
  0.7 1.2 %slice.8.refs_0_ = bf16[1024,256]{1,0:T(8,128)(2,1)S(1)} slice(bf16[1024,512]{1,0:T(8,128)(2,1)} %bitcast.27), slice={[0:1024], [0:256]} | slice | bytes 1048576 | tf_op jit(solution)/shard_map/slice | solution.py:202
  1.9 0.5 collective-permute-start.3
  2.4 1.1 %slice.9.refs_1_ = bf16[1024,256]{1,0:T(8,128)(2,1)S(1)} slice(bf16[1024,512]{1,0:T(8,128)(2,1)} %bitcast.28), slice={[0:1024], [256:512]} | slice | bytes 1048576 | tf_op jit(solution)/shard_map/slice | solution.py:202
  3.5 2.7 %collective-permute-start = (bf16[1024,256]{1,0:T(8,128)(2,1)S(1)}, bf16[1024,256]{1,0:T(8,128)(2,1)S(1)}, u32[]{:S(2)}, u32[]{:S(2)}) collective-permute-start(bf16[1024,256]{1,0:T(8,128)(2,1)S(1)} %slice.9.refs_1_), channel_id=1, source_target_pairs={{0,2},{2,4},{4,6},{6,8},{8,10},{10,12},{12,14},{14,16},{16,18},{18... | collective-permute-start | bytes 1572872 | tf_op jit(solution)/shard_map/ppermute | solution.py:23
  6.2 0.0 copy-done.4
  6.2 1.1 %copy-done.1 = bf16[768,512]{1,0:T(8,128)(2,1)S(1)} copy-done((bf16[768,512]{1,0:T(8,128)(2,1)S(1)}, bf16[768,512]{1,0:T(8,128)(2,1)}, u32[]{:S(2)}) %copy-start.1) | copy-done | bytes 786456
  7.3 1.9 %shard_map.68 = (f32[1024,256]{1,0:T(8,128)S(1)}, f32[1024,256]{1,0:T(8,128)S(1)}, f32[1024,256]{1,0:T(8,128)S(1)}, f32[1024,256]{1,0:T(8,128)S(1)}) custom-call(s32[1,3]{1,0:T(1,128)S(1)} %copy-done.4, s32[2,3]{1,0:T(2,128)S(1)} %bitcast.15, bf16[768,1024]{1,0:T(8,128)(2,1)S(1)} %copy-done, bf16[768,512]{1,0:T(8,128)(2,1)S(1)} %copy-done.1, ...), custom_call_target="tpu_custom_call" | custom-call | tf_op jit(solution)/shard_map/pallas_call | solution.py:157
  9.2 5.1 %collective-permute-done.3.arrived = bf16[1024,256]{1,0:T(8,128)(2,1)S(1)} collective-permute-done((bf16[1024,256]{1,0:T(8,128)(2,1)S(1)}, bf16[1024,256]{1,0:T(8,128)(2,1)S(1)}, u32[]{:S(2)}, u32[]{:S(2)}) %collective-permute-start.3) | collective-permute-done | bytes 524320 | tf_op jit(solution)/shard_map/ppermute | solution.py:23
  14.3 0.7 shard_map.73
  15.0 0.1 collective-permute-start.4
  15.0 4.8 %collective-permute-done.arrived = bf16[1024,256]{1,0:T(8,128)(2,1)S(1)} collective-permute-done((bf16[1024,256]{1,0:T(8,128)(2,1)S(1)}, bf16[1024,256]{1,0:T(8,128)(2,1)S(1)}, u32[]{:S(2)}, u32[]{:S(2)}) %collective-permute-start) | collective-permute-done | bytes 524320 | tf_op jit(solution)/shard_map/ppermute | solution.py:23
  19.9 0.7 shard_map.69
  20.6 0.1 collective-permute-start.1
  20.6 1.5 %shard_map.74 = (f32[1024,256]{1,0:T(8,128)S(1)}, f32[1024,256]{1,0:T(8,128)S(1)}) custom-call(s32[1,3]{1,0:T(1,128)S(1)} %copy-done.4, s32[2,3]{1,0:T(2,128)S(1)} %bitcast.18, bf16[768,1024]{1,0:T(8,128)(2,1)S(1)} %copy-done, bf16[768,512]{1,0:T(8,128)(2,1)S(1)} %copy-done.2, bf16[1024,256]{1,0:T(8,128)(2,1)S(1)} %get-tuple-element.44.rounded, ...), custom_call_target="tpu_custom_call" | custom-call | tf_op jit(solution)/shard_map/pallas_call | solution.py:157
  22.1 10.4 %collective-permute-done.4.arrived = bf16[1024,256]{1,0:T(8,128)(2,1)S(1)} collective-permute-done((bf16[1024,256]{1,0:T(8,128)(2,1)S(1)}, bf16[1024,256]{1,0:T(8,128)(2,1)S(1)}, u32[]{:S(2)}, u32[]{:S(2)}) %collective-permute-start.4) | collective-permute-done | bytes 524320 | tf_op jit(solution)/shard_map/ppermute | solution.py:23
  32.5 0.7 shard_map.75
  33.2 1.8 %shard_map.76 = (f32[1024,256]{1,0:T(8,128)S(1)}, f32[8,64,256]{2,1,0:T(8,128)S(1)}, f32[8,64,256]{2,1,0:T(8,128)S(1)}) custom-call(s32[1,3]{1,0:T(1,128)S(1)} %copy-done.4, s32[2,3]{1,0:T(2,128)S(1)} %bitcast.20, bf16[768,1024]{1,0:T(8,128)(2,1)S(1)} %copy-done, bf16[768,512]{1,0:T(8,128)(2,1)S(1)} %copy-done.2, ...), custom_call_target="tpu_custom_call" | custom-call | tf_op jit(solution)/shard_map/pallas_call | solution.py:157
  35.0 0.1 collective-permute-start.6
  35.0 1.5 %shard_map.70 = (f32[1024,256]{1,0:T(8,128)S(1)}, f32[1024,256]{1,0:T(8,128)S(1)}) custom-call(s32[1,3]{1,0:T(1,128)S(1)} %copy-done.4, s32[2,3]{1,0:T(2,128)S(1)} %bitcast.21, bf16[768,1024]{1,0:T(8,128)(2,1)S(1)} %copy-done, bf16[768,512]{1,0:T(8,128)(2,1)S(1)} %copy-done.2, bf16[1024,256]{1,0:T(8,128)(2,1)S(1)} %get-tuple-element.35.rounded, ...), custom_call_target="tpu_custom_call" | custom-call | tf_op jit(solution)/shard_map/pallas_call | solution.py:157
  36.5 5.8 %collective-permute-done.1.arrived = bf16[1024,256]{1,0:T(8,128)(2,1)S(1)} collective-permute-done((bf16[1024,256]{1,0:T(8,128)(2,1)S(1)}, bf16[1024,256]{1,0:T(8,128)(2,1)S(1)}, u32[]{:S(2)}, u32[]{:S(2)}) %collective-permute-start.1) | collective-permute-done | bytes 524320 | tf_op jit(solution)/shard_map/ppermute | solution.py:23
  42.3 0.7 shard_map.71
  43.0 1.8 %shard_map.72 = (f32[1024,256]{1,0:T(8,128)S(1)}, f32[8,64,256]{2,1,0:T(8,128)S(1)}, f32[8,64,256]{2,1,0:T(8,128)S(1)}) custom-call(s32[1,3]{1,0:T(1,128)S(1)} %copy-done.4, s32[2,3]{1,0:T(2,128)S(1)} %bitcast.23, bf16[768,1024]{1,0:T(8,128)(2,1)S(1)} %copy-done, bf16[768,512]{1,0:T(8,128)(2,1)S(1)} %copy-done.2, ...), custom_call_target="tpu_custom_call" | custom-call | tf_op jit(solution)/shard_map/pallas_call | solution.py:157
  44.8 0.1 collective-permute-start.8
  44.9 0.1 collective-permute-start.5
  44.9 1.5 %collective-permute-start.2 = (bf16[1024,256]{1,0:T(8,128)(2,1)S(1)}, bf16[1024,256]{1,0:T(8,128)(2,1)S(1)}, u32[]{:S(2)}, u32[]{:S(2)}) collective-permute-start(bf16[1024,256]{1,0:T(8,128)(2,1)S(1)} %get-tuple-element.39.rounded), channel_id=1, source_target_pairs={{0,8},{2,10},{4,12},{6,14},{8,16},{10,18},{12,20},{14,22},{16,24},... | collective-permute-start | bytes 1572872 | tf_op jit(solution)/shard_map/ppermute | solution.py:23
  46.5 0.0 collective-permute-done.6
  46.5 0.1 shard_map.79
  46.5 1.6 %collective-permute-start.7 = (bf16[8,32,256]{2,1,0:T(8,128)(2,1)S(1)}, bf16[8,32,256]{2,1,0:T(8,128)(2,1)S(1)}, u32[]{:S(2)}, u32[]{:S(2)}) collective-permute-start(bf16[8,32,256]{2,1,0:T(8,128)(2,1)S(1)} %get-tuple-element.55), channel_id=1, source_target_pairs={{0,1},{1,0},{2,3},{3,2},{4,5},{5,4},{6,7},{7,6},{8,9},{9,8},{10,11... | collective-permute-start | bytes 393224 | tf_op jit(solution)/shard_map/ppermute | solution.py:28
  48.1 0.0 collective-permute-done.8
  48.1 3.6 %collective-permute-done.7 = bf16[8,32,256]{2,1,0:T(8,128)(2,1)S(1)} collective-permute-done((bf16[8,32,256]{2,1,0:T(8,128)(2,1)S(1)}, bf16[8,32,256]{2,1,0:T(8,128)(2,1)S(1)}, u32[]{:S(2)}, u32[]{:S(2)}) %collective-permute-start.7) | collective-permute-done | bytes 131104 | tf_op jit(solution)/shard_map/ppermute | solution.py:28
  51.7 0.1 shard_map.80
  51.8 0.5 collective-permute-start.9
  52.4 1.5 %collective-permute-start.10 = (bf16[4,32,256]{2,1,0:T(8,128)(2,1)S(1)}, bf16[4,32,256]{2,1,0:T(8,128)(2,1)S(1)}, u32[]{:S(2)}, u32[]{:S(2)}) collective-permute-start(bf16[4,32,256]{2,1,0:T(8,128)(2,1)S(1)} %get-tuple-element.60), channel_id=1, source_target_pairs={{0,1},{1,0},{2,3},{3,2},{4,5},{5,4},{6,7},{7,6},{8,9},{9,8},{10,11... | collective-permute-start | bytes 196616 | tf_op jit(solution)/shard_map/ppermute | solution.py:28
  53.9 1.5 %collective-permute-start.11 = (bf16[4,32,256]{2,1,0:T(8,128)(2,1)S(1)}, bf16[4,32,256]{2,1,0:T(8,128)(2,1)S(1)}, u32[]{:S(2)}, u32[]{:S(2)}) collective-permute-start(bf16[4,32,256]{2,1,0:T(8,128)(2,1)S(1)} %get-tuple-element.61), channel_id=1, source_target_pairs={{0,5},{1,4},{2,7},{3,6},{4,1},{5,0},{6,3},{7,2},{8,13},{9,12},{10,... | collective-permute-start | bytes 196616 | tf_op jit(solution)/shard_map/ppermute | solution.py:266
  55.4 1.8 %collective-permute-done.10.from_x = bf16[4,32,256]{2,1,0:T(8,128)(2,1)S(1)} collective-permute-done((bf16[4,32,256]{2,1,0:T(8,128)(2,1)S(1)}, bf16[4,32,256]{2,1,0:T(8,128)(2,1)S(1)}, u32[]{:S(2)}, u32[]{:S(2)}) %collective-permute-start.10) | collective-permute-done | bytes 65568 | tf_op jit(solution)/shard_map/ppermute | solution.py:28
  57.2 1.9 %collective-permute-done.11.from_xy = bf16[4,32,256]{2,1,0:T(8,128)(2,1)S(1)} collective-permute-done((bf16[4,32,256]{2,1,0:T(8,128)(2,1)S(1)}, bf16[4,32,256]{2,1,0:T(8,128)(2,1)S(1)}, u32[]{:S(2)}, u32[]{:S(2)}) %collective-permute-start.11) | collective-permute-done | bytes 65568 | tf_op jit(solution)/shard_map/ppermute | solution.py:266
  59.0 0.0 collective-permute-done.9.from_y
  59.1 1.6 %collective-permute-start.12 = (bf16[32,512]{1,0:T(8,128)(2,1)S(1)}, bf16[32,512]{1,0:T(8,128)(2,1)S(1)}, u32[]{:S(2)}, u32[]{:S(2)}) collective-permute-start(bf16[32,512]{1,0:T(8,128)(2,1)S(1)} %get-tuple-element.63), channel_id=1, source_target_pairs={{0,8},{2,10},{4,12},{6,14},{8,0},{10,2},{12,4},{14,6},{16,24},{18,... | collective-permute-start | bytes 98312 | tf_op jit(solution)/shard_map/ppermute | solution.py:28
  60.7 1.8 %collective-permute-start.13 = (bf16[32,512]{1,0:T(8,128)(2,1)S(1)}, bf16[32,512]{1,0:T(8,128)(2,1)S(1)}, u32[]{:S(2)}, u32[]{:S(2)}) collective-permute-start(bf16[32,512]{1,0:T(8,128)(2,1)S(1)} %get-tuple-element.64), channel_id=1, source_target_pairs={{0,16},{2,18},{4,20},{6,22},{8,24},{10,26},{12,28},{14,30},{16,0},... | collective-permute-start | bytes 98312 | tf_op jit(solution)/shard_map/ppermute | solution.py:28
  62.5 1.2 %collective-permute-start.14 = (bf16[32,512]{1,0:T(8,128)(2,1)S(1)}, bf16[32,512]{1,0:T(8,128)(2,1)S(1)}, u32[]{:S(2)}, u32[]{:S(2)}) collective-permute-start(bf16[32,512]{1,0:T(8,128)(2,1)S(1)} %get-tuple-element.65), channel_id=1, source_target_pairs={{0,24},{2,26},{4,28},{6,30},{8,16},{10,18},{12,20},{14,22},{16,8},... | collective-permute-start | bytes 98312 | tf_op jit(solution)/shard_map/ppermute | solution.py:28
  63.7 0.0 collective-permute-done.5.arrived
  63.7 1.5 %shard_map.77.refs_0_ = bf16[1024,512]{1,0:T(8,128)(2,1)} custom-call(s32[2,3]{1,0:T(2,128)S(1)} %bitcast.24, f32[1024,256]{1,0:T(8,128)S(1)} %get-tuple-element.51.base, bf16[1024,256]{1,0:T(8,128)(2,1)S(1)} %collective-permute-done.5.arrived), custom_call_target="tpu_custom_call" | custom-call | tf_op jit(solution)/shard_map/pallas_call | solution.py:157
  65.1 7.7 %collective-permute-done.2.arrived = bf16[1024,256]{1,0:T(8,128)(2,1)S(1)} collective-permute-done((bf16[1024,256]{1,0:T(8,128)(2,1)S(1)}, bf16[1024,256]{1,0:T(8,128)(2,1)S(1)}, u32[]{:S(2)}, u32[]{:S(2)}) %collective-permute-start.2) | collective-permute-done | bytes 524320 | tf_op jit(solution)/shard_map/ppermute | solution.py:23
  72.8 1.5 %shard_map.78 = bf16[1024,512]{1,0:T(8,128)(2,1)} custom-call(s32[2,3]{1,0:T(2,128)S(1)} %bitcast.25, f32[1024,256]{1,0:T(8,128)S(1)} %get-tuple-element.42.base, bf16[1024,256]{1,0:T(8,128)(2,1)S(1)} %collective-permute-done.2.arrived, bf16[1024,512]{1,0:T(8,128)(2,1)} %shard_map.77.refs_0_), custom_call_target="tpu_custom_call", output_to_operand_aliasing={{}: (3, {})} | custom-call | tf_op jit(solution)/shard_map/pallas_call | solution.py:157
  74.3 0.0 collective-permute-done.12.refs_0_
  74.3 0.2 collective-permute-done.13.refs_1_
  74.5 0.0 collective-permute-done.14.refs_2_
  74.5 0.6 shard_map.82
  (9 shorter events, 0.1 us)
Async XLA Ops:
  0.6 5.5 %copy-start.4 = (s32[1,3]{1,0:T(1,128)S(1)}, s32[1,3]{1,0:T(1,128)}, u32[]{:S(2)}) copy-start(s32[1,3]{1,0:T(1,128)} %order.9) | copy-start | bytes 40
  0.6 5.5 %copy-start = (bf16[768,1024]{1,0:T(8,128)(2,1)S(1)}, bf16[768,1024]{1,0:T(8,128)(2,1)}, u32[]{:S(2)}) copy-start(bf16[768,1024]{1,0:T(8,128)(2,1)} %x.9) | copy-start | bytes 4718596
  0.7 5.5 %copy-start.3 = (s32[3,2]{0,1:T(2,128)S(1)}, s32[3,2]{0,1:T(2,128)}, u32[]{:S(2)}) copy-start(s32[3,2]{0,1:T(2,128)} %param.8) | copy-start | bytes 76
  1.9 12.4 %collective-permute-start.3 = (bf16[1024,256]{1,0:T(8,128)(2,1)S(1)}, bf16[1024,256]{1,0:T(8,128)(2,1)S(1)}, u32[]{:S(2)}, u32[]{:S(2)}) collective-permute-start(bf16[1024,256]{1,0:T(8,128)(2,1)S(1)} %slice.8.refs_0_), channel_id=1, source_target_pairs={{0,2},{2,4},{4,6},{6,8},{8,10},{10,12},{12,14},{14,16},{16,18},{18... | collective-permute-start | bytes 1572872 | tf_op jit(solution)/shard_map/ppermute | solution.py:23
  3.5 16.4 %collective-permute-start = (bf16[1024,256]{1,0:T(8,128)(2,1)S(1)}, bf16[1024,256]{1,0:T(8,128)(2,1)S(1)}, u32[]{:S(2)}, u32[]{:S(2)}) collective-permute-start(bf16[1024,256]{1,0:T(8,128)(2,1)S(1)} %slice.9.refs_1_), channel_id=1, source_target_pairs={{0,2},{2,4},{4,6},{6,8},{8,10},{10,12},{12,14},{14,16},{16,18},{18... | collective-permute-start | bytes 1572872 | tf_op jit(solution)/shard_map/ppermute | solution.py:23
  6.2 1.1 %copy-start.1 = (bf16[768,512]{1,0:T(8,128)(2,1)S(1)}, bf16[768,512]{1,0:T(8,128)(2,1)}, u32[]{:S(2)}) copy-start(bf16[768,512]{1,0:T(8,128)(2,1)} %t.9) | copy-start | bytes 2359300
  14.2 6.4 %copy-start.2 = (bf16[768,512]{1,0:T(8,128)(2,1)S(1)}, bf16[768,512]{1,0:T(8,128)(2,1)}, u32[]{:S(2)}) copy-start(bf16[768,512]{1,0:T(8,128)(2,1)} %t.9) | copy-start | bytes 2359300
  15.0 17.5 %collective-permute-start.4 = (bf16[1024,256]{1,0:T(8,128)(2,1)S(1)}, bf16[1024,256]{1,0:T(8,128)(2,1)S(1)}, u32[]{:S(2)}, u32[]{:S(2)}) collective-permute-start(bf16[1024,256]{1,0:T(8,128)(2,1)S(1)} %get-tuple-element.44.rounded), channel_id=1, source_target_pairs={{0,4},{2,6},{4,8},{6,10},{8,12},{10,14},{12,16},{14,18},{16,20},{1... | collective-permute-start | bytes 1572872 | tf_op jit(solution)/shard_map/ppermute | solution.py:23
  20.6 21.8 %collective-permute-start.1 = (bf16[1024,256]{1,0:T(8,128)(2,1)S(1)}, bf16[1024,256]{1,0:T(8,128)(2,1)S(1)}, u32[]{:S(2)}, u32[]{:S(2)}) collective-permute-start(bf16[1024,256]{1,0:T(8,128)(2,1)S(1)} %get-tuple-element.35.rounded), channel_id=1, source_target_pairs={{0,4},{2,6},{4,8},{6,10},{8,12},{10,14},{12,16},{14,18},{16,20},{1... | collective-permute-start | bytes 1572872 | tf_op jit(solution)/shard_map/ppermute | solution.py:23
  35.0 11.5 %collective-permute-start.6 = (f32[8,64,256]{2,1,0:T(8,128)S(1)}, f32[8,64,256]{2,1,0:T(8,128)S(1)}, u32[]{:S(2)}, u32[]{:S(2)}) collective-permute-start(f32[8,64,256]{2,1,0:T(8,128)S(1)} %get-tuple-element.53), channel_id=1, source_target_pairs={{0,2},{2,0},{4,6},{6,4},{8,10},{10,8},{12,14},{14,12},{16,18},{18,... | collective-permute-start | bytes 1572872 | tf_op jit(solution)/shard_map/ppermute | solution.py:28
  44.8 3.3 %collective-permute-start.8 = (f32[8,64,256]{2,1,0:T(8,128)S(1)}, f32[8,64,256]{2,1,0:T(8,128)S(1)}, u32[]{:S(2)}, u32[]{:S(2)}) collective-permute-start(f32[8,64,256]{2,1,0:T(8,128)S(1)} %get-tuple-element.57), channel_id=1, source_target_pairs={{0,2},{2,0},{4,6},{6,4},{8,10},{10,8},{12,14},{14,12},{16,18},{18,... | collective-permute-start | bytes 1572872 | tf_op jit(solution)/shard_map/ppermute | solution.py:28
  44.9 18.8 %collective-permute-start.5 = (bf16[1024,256]{1,0:T(8,128)(2,1)S(1)}, bf16[1024,256]{1,0:T(8,128)(2,1)S(1)}, u32[]{:S(2)}, u32[]{:S(2)}) collective-permute-start(bf16[1024,256]{1,0:T(8,128)(2,1)S(1)} %get-tuple-element.48.rounded), channel_id=1, source_target_pairs={{0,8},{2,10},{4,12},{6,14},{8,16},{10,18},{12,20},{14,22},{16,24},... | collective-permute-start | bytes 1572872 | tf_op jit(solution)/shard_map/ppermute | solution.py:23
  44.9 27.9 %collective-permute-start.2 = (bf16[1024,256]{1,0:T(8,128)(2,1)S(1)}, bf16[1024,256]{1,0:T(8,128)(2,1)S(1)}, u32[]{:S(2)}, u32[]{:S(2)}) collective-permute-start(bf16[1024,256]{1,0:T(8,128)(2,1)S(1)} %get-tuple-element.39.rounded), channel_id=1, source_target_pairs={{0,8},{2,10},{4,12},{6,14},{8,16},{10,18},{12,20},{14,22},{16,24},... | collective-permute-start | bytes 1572872 | tf_op jit(solution)/shard_map/ppermute | solution.py:23
  46.5 5.2 %collective-permute-start.7 = (bf16[8,32,256]{2,1,0:T(8,128)(2,1)S(1)}, bf16[8,32,256]{2,1,0:T(8,128)(2,1)S(1)}, u32[]{:S(2)}, u32[]{:S(2)}) collective-permute-start(bf16[8,32,256]{2,1,0:T(8,128)(2,1)S(1)} %get-tuple-element.55), channel_id=1, source_target_pairs={{0,1},{1,0},{2,3},{3,2},{4,5},{5,4},{6,7},{7,6},{8,9},{9,8},{10,11... | collective-permute-start | bytes 393224 | tf_op jit(solution)/shard_map/ppermute | solution.py:28
  51.8 7.2 %collective-permute-start.9 = (bf16[4,32,512]{2,1,0:T(8,128)(2,1)S(1)}, bf16[4,32,512]{2,1,0:T(8,128)(2,1)S(1)}, u32[]{:S(2)}, u32[]{:S(2)}) collective-permute-start(bf16[4,32,512]{2,1,0:T(8,128)(2,1)S(1)} %get-tuple-element.59), channel_id=1, source_target_pairs={{0,4},{2,6},{4,0},{6,2},{8,12},{10,14},{12,8},{14,10},{16,20},{18,... | collective-permute-start | bytes 393224 | tf_op jit(solution)/shard_map/ppermute | solution.py:28
  52.4 4.8 %collective-permute-start.10 = (bf16[4,32,256]{2,1,0:T(8,128)(2,1)S(1)}, bf16[4,32,256]{2,1,0:T(8,128)(2,1)S(1)}, u32[]{:S(2)}, u32[]{:S(2)}) collective-permute-start(bf16[4,32,256]{2,1,0:T(8,128)(2,1)S(1)} %get-tuple-element.60), channel_id=1, source_target_pairs={{0,1},{1,0},{2,3},{3,2},{4,5},{5,4},{6,7},{7,6},{8,9},{9,8},{10,11... | collective-permute-start | bytes 196616 | tf_op jit(solution)/shard_map/ppermute | solution.py:28
  53.9 5.2 %collective-permute-start.11 = (bf16[4,32,256]{2,1,0:T(8,128)(2,1)S(1)}, bf16[4,32,256]{2,1,0:T(8,128)(2,1)S(1)}, u32[]{:S(2)}, u32[]{:S(2)}) collective-permute-start(bf16[4,32,256]{2,1,0:T(8,128)(2,1)S(1)} %get-tuple-element.61), channel_id=1, source_target_pairs={{0,5},{1,4},{2,7},{3,6},{4,1},{5,0},{6,3},{7,2},{8,13},{9,12},{10,... | collective-permute-start | bytes 196616 | tf_op jit(solution)/shard_map/ppermute | solution.py:266
  59.1 15.2 %collective-permute-start.12 = (bf16[32,512]{1,0:T(8,128)(2,1)S(1)}, bf16[32,512]{1,0:T(8,128)(2,1)S(1)}, u32[]{:S(2)}, u32[]{:S(2)}) collective-permute-start(bf16[32,512]{1,0:T(8,128)(2,1)S(1)} %get-tuple-element.63), channel_id=1, source_target_pairs={{0,8},{2,10},{4,12},{6,14},{8,0},{10,2},{12,4},{14,6},{16,24},{18,... | collective-permute-start | bytes 98312 | tf_op jit(solution)/shard_map/ppermute | solution.py:28
  60.7 13.8 %collective-permute-start.13 = (bf16[32,512]{1,0:T(8,128)(2,1)S(1)}, bf16[32,512]{1,0:T(8,128)(2,1)S(1)}, u32[]{:S(2)}, u32[]{:S(2)}) collective-permute-start(bf16[32,512]{1,0:T(8,128)(2,1)S(1)} %get-tuple-element.64), channel_id=1, source_target_pairs={{0,16},{2,18},{4,20},{6,22},{8,24},{10,26},{12,28},{14,30},{16,0},... | collective-permute-start | bytes 98312 | tf_op jit(solution)/shard_map/ppermute | solution.py:28
  62.5 12.0 %collective-permute-start.14 = (bf16[32,512]{1,0:T(8,128)(2,1)S(1)}, bf16[32,512]{1,0:T(8,128)(2,1)S(1)}, u32[]{:S(2)}, u32[]{:S(2)}) collective-permute-start(bf16[32,512]{1,0:T(8,128)(2,1)S(1)} %get-tuple-element.65), channel_id=1, source_target_pairs={{0,24},{2,26},{4,28},{6,30},{8,16},{10,18},{12,20},{14,22},{16,8},... | collective-permute-start | bytes 98312 | tf_op jit(solution)/shard_map/ppermute | solution.py:28

commit v8 on v7

--- a/solution.py
+++ b/solution.py
@@ -28,11 +28,8 @@
     return lax.ppermute(value, axis, [(source, source ^ bit) for source in range(count)])
 
 
-def shares(plan_ref, step):
-    own = plan_ref[0, step].astype(jnp.float32)
-    peer = plan_ref[1, step].astype(jnp.float32)
-    own, peer = jnp.full((1, 1), own), jnp.full((1, 1), peer)
-    return own / (own + peer), peer / (own + peer)
+def shares(mix, step):
+    return mix[2 * step:2 * step + 1, 0:1], mix[2 * step + 1:2 * step + 2, 0:1]
 
 
 def gradient_of(batch_in, batch_out, rounded):
@@ -49,35 +46,39 @@
     return product * fan_scale
 
 
-def shard_of(order, x, t, step, columns):
+def first_kernel(order, plan, x, t, *refs):
+    weights, (mix, *shards), outs = refs[:HALVES], refs[HALVES:HALVES + 2 * STEPS - 1], refs[HALVES + 2 * STEPS - 1:]
     batch = x.shape[0] // STEPS
-    rows = pl.ds(pl.multiple_of(order[0, step] * batch, batch), batch)
-    return x[rows, :], t[rows, columns]
-
-
-def first_kernel(order, plan, x, t, *refs):
-    own, _ = shares(plan, 0)
-    weights, outs = refs[:HALVES], refs[HALVES:]
+    rows = [pl.ds(pl.multiple_of(order[0, step] * batch, batch), batch) for step in range(STEPS)]
+    mix[...] = jnp.zeros_like(mix)
+    for step in range(STEPS):
+        own, peer = [jnp.full((1, mix.shape[1]), plan[i, step].astype(jnp.float32)) for i in range(2)]
+        mix[2 * step:2 * step + 1, :] = own / (own + peer)
+        mix[2 * step + 1:2 * step + 2, :] = peer / (own + peer)
+    own, _ = shares(mix, 0)
     width = weights[0].shape[1]
     for half, w in enumerate(weights):
         base, velocity = outs[2 * half:2 * half + 2]
         columns = slice(half * width, (half + 1) * width)
-        gradient = gradient_of(*shard_of(order, x, t, 0, columns), w[...])
+        gradient = gradient_of(x[rows[0], :], t[rows[0], columns], w[...])
         velocity[...] = gradient
         base[...] = own * w[...].astype(jnp.float32) - learning_rate * gradient
-
-
-def middle_kernel(columns, order, plan, x, t, rounded, master, velocity_in, base, velocity):
-    own, _ = shares(plan, 1)
-    v = momentum_decay * velocity_in[...] + gradient_of(*shard_of(order, x, t, 1, columns), rounded[...])
+    for step in range(1, STEPS):
+        shards[2 * step - 2][...] = x[rows[step], :]
+        shards[2 * step - 1][...] = t[rows[step], :]
+
+
+def middle_kernel(columns, mix, x, t, rounded, master, velocity_in, base, velocity):
+    own, _ = shares(mix, 1)
+    v = momentum_decay * velocity_in[...] + gradient_of(x[...], t[:, columns], rounded[...])
     velocity[...] = v
     base[...] = own * master[...] - learning_rate * v
 
 
-def last_kernel(columns, split, order, plan, x, t, rounded, master, velocity_in, base, *outs):
-    own, last_peer = shares(plan, STEPS - 1)
+def last_kernel(columns, split, mix, x, t, rounded, master, velocity_in, base, *outs):
+    own, last_peer = shares(mix, STEPS - 1)
     r = rounded[...]
-    v = momentum_decay * velocity_in[...] + gradient_of(*shard_of(order, x, t, STEPS - 1, columns), r)
+    v = momentum_decay * velocity_in[...] + gradient_of(x[...], t[:, columns], r)
     b = own * master[...] - learning_rate * v
     base[...] = b
     part = b + last_peer * r.astype(jnp.float32)
@@ -91,15 +92,15 @@
     give[...] = held[:, pl.ds(1 - mine, 1)].reshape(give.shape)
 
 
-def round_kernel(step, plan, base, arrived, rounded, master):
-    _, peer = shares(plan, step)
+def round_kernel(step, mix, base, arrived, rounded, master):
+    _, peer = shares(mix, step)
     total = base[...] + peer * arrived[...].astype(jnp.float32)
     rounded[...] = total.astype(jnp.bfloat16)
     master[...] = total
 
 
-def finish_kernel(plan, base, arrived, *refs):
-    _, peer = shares(plan, STEPS - 1)
+def finish_kernel(mix, base, arrived, *refs):
+    _, peer = shares(mix, STEPS - 1)
     refs[-1][...] = (base[...] + peer * arrived[...].astype(jnp.float32)).astype(jnp.bfloat16)
 
 
@@ -202,17 +203,23 @@
         pieces.append(weights[:, columns[half]])
         weights = lax.optimization_barrier(weights)
         arrived0.append(shifted(pieces[half], "gossip", 1))
-    firsts = call(first_kernel, [order, plan, inputs, targets] + pieces, [half_f32] * (2 * HALVES))
+    batch = inputs.shape[0] // STEPS
+    shards = [((batch, din), inputs.dtype), ((batch, dout), targets.dtype)] * (STEPS - 1)
+    outs = [((-(-2 * STEPS // 8) * 8, 128), jnp.float32)] + shards + [half_f32] * (2 * HALVES)
+    mix, *rest = call(first_kernel, [order, plan, inputs, targets] + pieces, outs)
+    shards, firsts = rest[:len(shards)], rest[len(shards):]
     for half in range(HALVES):
         rounds0.append(
-            call(functools.partial(round_kernel, 0), [plan, firsts[2 * half], arrived0[half]], [half_bf16, half_f32])
+            call(
+                functools.partial(round_kernel, 0), [mix, firsts[2 * half], arrived0[half]], [half_bf16, half_f32]
+            )
         )
         arrived1.append(shifted(rounds0[half][0], "gossip", 2))
     for half in range(HALVES):
         middles.append(
             call(
                 functools.partial(middle_kernel, columns[half]),
-                [order, plan, inputs, targets] + list(rounds0[half]) + [firsts[2 * half + 1]],
+                [mix] + shards[:2] + list(rounds0[half]) + [firsts[2 * half + 1]],
                 [half_f32] * 2,
             )
         )
@@ -220,7 +227,7 @@
     for half in range(HALVES):
         base1, velocity1 = middles[half]
         rounded2, master2 = call(
-            functools.partial(round_kernel, 1), [plan, base1, arrived1[half]], [half_bf16, half_f32]
+            functools.partial(round_kernel, 1), [mix, base1, arrived1[half]], [half_bf16, half_f32]
         )
         arrived2 = shifted(rounded2, "gossip", 4)
         outs, scratch = [half_f32] * 2, ()
@@ -230,7 +237,7 @@
             scratch = (pltpu.VMEM((pair[0], 2) + pair[1:], jnp.float32),)
         base2, *part = call(
             functools.partial(last_kernel, columns[half], split),
-            [order, plan, inputs, targets, rounded2, master2, velocity1],
+            [mix] + shards[2:] + [rounded2, master2, velocity1],
             outs,
             scratch,
         )
@@ -276,7 +283,7 @@
     for half in range(HALVES):
         replica_weights = call(
             finish_kernel,
-            [plan, *last[2 * half:2 * half + 2], *replica_weights],
+            [mix, *last[2 * half:2 * half + 2], *replica_weights],
             [result],
             out_specs=[pl.BlockSpec((din, width), lambda i, half=half: (0, half))],
             in_place=3 if half else None,

time: 75.4 us -> 74.5 us (0.988)
  Pallas kernels: 14.9 us -> 10.5 us
  waiting for transfers between devices: 41.3 us -> 44.6 us
    pallas_call x15, Pallas kernels: 14.9 us -> 10.5 us  [call(): pl.pallas_call(kernel, grid=(1,) if out_specs else (), in_specs=in_specs,...]
    ppermute x6, waiting for transfers between devices: 33.9 us -> 36.8 us  [shifted(): return lax.ppermute(value, axis, pairs)]
  transfers between devices with their start and end apart: 15 -> 15, of which waited for: 9 -> 9; matrix products, arithmetic and copies ran while one was open for 1% -> 1% of each run, Pallas kernels for 19% -> 13%
where the time goes in v8:
time: 74.5 us; the launch traced here: 74.2 us
  waiting for transfers between devices  44.6 us (60%)
  starting transfers between devices  15 us (20%)
  Pallas kernels  10.5 us (14%)
  local copies, waits for them, and re-layouts  3.41 us (5%)
  between operations  0.76 us (1%)
    ppermute x6, waiting for transfers between devices, shifted(): return lax.ppermute(value, axis, pairs)  36.8 us
    pallas_call x15, Pallas kernels, call(): pl.pallas_call(kernel, grid=(1,) if out_specs else (), in_specs=in_specs,...  10.5 us
    ppermute x8, starting transfers between devices, flipped(): lax.ppermute(value, axis, [(source, source ^ bit) for source in range(cou...  8.45 us
    ppermute x8, waiting for transfers between devices, flipped(): lax.ppermute(value, axis, [(source, source ^ bit) for source in range(cou...  5.43 us
    ppermute x6, starting transfers between devices, shifted(): return lax.ppermute(value, axis, pairs)  5.13 us
    ppermute x1, waiting for transfers between devices, steps(): from_xy = lax.ppermute(give_xy, ('gossip', 'group'), pairs)  2.39 us
    slice x2, local copies, waits for them, and re-layouts, steps(): pieces.append(weights[:, columns[half]])  2.27 us
  transfers between devices with their start and end apart: 15, of which 9 were waited for; matrix products, arithmetic and copies ran while one was open for 1% of the time, Pallas kernels for 13%

profile of v8, /device:TPU:0, one launch (start us, length us, event | category | flops | bytes accessed | tf_op | source)
XLA Modules:
  0.0 74.2 jit_solution(13355237182326102704)
XLA Ops:
  0.7 1.2 %slice.8.refs_0_ = bf16[1024,256]{1,0:T(8,128)(2,1)S(1)} slice(bf16[1024,512]{1,0:T(8,128)(2,1)} %bitcast.17), slice={[0:1024], [0:256]} | slice | bytes 1048576 | tf_op jit(solution)/shard_map/slice | solution.py:203
  1.9 0.5 collective-permute-start.3
  2.4 1.1 %slice.9.refs_1_ = bf16[1024,256]{1,0:T(8,128)(2,1)S(1)} slice(bf16[1024,512]{1,0:T(8,128)(2,1)} %bitcast.18), slice={[0:1024], [256:512]} | slice | bytes 1048576 | tf_op jit(solution)/shard_map/slice | solution.py:203
  3.5 2.7 %collective-permute-start = (bf16[1024,256]{1,0:T(8,128)(2,1)S(1)}, bf16[1024,256]{1,0:T(8,128)(2,1)S(1)}, u32[]{:S(2)}, u32[]{:S(2)}) collective-permute-start(bf16[1024,256]{1,0:T(8,128)(2,1)S(1)} %slice.9.refs_1_), channel_id=1, source_target_pairs={{0,2},{2,4},{4,6},{6,8},{8,10},{10,12},{12,14},{14,16},{16,18},{18... | collective-permute-start | bytes 1572872 | tf_op jit(solution)/shard_map/ppermute | solution.py:23
  6.2 0.0 copy-done.3
  6.2 1.1 %copy-done.1 = bf16[768,512]{1,0:T(8,128)(2,1)S(1)} copy-done((bf16[768,512]{1,0:T(8,128)(2,1)S(1)}, bf16[768,512]{1,0:T(8,128)(2,1)}, u32[]{:S(2)}) %copy-start.1) | copy-done | bytes 786456
  7.3 1.9 %shard_map.68 = (f32[8,128]{1,0:T(8,128)S(1)}, bf16[256,1024]{1,0:T(8,128)(2,1)S(1)}, bf16[256,512]{1,0:T(8,128)(2,1)S(1)}, bf16[256,1024]{1,0:T(8,128)(2,1)S(1)...) custom-call(s32[1,3]{1,0:T(1,128)S(1)} %copy-done.3, ...), custom_call_target="tpu_custom_call" | custom-call | tf_op jit(solution)/shard_map/pallas_call | solution.py:158
  9.2 5.0 %collective-permute-done.3.arrived = bf16[1024,256]{1,0:T(8,128)(2,1)S(1)} collective-permute-done((bf16[1024,256]{1,0:T(8,128)(2,1)S(1)}, bf16[1024,256]{1,0:T(8,128)(2,1)S(1)}, u32[]{:S(2)}, u32[]{:S(2)}) %collective-permute-start.3) | collective-permute-done | bytes 524320 | tf_op jit(solution)/shard_map/ppermute | solution.py:23
  14.3 0.3 shard_map.73
  14.6 0.1 collective-permute-start.4
  14.6 5.2 %collective-permute-done.arrived = bf16[1024,256]{1,0:T(8,128)(2,1)S(1)} collective-permute-done((bf16[1024,256]{1,0:T(8,128)(2,1)S(1)}, bf16[1024,256]{1,0:T(8,128)(2,1)S(1)}, u32[]{:S(2)}, u32[]{:S(2)}) %collective-permute-start) | collective-permute-done | bytes 524320 | tf_op jit(solution)/shard_map/ppermute | solution.py:23
  19.9 0.3 shard_map.69
  20.2 0.3 collective-permute-start.1
  20.4 0.9 %shard_map.74 = (f32[1024,256]{1,0:T(8,128)S(1)}, f32[1024,256]{1,0:T(8,128)S(1)}) custom-call(f32[8,128]{1,0:T(8,128)S(1)} %get-tuple-element.39.mix, bf16[256,1024]{1,0:T(8,128)(2,1)S(1)} %get-tuple-element.42.x, bf16[256,512]{1,0:T(8,128)(2,1)S(1)} %get-tuple-element.43.t, bf16[1024,256]{1,0:T(8,128)(2,1)S(1)} %get-tuple-element.54.rounded, ...), custom_call_target="tpu_custom_call" | custom-call | tf_op jit(solution)/shard_map/pallas_call | solution.py:158
  21.4 10.7 %collective-permute-done.4.arrived = bf16[1024,256]{1,0:T(8,128)(2,1)S(1)} collective-permute-done((bf16[1024,256]{1,0:T(8,128)(2,1)S(1)}, bf16[1024,256]{1,0:T(8,128)(2,1)S(1)}, u32[]{:S(2)}, u32[]{:S(2)}) %collective-permute-start.4) | collective-permute-done | bytes 524320 | tf_op jit(solution)/shard_map/ppermute | solution.py:23
  32.1 0.3 shard_map.75
  32.4 1.2 %shard_map.76 = (f32[1024,256]{1,0:T(8,128)S(1)}, f32[8,64,256]{2,1,0:T(8,128)S(1)}, f32[8,64,256]{2,1,0:T(8,128)S(1)}) custom-call(f32[8,128]{1,0:T(8,128)S(1)} %get-tuple-element.39.mix, bf16[256,1024]{1,0:T(8,128)(2,1)S(1)} %get-tuple-element.40.x, bf16[256,512]{1,0:T(8,128)(2,1)S(1)} %get-tuple-element.41.t, ...), custom_call_target="tpu_custom_call" | custom-call | tf_op jit(solution)/shard_map/pallas_call | solution.py:158
  33.7 0.1 collective-permute-start.6
  33.7 0.9 %shard_map.70 = (f32[1024,256]{1,0:T(8,128)S(1)}, f32[1024,256]{1,0:T(8,128)S(1)}) custom-call(f32[8,128]{1,0:T(8,128)S(1)} %get-tuple-element.39.mix, bf16[256,1024]{1,0:T(8,128)(2,1)S(1)} %get-tuple-element.42.x, bf16[256,512]{1,0:T(8,128)(2,1)S(1)} %get-tuple-element.43.t, bf16[1024,256]{1,0:T(8,128)(2,1)S(1)} %get-tuple-element.45.rounded, ...), custom_call_target="tpu_custom_call" | custom-call | tf_op jit(solution)/shard_map/pallas_call | solution.py:158
  34.7 7.7 %collective-permute-done.1.arrived = bf16[1024,256]{1,0:T(8,128)(2,1)S(1)} collective-permute-done((bf16[1024,256]{1,0:T(8,128)(2,1)S(1)}, bf16[1024,256]{1,0:T(8,128)(2,1)S(1)}, u32[]{:S(2)}, u32[]{:S(2)}) %collective-permute-start.1) | collective-permute-done | bytes 524320 | tf_op jit(solution)/shard_map/ppermute | solution.py:23
  42.3 0.3 shard_map.71
  42.7 1.2 %shard_map.72 = (f32[1024,256]{1,0:T(8,128)S(1)}, f32[8,64,256]{2,1,0:T(8,128)S(1)}, f32[8,64,256]{2,1,0:T(8,128)S(1)}) custom-call(f32[8,128]{1,0:T(8,128)S(1)} %get-tuple-element.39.mix, bf16[256,1024]{1,0:T(8,128)(2,1)S(1)} %get-tuple-element.40.x, bf16[256,512]{1,0:T(8,128)(2,1)S(1)} %get-tuple-element.41.t, ...), custom_call_target="tpu_custom_call" | custom-call | tf_op jit(solution)/shard_map/pallas_call | solution.py:158
  43.9 0.1 collective-permute-start.8
  44.0 0.1 collective-permute-start.5
  44.0 1.5 %collective-permute-start.2 = (bf16[1024,256]{1,0:T(8,128)(2,1)S(1)}, bf16[1024,256]{1,0:T(8,128)(2,1)S(1)}, u32[]{:S(2)}, u32[]{:S(2)}) collective-permute-start(bf16[1024,256]{1,0:T(8,128)(2,1)S(1)} %get-tuple-element.49.rounded), channel_id=1, source_target_pairs={{0,8},{2,10},{4,12},{6,14},{8,16},{10,18},{12,20},{14,22},{16,24},... | collective-permute-start | bytes 1572872 | tf_op jit(solution)/shard_map/ppermute | solution.py:23
  45.6 0.0 collective-permute-done.6
  45.6 0.1 shard_map.79
  45.7 1.6 %collective-permute-start.7 = (bf16[8,32,256]{2,1,0:T(8,128)(2,1)S(1)}, bf16[8,32,256]{2,1,0:T(8,128)(2,1)S(1)}, u32[]{:S(2)}, u32[]{:S(2)}) collective-permute-start(bf16[8,32,256]{2,1,0:T(8,128)(2,1)S(1)} %get-tuple-element.65), channel_id=1, source_target_pairs={{0,1},{1,0},{2,3},{3,2},{4,5},{5,4},{6,7},{7,6},{8,9},{9,8},{10,11... | collective-permute-start | bytes 393224 | tf_op jit(solution)/shard_map/ppermute | solution.py:28
  47.2 0.0 collective-permute-done.8
  47.2 3.5 %collective-permute-done.7 = bf16[8,32,256]{2,1,0:T(8,128)(2,1)S(1)} collective-permute-done((bf16[8,32,256]{2,1,0:T(8,128)(2,1)S(1)}, bf16[8,32,256]{2,1,0:T(8,128)(2,1)S(1)}, u32[]{:S(2)}, u32[]{:S(2)}) %collective-permute-start.7) | collective-permute-done | bytes 131104 | tf_op jit(solution)/shard_map/ppermute | solution.py:28
  50.7 0.1 shard_map.80
  50.8 0.7 collective-permute-start.9
  51.5 1.5 %collective-permute-start.10 = (bf16[4,32,256]{2,1,0:T(8,128)(2,1)S(1)}, bf16[4,32,256]{2,1,0:T(8,128)(2,1)S(1)}, u32[]{:S(2)}, u32[]{:S(2)}) collective-permute-start(bf16[4,32,256]{2,1,0:T(8,128)(2,1)S(1)} %get-tuple-element.70), channel_id=1, source_target_pairs={{0,1},{1,0},{2,3},{3,2},{4,5},{5,4},{6,7},{7,6},{8,9},{9,8},{10,11... | collective-permute-start | bytes 196616 | tf_op jit(solution)/shard_map/ppermute | solution.py:28
  52.9 1.4 %collective-permute-start.11 = (bf16[4,32,256]{2,1,0:T(8,128)(2,1)S(1)}, bf16[4,32,256]{2,1,0:T(8,128)(2,1)S(1)}, u32[]{:S(2)}, u32[]{:S(2)}) collective-permute-start(bf16[4,32,256]{2,1,0:T(8,128)(2,1)S(1)} %get-tuple-element.71), channel_id=1, source_target_pairs={{0,5},{1,4},{2,7},{3,6},{4,1},{5,0},{6,3},{7,2},{8,13},{9,12},{10,... | collective-permute-start | bytes 196616 | tf_op jit(solution)/shard_map/ppermute | solution.py:273
  54.3 1.4 %collective-permute-done.10.from_x = bf16[4,32,256]{2,1,0:T(8,128)(2,1)S(1)} collective-permute-done((bf16[4,32,256]{2,1,0:T(8,128)(2,1)S(1)}, bf16[4,32,256]{2,1,0:T(8,128)(2,1)S(1)}, u32[]{:S(2)}, u32[]{:S(2)}) %collective-permute-start.10) | collective-permute-done | bytes 65568 | tf_op jit(solution)/shard_map/ppermute | solution.py:28
  55.7 2.4 %collective-permute-done.11.from_xy = bf16[4,32,256]{2,1,0:T(8,128)(2,1)S(1)} collective-permute-done((bf16[4,32,256]{2,1,0:T(8,128)(2,1)S(1)}, bf16[4,32,256]{2,1,0:T(8,128)(2,1)S(1)}, u32[]{:S(2)}, u32[]{:S(2)}) %collective-permute-start.11) | collective-permute-done | bytes 65568 | tf_op jit(solution)/shard_map/ppermute | solution.py:273
  58.1 0.0 collective-permute-done.9.from_y
  58.2 1.6 %collective-permute-start.12 = (bf16[32,512]{1,0:T(8,128)(2,1)S(1)}, bf16[32,512]{1,0:T(8,128)(2,1)S(1)}, u32[]{:S(2)}, u32[]{:S(2)}) collective-permute-start(bf16[32,512]{1,0:T(8,128)(2,1)S(1)} %get-tuple-element.73), channel_id=1, source_target_pairs={{0,8},{2,10},{4,12},{6,14},{8,0},{10,2},{12,4},{14,6},{16,24},{18,... | collective-permute-start | bytes 98312 | tf_op jit(solution)/shard_map/ppermute | solution.py:28
  59.8 1.8 %collective-permute-start.13 = (bf16[32,512]{1,0:T(8,128)(2,1)S(1)}, bf16[32,512]{1,0:T(8,128)(2,1)S(1)}, u32[]{:S(2)}, u32[]{:S(2)}) collective-permute-start(bf16[32,512]{1,0:T(8,128)(2,1)S(1)} %get-tuple-element.74), channel_id=1, source_target_pairs={{0,16},{2,18},{4,20},{6,22},{8,24},{10,26},{12,28},{14,30},{16,0},... | collective-permute-start | bytes 98312 | tf_op jit(solution)/shard_map/ppermute | solution.py:28
  61.6 1.2 %collective-permute-start.14 = (bf16[32,512]{1,0:T(8,128)(2,1)S(1)}, bf16[32,512]{1,0:T(8,128)(2,1)S(1)}, u32[]{:S(2)}, u32[]{:S(2)}) collective-permute-start(bf16[32,512]{1,0:T(8,128)(2,1)S(1)} %get-tuple-element.75), channel_id=1, source_target_pairs={{0,24},{2,26},{4,28},{6,30},{8,16},{10,18},{12,20},{14,22},{16,8},... | collective-permute-start | bytes 98312 | tf_op jit(solution)/shard_map/ppermute | solution.py:28
  62.7 0.0 collective-permute-done.5.arrived
  62.7 1.1 %shard_map.77.refs_0_ = bf16[1024,512]{1,0:T(8,128)(2,1)} custom-call(f32[8,128]{1,0:T(8,128)S(1)} %get-tuple-element.39.mix, f32[1024,256]{1,0:T(8,128)S(1)} %get-tuple-element.61.base, bf16[1024,256]{1,0:T(8,128)(2,1)S(1)} %collective-permute-done.5.arrived), custom_call_target="tpu_custom_call" | custom-call | tf_op jit(solution)/shard_map/pallas_call | solution.py:158
  63.8 8.1 %collective-permute-done.2.arrived = bf16[1024,256]{1,0:T(8,128)(2,1)S(1)} collective-permute-done((bf16[1024,256]{1,0:T(8,128)(2,1)S(1)}, bf16[1024,256]{1,0:T(8,128)(2,1)S(1)}, u32[]{:S(2)}, u32[]{:S(2)}) %collective-permute-start.2) | collective-permute-done | bytes 524320 | tf_op jit(solution)/shard_map/ppermute | solution.py:23
  71.9 1.1 %shard_map.78 = bf16[1024,512]{1,0:T(8,128)(2,1)} custom-call(f32[8,128]{1,0:T(8,128)S(1)} %get-tuple-element.39.mix, f32[1024,256]{1,0:T(8,128)S(1)} %get-tuple-element.52.base, bf16[1024,256]{1,0:T(8,128)(2,1)S(1)} %collective-permute-done.2.arrived, bf16[1024,512]{1,0:T(8,128)(2,1)} %shard_map.77.refs_0_), custom_call_target="tpu_custom_call", output_to_operand_aliasing={{}: (3, {})} | custom-call | tf_op jit(solution)/shard_map/pallas_call | solution.py:158
  73.0 0.0 collective-permute-done.12.refs_0_
  73.1 0.5 collective-permute-done.13.refs_1_
  73.6 0.0 collective-permute-done.14.refs_2_
  73.6 0.7 shard_map.82
  (7 shorter events, 0.1 us)
Async XLA Ops:
  0.6 5.5 %copy-start.3 = (s32[1,3]{1,0:T(1,128)S(1)}, s32[1,3]{1,0:T(1,128)}, u32[]{:S(2)}) copy-start(s32[1,3]{1,0:T(1,128)} %order.1) | copy-start | bytes 40
  0.6 5.5 %copy-start.2 = (s32[3,2]{0,1:T(2,128)S(1)}, s32[3,2]{0,1:T(2,128)}, u32[]{:S(2)}) copy-start(s32[3,2]{0,1:T(2,128)} %param.8) | copy-start | bytes 76
  0.7 5.5 %copy-start = (bf16[768,1024]{1,0:T(8,128)(2,1)S(1)}, bf16[768,1024]{1,0:T(8,128)(2,1)}, u32[]{:S(2)}) copy-start(bf16[768,1024]{1,0:T(8,128)(2,1)} %x.1) | copy-start | bytes 4718596
  1.9 12.4 %collective-permute-start.3 = (bf16[1024,256]{1,0:T(8,128)(2,1)S(1)}, bf16[1024,256]{1,0:T(8,128)(2,1)S(1)}, u32[]{:S(2)}, u32[]{:S(2)}) collective-permute-start(bf16[1024,256]{1,0:T(8,128)(2,1)S(1)} %slice.8.refs_0_), channel_id=1, source_target_pairs={{0,2},{2,4},{4,6},{6,8},{8,10},{10,12},{12,14},{14,16},{16,18},{18... | collective-permute-start | bytes 1572872 | tf_op jit(solution)/shard_map/ppermute | solution.py:23
  3.5 16.4 %collective-permute-start = (bf16[1024,256]{1,0:T(8,128)(2,1)S(1)}, bf16[1024,256]{1,0:T(8,128)(2,1)S(1)}, u32[]{:S(2)}, u32[]{:S(2)}) collective-permute-start(bf16[1024,256]{1,0:T(8,128)(2,1)S(1)} %slice.9.refs_1_), channel_id=1, source_target_pairs={{0,2},{2,4},{4,6},{6,8},{8,10},{10,12},{12,14},{14,16},{16,18},{18... | collective-permute-start | bytes 1572872 | tf_op jit(solution)/shard_map/ppermute | solution.py:23
  6.2 1.1 %copy-start.1 = (bf16[768,512]{1,0:T(8,128)(2,1)S(1)}, bf16[768,512]{1,0:T(8,128)(2,1)}, u32[]{:S(2)}) copy-start(bf16[768,512]{1,0:T(8,128)(2,1)} %t.1) | copy-start | bytes 2359300
  14.6 17.5 %collective-permute-start.4 = (bf16[1024,256]{1,0:T(8,128)(2,1)S(1)}, bf16[1024,256]{1,0:T(8,128)(2,1)S(1)}, u32[]{:S(2)}, u32[]{:S(2)}) collective-permute-start(bf16[1024,256]{1,0:T(8,128)(2,1)S(1)} %get-tuple-element.54.rounded), channel_id=1, source_target_pairs={{0,4},{2,6},{4,8},{6,10},{8,12},{10,14},{12,16},{14,18},{16,20},{1... | collective-permute-start | bytes 1572872 | tf_op jit(solution)/shard_map/ppermute | solution.py:23
  20.2 22.2 %collective-permute-start.1 = (bf16[1024,256]{1,0:T(8,128)(2,1)S(1)}, bf16[1024,256]{1,0:T(8,128)(2,1)S(1)}, u32[]{:S(2)}, u32[]{:S(2)}) collective-permute-start(bf16[1024,256]{1,0:T(8,128)(2,1)S(1)} %get-tuple-element.45.rounded), channel_id=1, source_target_pairs={{0,4},{2,6},{4,8},{6,10},{8,12},{10,14},{12,16},{14,18},{16,20},{1... | collective-permute-start | bytes 1572872 | tf_op jit(solution)/shard_map/ppermute | solution.py:23
  33.7 11.9 %collective-permute-start.6 = (f32[8,64,256]{2,1,0:T(8,128)S(1)}, f32[8,64,256]{2,1,0:T(8,128)S(1)}, u32[]{:S(2)}, u32[]{:S(2)}) collective-permute-start(f32[8,64,256]{2,1,0:T(8,128)S(1)} %get-tuple-element.63), channel_id=1, source_target_pairs={{0,2},{2,0},{4,6},{6,4},{8,10},{10,8},{12,14},{14,12},{16,18},{18,... | collective-permute-start | bytes 1572872 | tf_op jit(solution)/shard_map/ppermute | solution.py:28
  43.9 3.3 %collective-permute-start.8 = (f32[8,64,256]{2,1,0:T(8,128)S(1)}, f32[8,64,256]{2,1,0:T(8,128)S(1)}, u32[]{:S(2)}, u32[]{:S(2)}) collective-permute-start(f32[8,64,256]{2,1,0:T(8,128)S(1)} %get-tuple-element.67), channel_id=1, source_target_pairs={{0,2},{2,0},{4,6},{6,4},{8,10},{10,8},{12,14},{14,12},{16,18},{18,... | collective-permute-start | bytes 1572872 | tf_op jit(solution)/shard_map/ppermute | solution.py:28
  44.0 18.8 %collective-permute-start.5 = (bf16[1024,256]{1,0:T(8,128)(2,1)S(1)}, bf16[1024,256]{1,0:T(8,128)(2,1)S(1)}, u32[]{:S(2)}, u32[]{:S(2)}) collective-permute-start(bf16[1024,256]{1,0:T(8,128)(2,1)S(1)} %get-tuple-element.58.rounded), channel_id=1, source_target_pairs={{0,8},{2,10},{4,12},{6,14},{8,16},{10,18},{12,20},{14,22},{16,24},... | collective-permute-start | bytes 1572872 | tf_op jit(solution)/shard_map/ppermute | solution.py:23
  44.0 27.9 %collective-permute-start.2 = (bf16[1024,256]{1,0:T(8,128)(2,1)S(1)}, bf16[1024,256]{1,0:T(8,128)(2,1)S(1)}, u32[]{:S(2)}, u32[]{:S(2)}) collective-permute-start(bf16[1024,256]{1,0:T(8,128)(2,1)S(1)} %get-tuple-element.49.rounded), channel_id=1, source_target_pairs={{0,8},{2,10},{4,12},{6,14},{8,16},{10,18},{12,20},{14,22},{16,24},... | collective-permute-start | bytes 1572872 | tf_op jit(solution)/shard_map/ppermute | solution.py:23
  45.7 5.0 %collective-permute-start.7 = (bf16[8,32,256]{2,1,0:T(8,128)(2,1)S(1)}, bf16[8,32,256]{2,1,0:T(8,128)(2,1)S(1)}, u32[]{:S(2)}, u32[]{:S(2)}) collective-permute-start(bf16[8,32,256]{2,1,0:T(8,128)(2,1)S(1)} %get-tuple-element.65), channel_id=1, source_target_pairs={{0,1},{1,0},{2,3},{3,2},{4,5},{5,4},{6,7},{7,6},{8,9},{9,8},{10,11... | collective-permute-start | bytes 393224 | tf_op jit(solution)/shard_map/ppermute | solution.py:28
  50.8 7.3 %collective-permute-start.9 = (bf16[4,32,512]{2,1,0:T(8,128)(2,1)S(1)}, bf16[4,32,512]{2,1,0:T(8,128)(2,1)S(1)}, u32[]{:S(2)}, u32[]{:S(2)}) collective-permute-start(bf16[4,32,512]{2,1,0:T(8,128)(2,1)S(1)} %get-tuple-element.69), channel_id=1, source_target_pairs={{0,4},{2,6},{4,0},{6,2},{8,12},{10,14},{12,8},{14,10},{16,20},{18,... | collective-permute-start | bytes 393224 | tf_op jit(solution)/shard_map/ppermute | solution.py:28
  51.5 4.3 %collective-permute-start.10 = (bf16[4,32,256]{2,1,0:T(8,128)(2,1)S(1)}, bf16[4,32,256]{2,1,0:T(8,128)(2,1)S(1)}, u32[]{:S(2)}, u32[]{:S(2)}) collective-permute-start(bf16[4,32,256]{2,1,0:T(8,128)(2,1)S(1)} %get-tuple-element.70), channel_id=1, source_target_pairs={{0,1},{1,0},{2,3},{3,2},{4,5},{5,4},{6,7},{7,6},{8,9},{9,8},{10,11... | collective-permute-start | bytes 196616 | tf_op jit(solution)/shard_map/ppermute | solution.py:28
  52.9 5.2 %collective-permute-start.11 = (bf16[4,32,256]{2,1,0:T(8,128)(2,1)S(1)}, bf16[4,32,256]{2,1,0:T(8,128)(2,1)S(1)}, u32[]{:S(2)}, u32[]{:S(2)}) collective-permute-start(bf16[4,32,256]{2,1,0:T(8,128)(2,1)S(1)} %get-tuple-element.71), channel_id=1, source_target_pairs={{0,5},{1,4},{2,7},{3,6},{4,1},{5,0},{6,3},{7,2},{8,13},{9,12},{10,... | collective-permute-start | bytes 196616 | tf_op jit(solution)/shard_map/ppermute | solution.py:273
  58.2 14.9 %collective-permute-start.12 = (bf16[32,512]{1,0:T(8,128)(2,1)S(1)}, bf16[32,512]{1,0:T(8,128)(2,1)S(1)}, u32[]{:S(2)}, u32[]{:S(2)}) collective-permute-start(bf16[32,512]{1,0:T(8,128)(2,1)S(1)} %get-tuple-element.73), channel_id=1, source_target_pairs={{0,8},{2,10},{4,12},{6,14},{8,0},{10,2},{12,4},{14,6},{16,24},{18,... | collective-permute-start | bytes 98312 | tf_op jit(solution)/shard_map/ppermute | solution.py:28
  59.8 13.8 %collective-permute-start.13 = (bf16[32,512]{1,0:T(8,128)(2,1)S(1)}, bf16[32,512]{1,0:T(8,128)(2,1)S(1)}, u32[]{:S(2)}, u32[]{:S(2)}) collective-permute-start(bf16[32,512]{1,0:T(8,128)(2,1)S(1)} %get-tuple-element.74), channel_id=1, source_target_pairs={{0,16},{2,18},{4,20},{6,22},{8,24},{10,26},{12,28},{14,30},{16,0},... | collective-permute-start | bytes 98312 | tf_op jit(solution)/shard_map/ppermute | solution.py:28
  61.6 12.0 %collective-permute-start.14 = (bf16[32,512]{1,0:T(8,128)(2,1)S(1)}, bf16[32,512]{1,0:T(8,128)(2,1)S(1)}, u32[]{:S(2)}, u32[]{:S(2)}) collective-permute-start(bf16[32,512]{1,0:T(8,128)(2,1)S(1)} %get-tuple-element.75), channel_id=1, source_target_pairs={{0,24},{2,26},{4,28},{6,30},{8,16},{10,18},{12,20},{14,22},{16,8},... | collective-permute-start | bytes 98312 | tf_op jit(solution)/shard_map/ppermute | solution.py:28

commit v9 on v8

--- a/solution.py
+++ b/solution.py
@@ -21,6 +21,12 @@
     count = lax.axis_size(axis)
     pairs = [(source, (source + steps) % count) for source in range(count)]
     return lax.ppermute(value, axis, pairs)
+
+
+def moved(value, target):
+    count = lax.axis_size("gossip")
+    pairs = [(source, target(source) % count) for source in range(count) if target(source) is not None]
+    return lax.ppermute(value, "gossip", pairs)
 
 
 def flipped(value, axis, bit):
@@ -46,26 +52,37 @@
     return product * fan_scale
 
 
-def first_kernel(order, plan, x, t, *refs):
-    weights, (mix, *shards), outs = refs[:HALVES], refs[HALVES:HALVES + 2 * STEPS - 1], refs[HALVES + 2 * STEPS - 1:]
+def first_kernel(order, plan, x, t, weights, mix, *refs):
+    shards, outs = refs[:2 * STEPS - 2], refs[2 * STEPS - 2:-4]
+    x_first, t_first, w_held, arrivals = refs[-4:]
+    shards = (x_first, t_first) + shards
     batch = x.shape[0] // STEPS
-    rows = [pl.ds(pl.multiple_of(order[0, step] * batch, batch), batch) for step in range(STEPS)]
+    copies = [pltpu.make_async_copy(weights, w_held, arrivals.at[2 * STEPS])]
+    for step in range(STEPS):
+        rows = pl.ds(pl.multiple_of(order[0, step] * batch, batch), batch)
+        for i, source in enumerate((x, t)):
+            at = 2 * step + i
+            copies.append(pltpu.make_async_copy(source.at[rows, :], shards[at], arrivals.at[at]))
+    for copy in copies:
+        copy.start()
     mix[...] = jnp.zeros_like(mix)
     for step in range(STEPS):
         own, peer = [jnp.full((1, mix.shape[1]), plan[i, step].astype(jnp.float32)) for i in range(2)]
         mix[2 * step:2 * step + 1, :] = own / (own + peer)
         mix[2 * step + 1:2 * step + 2, :] = peer / (own + peer)
     own, _ = shares(mix, 0)
-    width = weights[0].shape[1]
-    for half, w in enumerate(weights):
+    width = weights.shape[1] // HALVES
+    for copy in copies[:3]:
+        copy.wait()
+    for half in range(HALVES):
         base, velocity = outs[2 * half:2 * half + 2]
         columns = slice(half * width, (half + 1) * width)
-        gradient = gradient_of(x[rows[0], :], t[rows[0], columns], w[...])
+        w = w_held[:, columns]
+        gradient = gradient_of(x_first[...], t_first[:, columns], w)
         velocity[...] = gradient
-        base[...] = own * w[...].astype(jnp.float32) - learning_rate * gradient
-    for step in range(1, STEPS):
-        shards[2 * step - 2][...] = x[rows[step], :]
-        shards[2 * step - 1][...] = t[rows[step], :]
+        base[...] = own * w.astype(jnp.float32) - learning_rate * gradient
+    for copy in copies[3:]:
+        copy.wait()
 
 
 def middle_kernel(columns, mix, x, t, rounded, master, velocity_in, base, velocity):
@@ -92,11 +109,22 @@
     give[...] = held[:, pl.ds(1 - mine, 1)].reshape(give.shape)
 
 
-def round_kernel(step, mix, base, arrived, rounded, master):
+def early_kernel(columns, mix, base, arrived, rounded):
+    _, peer = shares(mix, 0)
+    rounded[...] = (base[...] + peer * arrived[:, columns].astype(jnp.float32)).astype(jnp.bfloat16)
+
+
+def round_kernel(step, columns, mix, base, core_0, core_1, rounded, master):
     _, peer = shares(mix, step)
-    total = base[...] + peer * arrived[...].astype(jnp.float32)
-    rounded[...] = total.astype(jnp.bfloat16)
-    master[...] = total
+    core = lax.axis_index("gossip") & 1
+
+    def add(arrived):
+        total = base[...] + peer * arrived[:, columns].astype(jnp.float32)
+        rounded[...] = total.astype(jnp.bfloat16)
+        master[...] = total
+
+    pl.when(core == 0)(functools.partial(add, core_0))
+    pl.when(core == 1)(functools.partial(add, core_1))
 
 
 def finish_kernel(mix, base, arrived, *refs):
@@ -149,8 +177,8 @@
 IN_SMEM = pl.BlockSpec(memory_space=pltpu.SMEM)
 
 
-def call(kernel, ins, outs, scratch=(), out_specs=None, in_place=None):
-    in_specs = [IN_SMEM if array.dtype == jnp.int32 else IN_VMEM for array in ins]
+def call(kernel, ins, outs, scratch=(), out_specs=None, in_place=None, in_specs=None):
+    in_specs = in_specs or [IN_SMEM if array.dtype == jnp.int32 else IN_VMEM for array in ins]
     aliases = {}
     if in_place is not None:
         in_specs[in_place] = pl.BlockSpec(memory_space=pl.ANY)
@@ -198,23 +226,32 @@
     half_f32, half_bf16 = ((din, width), jnp.float32), ((din, width), jnp.bfloat16)
 
     plan = plan.T
-    pieces, arrived0, rounds0, arrived1, middles = [], [], [], [], []
-    for half in range(HALVES):
-        pieces.append(weights[:, columns[half]])
-        weights = lax.optimization_barrier(weights)
-        arrived0.append(shifted(pieces[half], "gossip", 1))
+    leads, rounds0, arrived1, middles = [], [], [], []
+    ship = moved(weights, lambda at: at + 1 if at & 1 else None)
+    chip = moved(weights, lambda at: None if at & 1 else at + 1)
     batch = inputs.shape[0] // STEPS
     shards = [((batch, din), inputs.dtype), ((batch, dout), targets.dtype)] * (STEPS - 1)
     outs = [((-(-2 * STEPS // 8) * 8, 128), jnp.float32)] + shards + [half_f32] * (2 * HALVES)
-    mix, *rest = call(first_kernel, [order, plan, inputs, targets] + pieces, outs)
+    in_hbm = [pltpu.with_memory_space_constraint(array, pltpu.HBM) for array in (order, plan, inputs, targets, weights)]
+    held = [pltpu.VMEM(*shard) for shard in shards[:2]] + [pltpu.VMEM(weights.shape, weights.dtype)]
+    mix, *rest = call(
+        first_kernel, in_hbm, outs, held + [pltpu.SemaphoreType.DMA((2 * STEPS + 1,))],
+        in_specs=[IN_SMEM] * 2 + [pl.BlockSpec(memory_space=pltpu.HBM)] * 3,
+    )
     shards, firsts = rest[:len(shards)], rest[len(shards):]
+    for half in range(HALVES):
+        (early,) = call(
+            functools.partial(early_kernel, columns[half]), [mix, firsts[2 * half], chip], [half_bf16]
+        )
+        leads.append(moved(early, lambda at: at + 2 if at & 1 else None))
     for half in range(HALVES):
         rounds0.append(
             call(
-                functools.partial(round_kernel, 0), [mix, firsts[2 * half], arrived0[half]], [half_bf16, half_f32]
+                functools.partial(round_kernel, 0, columns[half]), [mix, firsts[2 * half], ship, chip],
+                [half_bf16, half_f32],
             )
         )
-        arrived1.append(shifted(rounds0[half][0], "gossip", 2))
+        arrived1.append(moved(rounds0[half][0], lambda at: None if at & 1 else at + 2))
     for half in range(HALVES):
         middles.append(
             call(
@@ -227,7 +264,8 @@
     for half in range(HALVES):
         base1, velocity1 = middles[half]
         rounded2, master2 = call(
-            functools.partial(round_kernel, 1), [mix, base1, arrived1[half]], [half_bf16, half_f32]
+            functools.partial(round_kernel, 1, slice(None)), [mix, base1, arrived1[half], leads[half]],
+            [half_bf16, half_f32],
         )
         arrived2 = shifted(rounded2, "gossip", 4)
         outs, scratch = [half_f32] * 2, ()

time: 74.5 us -> 82.6 us (1.11)
  starting transfers between devices: 15 us -> 22.1 us
  local copies, waits for them, and re-layouts: 3.41 us -> 0 us
  Pallas kernels: 10.5 us -> 12.7 us
  waiting for transfers between devices: 44.6 us -> 46.8 us
    ppermute x0 -> x6, waiting for transfers between devices: none -> 30.6 us  [moved(): return lax.ppermute(value, 'gossip', pairs)]
    ppermute x6 -> x2, waiting for transfers between devices: 36.8 us -> 8.13 us  [shifted(): return lax.ppermute(value, axis, pairs)]
    ppermute x0 -> x6, starting transfers between devices: none -> 11 us  [moved(): return lax.ppermute(value, 'gossip', pairs)]
    ppermute x6 -> x2, starting transfers between devices: 5.13 us -> 1.4 us  [shifted(): return lax.ppermute(value, axis, pairs)]
    slice x2 -> x0, local copies, waits for them, and re-layouts: 2.27 us -> none  [steps(): pieces.append(weights[:, columns[half]])]
    pallas_call x15 -> x17, Pallas kernels: 10.5 us -> 12.7 us  [call(): pl.pallas_call(kernel, grid=(1,) if out_specs else (), in_specs=in_specs,...]
    unnamed x8 -> x0, local copies, waits for them, and re-layouts: 1.14 us -> none
    ppermute x8, waiting for transfers between devices: 5.43 us -> 6.28 us  [flipped(): lax.ppermute(value, axis, [(source, source ^ bit) for source in range(cou...]
  transfers between devices with their start and end apart: 15 -> 17, of which waited for: 9 -> 8; matrix products, arithmetic and copies ran while one was open for 1% -> 0% of each run, Pallas kernels for 13% -> 14%
where the time goes in v9:
time: 82.6 us; the launch traced here: 82.4 us
  waiting for transfers between devices  46.8 us (57%)
  starting transfers between devices  22.1 us (27%)
  Pallas kernels  12.7 us (15%)
    ppermute x6, waiting for transfers between devices, moved(): return lax.ppermute(value, 'gossip', pairs)  30.6 us
    pallas_call x17, Pallas kernels, call(): pl.pallas_call(kernel, grid=(1,) if out_specs else (), in_specs=in_specs,...  12.7 us
    ppermute x6, starting transfers between devices, moved(): return lax.ppermute(value, 'gossip', pairs)  11 us
    ppermute x8, starting transfers between devices, flipped(): lax.ppermute(value, axis, [(source, source ^ bit) for source in range(cou...  8.33 us
    ppermute x2, waiting for transfers between devices, shifted(): return lax.ppermute(value, axis, pairs)  8.13 us
    ppermute x8, waiting for transfers between devices, flipped(): lax.ppermute(value, axis, [(source, source ^ bit) for source in range(cou...  6.28 us
    ppermute x1, waiting for transfers between devices, steps(): from_xy = lax.ppermute(give_xy, ('gossip', 'group'), pairs)  1.85 us
  transfers between devices with their start and end apart: 17, of which 8 were waited for; matrix products, arithmetic and copies ran while one was open for 0% of the time, Pallas kernels for 14%

profile of v9, /device:TPU:0, one launch (start us, length us, event | category | flops | bytes accessed | tf_op | source)
XLA Modules:
  0.0 82.4 jit_solution(8012512181799247611)
XLA Ops:
  0.6 2.5 %collective-permute-start.1 = (bf16[1024,512]{1,0:T(8,128)(2,1)}, bf16[1024,512]{1,0:T(8,128)(2,1)S(1)}, u32[]{:S(2)}, u32[]{:S(2)}) collective-permute-start(bf16[1024,512]{1,0:T(8,128)(2,1)} %bitcast.16), channel_id=1, source_target_pairs={{0,2},{4,6},{8,10},{12,14},{16,18},{20,22},{24,26},{28,30},{1,3},{... | collective-permute-start | bytes 3145736 | tf_op jit(solution)/shard_map/ppermute | solution.py:29
  3.1 1.3 %collective-permute-start = (bf16[1024,512]{1,0:T(8,128)(2,1)}, bf16[1024,512]{1,0:T(8,128)(2,1)S(1)}, u32[]{:S(2)}, u32[]{:S(2)}) collective-permute-start(bf16[1024,512]{1,0:T(8,128)(2,1)} %bitcast.17), channel_id=1, source_target_pairs={{2,4},{6,8},{10,12},{14,16},{18,20},{22,24},{26,28},{30,0},{3,5},{... | collective-permute-start | bytes 3145736 | tf_op jit(solution)/shard_map/ppermute | solution.py:29
  4.4 3.5 %shard_map.68 = (f32[8,128]{1,0:T(8,128)S(1)}, bf16[256,1024]{1,0:T(8,128)(2,1)S(1)}, bf16[256,512]{1,0:T(8,128)(2,1)S(1)}, bf16[256,1024]{1,0:T(8,128)(2,1)S(1)...) custom-call(s32[1,3]{1,0:T(1,128)} %order.1, ...), custom_call_target="tpu_custom_call" | custom-call | tf_op jit(solution)/shard_map/pallas_call | solution.py:186
  7.9 0.0 collective-permute-done.1.core_1.arrived
  7.9 14.2 %collective-permute-done.core_0 = bf16[1024,512]{1,0:T(8,128)(2,1)S(1)} collective-permute-done((bf16[1024,512]{1,0:T(8,128)(2,1)}, bf16[1024,512]{1,0:T(8,128)(2,1)S(1)}, u32[]{:S(2)}, u32[]{:S(2)}) %collective-permute-start) | collective-permute-done | bytes 1048608 | tf_op jit(solution)/shard_map/ppermute | solution.py:29
  22.1 0.3 shard_map.74
  22.4 1.9 %collective-permute-start.5 = (bf16[1024,256]{1,0:T(8,128)(2,1)S(1)}, bf16[1024,256]{1,0:T(8,128)(2,1)S(1)}, u32[]{:S(2)}, u32[]{:S(2)}) collective-permute-start(bf16[1024,256]{1,0:T(8,128)(2,1)S(1)} %get-tuple-element.54.rounded), channel_id=1, source_target_pairs={{0,4},{4,8},{8,12},{12,16},{16,20},{20,24},{24,28},{28,0},{1,5},{5... | collective-permute-start | bytes 1572872 | tf_op jit(solution)/shard_map/ppermute | solution.py:29
  24.4 0.3 shard_map.76
  24.7 0.7 collective-permute-start.6
  25.4 0.3 shard_map.69
  25.7 4.0 %collective-permute-start.2 = (bf16[1024,256]{1,0:T(8,128)(2,1)S(1)}, bf16[1024,256]{1,0:T(8,128)(2,1)S(1)}, u32[]{:S(2)}, u32[]{:S(2)}) collective-permute-start(bf16[1024,256]{1,0:T(8,128)(2,1)S(1)} %get-tuple-element.45.rounded), channel_id=1, source_target_pairs={{0,4},{4,8},{8,12},{12,16},{16,20},{20,24},{24,28},{28,0},{1,5},{5... | collective-permute-start | bytes 1572872 | tf_op jit(solution)/shard_map/ppermute | solution.py:29
  29.7 0.3 shard_map.71
  30.0 0.7 collective-permute-start.3
  30.7 0.9 %shard_map.75 = (f32[1024,256]{1,0:T(8,128)S(1)}, f32[1024,256]{1,0:T(8,128)S(1)}) custom-call(f32[8,128]{1,0:T(8,128)S(1)} %get-tuple-element.39.mix, bf16[256,1024]{1,0:T(8,128)(2,1)S(1)} %get-tuple-element.42.x, bf16[256,512]{1,0:T(8,128)(2,1)S(1)} %get-tuple-element.43.t, bf16[1024,256]{1,0:T(8,128)(2,1)S(1)} %get-tuple-element.54.rounded, ...), custom_call_target="tpu_custom_call" | custom-call | tf_op jit(solution)/shard_map/pallas_call | solution.py:186
  31.6 10.2 %collective-permute-done.5.core_0 = bf16[1024,256]{1,0:T(8,128)(2,1)S(1)} collective-permute-done((bf16[1024,256]{1,0:T(8,128)(2,1)S(1)}, bf16[1024,256]{1,0:T(8,128)(2,1)S(1)}, u32[]{:S(2)}, u32[]{:S(2)}) %collective-permute-start.5) | collective-permute-done | bytes 524320 | tf_op jit(solution)/shard_map/ppermute | solution.py:29
  41.8 0.0 collective-permute-done.6.core_1
  41.8 0.3 shard_map.77
  42.1 1.2 %shard_map.78 = (f32[1024,256]{1,0:T(8,128)S(1)}, f32[8,64,256]{2,1,0:T(8,128)S(1)}, f32[8,64,256]{2,1,0:T(8,128)S(1)}) custom-call(f32[8,128]{1,0:T(8,128)S(1)} %get-tuple-element.39.mix, bf16[256,1024]{1,0:T(8,128)(2,1)S(1)} %get-tuple-element.40.x, bf16[256,512]{1,0:T(8,128)(2,1)S(1)} %get-tuple-element.41.t, ...), custom_call_target="tpu_custom_call" | custom-call | tf_op jit(solution)/shard_map/pallas_call | solution.py:186
  43.4 0.1 collective-permute-start.8
  43.5 0.9 %shard_map.70 = (f32[1024,256]{1,0:T(8,128)S(1)}, f32[1024,256]{1,0:T(8,128)S(1)}) custom-call(f32[8,128]{1,0:T(8,128)S(1)} %get-tuple-element.39.mix, bf16[256,1024]{1,0:T(8,128)(2,1)S(1)} %get-tuple-element.42.x, bf16[256,512]{1,0:T(8,128)(2,1)S(1)} %get-tuple-element.43.t, bf16[1024,256]{1,0:T(8,128)(2,1)S(1)} %get-tuple-element.45.rounded, ...), custom_call_target="tpu_custom_call" | custom-call | tf_op jit(solution)/shard_map/pallas_call | solution.py:186
  44.4 6.1 %collective-permute-done.2.core_0 = bf16[1024,256]{1,0:T(8,128)(2,1)S(1)} collective-permute-done((bf16[1024,256]{1,0:T(8,128)(2,1)S(1)}, bf16[1024,256]{1,0:T(8,128)(2,1)S(1)}, u32[]{:S(2)}, u32[]{:S(2)}) %collective-permute-start.2) | collective-permute-done | bytes 524320 | tf_op jit(solution)/shard_map/ppermute | solution.py:29
  50.5 0.0 collective-permute-done.3.core_1
  50.5 0.3 shard_map.72
  50.8 1.2 %shard_map.73 = (f32[1024,256]{1,0:T(8,128)S(1)}, f32[8,64,256]{2,1,0:T(8,128)S(1)}, f32[8,64,256]{2,1,0:T(8,128)S(1)}) custom-call(f32[8,128]{1,0:T(8,128)S(1)} %get-tuple-element.39.mix, bf16[256,1024]{1,0:T(8,128)(2,1)S(1)} %get-tuple-element.40.x, bf16[256,512]{1,0:T(8,128)(2,1)S(1)} %get-tuple-element.41.t, ...), custom_call_target="tpu_custom_call" | custom-call | tf_op jit(solution)/shard_map/pallas_call | solution.py:186
  52.1 0.1 collective-permute-start.10
  52.1 0.1 collective-permute-start.7
  52.2 1.3 %collective-permute-start.4 = (bf16[1024,256]{1,0:T(8,128)(2,1)S(1)}, bf16[1024,256]{1,0:T(8,128)(2,1)S(1)}, u32[]{:S(2)}, u32[]{:S(2)}) collective-permute-start(bf16[1024,256]{1,0:T(8,128)(2,1)S(1)} %get-tuple-element.49.rounded), channel_id=1, source_target_pairs={{0,8},{2,10},{4,12},{6,14},{8,16},{10,18},{12,20},{14,22},{16,24},... | collective-permute-start | bytes 1572872 | tf_op jit(solution)/shard_map/ppermute | solution.py:23
  53.5 0.0 collective-permute-done.8
  53.6 0.1 shard_map.81
  53.6 1.6 %collective-permute-start.9 = (bf16[8,32,256]{2,1,0:T(8,128)(2,1)S(1)}, bf16[8,32,256]{2,1,0:T(8,128)(2,1)S(1)}, u32[]{:S(2)}, u32[]{:S(2)}) collective-permute-start(bf16[8,32,256]{2,1,0:T(8,128)(2,1)S(1)} %get-tuple-element.65), channel_id=1, source_target_pairs={{0,1},{1,0},{2,3},{3,2},{4,5},{5,4},{6,7},{7,6},{8,9},{9,8},{10,11... | collective-permute-start | bytes 393224 | tf_op jit(solution)/shard_map/ppermute | solution.py:34
  55.2 3.8 %collective-permute-done.9 = bf16[8,32,256]{2,1,0:T(8,128)(2,1)S(1)} collective-permute-done((bf16[8,32,256]{2,1,0:T(8,128)(2,1)S(1)}, bf16[8,32,256]{2,1,0:T(8,128)(2,1)S(1)}, u32[]{:S(2)}, u32[]{:S(2)}) %collective-permute-start.9) | collective-permute-done | bytes 131104 | tf_op jit(solution)/shard_map/ppermute | solution.py:34
  59.0 0.1 shard_map.82
  59.0 0.7 collective-permute-start.11
  59.7 1.5 %collective-permute-start.12 = (bf16[4,32,256]{2,1,0:T(8,128)(2,1)S(1)}, bf16[4,32,256]{2,1,0:T(8,128)(2,1)S(1)}, u32[]{:S(2)}, u32[]{:S(2)}) collective-permute-start(bf16[4,32,256]{2,1,0:T(8,128)(2,1)S(1)} %get-tuple-element.70), channel_id=1, source_target_pairs={{0,1},{1,0},{2,3},{3,2},{4,5},{5,4},{6,7},{7,6},{8,9},{9,8},{10,11... | collective-permute-start | bytes 196616 | tf_op jit(solution)/shard_map/ppermute | solution.py:34
  61.2 1.4 %collective-permute-start.13 = (bf16[4,32,256]{2,1,0:T(8,128)(2,1)S(1)}, bf16[4,32,256]{2,1,0:T(8,128)(2,1)S(1)}, u32[]{:S(2)}, u32[]{:S(2)}) collective-permute-start(bf16[4,32,256]{2,1,0:T(8,128)(2,1)S(1)} %get-tuple-element.71), channel_id=1, source_target_pairs={{0,5},{1,4},{2,7},{3,6},{4,1},{5,0},{6,3},{7,2},{8,13},{9,12},{10,... | collective-permute-start | bytes 196616 | tf_op jit(solution)/shard_map/ppermute | solution.py:311
  62.6 1.9 %collective-permute-done.12.from_x = bf16[4,32,256]{2,1,0:T(8,128)(2,1)S(1)} collective-permute-done((bf16[4,32,256]{2,1,0:T(8,128)(2,1)S(1)}, bf16[4,32,256]{2,1,0:T(8,128)(2,1)S(1)}, u32[]{:S(2)}, u32[]{:S(2)}) %collective-permute-start.12) | collective-permute-done | bytes 65568 | tf_op jit(solution)/shard_map/ppermute | solution.py:34
  64.5 1.9 %collective-permute-done.13.from_xy = bf16[4,32,256]{2,1,0:T(8,128)(2,1)S(1)} collective-permute-done((bf16[4,32,256]{2,1,0:T(8,128)(2,1)S(1)}, bf16[4,32,256]{2,1,0:T(8,128)(2,1)S(1)}, u32[]{:S(2)}, u32[]{:S(2)}) %collective-permute-start.13) | collective-permute-done | bytes 65568 | tf_op jit(solution)/shard_map/ppermute | solution.py:311
  66.4 0.1 shard_map.83
  66.4 1.1 %collective-permute-start.14 = (bf16[32,512]{1,0:T(8,128)(2,1)S(1)}, bf16[32,512]{1,0:T(8,128)(2,1)S(1)}, u32[]{:S(2)}, u32[]{:S(2)}) collective-permute-start(bf16[32,512]{1,0:T(8,128)(2,1)S(1)} %get-tuple-element.73), channel_id=1, source_target_pairs={{0,8},{2,10},{4,12},{6,14},{8,0},{10,2},{12,4},{14,6},{16,24},{18,... | collective-permute-start | bytes 98312 | tf_op jit(solution)/shard_map/ppermute | solution.py:34
  67.5 1.8 %collective-permute-start.15 = (bf16[32,512]{1,0:T(8,128)(2,1)S(1)}, bf16[32,512]{1,0:T(8,128)(2,1)S(1)}, u32[]{:S(2)}, u32[]{:S(2)}) collective-permute-start(bf16[32,512]{1,0:T(8,128)(2,1)S(1)} %get-tuple-element.74), channel_id=1, source_target_pairs={{0,16},{2,18},{4,20},{6,22},{8,24},{10,26},{12,28},{14,30},{16,0},... | collective-permute-start | bytes 98312 | tf_op jit(solution)/shard_map/ppermute | solution.py:34
  69.3 1.6 %collective-permute-start.16 = (bf16[32,512]{1,0:T(8,128)(2,1)S(1)}, bf16[32,512]{1,0:T(8,128)(2,1)S(1)}, u32[]{:S(2)}, u32[]{:S(2)}) collective-permute-start(bf16[32,512]{1,0:T(8,128)(2,1)S(1)} %get-tuple-element.75), channel_id=1, source_target_pairs={{0,24},{2,26},{4,28},{6,30},{8,16},{10,18},{12,20},{14,22},{16,8},... | collective-permute-start | bytes 98312 | tf_op jit(solution)/shard_map/ppermute | solution.py:34
  70.9 1.1 %shard_map.79.refs_0_ = bf16[1024,512]{1,0:T(8,128)(2,1)} custom-call(f32[8,128]{1,0:T(8,128)S(1)} %get-tuple-element.39.mix, f32[1024,256]{1,0:T(8,128)S(1)} %get-tuple-element.61.base, bf16[1024,256]{1,0:T(8,128)(2,1)S(1)} %collective-permute-done.7.arrived), custom_call_target="tpu_custom_call" | custom-call | tf_op jit(solution)/shard_map/pallas_call | solution.py:186
  72.0 8.1 %collective-permute-done.4.arrived = bf16[1024,256]{1,0:T(8,128)(2,1)S(1)} collective-permute-done((bf16[1024,256]{1,0:T(8,128)(2,1)S(1)}, bf16[1024,256]{1,0:T(8,128)(2,1)S(1)}, u32[]{:S(2)}, u32[]{:S(2)}) %collective-permute-start.4) | collective-permute-done | bytes 524320 | tf_op jit(solution)/shard_map/ppermute | solution.py:23
  80.1 1.1 %shard_map.80 = bf16[1024,512]{1,0:T(8,128)(2,1)} custom-call(f32[8,128]{1,0:T(8,128)S(1)} %get-tuple-element.39.mix, f32[1024,256]{1,0:T(8,128)S(1)} %get-tuple-element.52.base, bf16[1024,256]{1,0:T(8,128)(2,1)S(1)} %collective-permute-done.4.arrived, bf16[1024,512]{1,0:T(8,128)(2,1)} %shard_map.79.refs_0_), custom_call_target="tpu_custom_call", output_to_operand_aliasing={{}: (3, {})} | custom-call | tf_op jit(solution)/shard_map/pallas_call | solution.py:186
  81.2 0.0 collective-permute-done.14.refs_0_
  81.2 0.5 collective-permute-done.15.refs_1_
  81.7 0.0 collective-permute-done.16.refs_2_
  81.7 0.6 shard_map.84
  (3 shorter events, 0.0 us)
Async XLA Ops:
  0.6 7.3 %collective-permute-start.1 = (bf16[1024,512]{1,0:T(8,128)(2,1)}, bf16[1024,512]{1,0:T(8,128)(2,1)S(1)}, u32[]{:S(2)}, u32[]{:S(2)}) collective-permute-start(bf16[1024,512]{1,0:T(8,128)(2,1)} %bitcast.16), channel_id=1, source_target_pairs={{0,2},{4,6},{8,10},{12,14},{16,18},{20,22},{24,26},{28,30},{1,3},{... | collective-permute-start | bytes 3145736 | tf_op jit(solution)/shard_map/ppermute | solution.py:29
  3.1 19.0 %collective-permute-start = (bf16[1024,512]{1,0:T(8,128)(2,1)}, bf16[1024,512]{1,0:T(8,128)(2,1)S(1)}, u32[]{:S(2)}, u32[]{:S(2)}) collective-permute-start(bf16[1024,512]{1,0:T(8,128)(2,1)} %bitcast.17), channel_id=1, source_target_pairs={{2,4},{6,8},{10,12},{14,16},{18,20},{22,24},{26,28},{30,0},{3,5},{... | collective-permute-start | bytes 3145736 | tf_op jit(solution)/shard_map/ppermute | solution.py:29
  22.4 19.4 %collective-permute-start.5 = (bf16[1024,256]{1,0:T(8,128)(2,1)S(1)}, bf16[1024,256]{1,0:T(8,128)(2,1)S(1)}, u32[]{:S(2)}, u32[]{:S(2)}) collective-permute-start(bf16[1024,256]{1,0:T(8,128)(2,1)S(1)} %get-tuple-element.54.rounded), channel_id=1, source_target_pairs={{0,4},{4,8},{8,12},{12,16},{16,20},{20,24},{24,28},{28,0},{1,5},{5... | collective-permute-start | bytes 1572872 | tf_op jit(solution)/shard_map/ppermute | solution.py:29
  24.7 17.2 %collective-permute-start.6 = (bf16[1024,256]{1,0:T(8,128)(2,1)S(1)}, bf16[1024,256]{1,0:T(8,128)(2,1)S(1)}, u32[]{:S(2)}, u32[]{:S(2)}) collective-permute-start(bf16[1024,256]{1,0:T(8,128)(2,1)S(1)} %shard_map.76), channel_id=1, source_target_pairs={{2,6},{6,10},{10,14},{14,18},{18,22},{22,26},{26,30},{30,2},{3,7},... | collective-permute-start | bytes 1572872 | tf_op jit(solution)/shard_map/ppermute | solution.py:29
  25.7 24.8 %collective-permute-start.2 = (bf16[1024,256]{1,0:T(8,128)(2,1)S(1)}, bf16[1024,256]{1,0:T(8,128)(2,1)S(1)}, u32[]{:S(2)}, u32[]{:S(2)}) collective-permute-start(bf16[1024,256]{1,0:T(8,128)(2,1)S(1)} %get-tuple-element.45.rounded), channel_id=1, source_target_pairs={{0,4},{4,8},{8,12},{12,16},{16,20},{20,24},{24,28},{28,0},{1,5},{5... | collective-permute-start | bytes 1572872 | tf_op jit(solution)/shard_map/ppermute | solution.py:29
  30.0 20.5 %collective-permute-start.3 = (bf16[1024,256]{1,0:T(8,128)(2,1)S(1)}, bf16[1024,256]{1,0:T(8,128)(2,1)S(1)}, u32[]{:S(2)}, u32[]{:S(2)}) collective-permute-start(bf16[1024,256]{1,0:T(8,128)(2,1)S(1)} %shard_map.71), channel_id=1, source_target_pairs={{2,6},{6,10},{10,14},{14,18},{18,22},{22,26},{26,30},{30,2},{3,7},... | collective-permute-start | bytes 1572872 | tf_op jit(solution)/shard_map/ppermute | solution.py:29
  43.4 10.2 %collective-permute-start.8 = (f32[8,64,256]{2,1,0:T(8,128)S(1)}, f32[8,64,256]{2,1,0:T(8,128)S(1)}, u32[]{:S(2)}, u32[]{:S(2)}) collective-permute-start(f32[8,64,256]{2,1,0:T(8,128)S(1)} %get-tuple-element.63), channel_id=1, source_target_pairs={{0,2},{2,0},{4,6},{6,4},{8,10},{10,8},{12,14},{14,12},{16,18},{18,... | collective-permute-start | bytes 1572872 | tf_op jit(solution)/shard_map/ppermute | solution.py:34
  52.1 3.1 %collective-permute-start.10 = (f32[8,64,256]{2,1,0:T(8,128)S(1)}, f32[8,64,256]{2,1,0:T(8,128)S(1)}, u32[]{:S(2)}, u32[]{:S(2)}) collective-permute-start(f32[8,64,256]{2,1,0:T(8,128)S(1)} %get-tuple-element.67), channel_id=1, source_target_pairs={{0,2},{2,0},{4,6},{6,4},{8,10},{10,8},{12,14},{14,12},{16,18},{18,... | collective-permute-start | bytes 1572872 | tf_op jit(solution)/shard_map/ppermute | solution.py:34
  52.1 18.8 %collective-permute-start.7 = (bf16[1024,256]{1,0:T(8,128)(2,1)S(1)}, bf16[1024,256]{1,0:T(8,128)(2,1)S(1)}, u32[]{:S(2)}, u32[]{:S(2)}) collective-permute-start(bf16[1024,256]{1,0:T(8,128)(2,1)S(1)} %get-tuple-element.58.rounded), channel_id=1, source_target_pairs={{0,8},{2,10},{4,12},{6,14},{8,16},{10,18},{12,20},{14,22},{16,24},... | collective-permute-start | bytes 1572872 | tf_op jit(solution)/shard_map/ppermute | solution.py:23
  52.2 27.9 %collective-permute-start.4 = (bf16[1024,256]{1,0:T(8,128)(2,1)S(1)}, bf16[1024,256]{1,0:T(8,128)(2,1)S(1)}, u32[]{:S(2)}, u32[]{:S(2)}) collective-permute-start(bf16[1024,256]{1,0:T(8,128)(2,1)S(1)} %get-tuple-element.49.rounded), channel_id=1, source_target_pairs={{0,8},{2,10},{4,12},{6,14},{8,16},{10,18},{12,20},{14,22},{16,24},... | collective-permute-start | bytes 1572872 | tf_op jit(solution)/shard_map/ppermute | solution.py:23
  53.6 5.4 %collective-permute-start.9 = (bf16[8,32,256]{2,1,0:T(8,128)(2,1)S(1)}, bf16[8,32,256]{2,1,0:T(8,128)(2,1)S(1)}, u32[]{:S(2)}, u32[]{:S(2)}) collective-permute-start(bf16[8,32,256]{2,1,0:T(8,128)(2,1)S(1)} %get-tuple-element.65), channel_id=1, source_target_pairs={{0,1},{1,0},{2,3},{3,2},{4,5},{5,4},{6,7},{7,6},{8,9},{9,8},{10,11... | collective-permute-start | bytes 393224 | tf_op jit(solution)/shard_map/ppermute | solution.py:34
  59.0 7.3 %collective-permute-start.11 = (bf16[4,32,512]{2,1,0:T(8,128)(2,1)S(1)}, bf16[4,32,512]{2,1,0:T(8,128)(2,1)S(1)}, u32[]{:S(2)}, u32[]{:S(2)}) collective-permute-start(bf16[4,32,512]{2,1,0:T(8,128)(2,1)S(1)} %get-tuple-element.69), channel_id=1, source_target_pairs={{0,4},{2,6},{4,0},{6,2},{8,12},{10,14},{12,8},{14,10},{16,20},{18,... | collective-permute-start | bytes 393224 | tf_op jit(solution)/shard_map/ppermute | solution.py:34
  59.7 4.8 %collective-permute-start.12 = (bf16[4,32,256]{2,1,0:T(8,128)(2,1)S(1)}, bf16[4,32,256]{2,1,0:T(8,128)(2,1)S(1)}, u32[]{:S(2)}, u32[]{:S(2)}) collective-permute-start(bf16[4,32,256]{2,1,0:T(8,128)(2,1)S(1)} %get-tuple-element.70), channel_id=1, source_target_pairs={{0,1},{1,0},{2,3},{3,2},{4,5},{5,4},{6,7},{7,6},{8,9},{9,8},{10,11... | collective-permute-start | bytes 196616 | tf_op jit(solution)/shard_map/ppermute | solution.py:34
  61.2 5.2 %collective-permute-start.13 = (bf16[4,32,256]{2,1,0:T(8,128)(2,1)S(1)}, bf16[4,32,256]{2,1,0:T(8,128)(2,1)S(1)}, u32[]{:S(2)}, u32[]{:S(2)}) collective-permute-start(bf16[4,32,256]{2,1,0:T(8,128)(2,1)S(1)} %get-tuple-element.71), channel_id=1, source_target_pairs={{0,5},{1,4},{2,7},{3,6},{4,1},{5,0},{6,3},{7,2},{8,13},{9,12},{10,... | collective-permute-start | bytes 196616 | tf_op jit(solution)/shard_map/ppermute | solution.py:311
  66.4 14.8 %collective-permute-start.14 = (bf16[32,512]{1,0:T(8,128)(2,1)S(1)}, bf16[32,512]{1,0:T(8,128)(2,1)S(1)}, u32[]{:S(2)}, u32[]{:S(2)}) collective-permute-start(bf16[32,512]{1,0:T(8,128)(2,1)S(1)} %get-tuple-element.73), channel_id=1, source_target_pairs={{0,8},{2,10},{4,12},{6,14},{8,0},{10,2},{12,4},{14,6},{16,24},{18,... | collective-permute-start | bytes 98312 | tf_op jit(solution)/shard_map/ppermute | solution.py:34
  67.5 14.2 %collective-permute-start.15 = (bf16[32,512]{1,0:T(8,128)(2,1)S(1)}, bf16[32,512]{1,0:T(8,128)(2,1)S(1)}, u32[]{:S(2)}, u32[]{:S(2)}) collective-permute-start(bf16[32,512]{1,0:T(8,128)(2,1)S(1)} %get-tuple-element.74), channel_id=1, source_target_pairs={{0,16},{2,18},{4,20},{6,22},{8,24},{10,26},{12,28},{14,30},{16,0},... | collective-permute-start | bytes 98312 | tf_op jit(solution)/shard_map/ppermute | solution.py:34
  69.3 12.4 %collective-permute-start.16 = (bf16[32,512]{1,0:T(8,128)(2,1)S(1)}, bf16[32,512]{1,0:T(8,128)(2,1)S(1)}, u32[]{:S(2)}, u32[]{:S(2)}) collective-permute-start(bf16[32,512]{1,0:T(8,128)(2,1)S(1)} %get-tuple-element.75), channel_id=1, source_target_pairs={{0,24},{2,26},{4,28},{6,30},{8,16},{10,18},{12,20},{14,22},{16,8},... | collective-permute-start | bytes 98312 | tf_op jit(solution)/shard_map/ppermute | solution.py:34

commit v10 on v8

--- a/solution.py
+++ b/solution.py
@@ -21,6 +21,12 @@
     count = lax.axis_size(axis)
     pairs = [(source, (source + steps) % count) for source in range(count)]
     return lax.ppermute(value, axis, pairs)
+
+
+def moved(value, target):
+    count = lax.axis_size("gossip")
+    pairs = [(source, target(source) % count) for source in range(count) if target(source) is not None]
+    return lax.ppermute(value, "gossip", pairs)
 
 
 def flipped(value, axis, bit):
@@ -92,16 +98,45 @@
     give[...] = held[:, pl.ds(1 - mine, 1)].reshape(give.shape)
 
 
-def round_kernel(step, mix, base, arrived, rounded, master):
+def round_kernel(step, mix, base, arrived, rounded, master, *pieces):
     _, peer = shares(mix, step)
     total = base[...] + peer * arrived[...].astype(jnp.float32)
     rounded[...] = total.astype(jnp.bfloat16)
     master[...] = total
-
-
-def finish_kernel(mix, base, arrived, *refs):
+    for i, piece in enumerate(pieces):
+        width = piece.shape[1]
+        piece[...] = rounded[:, i * width:(i + 1) * width]
+
+
+def gather_kernel(step, mix, base, direct, hop, relay, lead, rounded, master):
+    _, peer = shares(mix, step)
+    at = lax.axis_index("gossip")
+    core, chip = at & 1, (at >> 1) & 1
+
+    def add(columns, arrived):
+        total = base[:, columns] + peer * arrived[...].astype(jnp.float32)
+        rounded[:, columns] = total.astype(jnp.bfloat16)
+        master[:, columns] = total
+
+    width = hop.shape[1]
+    pl.when(core == 0)(lambda: add(slice(None), direct))
+    pl.when((core == 1) & (chip == 1))(lambda: add(slice(0, width), hop))
+    pl.when((core == 1) & (chip == 0))(lambda: add(slice(0, width), relay))
+    pl.when(core == 1)(lambda: add(slice(width, None), lead))
+
+
+def finish_kernel(count, mix, base, *refs):
     _, peer = shares(mix, STEPS - 1)
-    refs[-1][...] = (base[...] + peer * arrived[...].astype(jnp.float32)).astype(jnp.bfloat16)
+    core = lax.axis_index("gossip") & 1
+
+    def add(arrived):
+        refs[-1][...] = (base[...] + peer * arrived[...].astype(jnp.float32)).astype(jnp.bfloat16)
+
+    if count == 1:
+        add(refs[0])
+    else:
+        for i in range(count):
+            pl.when(core == i)(functools.partial(add, refs[i]))
 
 
 def leg_kernel(axis, bit, kept, arrived, keep, give):
@@ -209,12 +244,18 @@
     mix, *rest = call(first_kernel, [order, plan, inputs, targets] + pieces, outs)
     shards, firsts = rest[:len(shards)], rest[len(shards):]
     for half in range(HALVES):
-        rounds0.append(
-            call(
-                functools.partial(round_kernel, 0), [mix, firsts[2 * half], arrived0[half]], [half_bf16, half_f32]
-            )
-        )
-        arrived1.append(shifted(rounds0[half][0], "gossip", 2))
+        quarter, extra = width // 2, half == HALVES - 1
+        outs = [half_bf16, half_f32] + [((din, quarter), jnp.bfloat16)] * (2 * extra)
+        rounded, master, *quarters = call(
+            functools.partial(round_kernel, 0), [mix, firsts[2 * half], arrived0[half]], outs
+        )
+        rounds0.append((rounded, master))
+        if not extra:
+            arrived1.append([shifted(rounded, "gossip", 2)])
+            continue
+        hop = moved(quarters[0], lambda at: at ^ 2 if at & 1 else None)
+        lead = moved(quarters[1], lambda at: at + 2 if at & 1 else None)
+        direct = moved(rounded, lambda at: None if at & 1 else at + 2)
     for half in range(HALVES):
         middles.append(
             call(
@@ -226,10 +267,18 @@
     parts, last = [], []
     for half in range(HALVES):
         base1, velocity1 = middles[half]
+        kernel = round_kernel if half < HALVES - 1 else gather_kernel
         rounded2, master2 = call(
-            functools.partial(round_kernel, 1), [mix, base1, arrived1[half]], [half_bf16, half_f32]
-        )
-        arrived2 = shifted(rounded2, "gossip", 4)
+            functools.partial(kernel, 1), [mix, base1] + arrived1[half], [half_bf16, half_f32]
+        )
+        if half < HALVES - 1:
+            core_0 = moved(rounded2, lambda at: None if at & 1 else at + 4)
+            relay = moved(hop, lambda at: at + 4 if at & 3 == 1 else None)
+            arrived1.append([direct, hop, relay, lead])
+            core_1 = moved(rounded2, lambda at: at + 4 if at & 1 else None)
+            arrived2 = [core_0, core_1]
+        else:
+            arrived2 = [shifted(rounded2, "gossip", 4)]
         outs, scratch = [half_f32] * 2, ()
         if split:
             pair = (n_gossip // 2, n_group * own_rows, width)
@@ -241,7 +290,7 @@
             outs,
             scratch,
         )
-        last += [base2, arrived2]
+        last.append([base2] + arrived2)
         if not split:
             parts.append(part[0])
             continue
@@ -281,12 +330,13 @@
         mean_weights = scattered_sum(jnp.concatenate(parts, axis=1)) / replicas
     result, replica_weights = ((din, dout), jnp.bfloat16), []
     for half in range(HALVES):
+        ins = [mix] + last[half] + list(replica_weights)
         replica_weights = call(
-            finish_kernel,
-            [mix, *last[2 * half:2 * half + 2], *replica_weights],
+            functools.partial(finish_kernel, len(last[half]) - 1),
+            ins,
             [result],
             out_specs=[pl.BlockSpec((din, width), lambda i, half=half: (0, half))],
-            in_place=3 if half else None,
+            in_place=len(ins) - 1 if half else None,
         )
     if split:
         (mean_weights,) = call(functools.partial(mean_kernel, replicas), [keep] + gots, [(shape, jnp.float32)])

time: 74.5 us -> 85.4 us (1.15)
  starting transfers between devices: 15 us -> 35.6 us
  waiting for transfers between devices: 44.6 us -> 34.5 us
    ppermute x8, starting transfers between devices: 8.45 us -> 25.5 us  [flipped(): lax.ppermute(value, axis, [(source, source ^ bit) for source in range(cou...]
    ppermute x6 -> x4, waiting for transfers between devices: 36.8 us -> 22.4 us  [shifted(): return lax.ppermute(value, axis, pairs)]
    ppermute x0 -> x6, starting transfers between devices: none -> 6.75 us  [moved(): return lax.ppermute(value, 'gossip', pairs)]
    ppermute x1, waiting for transfers between devices: 2.39 us -> 5.16 us  [steps(): from_xy = lax.ppermute(give_xy, ('gossip', 'group'), pairs)]
    ppermute x6 -> x4, starting transfers between devices: 5.13 us -> 3.33 us  [shifted(): return lax.ppermute(value, axis, pairs)]
    ppermute x8, waiting for transfers between devices: 5.43 us -> 6.99 us  [flipped(): lax.ppermute(value, axis, [(source, source ^ bit) for source in range(cou...]
    ppermute x1, starting transfers between devices: 1.38 us -> 0.01 us  [steps(): from_xy = lax.ppermute(give_xy, ('gossip', 'group'), pairs)]
  transfers between devices with their start and end apart: 15 -> 19, of which waited for: 9 -> 8; matrix products, arithmetic and copies ran while one was open for 1% -> 1% of each run, Pallas kernels for 13% -> 12%
where the time goes in v10:
time: 85.4 us; the launch traced here: 85.1 us
  starting transfers between devices  35.6 us (42%)
  waiting for transfers between devices  34.5 us (40%)
  Pallas kernels  10.7 us (13%)
  local copies, waits for them, and re-layouts  3.41 us (4%)
    ppermute x8, starting transfers between devices, flipped(): lax.ppermute(value, axis, [(source, source ^ bit) for source in range(cou...  25.5 us
    ppermute x4, waiting for transfers between devices, shifted(): return lax.ppermute(value, axis, pairs)  22.4 us
    pallas_call x15, Pallas kernels, call(): pl.pallas_call(kernel, grid=(1,) if out_specs else (), in_specs=in_specs,...  10.7 us
    ppermute x8, waiting for transfers between devices, flipped(): lax.ppermute(value, axis, [(source, source ^ bit) for source in range(cou...  6.99 us
    ppermute x6, starting transfers between devices, moved(): return lax.ppermute(value, 'gossip', pairs)  6.75 us
    ppermute x1, waiting for transfers between devices, steps(): from_xy = lax.ppermute(give_xy, ('gossip', 'group'), pairs)  5.16 us
    ppermute x4, starting transfers between devices, shifted(): return lax.ppermute(value, axis, pairs)  3.33 us
    slice x2, local copies, waits for them, and re-layouts, steps(): pieces.append(weights[:, columns[half]])  2.27 us
  transfers between devices with their start and end apart: 19, of which 8 were waited for; matrix products, arithmetic and copies ran while one was open for 1% of the time, Pallas kernels for 12%

profile of v10, /device:TPU:0, one launch (start us, length us, event | category | flops | bytes accessed | tf_op | source)
XLA Modules:
  0.0 85.1 jit_solution(5665992032089510526)
XLA Ops:
  0.7 1.2 %slice.8.refs_0_ = bf16[1024,256]{1,0:T(8,128)(2,1)S(1)} slice(bf16[1024,512]{1,0:T(8,128)(2,1)} %bitcast.17), slice={[0:1024], [0:256]} | slice | bytes 1048576 | tf_op jit(solution)/shard_map/slice | solution.py:238
  1.9 0.5 collective-permute-start.6
  2.4 1.1 %slice.9.refs_1_ = bf16[1024,256]{1,0:T(8,128)(2,1)S(1)} slice(bf16[1024,512]{1,0:T(8,128)(2,1)} %bitcast.18), slice={[0:1024], [256:512]} | slice | bytes 1048576 | tf_op jit(solution)/shard_map/slice | solution.py:238
  3.5 2.7 %collective-permute-start = (bf16[1024,256]{1,0:T(8,128)(2,1)S(1)}, bf16[1024,256]{1,0:T(8,128)(2,1)S(1)}, u32[]{:S(2)}, u32[]{:S(2)}) collective-permute-start(bf16[1024,256]{1,0:T(8,128)(2,1)S(1)} %slice.9.refs_1_), channel_id=1, source_target_pairs={{0,2},{2,4},{4,6},{6,8},{8,10},{10,12},{12,14},{14,16},{16,18},{18... | collective-permute-start | bytes 1572872 | tf_op jit(solution)/shard_map/ppermute | solution.py:23
  6.2 1.1 %copy-done.1 = bf16[768,512]{1,0:T(8,128)(2,1)S(1)} copy-done((bf16[768,512]{1,0:T(8,128)(2,1)S(1)}, bf16[768,512]{1,0:T(8,128)(2,1)}, u32[]{:S(2)}) %copy-start.1) | copy-done | bytes 786456
  7.3 1.9 %shard_map.68 = (f32[8,128]{1,0:T(8,128)S(1)}, bf16[256,1024]{1,0:T(8,128)(2,1)S(1)}, bf16[256,512]{1,0:T(8,128)(2,1)S(1)}, bf16[256,1024]{1,0:T(8,128)(2,1)S(1)...) custom-call(s32[1,3]{1,0:T(1,128)S(1)} %copy-done.3, ...), custom_call_target="tpu_custom_call" | custom-call | tf_op jit(solution)/shard_map/pallas_call | solution.py:193
  9.2 5.0 %collective-permute-done.6.arrived = bf16[1024,256]{1,0:T(8,128)(2,1)S(1)} collective-permute-done((bf16[1024,256]{1,0:T(8,128)(2,1)S(1)}, bf16[1024,256]{1,0:T(8,128)(2,1)S(1)}, u32[]{:S(2)}, u32[]{:S(2)}) %collective-permute-start.6) | collective-permute-done | bytes 524320 | tf_op jit(solution)/shard_map/ppermute | solution.py:23
  14.2 0.3 shard_map.73
  14.6 0.1 collective-permute-start.7
  14.6 5.2 %collective-permute-done.arrived = bf16[1024,256]{1,0:T(8,128)(2,1)S(1)} collective-permute-done((bf16[1024,256]{1,0:T(8,128)(2,1)S(1)}, bf16[1024,256]{1,0:T(8,128)(2,1)S(1)}, u32[]{:S(2)}, u32[]{:S(2)}) %collective-permute-start) | collective-permute-done | bytes 524320 | tf_op jit(solution)/shard_map/ppermute | solution.py:23
  19.9 0.4 shard_map.69
  20.3 0.7 collective-permute-start.2
  21.0 2.1 %collective-permute-start.1 = (bf16[1024,256]{1,0:T(8,128)(2,1)S(1)}, bf16[1024,256]{1,0:T(8,128)(2,1)S(1)}, u32[]{:S(2)}, u32[]{:S(2)}) collective-permute-start(bf16[1024,256]{1,0:T(8,128)(2,1)S(1)} %get-tuple-element.47.rounded), channel_id=1, source_target_pairs={{0,4},{4,8},{8,12},{12,16},{16,20},{20,24},{24,28},{28,0},{1,5},{5... | collective-permute-start | bytes 1572872 | tf_op jit(solution)/shard_map/ppermute | solution.py:29
  23.1 0.7 collective-permute-start.4
  23.8 0.0 collective-permute-done.2.hop
  23.8 0.7 collective-permute-start.3
  24.5 0.9 %shard_map.74 = (f32[1024,256]{1,0:T(8,128)S(1)}, f32[1024,256]{1,0:T(8,128)S(1)}) custom-call(f32[8,128]{1,0:T(8,128)S(1)} %get-tuple-element.41.mix, bf16[256,1024]{1,0:T(8,128)(2,1)S(1)} %get-tuple-element.44.x, bf16[256,512]{1,0:T(8,128)(2,1)S(1)} %get-tuple-element.45.t, bf16[1024,256]{1,0:T(8,128)(2,1)S(1)} %get-tuple-element.58.rounded, ...), custom_call_target="tpu_custom_call" | custom-call | tf_op jit(solution)/shard_map/pallas_call | solution.py:193
  25.4 6.8 %collective-permute-done.7.arrived = bf16[1024,256]{1,0:T(8,128)(2,1)S(1)} collective-permute-done((bf16[1024,256]{1,0:T(8,128)(2,1)S(1)}, bf16[1024,256]{1,0:T(8,128)(2,1)S(1)}, u32[]{:S(2)}, u32[]{:S(2)}) %collective-permute-start.7) | collective-permute-done | bytes 524320 | tf_op jit(solution)/shard_map/ppermute | solution.py:23
  32.2 0.3 shard_map.75
  32.5 1.2 %shard_map.76 = (f32[1024,256]{1,0:T(8,128)S(1)}, f32[8,64,256]{2,1,0:T(8,128)S(1)}, f32[8,64,256]{2,1,0:T(8,128)S(1)}) custom-call(f32[8,128]{1,0:T(8,128)S(1)} %get-tuple-element.41.mix, bf16[256,1024]{1,0:T(8,128)(2,1)S(1)} %get-tuple-element.42.x, bf16[256,512]{1,0:T(8,128)(2,1)S(1)} %get-tuple-element.43.t, ...), custom_call_target="tpu_custom_call" | custom-call | tf_op jit(solution)/shard_map/pallas_call | solution.py:193
  33.8 12.9 %collective-permute-start.10 = (f32[8,64,256]{2,1,0:T(8,128)S(1)}, f32[8,64,256]{2,1,0:T(8,128)S(1)}, u32[]{:S(2)}, u32[]{:S(2)}) collective-permute-start(f32[8,64,256]{2,1,0:T(8,128)S(1)} %get-tuple-element.67), channel_id=1, source_target_pairs={{0,2},{2,0},{4,6},{6,4},{8,10},{10,8},{12,14},{14,12},{16,18},{18,... | collective-permute-start | bytes 1572872 | tf_op jit(solution)/shard_map/ppermute | solution.py:34
  46.6 0.9 %shard_map.70 = (f32[1024,256]{1,0:T(8,128)S(1)}, f32[1024,256]{1,0:T(8,128)S(1)}) custom-call(f32[8,128]{1,0:T(8,128)S(1)} %get-tuple-element.41.mix, bf16[256,1024]{1,0:T(8,128)(2,1)S(1)} %get-tuple-element.44.x, bf16[256,512]{1,0:T(8,128)(2,1)S(1)} %get-tuple-element.45.t, bf16[1024,256]{1,0:T(8,128)(2,1)S(1)} %get-tuple-element.47.rounded, ...), custom_call_target="tpu_custom_call" | custom-call | tf_op jit(solution)/shard_map/pallas_call | solution.py:193
  47.6 0.0 collective-permute-done.3.relay
  47.6 0.0 collective-permute-done.1.direct
  47.6 0.3 shard_map.71
  47.9 1.2 %shard_map.72 = (f32[1024,256]{1,0:T(8,128)S(1)}, f32[8,64,256]{2,1,0:T(8,128)S(1)}, f32[8,64,256]{2,1,0:T(8,128)S(1)}) custom-call(f32[8,128]{1,0:T(8,128)S(1)} %get-tuple-element.41.mix, bf16[256,1024]{1,0:T(8,128)(2,1)S(1)} %get-tuple-element.42.x, bf16[256,512]{1,0:T(8,128)(2,1)S(1)} %get-tuple-element.43.t, ...), custom_call_target="tpu_custom_call" | custom-call | tf_op jit(solution)/shard_map/pallas_call | solution.py:193
  49.2 3.5 %collective-permute-start.12 = (f32[8,64,256]{2,1,0:T(8,128)S(1)}, f32[8,64,256]{2,1,0:T(8,128)S(1)}, u32[]{:S(2)}, u32[]{:S(2)}) collective-permute-start(f32[8,64,256]{2,1,0:T(8,128)S(1)} %get-tuple-element.71), channel_id=1, source_target_pairs={{0,2},{2,0},{4,6},{6,4},{8,10},{10,8},{12,14},{14,12},{16,18},{18,... | collective-permute-start | bytes 1572872 | tf_op jit(solution)/shard_map/ppermute | solution.py:34
  52.7 1.9 %collective-permute-start.8 = (bf16[1024,256]{1,0:T(8,128)(2,1)S(1)}, bf16[1024,256]{1,0:T(8,128)(2,1)S(1)}, u32[]{:S(2)}, u32[]{:S(2)}) collective-permute-start(bf16[1024,256]{1,0:T(8,128)(2,1)S(1)} %get-tuple-element.62.rounded), channel_id=1, source_target_pairs={{0,8},{4,12},{8,16},{12,20},{16,24},{20,28},{24,0},{28,4},{1,9},{5... | collective-permute-start | bytes 1572872 | tf_op jit(solution)/shard_map/ppermute | solution.py:29
  54.6 0.7 collective-permute-start.9
  55.3 0.1 collective-permute-start.5
  55.4 0.1 shard_map.79
  55.5 2.0 %collective-permute-start.11 = (bf16[8,32,256]{2,1,0:T(8,128)(2,1)S(1)}, bf16[8,32,256]{2,1,0:T(8,128)(2,1)S(1)}, u32[]{:S(2)}, u32[]{:S(2)}) collective-permute-start(bf16[8,32,256]{2,1,0:T(8,128)(2,1)S(1)} %get-tuple-element.69), channel_id=1, source_target_pairs={{0,1},{1,0},{2,3},{3,2},{4,5},{5,4},{6,7},{7,6},{8,9},{9,8},{10,11... | collective-permute-start | bytes 393224 | tf_op jit(solution)/shard_map/ppermute | solution.py:34
  57.5 3.7 %collective-permute-done.11 = bf16[8,32,256]{2,1,0:T(8,128)(2,1)S(1)} collective-permute-done((bf16[8,32,256]{2,1,0:T(8,128)(2,1)S(1)}, bf16[8,32,256]{2,1,0:T(8,128)(2,1)S(1)}, u32[]{:S(2)}, u32[]{:S(2)}) %collective-permute-start.11) | collective-permute-done | bytes 131104 | tf_op jit(solution)/shard_map/ppermute | solution.py:34
  61.2 0.1 shard_map.80
  61.3 1.8 %collective-permute-start.14 = (bf16[4,32,256]{2,1,0:T(8,128)(2,1)S(1)}, bf16[4,32,256]{2,1,0:T(8,128)(2,1)S(1)}, u32[]{:S(2)}, u32[]{:S(2)}) collective-permute-start(bf16[4,32,256]{2,1,0:T(8,128)(2,1)S(1)} %get-tuple-element.74), channel_id=1, source_target_pairs={{0,1},{1,0},{2,3},{3,2},{4,5},{5,4},{6,7},{7,6},{8,9},{9,8},{10,11... | collective-permute-start | bytes 196616 | tf_op jit(solution)/shard_map/ppermute | solution.py:34
  63.1 0.0 collective-permute-start.13
  63.1 2.5 %collective-permute-done.14.from_x = bf16[4,32,256]{2,1,0:T(8,128)(2,1)S(1)} collective-permute-done((bf16[4,32,256]{2,1,0:T(8,128)(2,1)S(1)}, bf16[4,32,256]{2,1,0:T(8,128)(2,1)S(1)}, u32[]{:S(2)}, u32[]{:S(2)}) %collective-permute-start.14) | collective-permute-done | bytes 65568 | tf_op jit(solution)/shard_map/ppermute | solution.py:34
  65.6 0.0 collective-permute-start.15
  65.6 5.2 %collective-permute-done.15.from_xy = bf16[4,32,256]{2,1,0:T(8,128)(2,1)S(1)} collective-permute-done((bf16[4,32,256]{2,1,0:T(8,128)(2,1)S(1)}, bf16[4,32,256]{2,1,0:T(8,128)(2,1)S(1)}, u32[]{:S(2)}, u32[]{:S(2)}) %collective-permute-start.15) | collective-permute-done | bytes 65568 | tf_op jit(solution)/shard_map/ppermute | solution.py:322
  70.9 1.1 %collective-permute-start.16 = (bf16[32,512]{1,0:T(8,128)(2,1)S(1)}, bf16[32,512]{1,0:T(8,128)(2,1)S(1)}, u32[]{:S(2)}, u32[]{:S(2)}) collective-permute-start(bf16[32,512]{1,0:T(8,128)(2,1)S(1)} %get-tuple-element.77), channel_id=1, source_target_pairs={{0,8},{2,10},{4,12},{6,14},{8,0},{10,2},{12,4},{14,6},{16,24},{18,... | collective-permute-start | bytes 98312 | tf_op jit(solution)/shard_map/ppermute | solution.py:34
  72.0 3.0 %collective-permute-start.17 = (bf16[32,512]{1,0:T(8,128)(2,1)S(1)}, bf16[32,512]{1,0:T(8,128)(2,1)S(1)}, u32[]{:S(2)}, u32[]{:S(2)}) collective-permute-start(bf16[32,512]{1,0:T(8,128)(2,1)S(1)} %get-tuple-element.78), channel_id=1, source_target_pairs={{0,16},{2,18},{4,20},{6,22},{8,24},{10,26},{12,28},{14,30},{16,0},... | collective-permute-start | bytes 98312 | tf_op jit(solution)/shard_map/ppermute | solution.py:34
  75.0 1.2 %collective-permute-start.18 = (bf16[32,512]{1,0:T(8,128)(2,1)S(1)}, bf16[32,512]{1,0:T(8,128)(2,1)S(1)}, u32[]{:S(2)}, u32[]{:S(2)}) collective-permute-start(bf16[32,512]{1,0:T(8,128)(2,1)S(1)} %get-tuple-element.79), channel_id=1, source_target_pairs={{0,24},{2,26},{4,28},{6,30},{8,16},{10,18},{12,20},{14,22},{16,8},... | collective-permute-start | bytes 98312 | tf_op jit(solution)/shard_map/ppermute | solution.py:34
  76.2 1.1 %shard_map.77.refs_1_ = bf16[1024,512]{1,0:T(8,128)(2,1)} custom-call(f32[8,128]{1,0:T(8,128)S(1)} %get-tuple-element.41.mix, f32[1024,256]{1,0:T(8,128)S(1)} %get-tuple-element.65.base, bf16[1024,256]{1,0:T(8,128)(2,1)S(1)} %collective-permute-done.8.refs_0_, bf16[1024,256]{1,0:T(8,128)(2,1)S(1)} %collective-permute-done.9.refs_1_), custom_call_target="tpu_custom_call" | custom-call | tf_op jit(solution)/shard_map/pallas_call | solution.py:193
  77.3 5.3 %collective-permute-done.5.refs_0_ = bf16[1024,256]{1,0:T(8,128)(2,1)S(1)} collective-permute-done((bf16[1024,256]{1,0:T(8,128)(2,1)S(1)}, bf16[1024,256]{1,0:T(8,128)(2,1)S(1)}, u32[]{:S(2)}, u32[]{:S(2)}) %collective-permute-start.5) | collective-permute-done | bytes 524320 | tf_op jit(solution)/shard_map/ppermute | solution.py:23
  82.6 1.1 %shard_map.78 = bf16[1024,512]{1,0:T(8,128)(2,1)} custom-call(f32[8,128]{1,0:T(8,128)S(1)} %get-tuple-element.41.mix, f32[1024,256]{1,0:T(8,128)S(1)} %get-tuple-element.56.base, bf16[1024,256]{1,0:T(8,128)(2,1)S(1)} %collective-permute-done.5.refs_0_, bf16[1024,512]{1,0:T(8,128)(2,1)} %shard_map.77.refs_1_), custom_call_target="tpu_custom_call", output_to_operand_aliasing={{}: (3, {})} | custom-call | tf_op jit(solution)/shard_map/pallas_call | solution.py:193
  83.7 0.0 collective-permute-done.16.refs_0_
  83.7 0.7 collective-permute-done.17.refs_1_
  84.4 0.7 shard_map.82
  (15 shorter events, 0.1 us)
Async XLA Ops:
  0.6 5.5 %copy-start.2 = (s32[3,2]{0,1:T(2,128)S(1)}, s32[3,2]{0,1:T(2,128)}, u32[]{:S(2)}) copy-start(s32[3,2]{0,1:T(2,128)} %param.8) | copy-start | bytes 76
  0.6 5.5 %copy-start = (bf16[768,1024]{1,0:T(8,128)(2,1)S(1)}, bf16[768,1024]{1,0:T(8,128)(2,1)}, u32[]{:S(2)}) copy-start(bf16[768,1024]{1,0:T(8,128)(2,1)} %x.1) | copy-start | bytes 4718596
  0.7 5.5 %copy-start.3 = (s32[1,3]{1,0:T(1,128)S(1)}, s32[1,3]{1,0:T(1,128)}, u32[]{:S(2)}) copy-start(s32[1,3]{1,0:T(1,128)} %order.1) | copy-start | bytes 40
  1.9 12.4 %collective-permute-start.6 = (bf16[1024,256]{1,0:T(8,128)(2,1)S(1)}, bf16[1024,256]{1,0:T(8,128)(2,1)S(1)}, u32[]{:S(2)}, u32[]{:S(2)}) collective-permute-start(bf16[1024,256]{1,0:T(8,128)(2,1)S(1)} %slice.8.refs_0_), channel_id=1, source_target_pairs={{0,2},{2,4},{4,6},{6,8},{8,10},{10,12},{12,14},{14,16},{16,18},{18... | collective-permute-start | bytes 1572872 | tf_op jit(solution)/shard_map/ppermute | solution.py:23
  3.5 16.4 %collective-permute-start = (bf16[1024,256]{1,0:T(8,128)(2,1)S(1)}, bf16[1024,256]{1,0:T(8,128)(2,1)S(1)}, u32[]{:S(2)}, u32[]{:S(2)}) collective-permute-start(bf16[1024,256]{1,0:T(8,128)(2,1)S(1)} %slice.9.refs_1_), channel_id=1, source_target_pairs={{0,2},{2,4},{4,6},{6,8},{8,10},{10,12},{12,14},{14,16},{16,18},{18... | collective-permute-start | bytes 1572872 | tf_op jit(solution)/shard_map/ppermute | solution.py:23
  6.2 1.1 %copy-start.1 = (bf16[768,512]{1,0:T(8,128)(2,1)S(1)}, bf16[768,512]{1,0:T(8,128)(2,1)}, u32[]{:S(2)}) copy-start(bf16[768,512]{1,0:T(8,128)(2,1)} %t.1) | copy-start | bytes 2359300
  14.6 17.6 %collective-permute-start.7 = (bf16[1024,256]{1,0:T(8,128)(2,1)S(1)}, bf16[1024,256]{1,0:T(8,128)(2,1)S(1)}, u32[]{:S(2)}, u32[]{:S(2)}) collective-permute-start(bf16[1024,256]{1,0:T(8,128)(2,1)S(1)} %get-tuple-element.58.rounded), channel_id=1, source_target_pairs={{0,4},{2,6},{4,8},{6,10},{8,12},{10,14},{12,16},{14,18},{16,20},{1... | collective-permute-start | bytes 1572872 | tf_op jit(solution)/shard_map/ppermute | solution.py:23
  20.3 3.5 %collective-permute-start.2 = (bf16[1024,128]{1,0:T(8,128)(2,1)S(1)}, bf16[1024,128]{1,0:T(8,128)(2,1)S(1)}, u32[]{:S(2)}, u32[]{:S(2)}) collective-permute-start(bf16[1024,128]{1,0:T(8,128)(2,1)S(1)} %get-tuple-element.51), channel_id=1, source_target_pairs={{2,6},{6,2},{10,14},{14,10},{18,22},{22,18},{26,30},{30,26},{3,7},... | collective-permute-start | bytes 786440 | tf_op jit(solution)/shard_map/ppermute | solution.py:29
  21.0 26.6 %collective-permute-start.1 = (bf16[1024,256]{1,0:T(8,128)(2,1)S(1)}, bf16[1024,256]{1,0:T(8,128)(2,1)S(1)}, u32[]{:S(2)}, u32[]{:S(2)}) collective-permute-start(bf16[1024,256]{1,0:T(8,128)(2,1)S(1)} %get-tuple-element.47.rounded), channel_id=1, source_target_pairs={{0,4},{4,8},{8,12},{12,16},{16,20},{20,24},{24,28},{28,0},{1,5},{5... | collective-permute-start | bytes 1572872 | tf_op jit(solution)/shard_map/ppermute | solution.py:29
  23.1 24.5 %collective-permute-start.4 = (bf16[1024,128]{1,0:T(8,128)(2,1)S(1)}, bf16[1024,128]{1,0:T(8,128)(2,1)S(1)}, u32[]{:S(2)}, u32[]{:S(2)}) collective-permute-start(bf16[1024,128]{1,0:T(8,128)(2,1)S(1)} %get-tuple-element.52), channel_id=1, source_target_pairs={{2,6},{6,10},{10,14},{14,18},{18,22},{22,26},{26,30},{30,2},{3,7},... | collective-permute-start | bytes 786440 | tf_op jit(solution)/shard_map/ppermute | solution.py:29
  23.8 23.8 %collective-permute-start.3 = (bf16[1024,128]{1,0:T(8,128)(2,1)S(1)}, bf16[1024,128]{1,0:T(8,128)(2,1)S(1)}, u32[]{:S(2)}, u32[]{:S(2)}) collective-permute-start(bf16[1024,128]{1,0:T(8,128)(2,1)S(1)} %collective-permute-done.2.hop), channel_id=1, source_target_pairs={{2,10},{10,18},{18,26},{26,2},{3,11},{11,19},{19,27},{27,3}} | collective-permute-start | bytes 786440 | tf_op jit(solution)/shard_map/ppermute | solution.py:29
  33.8 21.7 %collective-permute-start.10 = (f32[8,64,256]{2,1,0:T(8,128)S(1)}, f32[8,64,256]{2,1,0:T(8,128)S(1)}, u32[]{:S(2)}, u32[]{:S(2)}) collective-permute-start(f32[8,64,256]{2,1,0:T(8,128)S(1)} %get-tuple-element.67), channel_id=1, source_target_pairs={{0,2},{2,0},{4,6},{6,4},{8,10},{10,8},{12,14},{14,12},{16,18},{18,... | collective-permute-start | bytes 1572872 | tf_op jit(solution)/shard_map/ppermute | solution.py:34
  49.2 8.3 %collective-permute-start.12 = (f32[8,64,256]{2,1,0:T(8,128)S(1)}, f32[8,64,256]{2,1,0:T(8,128)S(1)}, u32[]{:S(2)}, u32[]{:S(2)}) collective-permute-start(f32[8,64,256]{2,1,0:T(8,128)S(1)} %get-tuple-element.71), channel_id=1, source_target_pairs={{0,2},{2,0},{4,6},{6,4},{8,10},{10,8},{12,14},{14,12},{16,18},{18,... | collective-permute-start | bytes 1572872 | tf_op jit(solution)/shard_map/ppermute | solution.py:34
  52.7 22.3 %collective-permute-start.8 = (bf16[1024,256]{1,0:T(8,128)(2,1)S(1)}, bf16[1024,256]{1,0:T(8,128)(2,1)S(1)}, u32[]{:S(2)}, u32[]{:S(2)}) collective-permute-start(bf16[1024,256]{1,0:T(8,128)(2,1)S(1)} %get-tuple-element.62.rounded), channel_id=1, source_target_pairs={{0,8},{4,12},{8,16},{12,20},{16,24},{20,28},{24,0},{28,4},{1,9},{5... | collective-permute-start | bytes 1572872 | tf_op jit(solution)/shard_map/ppermute | solution.py:29
  54.6 21.5 %collective-permute-start.9 = (bf16[1024,256]{1,0:T(8,128)(2,1)S(1)}, bf16[1024,256]{1,0:T(8,128)(2,1)S(1)}, u32[]{:S(2)}, u32[]{:S(2)}) collective-permute-start(bf16[1024,256]{1,0:T(8,128)(2,1)S(1)} %get-tuple-element.62.rounded), channel_id=1, source_target_pairs={{2,10},{6,14},{10,18},{14,22},{18,26},{22,30},{26,2},{30,6},{3,11}... | collective-permute-start | bytes 1572872 | tf_op jit(solution)/shard_map/ppermute | solution.py:29
  55.3 27.2 %collective-permute-start.5 = (bf16[1024,256]{1,0:T(8,128)(2,1)S(1)}, bf16[1024,256]{1,0:T(8,128)(2,1)S(1)}, u32[]{:S(2)}, u32[]{:S(2)}) collective-permute-start(bf16[1024,256]{1,0:T(8,128)(2,1)S(1)} %get-tuple-element.53.rounded), channel_id=1, source_target_pairs={{0,8},{2,10},{4,12},{6,14},{8,16},{10,18},{12,20},{14,22},{16,24},... | collective-permute-start | bytes 1572872 | tf_op jit(solution)/shard_map/ppermute | solution.py:23
  55.5 5.7 %collective-permute-start.11 = (bf16[8,32,256]{2,1,0:T(8,128)(2,1)S(1)}, bf16[8,32,256]{2,1,0:T(8,128)(2,1)S(1)}, u32[]{:S(2)}, u32[]{:S(2)}) collective-permute-start(bf16[8,32,256]{2,1,0:T(8,128)(2,1)S(1)} %get-tuple-element.69), channel_id=1, source_target_pairs={{0,1},{1,0},{2,3},{3,2},{4,5},{5,4},{6,7},{7,6},{8,9},{9,8},{10,11... | collective-permute-start | bytes 393224 | tf_op jit(solution)/shard_map/ppermute | solution.py:34
  61.3 4.3 %collective-permute-start.14 = (bf16[4,32,256]{2,1,0:T(8,128)(2,1)S(1)}, bf16[4,32,256]{2,1,0:T(8,128)(2,1)S(1)}, u32[]{:S(2)}, u32[]{:S(2)}) collective-permute-start(bf16[4,32,256]{2,1,0:T(8,128)(2,1)S(1)} %get-tuple-element.74), channel_id=1, source_target_pairs={{0,1},{1,0},{2,3},{3,2},{4,5},{5,4},{6,7},{7,6},{8,9},{9,8},{10,11... | collective-permute-start | bytes 196616 | tf_op jit(solution)/shard_map/ppermute | solution.py:34
  63.1 7.7 %collective-permute-start.13 = (bf16[4,32,512]{2,1,0:T(8,128)(2,1)S(1)}, bf16[4,32,512]{2,1,0:T(8,128)(2,1)S(1)}, u32[]{:S(2)}, u32[]{:S(2)}) collective-permute-start(bf16[4,32,512]{2,1,0:T(8,128)(2,1)S(1)} %get-tuple-element.73), channel_id=1, source_target_pairs={{0,4},{2,6},{4,0},{6,2},{8,12},{10,14},{12,8},{14,10},{16,20},{18,... | collective-permute-start | bytes 393224 | tf_op jit(solution)/shard_map/ppermute | solution.py:34
  65.6 5.2 %collective-permute-start.15 = (bf16[4,32,256]{2,1,0:T(8,128)(2,1)S(1)}, bf16[4,32,256]{2,1,0:T(8,128)(2,1)S(1)}, u32[]{:S(2)}, u32[]{:S(2)}) collective-permute-start(bf16[4,32,256]{2,1,0:T(8,128)(2,1)S(1)} %get-tuple-element.75), channel_id=1, source_target_pairs={{0,5},{1,4},{2,7},{3,6},{4,1},{5,0},{6,3},{7,2},{8,13},{9,12},{10,... | collective-permute-start | bytes 196616 | tf_op jit(solution)/shard_map/ppermute | solution.py:322
  70.9 12.9 %collective-permute-start.16 = (bf16[32,512]{1,0:T(8,128)(2,1)S(1)}, bf16[32,512]{1,0:T(8,128)(2,1)S(1)}, u32[]{:S(2)}, u32[]{:S(2)}) collective-permute-start(bf16[32,512]{1,0:T(8,128)(2,1)S(1)} %get-tuple-element.77), channel_id=1, source_target_pairs={{0,8},{2,10},{4,12},{6,14},{8,0},{10,2},{12,4},{14,6},{16,24},{18,... | collective-permute-start | bytes 98312 | tf_op jit(solution)/shard_map/ppermute | solution.py:34
  72.0 12.5 %collective-permute-start.17 = (bf16[32,512]{1,0:T(8,128)(2,1)S(1)}, bf16[32,512]{1,0:T(8,128)(2,1)S(1)}, u32[]{:S(2)}, u32[]{:S(2)}) collective-permute-start(bf16[32,512]{1,0:T(8,128)(2,1)S(1)} %get-tuple-element.78), channel_id=1, source_target_pairs={{0,16},{2,18},{4,20},{6,22},{8,24},{10,26},{12,28},{14,30},{16,0},... | collective-permute-start | bytes 98312 | tf_op jit(solution)/shard_map/ppermute | solution.py:34
  75.0 9.4 %collective-permute-start.18 = (bf16[32,512]{1,0:T(8,128)(2,1)S(1)}, bf16[32,512]{1,0:T(8,128)(2,1)S(1)}, u32[]{:S(2)}, u32[]{:S(2)}) collective-permute-start(bf16[32,512]{1,0:T(8,128)(2,1)S(1)} %get-tuple-element.79), channel_id=1, source_target_pairs={{0,24},{2,26},{4,28},{6,30},{8,16},{10,18},{12,20},{14,22},{16,8},... | collective-permute-start | bytes 98312 | tf_op jit(solution)/shard_map/ppermute | solution.py:34

commit v11 on v8

--- a/solution.py
+++ b/solution.py
@@ -138,11 +138,13 @@
         out[:, width:] = (rows[:, :, width:] + late).reshape(out.shape[0], width).astype(out.dtype)
 
 
-def mean_kernel(replicas, keep, *refs):
+def final_kernel(replicas, mix, base, arrived, other_half, keep, *refs):
+    out, mean = refs[-2:]
+    finish_kernel(mix, base, arrived, other_half, out)
     total = keep[...]
-    for piece in refs[:-1]:
+    for piece in refs[:-2]:
         total = total + piece[...].astype(jnp.float32)
-    refs[-1][...] = total / replicas
+    mean[...] = total / replicas
 
 
 IN_VMEM = pl.BlockSpec(memory_space=pltpu.VMEM)
@@ -281,15 +283,16 @@
         mean_weights = scattered_sum(jnp.concatenate(parts, axis=1)) / replicas
     result, replica_weights = ((din, dout), jnp.bfloat16), []
     for half in range(HALVES):
-        replica_weights = call(
-            finish_kernel,
-            [mix, *last[2 * half:2 * half + 2], *replica_weights],
-            [result],
-            out_specs=[pl.BlockSpec((din, width), lambda i, half=half: (0, half))],
-            in_place=3 if half else None,
-        )
-    if split:
-        (mean_weights,) = call(functools.partial(mean_kernel, replicas), [keep] + gots, [(shape, jnp.float32)])
+        ins = [mix, *last[2 * half:2 * half + 2], *replica_weights]
+        block = pl.BlockSpec((din, width), lambda i, half=half: (0, half))
+        in_place = 3 if half else None
+        if split and half == HALVES - 1:
+            *replica_weights, mean_weights = call(
+                functools.partial(final_kernel, replicas), ins + [keep] + gots, [result, (shape, jnp.float32)],
+                out_specs=[block, IN_VMEM], in_place=in_place,
+            )
+        else:
+            replica_weights = call(finish_kernel, ins, [result], out_specs=[block], in_place=in_place)
     return (replica_weights[0][None], mean_weights)
 
 

time: 74.5 us -> 74.9 us (level)
  waiting for transfers between devices: 44.6 us -> 45.7 us
    ppermute x8, waiting for transfers between devices: 5.43 us -> 6.51 us  [flipped(): lax.ppermute(value, axis, [(source, source ^ bit) for source in range(cou...]
    pallas_call x15 -> x14, Pallas kernels: 10.5 us -> 9.85 us  [call(): pl.pallas_call(kernel, grid=(1,) if out_specs else (), in_specs=in_specs,...]
  transfers between devices with their start and end apart: 15 -> 15, of which waited for: 9 -> 10; matrix products, arithmetic and copies ran while one was open for 1% -> 1% of each run, Pallas kernels for 13% -> 12%
where the time goes in v11:
time: 74.9 us; the launch traced here: 74.7 us
  waiting for transfers between devices  45.7 us (61%)
  starting transfers between devices  15 us (20%)
  Pallas kernels  9.85 us (13%)
  local copies, waits for them, and re-layouts  3.41 us (5%)
  between operations  0.76 us (1%)
    ppermute x6, waiting for transfers between devices, shifted(): return lax.ppermute(value, axis, pairs)  36.8 us
    pallas_call x14, Pallas kernels, call(): pl.pallas_call(kernel, grid=(1,) if out_specs else (), in_specs=in_specs,...  9.85 us
    ppermute x8, starting transfers between devices, flipped(): lax.ppermute(value, axis, [(source, source ^ bit) for source in range(cou...  8.45 us
    ppermute x8, waiting for transfers between devices, flipped(): lax.ppermute(value, axis, [(source, source ^ bit) for source in range(cou...  6.51 us
    ppermute x6, starting transfers between devices, shifted(): return lax.ppermute(value, axis, pairs)  5.13 us
    ppermute x1, waiting for transfers between devices, steps(): from_xy = lax.ppermute(give_xy, ('gossip', 'group'), pairs)  2.39 us
    slice x2, local copies, waits for them, and re-layouts, steps(): pieces.append(weights[:, columns[half]])  2.27 us
  transfers between devices with their start and end apart: 15, of which 10 were waited for; matrix products, arithmetic and copies ran while one was open for 1% of the time, Pallas kernels for 12%

profile of v11, /device:TPU:0, one launch (start us, length us, event | category | flops | bytes accessed | tf_op | source)
XLA Modules:
  0.0 74.7 jit_solution(2816777009018906595)
XLA Ops:
  0.7 1.2 %slice.8.refs_0_ = bf16[1024,256]{1,0:T(8,128)(2,1)S(1)} slice(bf16[1024,512]{1,0:T(8,128)(2,1)} %bitcast.17), slice={[0:1024], [0:256]} | slice | bytes 1048576 | tf_op jit(solution)/shard_map/slice | solution.py:205
  1.9 0.5 collective-permute-start.3
  2.4 1.1 %slice.9.refs_1_ = bf16[1024,256]{1,0:T(8,128)(2,1)S(1)} slice(bf16[1024,512]{1,0:T(8,128)(2,1)} %bitcast.18), slice={[0:1024], [256:512]} | slice | bytes 1048576 | tf_op jit(solution)/shard_map/slice | solution.py:205
  3.5 2.7 %collective-permute-start = (bf16[1024,256]{1,0:T(8,128)(2,1)S(1)}, bf16[1024,256]{1,0:T(8,128)(2,1)S(1)}, u32[]{:S(2)}, u32[]{:S(2)}) collective-permute-start(bf16[1024,256]{1,0:T(8,128)(2,1)S(1)} %slice.9.refs_1_), channel_id=1, source_target_pairs={{0,2},{2,4},{4,6},{6,8},{8,10},{10,12},{12,14},{14,16},{16,18},{18... | collective-permute-start | bytes 1572872 | tf_op jit(solution)/shard_map/ppermute | solution.py:23
  6.2 0.0 copy-done.3
  6.2 0.0 copy-done
  6.2 1.1 %copy-done.1 = bf16[768,512]{1,0:T(8,128)(2,1)S(1)} copy-done((bf16[768,512]{1,0:T(8,128)(2,1)S(1)}, bf16[768,512]{1,0:T(8,128)(2,1)}, u32[]{:S(2)}) %copy-start.1) | copy-done | bytes 786456
  7.3 1.9 %shard_map.68 = (f32[8,128]{1,0:T(8,128)S(1)}, bf16[256,1024]{1,0:T(8,128)(2,1)S(1)}, bf16[256,512]{1,0:T(8,128)(2,1)S(1)}, bf16[256,1024]{1,0:T(8,128)(2,1)S(1)...) custom-call(s32[1,3]{1,0:T(1,128)S(1)} %copy-done.3, ...), custom_call_target="tpu_custom_call" | custom-call | tf_op jit(solution)/shard_map/pallas_call | solution.py:160
  9.2 5.0 %collective-permute-done.3.arrived = bf16[1024,256]{1,0:T(8,128)(2,1)S(1)} collective-permute-done((bf16[1024,256]{1,0:T(8,128)(2,1)S(1)}, bf16[1024,256]{1,0:T(8,128)(2,1)S(1)}, u32[]{:S(2)}, u32[]{:S(2)}) %collective-permute-start.3) | collective-permute-done | bytes 524320 | tf_op jit(solution)/shard_map/ppermute | solution.py:23
  14.3 0.3 shard_map.73
  14.6 0.1 collective-permute-start.4
  14.6 5.2 %collective-permute-done.arrived = bf16[1024,256]{1,0:T(8,128)(2,1)S(1)} collective-permute-done((bf16[1024,256]{1,0:T(8,128)(2,1)S(1)}, bf16[1024,256]{1,0:T(8,128)(2,1)S(1)}, u32[]{:S(2)}, u32[]{:S(2)}) %collective-permute-start) | collective-permute-done | bytes 524320 | tf_op jit(solution)/shard_map/ppermute | solution.py:23
  19.9 0.3 shard_map.69
  20.2 0.3 collective-permute-start.1
  20.4 0.9 %shard_map.74 = (f32[1024,256]{1,0:T(8,128)S(1)}, f32[1024,256]{1,0:T(8,128)S(1)}) custom-call(f32[8,128]{1,0:T(8,128)S(1)} %get-tuple-element.41.mix, bf16[256,1024]{1,0:T(8,128)(2,1)S(1)} %get-tuple-element.44.x, bf16[256,512]{1,0:T(8,128)(2,1)S(1)} %get-tuple-element.45.t, bf16[1024,256]{1,0:T(8,128)(2,1)S(1)} %get-tuple-element.56.rounded, ...), custom_call_target="tpu_custom_call" | custom-call | tf_op jit(solution)/shard_map/pallas_call | solution.py:160
  21.4 10.7 %collective-permute-done.4.arrived = bf16[1024,256]{1,0:T(8,128)(2,1)S(1)} collective-permute-done((bf16[1024,256]{1,0:T(8,128)(2,1)S(1)}, bf16[1024,256]{1,0:T(8,128)(2,1)S(1)}, u32[]{:S(2)}, u32[]{:S(2)}) %collective-permute-start.4) | collective-permute-done | bytes 524320 | tf_op jit(solution)/shard_map/ppermute | solution.py:23
  32.1 0.3 shard_map.75
  32.4 1.2 %shard_map.76 = (f32[1024,256]{1,0:T(8,128)S(1)}, f32[8,64,256]{2,1,0:T(8,128)S(1)}, f32[8,64,256]{2,1,0:T(8,128)S(1)}) custom-call(f32[8,128]{1,0:T(8,128)S(1)} %get-tuple-element.41.mix, bf16[256,1024]{1,0:T(8,128)(2,1)S(1)} %get-tuple-element.42.x, bf16[256,512]{1,0:T(8,128)(2,1)S(1)} %get-tuple-element.43.t, ...), custom_call_target="tpu_custom_call" | custom-call | tf_op jit(solution)/shard_map/pallas_call | solution.py:160
  33.7 0.1 collective-permute-start.6
  33.7 0.9 %shard_map.70 = (f32[1024,256]{1,0:T(8,128)S(1)}, f32[1024,256]{1,0:T(8,128)S(1)}) custom-call(f32[8,128]{1,0:T(8,128)S(1)} %get-tuple-element.41.mix, bf16[256,1024]{1,0:T(8,128)(2,1)S(1)} %get-tuple-element.44.x, bf16[256,512]{1,0:T(8,128)(2,1)S(1)} %get-tuple-element.45.t, bf16[1024,256]{1,0:T(8,128)(2,1)S(1)} %get-tuple-element.47.rounded, ...), custom_call_target="tpu_custom_call" | custom-call | tf_op jit(solution)/shard_map/pallas_call | solution.py:160
  34.7 7.7 %collective-permute-done.1.arrived = bf16[1024,256]{1,0:T(8,128)(2,1)S(1)} collective-permute-done((bf16[1024,256]{1,0:T(8,128)(2,1)S(1)}, bf16[1024,256]{1,0:T(8,128)(2,1)S(1)}, u32[]{:S(2)}, u32[]{:S(2)}) %collective-permute-start.1) | collective-permute-done | bytes 524320 | tf_op jit(solution)/shard_map/ppermute | solution.py:23
  42.3 0.3 shard_map.71
  42.7 1.2 %shard_map.72 = (f32[1024,256]{1,0:T(8,128)S(1)}, f32[8,64,256]{2,1,0:T(8,128)S(1)}, f32[8,64,256]{2,1,0:T(8,128)S(1)}) custom-call(f32[8,128]{1,0:T(8,128)S(1)} %get-tuple-element.41.mix, bf16[256,1024]{1,0:T(8,128)(2,1)S(1)} %get-tuple-element.42.x, bf16[256,512]{1,0:T(8,128)(2,1)S(1)} %get-tuple-element.43.t, ...), custom_call_target="tpu_custom_call" | custom-call | tf_op jit(solution)/shard_map/pallas_call | solution.py:160
  43.9 0.1 collective-permute-start.8
  44.0 0.1 collective-permute-start.5
  44.0 1.5 %collective-permute-start.2 = (bf16[1024,256]{1,0:T(8,128)(2,1)S(1)}, bf16[1024,256]{1,0:T(8,128)(2,1)S(1)}, u32[]{:S(2)}, u32[]{:S(2)}) collective-permute-start(bf16[1024,256]{1,0:T(8,128)(2,1)S(1)} %get-tuple-element.51.rounded), channel_id=1, source_target_pairs={{0,8},{2,10},{4,12},{6,14},{8,16},{10,18},{12,20},{14,22},{16,24},... | collective-permute-start | bytes 1572872 | tf_op jit(solution)/shard_map/ppermute | solution.py:23
  45.6 0.0 collective-permute-done.6
  45.6 0.1 shard_map.78
  45.7 1.6 %collective-permute-start.7 = (bf16[8,32,256]{2,1,0:T(8,128)(2,1)S(1)}, bf16[8,32,256]{2,1,0:T(8,128)(2,1)S(1)}, u32[]{:S(2)}, u32[]{:S(2)}) collective-permute-start(bf16[8,32,256]{2,1,0:T(8,128)(2,1)S(1)} %get-tuple-element.67), channel_id=1, source_target_pairs={{0,1},{1,0},{2,3},{3,2},{4,5},{5,4},{6,7},{7,6},{8,9},{9,8},{10,11... | collective-permute-start | bytes 393224 | tf_op jit(solution)/shard_map/ppermute | solution.py:28
  47.2 0.0 collective-permute-done.8
  47.2 3.5 %collective-permute-done.7 = bf16[8,32,256]{2,1,0:T(8,128)(2,1)S(1)} collective-permute-done((bf16[8,32,256]{2,1,0:T(8,128)(2,1)S(1)}, bf16[8,32,256]{2,1,0:T(8,128)(2,1)S(1)}, u32[]{:S(2)}, u32[]{:S(2)}) %collective-permute-start.7) | collective-permute-done | bytes 131104 | tf_op jit(solution)/shard_map/ppermute | solution.py:28
  50.7 0.1 shard_map.79
  50.8 0.7 collective-permute-start.9
  51.5 1.5 %collective-permute-start.10 = (bf16[4,32,256]{2,1,0:T(8,128)(2,1)S(1)}, bf16[4,32,256]{2,1,0:T(8,128)(2,1)S(1)}, u32[]{:S(2)}, u32[]{:S(2)}) collective-permute-start(bf16[4,32,256]{2,1,0:T(8,128)(2,1)S(1)} %get-tuple-element.72), channel_id=1, source_target_pairs={{0,1},{1,0},{2,3},{3,2},{4,5},{5,4},{6,7},{7,6},{8,9},{9,8},{10,11... | collective-permute-start | bytes 196616 | tf_op jit(solution)/shard_map/ppermute | solution.py:28
  52.9 1.4 %collective-permute-start.11 = (bf16[4,32,256]{2,1,0:T(8,128)(2,1)S(1)}, bf16[4,32,256]{2,1,0:T(8,128)(2,1)S(1)}, u32[]{:S(2)}, u32[]{:S(2)}) collective-permute-start(bf16[4,32,256]{2,1,0:T(8,128)(2,1)S(1)} %get-tuple-element.73), channel_id=1, source_target_pairs={{0,5},{1,4},{2,7},{3,6},{4,1},{5,0},{6,3},{7,2},{8,13},{9,12},{10,... | collective-permute-start | bytes 196616 | tf_op jit(solution)/shard_map/ppermute | solution.py:275
  54.3 1.4 %collective-permute-done.10.from_x = bf16[4,32,256]{2,1,0:T(8,128)(2,1)S(1)} collective-permute-done((bf16[4,32,256]{2,1,0:T(8,128)(2,1)S(1)}, bf16[4,32,256]{2,1,0:T(8,128)(2,1)S(1)}, u32[]{:S(2)}, u32[]{:S(2)}) %collective-permute-start.10) | collective-permute-done | bytes 65568 | tf_op jit(solution)/shard_map/ppermute | solution.py:28
  55.7 2.4 %collective-permute-done.11.from_xy = bf16[4,32,256]{2,1,0:T(8,128)(2,1)S(1)} collective-permute-done((bf16[4,32,256]{2,1,0:T(8,128)(2,1)S(1)}, bf16[4,32,256]{2,1,0:T(8,128)(2,1)S(1)}, u32[]{:S(2)}, u32[]{:S(2)}) %collective-permute-start.11) | collective-permute-done | bytes 65568 | tf_op jit(solution)/shard_map/ppermute | solution.py:275
  58.1 0.0 collective-permute-done.9.from_y
  58.2 1.6 %collective-permute-start.12 = (bf16[32,512]{1,0:T(8,128)(2,1)S(1)}, bf16[32,512]{1,0:T(8,128)(2,1)S(1)}, u32[]{:S(2)}, u32[]{:S(2)}) collective-permute-start(bf16[32,512]{1,0:T(8,128)(2,1)S(1)} %get-tuple-element.75), channel_id=1, source_target_pairs={{0,8},{2,10},{4,12},{6,14},{8,0},{10,2},{12,4},{14,6},{16,24},{18,... | collective-permute-start | bytes 98312 | tf_op jit(solution)/shard_map/ppermute | solution.py:28
  59.8 1.8 %collective-permute-start.13 = (bf16[32,512]{1,0:T(8,128)(2,1)S(1)}, bf16[32,512]{1,0:T(8,128)(2,1)S(1)}, u32[]{:S(2)}, u32[]{:S(2)}) collective-permute-start(bf16[32,512]{1,0:T(8,128)(2,1)S(1)} %get-tuple-element.76), channel_id=1, source_target_pairs={{0,16},{2,18},{4,20},{6,22},{8,24},{10,26},{12,28},{14,30},{16,0},... | collective-permute-start | bytes 98312 | tf_op jit(solution)/shard_map/ppermute | solution.py:28
  61.6 1.2 %collective-permute-start.14 = (bf16[32,512]{1,0:T(8,128)(2,1)S(1)}, bf16[32,512]{1,0:T(8,128)(2,1)S(1)}, u32[]{:S(2)}, u32[]{:S(2)}) collective-permute-start(bf16[32,512]{1,0:T(8,128)(2,1)S(1)} %get-tuple-element.77), channel_id=1, source_target_pairs={{0,24},{2,26},{4,28},{6,30},{8,16},{10,18},{12,20},{14,22},{16,8},... | collective-permute-start | bytes 98312 | tf_op jit(solution)/shard_map/ppermute | solution.py:28
  62.7 0.0 collective-permute-done.5.arrived
  62.7 1.1 %shard_map.77.other_half = bf16[1024,512]{1,0:T(8,128)(2,1)} custom-call(f32[8,128]{1,0:T(8,128)S(1)} %get-tuple-element.41.mix, f32[1024,256]{1,0:T(8,128)S(1)} %get-tuple-element.63.base, bf16[1024,256]{1,0:T(8,128)(2,1)S(1)} %collective-permute-done.5.arrived), custom_call_target="tpu_custom_call" | custom-call | tf_op jit(solution)/shard_map/pallas_call | solution.py:160
  63.8 8.1 %collective-permute-done.2.arrived = bf16[1024,256]{1,0:T(8,128)(2,1)S(1)} collective-permute-done((bf16[1024,256]{1,0:T(8,128)(2,1)S(1)}, bf16[1024,256]{1,0:T(8,128)(2,1)S(1)}, u32[]{:S(2)}, u32[]{:S(2)}) %collective-permute-start.2) | collective-permute-done | bytes 524320 | tf_op jit(solution)/shard_map/ppermute | solution.py:23
  71.9 1.1 %collective-permute-done.12.refs_0_ = bf16[32,512]{1,0:T(8,128)(2,1)S(1)} collective-permute-done((bf16[32,512]{1,0:T(8,128)(2,1)S(1)}, bf16[32,512]{1,0:T(8,128)(2,1)S(1)}, u32[]{:S(2)}, u32[]{:S(2)}) %collective-permute-start.12) | collective-permute-done | bytes 32800 | tf_op jit(solution)/shard_map/ppermute | solution.py:28
  73.1 0.5 collective-permute-done.13.refs_1_
  73.6 0.0 collective-permute-done.14.refs_2_
  73.6 1.1 %shard_map.81 = (bf16[1024,512]{1,0:T(8,128)(2,1)}, f32[32,512]{1,0:T(8,128)}) custom-call(f32[8,128]{1,0:T(8,128)S(1)} %get-tuple-element.41.mix, f32[1024,256]{1,0:T(8,128)S(1)} %get-tuple-element.54.base, bf16[1024,256]{1,0:T(8,128)(2,1)S(1)} %collective-permute-done.2.arrived, ...), custom_call_target="tpu_custom_call", output_to_operand_aliasing={{0}: (3, {})} | custom-call | tf_op jit(solution)/shard_map/pallas_call | solution.py:160
  (6 shorter events, 0.1 us)
Async XLA Ops:
  0.6 5.5 %copy-start.3 = (s32[1,3]{1,0:T(1,128)S(1)}, s32[1,3]{1,0:T(1,128)}, u32[]{:S(2)}) copy-start(s32[1,3]{1,0:T(1,128)} %order.1) | copy-start | bytes 40
  0.6 5.5 %copy-start.2 = (s32[3,2]{0,1:T(2,128)S(1)}, s32[3,2]{0,1:T(2,128)}, u32[]{:S(2)}) copy-start(s32[3,2]{0,1:T(2,128)} %param.8) | copy-start | bytes 76
  0.7 5.5 %copy-start = (bf16[768,1024]{1,0:T(8,128)(2,1)S(1)}, bf16[768,1024]{1,0:T(8,128)(2,1)}, u32[]{:S(2)}) copy-start(bf16[768,1024]{1,0:T(8,128)(2,1)} %x.1) | copy-start | bytes 4718596
  1.9 12.4 %collective-permute-start.3 = (bf16[1024,256]{1,0:T(8,128)(2,1)S(1)}, bf16[1024,256]{1,0:T(8,128)(2,1)S(1)}, u32[]{:S(2)}, u32[]{:S(2)}) collective-permute-start(bf16[1024,256]{1,0:T(8,128)(2,1)S(1)} %slice.8.refs_0_), channel_id=1, source_target_pairs={{0,2},{2,4},{4,6},{6,8},{8,10},{10,12},{12,14},{14,16},{16,18},{18... | collective-permute-start | bytes 1572872 | tf_op jit(solution)/shard_map/ppermute | solution.py:23
  3.5 16.4 %collective-permute-start = (bf16[1024,256]{1,0:T(8,128)(2,1)S(1)}, bf16[1024,256]{1,0:T(8,128)(2,1)S(1)}, u32[]{:S(2)}, u32[]{:S(2)}) collective-permute-start(bf16[1024,256]{1,0:T(8,128)(2,1)S(1)} %slice.9.refs_1_), channel_id=1, source_target_pairs={{0,2},{2,4},{4,6},{6,8},{8,10},{10,12},{12,14},{14,16},{16,18},{18... | collective-permute-start | bytes 1572872 | tf_op jit(solution)/shard_map/ppermute | solution.py:23
  6.2 1.1 %copy-start.1 = (bf16[768,512]{1,0:T(8,128)(2,1)S(1)}, bf16[768,512]{1,0:T(8,128)(2,1)}, u32[]{:S(2)}) copy-start(bf16[768,512]{1,0:T(8,128)(2,1)} %t.1) | copy-start | bytes 2359300
  14.6 17.5 %collective-permute-start.4 = (bf16[1024,256]{1,0:T(8,128)(2,1)S(1)}, bf16[1024,256]{1,0:T(8,128)(2,1)S(1)}, u32[]{:S(2)}, u32[]{:S(2)}) collective-permute-start(bf16[1024,256]{1,0:T(8,128)(2,1)S(1)} %get-tuple-element.56.rounded), channel_id=1, source_target_pairs={{0,4},{2,6},{4,8},{6,10},{8,12},{10,14},{12,16},{14,18},{16,20},{1... | collective-permute-start | bytes 1572872 | tf_op jit(solution)/shard_map/ppermute | solution.py:23
  20.2 22.2 %collective-permute-start.1 = (bf16[1024,256]{1,0:T(8,128)(2,1)S(1)}, bf16[1024,256]{1,0:T(8,128)(2,1)S(1)}, u32[]{:S(2)}, u32[]{:S(2)}) collective-permute-start(bf16[1024,256]{1,0:T(8,128)(2,1)S(1)} %get-tuple-element.47.rounded), channel_id=1, source_target_pairs={{0,4},{2,6},{4,8},{6,10},{8,12},{10,14},{12,16},{14,18},{16,20},{1... | collective-permute-start | bytes 1572872 | tf_op jit(solution)/shard_map/ppermute | solution.py:23
  33.7 11.9 %collective-permute-start.6 = (f32[8,64,256]{2,1,0:T(8,128)S(1)}, f32[8,64,256]{2,1,0:T(8,128)S(1)}, u32[]{:S(2)}, u32[]{:S(2)}) collective-permute-start(f32[8,64,256]{2,1,0:T(8,128)S(1)} %get-tuple-element.65), channel_id=1, source_target_pairs={{0,2},{2,0},{4,6},{6,4},{8,10},{10,8},{12,14},{14,12},{16,18},{18,... | collective-permute-start | bytes 1572872 | tf_op jit(solution)/shard_map/ppermute | solution.py:28
  43.9 3.3 %collective-permute-start.8 = (f32[8,64,256]{2,1,0:T(8,128)S(1)}, f32[8,64,256]{2,1,0:T(8,128)S(1)}, u32[]{:S(2)}, u32[]{:S(2)}) collective-permute-start(f32[8,64,256]{2,1,0:T(8,128)S(1)} %get-tuple-element.69), channel_id=1, source_target_pairs={{0,2},{2,0},{4,6},{6,4},{8,10},{10,8},{12,14},{14,12},{16,18},{18,... | collective-permute-start | bytes 1572872 | tf_op jit(solution)/shard_map/ppermute | solution.py:28
  44.0 18.8 %collective-permute-start.5 = (bf16[1024,256]{1,0:T(8,128)(2,1)S(1)}, bf16[1024,256]{1,0:T(8,128)(2,1)S(1)}, u32[]{:S(2)}, u32[]{:S(2)}) collective-permute-start(bf16[1024,256]{1,0:T(8,128)(2,1)S(1)} %get-tuple-element.60.rounded), channel_id=1, source_target_pairs={{0,8},{2,10},{4,12},{6,14},{8,16},{10,18},{12,20},{14,22},{16,24},... | collective-permute-start | bytes 1572872 | tf_op jit(solution)/shard_map/ppermute | solution.py:23
  44.0 27.9 %collective-permute-start.2 = (bf16[1024,256]{1,0:T(8,128)(2,1)S(1)}, bf16[1024,256]{1,0:T(8,128)(2,1)S(1)}, u32[]{:S(2)}, u32[]{:S(2)}) collective-permute-start(bf16[1024,256]{1,0:T(8,128)(2,1)S(1)} %get-tuple-element.51.rounded), channel_id=1, source_target_pairs={{0,8},{2,10},{4,12},{6,14},{8,16},{10,18},{12,20},{14,22},{16,24},... | collective-permute-start | bytes 1572872 | tf_op jit(solution)/shard_map/ppermute | solution.py:23
  45.7 5.0 %collective-permute-start.7 = (bf16[8,32,256]{2,1,0:T(8,128)(2,1)S(1)}, bf16[8,32,256]{2,1,0:T(8,128)(2,1)S(1)}, u32[]{:S(2)}, u32[]{:S(2)}) collective-permute-start(bf16[8,32,256]{2,1,0:T(8,128)(2,1)S(1)} %get-tuple-element.67), channel_id=1, source_target_pairs={{0,1},{1,0},{2,3},{3,2},{4,5},{5,4},{6,7},{7,6},{8,9},{9,8},{10,11... | collective-permute-start | bytes 393224 | tf_op jit(solution)/shard_map/ppermute | solution.py:28
  50.8 7.3 %collective-permute-start.9 = (bf16[4,32,512]{2,1,0:T(8,128)(2,1)S(1)}, bf16[4,32,512]{2,1,0:T(8,128)(2,1)S(1)}, u32[]{:S(2)}, u32[]{:S(2)}) collective-permute-start(bf16[4,32,512]{2,1,0:T(8,128)(2,1)S(1)} %get-tuple-element.71), channel_id=1, source_target_pairs={{0,4},{2,6},{4,0},{6,2},{8,12},{10,14},{12,8},{14,10},{16,20},{18,... | collective-permute-start | bytes 393224 | tf_op jit(solution)/shard_map/ppermute | solution.py:28
  51.5 4.3 %collective-permute-start.10 = (bf16[4,32,256]{2,1,0:T(8,128)(2,1)S(1)}, bf16[4,32,256]{2,1,0:T(8,128)(2,1)S(1)}, u32[]{:S(2)}, u32[]{:S(2)}) collective-permute-start(bf16[4,32,256]{2,1,0:T(8,128)(2,1)S(1)} %get-tuple-element.72), channel_id=1, source_target_pairs={{0,1},{1,0},{2,3},{3,2},{4,5},{5,4},{6,7},{7,6},{8,9},{9,8},{10,11... | collective-permute-start | bytes 196616 | tf_op jit(solution)/shard_map/ppermute | solution.py:28
  52.9 5.2 %collective-permute-start.11 = (bf16[4,32,256]{2,1,0:T(8,128)(2,1)S(1)}, bf16[4,32,256]{2,1,0:T(8,128)(2,1)S(1)}, u32[]{:S(2)}, u32[]{:S(2)}) collective-permute-start(bf16[4,32,256]{2,1,0:T(8,128)(2,1)S(1)} %get-tuple-element.73), channel_id=1, source_target_pairs={{0,5},{1,4},{2,7},{3,6},{4,1},{5,0},{6,3},{7,2},{8,13},{9,12},{10,... | collective-permute-start | bytes 196616 | tf_op jit(solution)/shard_map/ppermute | solution.py:275
  58.2 14.9 %collective-permute-start.12 = (bf16[32,512]{1,0:T(8,128)(2,1)S(1)}, bf16[32,512]{1,0:T(8,128)(2,1)S(1)}, u32[]{:S(2)}, u32[]{:S(2)}) collective-permute-start(bf16[32,512]{1,0:T(8,128)(2,1)S(1)} %get-tuple-element.75), channel_id=1, source_target_pairs={{0,8},{2,10},{4,12},{6,14},{8,0},{10,2},{12,4},{14,6},{16,24},{18,... | collective-permute-start | bytes 98312 | tf_op jit(solution)/shard_map/ppermute | solution.py:28
  59.8 13.8 %collective-permute-start.13 = (bf16[32,512]{1,0:T(8,128)(2,1)S(1)}, bf16[32,512]{1,0:T(8,128)(2,1)S(1)}, u32[]{:S(2)}, u32[]{:S(2)}) collective-permute-start(bf16[32,512]{1,0:T(8,128)(2,1)S(1)} %get-tuple-element.76), channel_id=1, source_target_pairs={{0,16},{2,18},{4,20},{6,22},{8,24},{10,26},{12,28},{14,30},{16,0},... | collective-permute-start | bytes 98312 | tf_op jit(solution)/shard_map/ppermute | solution.py:28
  61.6 12.0 %collective-permute-start.14 = (bf16[32,512]{1,0:T(8,128)(2,1)S(1)}, bf16[32,512]{1,0:T(8,128)(2,1)S(1)}, u32[]{:S(2)}, u32[]{:S(2)}) collective-permute-start(bf16[32,512]{1,0:T(8,128)(2,1)S(1)} %get-tuple-element.77), channel_id=1, source_target_pairs={{0,24},{2,26},{4,28},{6,30},{8,16},{10,18},{12,20},{14,22},{16,8},... | collective-permute-start | bytes 98312 | tf_op jit(solution)/shard_map/ppermute | solution.py:28

commit v12 on v8

--- a/solution.py
+++ b/solution.py
@@ -21,6 +21,12 @@
     count = lax.axis_size(axis)
     pairs = [(source, (source + steps) % count) for source in range(count)]
     return lax.ppermute(value, axis, pairs)
+
+
+def moved(value, target):
+    count = lax.axis_size("gossip")
+    pairs = [(source, target(source) % count) for source in range(count) if target(source) is not None]
+    return lax.ppermute(value, "gossip", pairs)
 
 
 def flipped(value, axis, bit):
@@ -46,8 +52,22 @@
     return product * fan_scale
 
 
+def piece_kernel(half, weights, piece, arrival):
+    core, width = lax.axis_index("gossip") & 1, piece.shape[1]
+
+    @pl.when(core == 1)
+    def _():
+        copy = pltpu.make_async_copy(weights.at[:, half * width:(half + 1) * width], piece, arrival)
+        copy.start()
+        copy.wait()
+
+    @pl.when(core == 0)
+    def _():
+        piece[...] = jnp.zeros_like(piece)
+
+
 def first_kernel(order, plan, x, t, *refs):
-    weights, (mix, *shards), outs = refs[:HALVES], refs[HALVES:HALVES + 2 * STEPS - 1], refs[HALVES + 2 * STEPS - 1:]
+    weights, (mix, *shards), outs = refs[0], refs[1:2 * STEPS], refs[2 * STEPS:]
     batch = x.shape[0] // STEPS
     rows = [pl.ds(pl.multiple_of(order[0, step] * batch, batch), batch) for step in range(STEPS)]
     mix[...] = jnp.zeros_like(mix)
@@ -56,13 +76,14 @@
         mix[2 * step:2 * step + 1, :] = own / (own + peer)
         mix[2 * step + 1:2 * step + 2, :] = peer / (own + peer)
     own, _ = shares(mix, 0)
-    width = weights[0].shape[1]
-    for half, w in enumerate(weights):
+    width = weights.shape[1] // HALVES
+    for half in range(HALVES):
         base, velocity = outs[2 * half:2 * half + 2]
         columns = slice(half * width, (half + 1) * width)
-        gradient = gradient_of(x[rows[0], :], t[rows[0], columns], w[...])
+        w = weights[:, columns]
+        gradient = gradient_of(x[rows[0], :], t[rows[0], columns], w)
         velocity[...] = gradient
-        base[...] = own * w[...].astype(jnp.float32) - learning_rate * gradient
+        base[...] = own * w.astype(jnp.float32) - learning_rate * gradient
     for step in range(1, STEPS):
         shards[2 * step - 2][...] = x[rows[step], :]
         shards[2 * step - 1][...] = t[rows[step], :]
@@ -92,16 +113,27 @@
     give[...] = held[:, pl.ds(1 - mine, 1)].reshape(give.shape)
 
 
-def round_kernel(step, mix, base, arrived, rounded, master):
+def first_round_kernel(columns, mix, base, from_chip, on_chip, rounded, master):
+    core = lax.axis_index("gossip") & 1
+    pl.when(core == 0)(lambda: round_kernel(0, mix, base, from_chip, rounded, master))
+    pl.when(core == 1)(lambda: round_kernel(0, mix, base, on_chip.at[:, columns], rounded, master))
+
+
+def round_kernel(step, mix, base, arrived, rounded, master, *row_parts):
     _, peer = shares(mix, step)
     total = base[...] + peer * arrived[...].astype(jnp.float32)
     rounded[...] = total.astype(jnp.bfloat16)
     master[...] = total
-
-
-def finish_kernel(mix, base, arrived, *refs):
+    row = 0
+    for part in row_parts:
+        part[...] = rounded[row:row + part.shape[0], :]
+        row += part.shape[0]
+
+
+def finish_kernel(row, mix, base, arrived, *refs):
     _, peer = shares(mix, STEPS - 1)
-    refs[-1][...] = (base[...] + peer * arrived[...].astype(jnp.float32)).astype(jnp.bfloat16)
+    rows = slice(row, row + arrived.shape[0])
+    refs[-1][...] = (base[rows, :] + peer * arrived[...].astype(jnp.float32)).astype(jnp.bfloat16)
 
 
 def leg_kernel(axis, bit, kept, arrived, keep, give):
@@ -149,8 +181,8 @@
 IN_SMEM = pl.BlockSpec(memory_space=pltpu.SMEM)
 
 
-def call(kernel, ins, outs, scratch=(), out_specs=None, in_place=None):
-    in_specs = [IN_SMEM if array.dtype == jnp.int32 else IN_VMEM for array in ins]
+def call(kernel, ins, outs, scratch=(), out_specs=None, in_place=None, in_specs=None):
+    in_specs = in_specs or [IN_SMEM if array.dtype == jnp.int32 else IN_VMEM for array in ins]
     aliases = {}
     if in_place is not None:
         in_specs[in_place] = pl.BlockSpec(memory_space=pl.ANY)
@@ -198,20 +230,27 @@
     half_f32, half_bf16 = ((din, width), jnp.float32), ((din, width), jnp.bfloat16)
 
     plan = plan.T
+    in_hbm = pltpu.with_memory_space_constraint(weights, pltpu.HBM)
     pieces, arrived0, rounds0, arrived1, middles = [], [], [], [], []
     for half in range(HALVES):
-        pieces.append(weights[:, columns[half]])
-        weights = lax.optimization_barrier(weights)
+        (piece,) = call(
+            functools.partial(piece_kernel, half), [in_hbm], [half_bf16], (pltpu.SemaphoreType.DMA,),
+            in_specs=[pl.BlockSpec(memory_space=pltpu.HBM)],
+        )
+        pieces.append(piece)
         arrived0.append(shifted(pieces[half], "gossip", 1))
+    on_chip = moved(weights, lambda at: None if at & 1 else at + 1)
     batch = inputs.shape[0] // STEPS
     shards = [((batch, din), inputs.dtype), ((batch, dout), targets.dtype)] * (STEPS - 1)
     outs = [((-(-2 * STEPS // 8) * 8, 128), jnp.float32)] + shards + [half_f32] * (2 * HALVES)
-    mix, *rest = call(first_kernel, [order, plan, inputs, targets] + pieces, outs)
+    mix, *rest = call(first_kernel, [order, plan, inputs, targets, weights], outs)
     shards, firsts = rest[:len(shards)], rest[len(shards):]
     for half in range(HALVES):
         rounds0.append(
             call(
-                functools.partial(round_kernel, 0), [mix, firsts[2 * half], arrived0[half]], [half_bf16, half_f32]
+                functools.partial(first_round_kernel, columns[half]),
+                [mix, firsts[2 * half], arrived0[half], on_chip],
+                [half_bf16, half_f32],
             )
         )
         arrived1.append(shifted(rounds0[half][0], "gossip", 2))
@@ -226,10 +265,13 @@
     parts, last = [], []
     for half in range(HALVES):
         base1, velocity1 = middles[half]
-        rounded2, master2 = call(
-            functools.partial(round_kernel, 1), [mix, base1, arrived1[half]], [half_bf16, half_f32]
-        )
-        arrived2 = shifted(rounded2, "gossip", 4)
+        heights = [din] if half < HALVES - 1 else [din - din // 4, din // 4]
+        row_parts = [((height, width), jnp.bfloat16) for height in heights]
+        rounded2, master2, *sent = call(
+            functools.partial(round_kernel, 1), [mix, base1, arrived1[half]],
+            [half_bf16, half_f32] + (row_parts if len(heights) > 1 else []),
+        )
+        arrived2 = shifted((sent or [rounded2])[0], "gossip", 4)
         outs, scratch = [half_f32] * 2, ()
         if split:
             pair = (n_gossip // 2, n_group * own_rows, width)
@@ -241,7 +283,7 @@
             outs,
             scratch,
         )
-        last += [base2, arrived2]
+        last.append((base2, arrived2))
         if not split:
             parts.append(part[0])
             continue
@@ -279,14 +321,18 @@
             gots.append(flipped(give, "gossip", 4 * other))
     else:
         mean_weights = scattered_sum(jnp.concatenate(parts, axis=1)) / replicas
+    arrived_tail = shifted(sent[1], "gossip", 4)
     result, replica_weights = ((din, dout), jnp.bfloat16), []
-    for half in range(HALVES):
+    for part in range(HALVES + 1):
+        half = min(part, HALVES - 1)
+        base2, arrived2 = last[half]
+        row = din - din // 4 if part == HALVES else 0
+        arrived2 = arrived_tail if row else arrived2
+        height = arrived2.shape[0]
+        block = pl.BlockSpec((height, width), lambda i, at=(row // height, half): at)
         replica_weights = call(
-            finish_kernel,
-            [mix, *last[2 * half:2 * half + 2], *replica_weights],
-            [result],
-            out_specs=[pl.BlockSpec((din, width), lambda i, half=half: (0, half))],
-            in_place=3 if half else None,
+            functools.partial(finish_kernel, row), [mix, base2, arrived2, *replica_weights], [result],
+            out_specs=[block], in_place=3 if part else None,
         )
     if split:
         (mean_weights,) = call(functools.partial(mean_kernel, replicas), [keep] + gots, [(shape, jnp.float32)])

time: 74.5 us -> 75.9 us (1.019)
  starting transfers between devices: 15 us -> 19.7 us
  local copies, waits for them, and re-layouts: 3.41 us -> 1.15 us
  waiting for transfers between devices: 44.6 us -> 42.8 us
  Pallas kernels: 10.5 us -> 11.3 us
    ppermute x0 -> x1, starting transfers between devices: none -> 2.73 us  [moved(): return lax.ppermute(value, 'gossip', pairs)]
    ppermute x6 -> x7, waiting for transfers between devices: 36.8 us -> 34.2 us  [shifted(): return lax.ppermute(value, axis, pairs)]
    slice x2 -> x0, local copies, waits for them, and re-layouts: 2.27 us -> none  [steps(): pieces.append(weights[:, columns[half]])]
    ppermute x6 -> x7, starting transfers between devices: 5.13 us -> 6.37 us  [shifted(): return lax.ppermute(value, axis, pairs)]
    ppermute x1, waiting for transfers between devices: 2.39 us -> 3.62 us  [steps(): from_xy = lax.ppermute(give_xy, ('gossip', 'group'), pairs)]
    pallas_call x15 -> x18, Pallas kernels: 10.5 us -> 11.3 us  [call(): pl.pallas_call(kernel, grid=(1,) if out_specs else (), in_specs=in_specs,...]
  transfers between devices with their start and end apart: 15 -> 17, of which waited for: 9 -> 11; matrix products, arithmetic and copies ran while one was open for 1% -> 0% of each run, Pallas kernels for 13% -> 14%
where the time goes in v12:
time: 75.9 us; the launch traced here: 75.7 us
  waiting for transfers between devices  42.8 us (56%)
  starting transfers between devices  19.7 us (26%)
  Pallas kernels  11.3 us (15%)
  local copies, waits for them, and re-layouts  1.15 us (2%)
  between operations  0.82 us (1%)
    ppermute x7, waiting for transfers between devices, shifted(): return lax.ppermute(value, axis, pairs)  34.2 us
    pallas_call x18, Pallas kernels, call(): pl.pallas_call(kernel, grid=(1,) if out_specs else (), in_specs=in_specs,...  11.3 us
    ppermute x8, starting transfers between devices, flipped(): lax.ppermute(value, axis, [(source, source ^ bit) for source in range(cou...  9.04 us
    ppermute x7, starting transfers between devices, shifted(): return lax.ppermute(value, axis, pairs)  6.37 us
    ppermute x8, waiting for transfers between devices, flipped(): lax.ppermute(value, axis, [(source, source ^ bit) for source in range(cou...  4.96 us
    ppermute x1, waiting for transfers between devices, steps(): from_xy = lax.ppermute(give_xy, ('gossip', 'group'), pairs)  3.62 us
    ppermute x1, starting transfers between devices, moved(): return lax.ppermute(value, 'gossip', pairs)  2.73 us
    ppermute x1, starting transfers between devices, steps(): from_xy = lax.ppermute(give_xy, ('gossip', 'group'), pairs)  1.55 us
  transfers between devices with their start and end apart: 17, of which 11 were waited for; matrix products, arithmetic and copies ran while one was open for 0% of the time, Pallas kernels for 14%

profile of v12, /device:TPU:0, one launch (start us, length us, event | category | flops | bytes accessed | tf_op | source)
XLA Modules:
  0.0 75.7 jit_solution(9347112421993703241)
XLA Ops:
  0.6 0.0 copy-start
  0.7 2.7 %collective-permute-start.1 = (bf16[1024,512]{1,0:T(8,128)(2,1)}, bf16[1024,512]{1,0:T(8,128)(2,1)S(1)}, u32[]{:S(2)}, u32[]{:S(2)}) collective-permute-start(bf16[1024,512]{1,0:T(8,128)(2,1)} %bitcast.9), channel_id=1, source_target_pairs={{0,2},{4,6},{8,10},{12,14},{16,18},{20,22},{24,26},{28,30},{1,3},{... | collective-permute-start | bytes 3145736 | tf_op jit(solution)/shard_map/ppermute | solution.py:29
  3.4 0.1 shard_map.74
  3.5 0.4 collective-permute-start.5
  3.9 3.2 %collective-permute-start = (bf16[1024,256]{1,0:T(8,128)(2,1)S(1)}, bf16[1024,256]{1,0:T(8,128)(2,1)S(1)}, u32[]{:S(2)}, u32[]{:S(2)}) collective-permute-start(bf16[1024,256]{1,0:T(8,128)(2,1)S(1)} %shard_map.69), channel_id=1, source_target_pairs={{0,2},{2,4},{4,6},{6,8},{8,10},{10,12},{12,14},{14,16},{16,18},{18... | collective-permute-start | bytes 1572872 | tf_op jit(solution)/shard_map/ppermute | solution.py:23
  7.1 0.0 copy-start.2
  7.1 1.1 %copy-done.2 = bf16[768,512]{1,0:T(8,128)(2,1)S(1)} copy-done((bf16[768,512]{1,0:T(8,128)(2,1)S(1)}, bf16[768,512]{1,0:T(8,128)(2,1)}, u32[]{:S(2)}) %copy-start.2) | copy-done | bytes 786456
  8.2 1.9 %shard_map.68 = (f32[8,128]{1,0:T(8,128)S(1)}, bf16[256,1024]{1,0:T(8,128)(2,1)S(1)}, bf16[256,512]{1,0:T(8,128)(2,1)S(1)}, bf16[256,1024]{1,0:T(8,128)(2,1)S(1)...) custom-call(s32[1,3]{1,0:T(1,128)S(1)} %copy-done.4, ...), custom_call_target="tpu_custom_call" | custom-call | tf_op jit(solution)/shard_map/pallas_call | solution.py:190
  10.2 5.5 %collective-permute-done.5.from_chip = bf16[1024,256]{1,0:T(8,128)(2,1)S(1)} collective-permute-done((bf16[1024,256]{1,0:T(8,128)(2,1)S(1)}, bf16[1024,256]{1,0:T(8,128)(2,1)S(1)}, u32[]{:S(2)}, u32[]{:S(2)}) %collective-permute-start.5) | collective-permute-done | bytes 524320 | tf_op jit(solution)/shard_map/ppermute | solution.py:23
  15.7 0.0 collective-permute-done.1.on_chip
  15.7 0.3 shard_map.75
  16.0 0.1 collective-permute-start.6
  16.1 5.2 %collective-permute-done.from_chip = bf16[1024,256]{1,0:T(8,128)(2,1)S(1)} collective-permute-done((bf16[1024,256]{1,0:T(8,128)(2,1)S(1)}, bf16[1024,256]{1,0:T(8,128)(2,1)S(1)}, u32[]{:S(2)}, u32[]{:S(2)}) %collective-permute-start) | collective-permute-done | bytes 524320 | tf_op jit(solution)/shard_map/ppermute | solution.py:23
  21.3 0.3 shard_map.70
  21.6 0.1 collective-permute-start.2
  21.7 0.9 %shard_map.76 = (f32[1024,256]{1,0:T(8,128)S(1)}, f32[1024,256]{1,0:T(8,128)S(1)}) custom-call(f32[8,128]{1,0:T(8,128)S(1)} %get-tuple-element.41.mix, bf16[256,1024]{1,0:T(8,128)(2,1)S(1)} %get-tuple-element.44.x, bf16[256,512]{1,0:T(8,128)(2,1)S(1)} %get-tuple-element.45.t, bf16[1024,256]{1,0:T(8,128)(2,1)S(1)} %get-tuple-element.58.rounded, ...), custom_call_target="tpu_custom_call" | custom-call | tf_op jit(solution)/shard_map/pallas_call | solution.py:190
  22.6 10.9 %collective-permute-done.6.arrived = bf16[1024,256]{1,0:T(8,128)(2,1)S(1)} collective-permute-done((bf16[1024,256]{1,0:T(8,128)(2,1)S(1)}, bf16[1024,256]{1,0:T(8,128)(2,1)S(1)}, u32[]{:S(2)}, u32[]{:S(2)}) %collective-permute-start.6) | collective-permute-done | bytes 524320 | tf_op jit(solution)/shard_map/ppermute | solution.py:23
  33.6 0.3 shard_map.77
  33.9 1.2 %shard_map.78 = (f32[1024,256]{1,0:T(8,128)S(1)}, f32[8,64,256]{2,1,0:T(8,128)S(1)}, f32[8,64,256]{2,1,0:T(8,128)S(1)}) custom-call(f32[8,128]{1,0:T(8,128)S(1)} %get-tuple-element.41.mix, bf16[256,1024]{1,0:T(8,128)(2,1)S(1)} %get-tuple-element.42.x, bf16[256,512]{1,0:T(8,128)(2,1)S(1)} %get-tuple-element.43.t, ...), custom_call_target="tpu_custom_call" | custom-call | tf_op jit(solution)/shard_map/pallas_call | solution.py:190
  35.1 0.1 collective-permute-start.8
  35.2 0.9 %shard_map.71 = (f32[1024,256]{1,0:T(8,128)S(1)}, f32[1024,256]{1,0:T(8,128)S(1)}) custom-call(f32[8,128]{1,0:T(8,128)S(1)} %get-tuple-element.41.mix, bf16[256,1024]{1,0:T(8,128)(2,1)S(1)} %get-tuple-element.44.x, bf16[256,512]{1,0:T(8,128)(2,1)S(1)} %get-tuple-element.45.t, bf16[1024,256]{1,0:T(8,128)(2,1)S(1)} %get-tuple-element.47.rounded, ...), custom_call_target="tpu_custom_call" | custom-call | tf_op jit(solution)/shard_map/pallas_call | solution.py:190
  36.1 7.7 %collective-permute-done.2.arrived = bf16[1024,256]{1,0:T(8,128)(2,1)S(1)} collective-permute-done((bf16[1024,256]{1,0:T(8,128)(2,1)S(1)}, bf16[1024,256]{1,0:T(8,128)(2,1)S(1)}, u32[]{:S(2)}, u32[]{:S(2)}) %collective-permute-start.2) | collective-permute-done | bytes 524320 | tf_op jit(solution)/shard_map/ppermute | solution.py:23
  43.8 0.3 shard_map.72
  44.1 1.2 %shard_map.73 = (f32[1024,256]{1,0:T(8,128)S(1)}, f32[8,64,256]{2,1,0:T(8,128)S(1)}, f32[8,64,256]{2,1,0:T(8,128)S(1)}) custom-call(f32[8,128]{1,0:T(8,128)S(1)} %get-tuple-element.41.mix, bf16[256,1024]{1,0:T(8,128)(2,1)S(1)} %get-tuple-element.42.x, bf16[256,512]{1,0:T(8,128)(2,1)S(1)} %get-tuple-element.43.t, ...), custom_call_target="tpu_custom_call" | custom-call | tf_op jit(solution)/shard_map/pallas_call | solution.py:190
  45.4 0.1 collective-permute-start.10
  45.5 0.1 collective-permute-start.7
  45.5 1.1 %collective-permute-start.4 = (bf16[768,256]{1,0:T(8,128)(2,1)S(1)}, bf16[768,256]{1,0:T(8,128)(2,1)S(1)}, u32[]{:S(2)}, u32[]{:S(2)}) collective-permute-start(bf16[768,256]{1,0:T(8,128)(2,1)S(1)} %get-tuple-element.56), channel_id=1, source_target_pairs={{0,8},{2,10},{4,12},{6,14},{8,16},{10,18},{12,20},{14,22},{16,24},... | collective-permute-start | bytes 1179656 | tf_op jit(solution)/shard_map/ppermute | solution.py:23
  46.6 0.1 shard_map.82
  46.6 1.6 %collective-permute-start.9 = (bf16[8,32,256]{2,1,0:T(8,128)(2,1)S(1)}, bf16[8,32,256]{2,1,0:T(8,128)(2,1)S(1)}, u32[]{:S(2)}, u32[]{:S(2)}) collective-permute-start(bf16[8,32,256]{2,1,0:T(8,128)(2,1)S(1)} %get-tuple-element.69), channel_id=1, source_target_pairs={{0,1},{1,0},{2,3},{3,2},{4,5},{5,4},{6,7},{7,6},{8,9},{9,8},{10,11... | collective-permute-start | bytes 393224 | tf_op jit(solution)/shard_map/ppermute | solution.py:34
  48.2 3.5 %collective-permute-done.9 = bf16[8,32,256]{2,1,0:T(8,128)(2,1)S(1)} collective-permute-done((bf16[8,32,256]{2,1,0:T(8,128)(2,1)S(1)}, bf16[8,32,256]{2,1,0:T(8,128)(2,1)S(1)}, u32[]{:S(2)}, u32[]{:S(2)}) %collective-permute-start.9) | collective-permute-done | bytes 131104 | tf_op jit(solution)/shard_map/ppermute | solution.py:34
  51.7 0.1 shard_map.83
  51.8 1.6 %collective-permute-start.12 = (bf16[4,32,256]{2,1,0:T(8,128)(2,1)S(1)}, bf16[4,32,256]{2,1,0:T(8,128)(2,1)S(1)}, u32[]{:S(2)}, u32[]{:S(2)}) collective-permute-start(bf16[4,32,256]{2,1,0:T(8,128)(2,1)S(1)} %get-tuple-element.74), channel_id=1, source_target_pairs={{0,1},{1,0},{2,3},{3,2},{4,5},{5,4},{6,7},{7,6},{8,9},{9,8},{10,11... | collective-permute-start | bytes 196616 | tf_op jit(solution)/shard_map/ppermute | solution.py:34
  53.3 0.6 collective-permute-start.11
  54.0 1.6 %collective-permute-start.3 = (bf16[256,256]{1,0:T(8,128)(2,1)S(1)}, bf16[256,256]{1,0:T(8,128)(2,1)S(1)}, u32[]{:S(2)}, u32[]{:S(2)}) collective-permute-start(bf16[256,256]{1,0:T(8,128)(2,1)S(1)} %get-tuple-element.55), channel_id=1, source_target_pairs={{0,8},{2,10},{4,12},{6,14},{8,16},{10,18},{12,20},{14,22},{16,24},... | collective-permute-start | bytes 393224 | tf_op jit(solution)/shard_map/ppermute | solution.py:23
  55.5 0.6 collective-permute-done.12.from_x
  56.1 1.5 %collective-permute-start.13 = (bf16[4,32,256]{2,1,0:T(8,128)(2,1)S(1)}, bf16[4,32,256]{2,1,0:T(8,128)(2,1)S(1)}, u32[]{:S(2)}, u32[]{:S(2)}) collective-permute-start(bf16[4,32,256]{2,1,0:T(8,128)(2,1)S(1)} %get-tuple-element.75), channel_id=1, source_target_pairs={{0,5},{1,4},{2,7},{3,6},{4,1},{5,0},{6,3},{7,2},{8,13},{9,12},{10,... | collective-permute-start | bytes 196616 | tf_op jit(solution)/shard_map/ppermute | solution.py:315
  57.7 3.6 %collective-permute-done.13.from_xy = bf16[4,32,256]{2,1,0:T(8,128)(2,1)S(1)} collective-permute-done((bf16[4,32,256]{2,1,0:T(8,128)(2,1)S(1)}, bf16[4,32,256]{2,1,0:T(8,128)(2,1)S(1)}, u32[]{:S(2)}, u32[]{:S(2)}) %collective-permute-start.13) | collective-permute-done | bytes 65568 | tf_op jit(solution)/shard_map/ppermute | solution.py:315
  61.3 1.6 %collective-permute-start.14 = (bf16[32,512]{1,0:T(8,128)(2,1)S(1)}, bf16[32,512]{1,0:T(8,128)(2,1)S(1)}, u32[]{:S(2)}, u32[]{:S(2)}) collective-permute-start(bf16[32,512]{1,0:T(8,128)(2,1)S(1)} %get-tuple-element.77), channel_id=1, source_target_pairs={{0,8},{2,10},{4,12},{6,14},{8,0},{10,2},{12,4},{14,6},{16,24},{18,... | collective-permute-start | bytes 98312 | tf_op jit(solution)/shard_map/ppermute | solution.py:34
  63.0 2.4 %collective-permute-start.15 = (bf16[32,512]{1,0:T(8,128)(2,1)S(1)}, bf16[32,512]{1,0:T(8,128)(2,1)S(1)}, u32[]{:S(2)}, u32[]{:S(2)}) collective-permute-start(bf16[32,512]{1,0:T(8,128)(2,1)S(1)} %get-tuple-element.78), channel_id=1, source_target_pairs={{0,16},{2,18},{4,20},{6,22},{8,24},{10,26},{12,28},{14,30},{16,0},... | collective-permute-start | bytes 98312 | tf_op jit(solution)/shard_map/ppermute | solution.py:34
  65.3 1.2 %collective-permute-start.16 = (bf16[32,512]{1,0:T(8,128)(2,1)S(1)}, bf16[32,512]{1,0:T(8,128)(2,1)S(1)}, u32[]{:S(2)}, u32[]{:S(2)}) collective-permute-start(bf16[32,512]{1,0:T(8,128)(2,1)S(1)} %get-tuple-element.79), channel_id=1, source_target_pairs={{0,24},{2,26},{4,28},{6,30},{8,16},{10,18},{12,20},{14,22},{16,8},... | collective-permute-start | bytes 98312 | tf_op jit(solution)/shard_map/ppermute | solution.py:34
  66.5 1.1 %shard_map.79.refs_0_ = bf16[1024,512]{1,0:T(8,128)(2,1)} custom-call(f32[8,128]{1,0:T(8,128)S(1)} %get-tuple-element.41.mix, f32[1024,256]{1,0:T(8,128)S(1)} %get-tuple-element.65.base, bf16[1024,256]{1,0:T(8,128)(2,1)S(1)} %collective-permute-done.7.arrived), custom_call_target="tpu_custom_call" | custom-call | tf_op jit(solution)/shard_map/pallas_call | solution.py:190
  67.6 3.1 %collective-permute-done.4.arrived = bf16[768,256]{1,0:T(8,128)(2,1)S(1)} collective-permute-done((bf16[768,256]{1,0:T(8,128)(2,1)S(1)}, bf16[768,256]{1,0:T(8,128)(2,1)S(1)}, u32[]{:S(2)}, u32[]{:S(2)}) %collective-permute-start.4) | collective-permute-done | bytes 393248 | tf_op jit(solution)/shard_map/ppermute | solution.py:23
  70.7 1.0 %shard_map.80.refs_0_ = bf16[1024,512]{1,0:T(8,128)(2,1)} custom-call(f32[8,128]{1,0:T(8,128)S(1)} %get-tuple-element.41.mix, f32[1024,256]{1,0:T(8,128)S(1)} %get-tuple-element.54.base, bf16[768,256]{1,0:T(8,128)(2,1)S(1)} %collective-permute-done.4.arrived, bf16[1024,512]{1,0:T(8,128)(2,1)} %shard_map.79.refs_0_), custom_call_target="tpu_custom_call", output_to_operand_aliasing={{}: (3, {})} | custom-call | tf_op jit(solution)/shard_map/pallas_call | solution.py:190
  71.7 1.7 %collective-permute-done.3.arrived = bf16[256,256]{1,0:T(8,128)(2,1)S(1)} collective-permute-done((bf16[256,256]{1,0:T(8,128)(2,1)S(1)}, bf16[256,256]{1,0:T(8,128)(2,1)S(1)}, u32[]{:S(2)}, u32[]{:S(2)}) %collective-permute-start.3) | collective-permute-done | bytes 131104 | tf_op jit(solution)/shard_map/ppermute | solution.py:23
  73.4 0.7 shard_map.81
  74.2 0.4 collective-permute-done.14.refs_0_
  74.5 0.5 collective-permute-done.15.refs_1_
  75.1 0.6 shard_map.85
  (14 shorter events, 0.1 us)
Async XLA Ops:
  0.6 6.5 %copy-start = (bf16[1,1024,512]{2,1,0:T(8,128)(2,1)S(1)}, bf16[1,1024,512]{2,1,0:T(8,128)(2,1)}, u32[]{:S(2)}) copy-start(bf16[1,1024,512]{2,1,0:T(8,128)(2,1)} %param.5) | copy-start | bytes 3145732
  0.6 6.5 %copy-start.1 = (bf16[768,1024]{1,0:T(8,128)(2,1)S(1)}, bf16[768,1024]{1,0:T(8,128)(2,1)}, u32[]{:S(2)}) copy-start(bf16[768,1024]{1,0:T(8,128)(2,1)} %x.1) | copy-start | bytes 4718596
  0.7 6.4 %copy-start.3 = (s32[3,2]{0,1:T(2,128)S(1)}, s32[3,2]{0,1:T(2,128)}, u32[]{:S(2)}) copy-start(s32[3,2]{0,1:T(2,128)} %param.8) | copy-start | bytes 76
  0.7 6.4 %copy-start.4 = (s32[1,3]{1,0:T(1,128)S(1)}, s32[1,3]{1,0:T(1,128)}, u32[]{:S(2)}) copy-start(s32[1,3]{1,0:T(1,128)} %order.1) | copy-start | bytes 40
  0.7 15.0 %collective-permute-start.1 = (bf16[1024,512]{1,0:T(8,128)(2,1)}, bf16[1024,512]{1,0:T(8,128)(2,1)S(1)}, u32[]{:S(2)}, u32[]{:S(2)}) collective-permute-start(bf16[1024,512]{1,0:T(8,128)(2,1)} %bitcast.9), channel_id=1, source_target_pairs={{0,2},{4,6},{8,10},{12,14},{16,18},{20,22},{24,26},{28,30},{1,3},{... | collective-permute-start | bytes 3145736 | tf_op jit(solution)/shard_map/ppermute | solution.py:29
  3.5 12.2 %collective-permute-start.5 = (bf16[1024,256]{1,0:T(8,128)(2,1)S(1)}, bf16[1024,256]{1,0:T(8,128)(2,1)S(1)}, u32[]{:S(2)}, u32[]{:S(2)}) collective-permute-start(bf16[1024,256]{1,0:T(8,128)(2,1)S(1)} %shard_map.74), channel_id=1, source_target_pairs={{0,2},{2,4},{4,6},{6,8},{8,10},{10,12},{12,14},{14,16},{16,18},{18... | collective-permute-start | bytes 1572872 | tf_op jit(solution)/shard_map/ppermute | solution.py:23
  3.9 17.4 %collective-permute-start = (bf16[1024,256]{1,0:T(8,128)(2,1)S(1)}, bf16[1024,256]{1,0:T(8,128)(2,1)S(1)}, u32[]{:S(2)}, u32[]{:S(2)}) collective-permute-start(bf16[1024,256]{1,0:T(8,128)(2,1)S(1)} %shard_map.69), channel_id=1, source_target_pairs={{0,2},{2,4},{4,6},{6,8},{8,10},{10,12},{12,14},{14,16},{16,18},{18... | collective-permute-start | bytes 1572872 | tf_op jit(solution)/shard_map/ppermute | solution.py:23
  7.1 1.1 %copy-start.2 = (bf16[768,512]{1,0:T(8,128)(2,1)S(1)}, bf16[768,512]{1,0:T(8,128)(2,1)}, u32[]{:S(2)}) copy-start(bf16[768,512]{1,0:T(8,128)(2,1)} %t.1) | copy-start | bytes 2359300
  16.0 17.5 %collective-permute-start.6 = (bf16[1024,256]{1,0:T(8,128)(2,1)S(1)}, bf16[1024,256]{1,0:T(8,128)(2,1)S(1)}, u32[]{:S(2)}, u32[]{:S(2)}) collective-permute-start(bf16[1024,256]{1,0:T(8,128)(2,1)S(1)} %get-tuple-element.58.rounded), channel_id=1, source_target_pairs={{0,4},{2,6},{4,8},{6,10},{8,12},{10,14},{12,16},{14,18},{16,20},{1... | collective-permute-start | bytes 1572872 | tf_op jit(solution)/shard_map/ppermute | solution.py:23
  21.6 22.2 %collective-permute-start.2 = (bf16[1024,256]{1,0:T(8,128)(2,1)S(1)}, bf16[1024,256]{1,0:T(8,128)(2,1)S(1)}, u32[]{:S(2)}, u32[]{:S(2)}) collective-permute-start(bf16[1024,256]{1,0:T(8,128)(2,1)S(1)} %get-tuple-element.47.rounded), channel_id=1, source_target_pairs={{0,4},{2,6},{4,8},{6,10},{8,12},{10,14},{12,16},{14,18},{16,20},{1... | collective-permute-start | bytes 1572872 | tf_op jit(solution)/shard_map/ppermute | solution.py:23
  35.1 11.5 %collective-permute-start.8 = (f32[8,64,256]{2,1,0:T(8,128)S(1)}, f32[8,64,256]{2,1,0:T(8,128)S(1)}, u32[]{:S(2)}, u32[]{:S(2)}) collective-permute-start(f32[8,64,256]{2,1,0:T(8,128)S(1)} %get-tuple-element.67), channel_id=1, source_target_pairs={{0,2},{2,0},{4,6},{6,4},{8,10},{10,8},{12,14},{14,12},{16,18},{18,... | collective-permute-start | bytes 1572872 | tf_op jit(solution)/shard_map/ppermute | solution.py:34
  45.4 2.8 %collective-permute-start.10 = (f32[8,64,256]{2,1,0:T(8,128)S(1)}, f32[8,64,256]{2,1,0:T(8,128)S(1)}, u32[]{:S(2)}, u32[]{:S(2)}) collective-permute-start(f32[8,64,256]{2,1,0:T(8,128)S(1)} %get-tuple-element.71), channel_id=1, source_target_pairs={{0,2},{2,0},{4,6},{6,4},{8,10},{10,8},{12,14},{14,12},{16,18},{18,... | collective-permute-start | bytes 1572872 | tf_op jit(solution)/shard_map/ppermute | solution.py:34
  45.5 19.9 %collective-permute-start.7 = (bf16[1024,256]{1,0:T(8,128)(2,1)S(1)}, bf16[1024,256]{1,0:T(8,128)(2,1)S(1)}, u32[]{:S(2)}, u32[]{:S(2)}) collective-permute-start(bf16[1024,256]{1,0:T(8,128)(2,1)S(1)} %get-tuple-element.62.rounded), channel_id=1, source_target_pairs={{0,8},{2,10},{4,12},{6,14},{8,16},{10,18},{12,20},{14,22},{16,24},... | collective-permute-start | bytes 1572872 | tf_op jit(solution)/shard_map/ppermute | solution.py:23
  45.5 25.2 %collective-permute-start.4 = (bf16[768,256]{1,0:T(8,128)(2,1)S(1)}, bf16[768,256]{1,0:T(8,128)(2,1)S(1)}, u32[]{:S(2)}, u32[]{:S(2)}) collective-permute-start(bf16[768,256]{1,0:T(8,128)(2,1)S(1)} %get-tuple-element.56), channel_id=1, source_target_pairs={{0,8},{2,10},{4,12},{6,14},{8,16},{10,18},{12,20},{14,22},{16,24},... | collective-permute-start | bytes 1179656 | tf_op jit(solution)/shard_map/ppermute | solution.py:23
  46.6 5.0 %collective-permute-start.9 = (bf16[8,32,256]{2,1,0:T(8,128)(2,1)S(1)}, bf16[8,32,256]{2,1,0:T(8,128)(2,1)S(1)}, u32[]{:S(2)}, u32[]{:S(2)}) collective-permute-start(bf16[8,32,256]{2,1,0:T(8,128)(2,1)S(1)} %get-tuple-element.69), channel_id=1, source_target_pairs={{0,1},{1,0},{2,3},{3,2},{4,5},{5,4},{6,7},{7,6},{8,9},{9,8},{10,11... | collective-permute-start | bytes 393224 | tf_op jit(solution)/shard_map/ppermute | solution.py:34
  51.8 4.3 %collective-permute-start.12 = (bf16[4,32,256]{2,1,0:T(8,128)(2,1)S(1)}, bf16[4,32,256]{2,1,0:T(8,128)(2,1)S(1)}, u32[]{:S(2)}, u32[]{:S(2)}) collective-permute-start(bf16[4,32,256]{2,1,0:T(8,128)(2,1)S(1)} %get-tuple-element.74), channel_id=1, source_target_pairs={{0,1},{1,0},{2,3},{3,2},{4,5},{5,4},{6,7},{7,6},{8,9},{9,8},{10,11... | collective-permute-start | bytes 196616 | tf_op jit(solution)/shard_map/ppermute | solution.py:34
  53.3 7.9 %collective-permute-start.11 = (bf16[4,32,512]{2,1,0:T(8,128)(2,1)S(1)}, bf16[4,32,512]{2,1,0:T(8,128)(2,1)S(1)}, u32[]{:S(2)}, u32[]{:S(2)}) collective-permute-start(bf16[4,32,512]{2,1,0:T(8,128)(2,1)S(1)} %get-tuple-element.73), channel_id=1, source_target_pairs={{0,4},{2,6},{4,0},{6,2},{8,12},{10,14},{12,8},{14,10},{16,20},{18,... | collective-permute-start | bytes 393224 | tf_op jit(solution)/shard_map/ppermute | solution.py:34
  54.0 19.5 %collective-permute-start.3 = (bf16[256,256]{1,0:T(8,128)(2,1)S(1)}, bf16[256,256]{1,0:T(8,128)(2,1)S(1)}, u32[]{:S(2)}, u32[]{:S(2)}) collective-permute-start(bf16[256,256]{1,0:T(8,128)(2,1)S(1)} %get-tuple-element.55), channel_id=1, source_target_pairs={{0,8},{2,10},{4,12},{6,14},{8,16},{10,18},{12,20},{14,22},{16,24},... | collective-permute-start | bytes 393224 | tf_op jit(solution)/shard_map/ppermute | solution.py:23
  56.1 5.2 %collective-permute-start.13 = (bf16[4,32,256]{2,1,0:T(8,128)(2,1)S(1)}, bf16[4,32,256]{2,1,0:T(8,128)(2,1)S(1)}, u32[]{:S(2)}, u32[]{:S(2)}) collective-permute-start(bf16[4,32,256]{2,1,0:T(8,128)(2,1)S(1)} %get-tuple-element.75), channel_id=1, source_target_pairs={{0,5},{1,4},{2,7},{3,6},{4,1},{5,0},{6,3},{7,2},{8,13},{9,12},{10,... | collective-permute-start | bytes 196616 | tf_op jit(solution)/shard_map/ppermute | solution.py:315
  61.3 13.2 %collective-permute-start.14 = (bf16[32,512]{1,0:T(8,128)(2,1)S(1)}, bf16[32,512]{1,0:T(8,128)(2,1)S(1)}, u32[]{:S(2)}, u32[]{:S(2)}) collective-permute-start(bf16[32,512]{1,0:T(8,128)(2,1)S(1)} %get-tuple-element.77), channel_id=1, source_target_pairs={{0,8},{2,10},{4,12},{6,14},{8,0},{10,2},{12,4},{14,6},{16,24},{18,... | collective-permute-start | bytes 98312 | tf_op jit(solution)/shard_map/ppermute | solution.py:34
  63.0 12.1 %collective-permute-start.15 = (bf16[32,512]{1,0:T(8,128)(2,1)S(1)}, bf16[32,512]{1,0:T(8,128)(2,1)S(1)}, u32[]{:S(2)}, u32[]{:S(2)}) collective-permute-start(bf16[32,512]{1,0:T(8,128)(2,1)S(1)} %get-tuple-element.78), channel_id=1, source_target_pairs={{0,16},{2,18},{4,20},{6,22},{8,24},{10,26},{12,28},{14,30},{16,0},... | collective-permute-start | bytes 98312 | tf_op jit(solution)/shard_map/ppermute | solution.py:34
  65.3 9.7 %collective-permute-start.16 = (bf16[32,512]{1,0:T(8,128)(2,1)S(1)}, bf16[32,512]{1,0:T(8,128)(2,1)S(1)}, u32[]{:S(2)}, u32[]{:S(2)}) collective-permute-start(bf16[32,512]{1,0:T(8,128)(2,1)S(1)} %get-tuple-element.79), channel_id=1, source_target_pairs={{0,24},{2,26},{4,28},{6,30},{8,16},{10,18},{12,20},{14,22},{16,8},... | collective-permute-start | bytes 98312 | tf_op jit(solution)/shard_map/ppermute | solution.py:34

commit v13 on v12

--- a/solution.py
+++ b/solution.py
@@ -119,21 +119,16 @@
     pl.when(core == 1)(lambda: round_kernel(0, mix, base, on_chip.at[:, columns], rounded, master))
 
 
-def round_kernel(step, mix, base, arrived, rounded, master, *row_parts):
+def round_kernel(step, mix, base, arrived, rounded, master):
     _, peer = shares(mix, step)
     total = base[...] + peer * arrived[...].astype(jnp.float32)
     rounded[...] = total.astype(jnp.bfloat16)
     master[...] = total
-    row = 0
-    for part in row_parts:
-        part[...] = rounded[row:row + part.shape[0], :]
-        row += part.shape[0]
-
-
-def finish_kernel(row, mix, base, arrived, *refs):
+
+
+def finish_kernel(mix, base, arrived, *refs):
     _, peer = shares(mix, STEPS - 1)
-    rows = slice(row, row + arrived.shape[0])
-    refs[-1][...] = (base[rows, :] + peer * arrived[...].astype(jnp.float32)).astype(jnp.bfloat16)
+    refs[-1][...] = (base[...] + peer * arrived[...].astype(jnp.float32)).astype(jnp.bfloat16)
 
 
 def leg_kernel(axis, bit, kept, arrived, keep, give):
@@ -145,29 +140,39 @@
 
 
 def corner_kernel(first, first_arrived, second, second_arrived, keep, give_y, give_x, give_xy):
-    y, x = (lax.axis_index("gossip") >> 1) & 1, lax.axis_index("group") & 1
-    width = first.shape[-1]
-    for out, row in ((keep, y), (give_y, 1 - y)):
-        at, column = pl.ds(row, 1), pl.ds(x, 1)
-        total = first[:, at] + first_arrived[:, at].astype(jnp.float32)
-        out[:, :, :width] = total.reshape(out.shape[:-1] + (width,)).astype(out.dtype)
-        total = second[:, at, column] + second_arrived[:, at, column]
-        out[:, :, width:] = total.reshape(out.shape[:-1] + (width,)).astype(out.dtype)
-    for out, row in ((give_x, y), (give_xy, 1 - y)):
-        at, column = pl.ds(row, 1), pl.ds(1 - x, 1)
-        total = second[:, at, column] + second_arrived[:, at, column]
-        out[...] = total.reshape(out.shape).astype(out.dtype)
+    at = lax.axis_index("gossip")
+    own, y, x = at >> 2, (at >> 1) & 1, lax.axis_index("group") & 1
+    width, half = first.shape[-1], first.shape[0] // 2
+    for near, wide, narrow in ((y, keep, give_x), (1 - y, give_y, give_xy)):
+        for i in range(half):
+            block = pl.ds(own ^ ((1 - near) * half + i), 1)
+            for row in range(2):
+                to = (slice(2 * i + row, 2 * i + row + 1), slice(None))
+                shape = (1, wide.shape[1], width)
+                total = first[block, row] + first_arrived[block, row].astype(jnp.float32)
+                wide[to + (slice(0, width),)] = total.reshape(shape).astype(wide.dtype)
+                for out, side, columns in ((wide, x, slice(width, None)), (narrow, 1 - x, slice(None))):
+                    column = pl.ds(side, 1)
+                    total = second[block, row, column] + second_arrived[block, row, column]
+                    out[to + (columns,)] = total.reshape(shape).astype(out.dtype)
 
 
 def spread_kernel(kept, from_y, from_x, from_xy, keep, *gives):
-    mine = lax.axis_index("gossip") >> 2
+    y = (lax.axis_index("gossip") >> 1) & 1
     width = from_x.shape[-1]
-    for other, out in enumerate((keep,) + gives):
-        at = pl.ds(mine ^ other, 1)
+
+    def block_of(place, out):
+        at = pl.ds(place, 1)
         rows = kept[at] + from_y[at].astype(jnp.float32)
         late = from_x[at].astype(jnp.float32) + from_xy[at].astype(jnp.float32)
         out[:, :width] = rows[:, :, :width].reshape(out.shape[0], width).astype(out.dtype)
         out[:, width:] = (rows[:, :, width:] + late).reshape(out.shape[0], width).astype(out.dtype)
+
+    block_of(1, keep)
+    keep[...] = jnp.where(y == 1, keep[...], 0.0)
+    for i in range(len(gives) // 2):
+        block_of(2 * i + y, gives[2 * i])
+        block_of(2 * i + 1 - y, gives[2 * i + 1])
 
 
 def mean_kernel(replicas, keep, *refs):
@@ -265,13 +270,10 @@
     parts, last = [], []
     for half in range(HALVES):
         base1, velocity1 = middles[half]
-        heights = [din] if half < HALVES - 1 else [din - din // 4, din // 4]
-        row_parts = [((height, width), jnp.bfloat16) for height in heights]
-        rounded2, master2, *sent = call(
-            functools.partial(round_kernel, 1), [mix, base1, arrived1[half]],
-            [half_bf16, half_f32] + (row_parts if len(heights) > 1 else []),
-        )
-        arrived2 = shifted((sent or [rounded2])[0], "gossip", 4)
+        rounded2, master2 = call(
+            functools.partial(round_kernel, 1), [mix, base1, arrived1[half]], [half_bf16, half_f32]
+        )
+        arrived2 = shifted(rounded2, "gossip", 4)
         outs, scratch = [half_f32] * 2, ()
         if split:
             pair = (n_gossip // 2, n_group * own_rows, width)
@@ -283,7 +285,7 @@
             outs,
             scratch,
         )
-        last.append((base2, arrived2))
+        last += [base2, arrived2]
         if not split:
             parts.append(part[0])
             continue
@@ -314,25 +316,29 @@
         pairs = [(source, source ^ (2 * n_group + 1)) for source in range(replicas)]
         from_xy = lax.ppermute(give_xy, ("gossip", "group"), pairs)
         shape = (own_rows, dout)
-        others = [(shape, jnp.bfloat16)] * (lead - 1)
+        others = [(shape, jnp.bfloat16)] * lead
         keep, *gives = call(spread_kernel, [keep, from_y, from_x, from_xy], [(shape, jnp.float32)] + others)
         gots = []
-        for other, give in enumerate(gives, 1):
-            gots.append(flipped(give, "gossip", 4 * other))
+        for i in range(lead // 2):
+            for cross in range(2):
+
+                def target(at, i=i, cross=cross):
+                    own, y, core = at >> 2, (at >> 1) & 1, at & 1
+                    if y and not i and not cross:
+                        return None
+                    return ((own ^ (i if y else lead // 2 + i)) << 2) | ((y ^ cross) << 1) | core
+
+                gots.append(moved(gives[2 * i + cross], target))
     else:
         mean_weights = scattered_sum(jnp.concatenate(parts, axis=1)) / replicas
-    arrived_tail = shifted(sent[1], "gossip", 4)
     result, replica_weights = ((din, dout), jnp.bfloat16), []
-    for part in range(HALVES + 1):
-        half = min(part, HALVES - 1)
-        base2, arrived2 = last[half]
-        row = din - din // 4 if part == HALVES else 0
-        arrived2 = arrived_tail if row else arrived2
-        height = arrived2.shape[0]
-        block = pl.BlockSpec((height, width), lambda i, at=(row // height, half): at)
+    for half in range(HALVES):
         replica_weights = call(
-            functools.partial(finish_kernel, row), [mix, base2, arrived2, *replica_weights], [result],
-            out_specs=[block], in_place=3 if part else None,
+            finish_kernel,
+            [mix, *last[2 * half:2 * half + 2], *replica_weights],
+            [result],
+            out_specs=[pl.BlockSpec((din, width), lambda i, half=half: (0, half))],
+            in_place=3 if half else None,
         )
     if split:
         (mean_weights,) = call(functools.partial(mean_kernel, replicas), [keep] + gots, [(shape, jnp.float32)])

time: 75.9 us -> 77.3 us (1.018)
  starting transfers between devices: 19.7 us -> 20.8 us
  waiting for transfers between devices: 42.8 us -> 43.6 us
    ppermute x1 -> x5, starting transfers between devices: 2.73 us -> 10.7 us  [moved(): return lax.ppermute(value, 'gossip', pairs)]
    ppermute x8 -> x5, starting transfers between devices: 9.04 us -> 3.87 us  [flipped(): lax.ppermute(value, axis, [(source, source ^ bit) for source in range(cou...]
    ppermute x1 -> x5, waiting for transfers between devices: 0.01 us -> 1.91 us  [moved(): return lax.ppermute(value, 'gossip', pairs)]
    ppermute x7 -> x6, starting transfers between devices: 6.37 us -> 4.79 us  [shifted(): return lax.ppermute(value, axis, pairs)]
    ppermute x1, waiting for transfers between devices: 3.62 us -> 2.39 us  [steps(): from_xy = lax.ppermute(give_xy, ('gossip', 'group'), pairs)]
    pallas_call x18 -> x17, Pallas kernels: 11.3 us -> 10.7 us  [call(): pl.pallas_call(kernel, grid=(1,) if out_specs else (), in_specs=in_specs,...]
    ppermute x7 -> x6, waiting for transfers between devices: 34.2 us -> 34.5 us  [shifted(): return lax.ppermute(value, axis, pairs)]
    ppermute x8 -> x5, waiting for transfers between devices: 4.96 us -> 4.88 us  [flipped(): lax.ppermute(value, axis, [(source, source ^ bit) for source in range(cou...]
  transfers between devices with their start and end apart: 17 -> 17, of which waited for: 11 -> 9; matrix products, arithmetic and copies ran while one was open for 0% -> 0% of each run, Pallas kernels for 14% -> 13%
where the time goes in v13:
time: 77.3 us; the launch traced here: 77 us
  waiting for transfers between devices  43.6 us (56%)
  starting transfers between devices  20.8 us (27%)
  Pallas kernels  10.7 us (14%)
  local copies, waits for them, and re-layouts  1.15 us (1%)
  between operations  0.82 us (1%)
    ppermute x6, waiting for transfers between devices, shifted(): return lax.ppermute(value, axis, pairs)  34.5 us
    ppermute x5, starting transfers between devices, moved(): return lax.ppermute(value, 'gossip', pairs)  10.7 us
    pallas_call x17, Pallas kernels, call(): pl.pallas_call(kernel, grid=(1,) if out_specs else (), in_specs=in_specs,...  10.7 us
    ppermute x5, waiting for transfers between devices, flipped(): lax.ppermute(value, axis, [(source, source ^ bit) for source in range(cou...  4.88 us
    ppermute x6, starting transfers between devices, shifted(): return lax.ppermute(value, axis, pairs)  4.79 us
    ppermute x5, starting transfers between devices, flipped(): lax.ppermute(value, axis, [(source, source ^ bit) for source in range(cou...  3.87 us
    ppermute x1, waiting for transfers between devices, steps(): from_xy = lax.ppermute(give_xy, ('gossip', 'group'), pairs)  2.39 us
    ppermute x5, waiting for transfers between devices, moved(): return lax.ppermute(value, 'gossip', pairs)  1.91 us
  transfers between devices with their start and end apart: 17, of which 9 were waited for; matrix products, arithmetic and copies ran while one was open for 0% of the time, Pallas kernels for 13%

profile of v13, /device:TPU:0, one launch (start us, length us, event | category | flops | bytes accessed | tf_op | source)
XLA Modules:
  0.0 77.0 jit_solution(3893987294642864657)
XLA Ops:
  0.6 0.0 copy-start
  0.7 2.7 %collective-permute-start.1 = (bf16[1024,512]{1,0:T(8,128)(2,1)}, bf16[1024,512]{1,0:T(8,128)(2,1)S(1)}, u32[]{:S(2)}, u32[]{:S(2)}) collective-permute-start(bf16[1024,512]{1,0:T(8,128)(2,1)} %bitcast.9), channel_id=1, source_target_pairs={{0,2},{4,6},{8,10},{12,14},{16,18},{20,22},{24,26},{28,30},{1,3},{... | collective-permute-start | bytes 3145736 | tf_op jit(solution)/shard_map/ppermute | solution.py:29
  3.4 0.1 shard_map.74
  3.5 0.4 collective-permute-start.4
  3.9 3.2 %collective-permute-start = (bf16[1024,256]{1,0:T(8,128)(2,1)S(1)}, bf16[1024,256]{1,0:T(8,128)(2,1)S(1)}, u32[]{:S(2)}, u32[]{:S(2)}) collective-permute-start(bf16[1024,256]{1,0:T(8,128)(2,1)S(1)} %shard_map.69), channel_id=1, source_target_pairs={{0,2},{2,4},{4,6},{6,8},{8,10},{10,12},{12,14},{14,16},{16,18},{18... | collective-permute-start | bytes 1572872 | tf_op jit(solution)/shard_map/ppermute | solution.py:23
  7.1 0.0 copy-start.2
  7.1 1.1 %copy-done.2 = bf16[768,512]{1,0:T(8,128)(2,1)S(1)} copy-done((bf16[768,512]{1,0:T(8,128)(2,1)S(1)}, bf16[768,512]{1,0:T(8,128)(2,1)}, u32[]{:S(2)}) %copy-start.2) | copy-done | bytes 786456
  8.2 1.9 %shard_map.68 = (f32[8,128]{1,0:T(8,128)S(1)}, bf16[256,1024]{1,0:T(8,128)(2,1)S(1)}, bf16[256,512]{1,0:T(8,128)(2,1)S(1)}, bf16[256,1024]{1,0:T(8,128)(2,1)S(1)...) custom-call(s32[1,3]{1,0:T(1,128)S(1)} %copy-done.4, ...), custom_call_target="tpu_custom_call" | custom-call | tf_op jit(solution)/shard_map/pallas_call | solution.py:195
  10.2 5.5 %collective-permute-done.4.from_chip = bf16[1024,256]{1,0:T(8,128)(2,1)S(1)} collective-permute-done((bf16[1024,256]{1,0:T(8,128)(2,1)S(1)}, bf16[1024,256]{1,0:T(8,128)(2,1)S(1)}, u32[]{:S(2)}, u32[]{:S(2)}) %collective-permute-start.4) | collective-permute-done | bytes 524320 | tf_op jit(solution)/shard_map/ppermute | solution.py:23
  15.7 0.0 collective-permute-done.1.on_chip
  15.7 0.3 shard_map.75
  16.0 0.1 collective-permute-start.5
  16.1 5.2 %collective-permute-done.from_chip = bf16[1024,256]{1,0:T(8,128)(2,1)S(1)} collective-permute-done((bf16[1024,256]{1,0:T(8,128)(2,1)S(1)}, bf16[1024,256]{1,0:T(8,128)(2,1)S(1)}, u32[]{:S(2)}, u32[]{:S(2)}) %collective-permute-start) | collective-permute-done | bytes 524320 | tf_op jit(solution)/shard_map/ppermute | solution.py:23
  21.3 0.3 shard_map.70
  21.6 0.1 collective-permute-start.2
  21.7 0.9 %shard_map.76 = (f32[1024,256]{1,0:T(8,128)S(1)}, f32[1024,256]{1,0:T(8,128)S(1)}) custom-call(f32[8,128]{1,0:T(8,128)S(1)} %get-tuple-element.40.mix, bf16[256,1024]{1,0:T(8,128)(2,1)S(1)} %get-tuple-element.43.x, bf16[256,512]{1,0:T(8,128)(2,1)S(1)} %get-tuple-element.44.t, bf16[1024,256]{1,0:T(8,128)(2,1)S(1)} %get-tuple-element.55.rounded, ...), custom_call_target="tpu_custom_call" | custom-call | tf_op jit(solution)/shard_map/pallas_call | solution.py:195
  22.6 10.9 %collective-permute-done.5.arrived = bf16[1024,256]{1,0:T(8,128)(2,1)S(1)} collective-permute-done((bf16[1024,256]{1,0:T(8,128)(2,1)S(1)}, bf16[1024,256]{1,0:T(8,128)(2,1)S(1)}, u32[]{:S(2)}, u32[]{:S(2)}) %collective-permute-start.5) | collective-permute-done | bytes 524320 | tf_op jit(solution)/shard_map/ppermute | solution.py:23
  33.6 0.3 shard_map.77
  33.9 1.2 %shard_map.78 = (f32[1024,256]{1,0:T(8,128)S(1)}, f32[8,64,256]{2,1,0:T(8,128)S(1)}, f32[8,64,256]{2,1,0:T(8,128)S(1)}) custom-call(f32[8,128]{1,0:T(8,128)S(1)} %get-tuple-element.40.mix, bf16[256,1024]{1,0:T(8,128)(2,1)S(1)} %get-tuple-element.41.x, bf16[256,512]{1,0:T(8,128)(2,1)S(1)} %get-tuple-element.42.t, ...), custom_call_target="tpu_custom_call" | custom-call | tf_op jit(solution)/shard_map/pallas_call | solution.py:195
  35.1 0.1 collective-permute-start.7
  35.2 0.9 %shard_map.71 = (f32[1024,256]{1,0:T(8,128)S(1)}, f32[1024,256]{1,0:T(8,128)S(1)}) custom-call(f32[8,128]{1,0:T(8,128)S(1)} %get-tuple-element.40.mix, bf16[256,1024]{1,0:T(8,128)(2,1)S(1)} %get-tuple-element.43.x, bf16[256,512]{1,0:T(8,128)(2,1)S(1)} %get-tuple-element.44.t, bf16[1024,256]{1,0:T(8,128)(2,1)S(1)} %get-tuple-element.46.rounded, ...), custom_call_target="tpu_custom_call" | custom-call | tf_op jit(solution)/shard_map/pallas_call | solution.py:195
  36.1 7.7 %collective-permute-done.2.arrived = bf16[1024,256]{1,0:T(8,128)(2,1)S(1)} collective-permute-done((bf16[1024,256]{1,0:T(8,128)(2,1)S(1)}, bf16[1024,256]{1,0:T(8,128)(2,1)S(1)}, u32[]{:S(2)}, u32[]{:S(2)}) %collective-permute-start.2) | collective-permute-done | bytes 524320 | tf_op jit(solution)/shard_map/ppermute | solution.py:23
  43.8 0.3 shard_map.72
  44.1 1.2 %shard_map.73 = (f32[1024,256]{1,0:T(8,128)S(1)}, f32[8,64,256]{2,1,0:T(8,128)S(1)}, f32[8,64,256]{2,1,0:T(8,128)S(1)}) custom-call(f32[8,128]{1,0:T(8,128)S(1)} %get-tuple-element.40.mix, bf16[256,1024]{1,0:T(8,128)(2,1)S(1)} %get-tuple-element.41.x, bf16[256,512]{1,0:T(8,128)(2,1)S(1)} %get-tuple-element.42.t, ...), custom_call_target="tpu_custom_call" | custom-call | tf_op jit(solution)/shard_map/pallas_call | solution.py:195
  45.3 0.1 collective-permute-start.9
  45.4 0.1 collective-permute-start.6
  45.5 1.1 %collective-permute-start.3 = (bf16[1024,256]{1,0:T(8,128)(2,1)S(1)}, bf16[1024,256]{1,0:T(8,128)(2,1)S(1)}, u32[]{:S(2)}, u32[]{:S(2)}) collective-permute-start(bf16[1024,256]{1,0:T(8,128)(2,1)S(1)} %get-tuple-element.50.rounded), channel_id=1, source_target_pairs={{0,8},{2,10},{4,12},{6,14},{8,16},{10,18},{12,20},{14,22},{16,24},... | collective-permute-start | bytes 1572872 | tf_op jit(solution)/shard_map/ppermute | solution.py:23
  46.5 0.1 shard_map.81
  46.6 1.6 %collective-permute-start.8 = (bf16[8,32,256]{2,1,0:T(8,128)(2,1)S(1)}, bf16[8,32,256]{2,1,0:T(8,128)(2,1)S(1)}, u32[]{:S(2)}, u32[]{:S(2)}) collective-permute-start(bf16[8,32,256]{2,1,0:T(8,128)(2,1)S(1)} %get-tuple-element.66), channel_id=1, source_target_pairs={{0,1},{1,0},{2,3},{3,2},{4,5},{5,4},{6,7},{7,6},{8,9},{9,8},{10,11... | collective-permute-start | bytes 393224 | tf_op jit(solution)/shard_map/ppermute | solution.py:34
  48.2 3.5 %collective-permute-done.8 = bf16[8,32,256]{2,1,0:T(8,128)(2,1)S(1)} collective-permute-done((bf16[8,32,256]{2,1,0:T(8,128)(2,1)S(1)}, bf16[8,32,256]{2,1,0:T(8,128)(2,1)S(1)}, u32[]{:S(2)}, u32[]{:S(2)}) %collective-permute-start.8) | collective-permute-done | bytes 131104 | tf_op jit(solution)/shard_map/ppermute | solution.py:34
  51.6 0.1 shard_map.82
  51.8 0.7 collective-permute-start.10
  52.5 1.5 %collective-permute-start.11 = (bf16[4,32,256]{2,1,0:T(8,128)(2,1)S(1)}, bf16[4,32,256]{2,1,0:T(8,128)(2,1)S(1)}, u32[]{:S(2)}, u32[]{:S(2)}) collective-permute-start(bf16[4,32,256]{2,1,0:T(8,128)(2,1)S(1)} %get-tuple-element.71), channel_id=1, source_target_pairs={{0,1},{1,0},{2,3},{3,2},{4,5},{5,4},{6,7},{7,6},{8,9},{9,8},{10,11... | collective-permute-start | bytes 196616 | tf_op jit(solution)/shard_map/ppermute | solution.py:34
  53.9 1.4 %collective-permute-start.12 = (bf16[4,32,256]{2,1,0:T(8,128)(2,1)S(1)}, bf16[4,32,256]{2,1,0:T(8,128)(2,1)S(1)}, u32[]{:S(2)}, u32[]{:S(2)}) collective-permute-start(bf16[4,32,256]{2,1,0:T(8,128)(2,1)S(1)} %get-tuple-element.72), channel_id=1, source_target_pairs={{0,5},{1,4},{2,7},{3,6},{4,1},{5,0},{6,3},{7,2},{8,13},{9,12},{10,... | collective-permute-start | bytes 196616 | tf_op jit(solution)/shard_map/ppermute | solution.py:317
  55.3 1.4 %collective-permute-done.11.from_x = bf16[4,32,256]{2,1,0:T(8,128)(2,1)S(1)} collective-permute-done((bf16[4,32,256]{2,1,0:T(8,128)(2,1)S(1)}, bf16[4,32,256]{2,1,0:T(8,128)(2,1)S(1)}, u32[]{:S(2)}, u32[]{:S(2)}) %collective-permute-start.11) | collective-permute-done | bytes 65568 | tf_op jit(solution)/shard_map/ppermute | solution.py:34
  56.7 2.4 %collective-permute-done.12.from_xy = bf16[4,32,256]{2,1,0:T(8,128)(2,1)S(1)} collective-permute-done((bf16[4,32,256]{2,1,0:T(8,128)(2,1)S(1)}, bf16[4,32,256]{2,1,0:T(8,128)(2,1)S(1)}, u32[]{:S(2)}, u32[]{:S(2)}) %collective-permute-start.12) | collective-permute-done | bytes 65568 | tf_op jit(solution)/shard_map/ppermute | solution.py:317
  59.1 0.0 collective-permute-done.10.from_y
  59.1 0.1 shard_map.83
  59.2 5.0 %collective-permute-start.13 = (bf16[32,512]{1,0:T(8,128)(2,1)S(1)}, bf16[32,512]{1,0:T(8,128)(2,1)S(1)}, u32[]{:S(2)}, u32[]{:S(2)}) collective-permute-start(bf16[32,512]{1,0:T(8,128)(2,1)S(1)} %get-tuple-element.74), channel_id=1, source_target_pairs={{0,16},{2,18},{8,24},{10,26},{16,0},{18,2},{24,8},{26,10},{1,17},{... | collective-permute-start | bytes 98312 | tf_op jit(solution)/shard_map/ppermute | solution.py:29
  64.2 0.2 collective-permute-start.14
  64.4 0.8 %collective-permute-start.15 = (bf16[32,512]{1,0:T(8,128)(2,1)S(1)}, bf16[32,512]{1,0:T(8,128)(2,1)S(1)}, u32[]{:S(2)}, u32[]{:S(2)}) collective-permute-start(bf16[32,512]{1,0:T(8,128)(2,1)S(1)} %get-tuple-element.76), channel_id=1, source_target_pairs={{0,24},{2,26},{4,12},{6,14},{8,16},{10,18},{12,4},{14,6},{16,8},{1... | collective-permute-start | bytes 98312 | tf_op jit(solution)/shard_map/ppermute | solution.py:29
  65.2 0.0 collective-permute-done.6.arrived
  65.2 2.0 %collective-permute-start.16 = (bf16[32,512]{1,0:T(8,128)(2,1)S(1)}, bf16[32,512]{1,0:T(8,128)(2,1)S(1)}, u32[]{:S(2)}, u32[]{:S(2)}) collective-permute-start(bf16[32,512]{1,0:T(8,128)(2,1)S(1)} %get-tuple-element.77), channel_id=1, source_target_pairs={{0,28},{2,30},{4,8},{6,10},{8,20},{10,22},{12,0},{14,2},{16,12},{1... | collective-permute-start | bytes 98312 | tf_op jit(solution)/shard_map/ppermute | solution.py:29
  67.2 1.1 %shard_map.79.refs_0_ = bf16[1024,512]{1,0:T(8,128)(2,1)} custom-call(f32[8,128]{1,0:T(8,128)S(1)} %get-tuple-element.40.mix, f32[1024,256]{1,0:T(8,128)S(1)} %get-tuple-element.62.base, bf16[1024,256]{1,0:T(8,128)(2,1)S(1)} %collective-permute-done.6.arrived), custom_call_target="tpu_custom_call" | custom-call | tf_op jit(solution)/shard_map/pallas_call | solution.py:195
  68.3 5.1 %collective-permute-done.3.arrived = bf16[1024,256]{1,0:T(8,128)(2,1)S(1)} collective-permute-done((bf16[1024,256]{1,0:T(8,128)(2,1)S(1)}, bf16[1024,256]{1,0:T(8,128)(2,1)S(1)}, u32[]{:S(2)}, u32[]{:S(2)}) %collective-permute-start.3) | collective-permute-done | bytes 524320 | tf_op jit(solution)/shard_map/ppermute | solution.py:23
  73.4 1.1 %shard_map.80 = bf16[1024,512]{1,0:T(8,128)(2,1)} custom-call(f32[8,128]{1,0:T(8,128)S(1)} %get-tuple-element.40.mix, f32[1024,256]{1,0:T(8,128)S(1)} %get-tuple-element.53.base, bf16[1024,256]{1,0:T(8,128)(2,1)S(1)} %collective-permute-done.3.arrived, bf16[1024,512]{1,0:T(8,128)(2,1)} %shard_map.79.refs_0_), custom_call_target="tpu_custom_call", output_to_operand_aliasing={{}: (3, {})} | custom-call | tf_op jit(solution)/shard_map/pallas_call | solution.py:195
  74.5 1.9 %collective-permute-done.13.refs_0_ = bf16[32,512]{1,0:T(8,128)(2,1)S(1)} collective-permute-done((bf16[32,512]{1,0:T(8,128)(2,1)S(1)}, bf16[32,512]{1,0:T(8,128)(2,1)S(1)}, u32[]{:S(2)}, u32[]{:S(2)}) %collective-permute-start.13) | collective-permute-done | bytes 32800 | tf_op jit(solution)/shard_map/ppermute | solution.py:29
  76.4 0.7 shard_map.84
  (13 shorter events, 0.1 us)
Async XLA Ops:
  0.6 6.5 %copy-start = (bf16[1,1024,512]{2,1,0:T(8,128)(2,1)S(1)}, bf16[1,1024,512]{2,1,0:T(8,128)(2,1)}, u32[]{:S(2)}) copy-start(bf16[1,1024,512]{2,1,0:T(8,128)(2,1)} %param.5) | copy-start | bytes 3145732
  0.6 6.5 %copy-start.1 = (bf16[768,1024]{1,0:T(8,128)(2,1)S(1)}, bf16[768,1024]{1,0:T(8,128)(2,1)}, u32[]{:S(2)}) copy-start(bf16[768,1024]{1,0:T(8,128)(2,1)} %x.1) | copy-start | bytes 4718596
  0.7 6.4 %copy-start.3 = (s32[3,2]{0,1:T(2,128)S(1)}, s32[3,2]{0,1:T(2,128)}, u32[]{:S(2)}) copy-start(s32[3,2]{0,1:T(2,128)} %param.8) | copy-start | bytes 76
  0.7 6.4 %copy-start.4 = (s32[1,3]{1,0:T(1,128)S(1)}, s32[1,3]{1,0:T(1,128)}, u32[]{:S(2)}) copy-start(s32[1,3]{1,0:T(1,128)} %order.1) | copy-start | bytes 40
  0.7 15.0 %collective-permute-start.1 = (bf16[1024,512]{1,0:T(8,128)(2,1)}, bf16[1024,512]{1,0:T(8,128)(2,1)S(1)}, u32[]{:S(2)}, u32[]{:S(2)}) collective-permute-start(bf16[1024,512]{1,0:T(8,128)(2,1)} %bitcast.9), channel_id=1, source_target_pairs={{0,2},{4,6},{8,10},{12,14},{16,18},{20,22},{24,26},{28,30},{1,3},{... | collective-permute-start | bytes 3145736 | tf_op jit(solution)/shard_map/ppermute | solution.py:29
  3.5 12.2 %collective-permute-start.4 = (bf16[1024,256]{1,0:T(8,128)(2,1)S(1)}, bf16[1024,256]{1,0:T(8,128)(2,1)S(1)}, u32[]{:S(2)}, u32[]{:S(2)}) collective-permute-start(bf16[1024,256]{1,0:T(8,128)(2,1)S(1)} %shard_map.74), channel_id=1, source_target_pairs={{0,2},{2,4},{4,6},{6,8},{8,10},{10,12},{12,14},{14,16},{16,18},{18... | collective-permute-start | bytes 1572872 | tf_op jit(solution)/shard_map/ppermute | solution.py:23
  3.9 17.4 %collective-permute-start = (bf16[1024,256]{1,0:T(8,128)(2,1)S(1)}, bf16[1024,256]{1,0:T(8,128)(2,1)S(1)}, u32[]{:S(2)}, u32[]{:S(2)}) collective-permute-start(bf16[1024,256]{1,0:T(8,128)(2,1)S(1)} %shard_map.69), channel_id=1, source_target_pairs={{0,2},{2,4},{4,6},{6,8},{8,10},{10,12},{12,14},{14,16},{16,18},{18... | collective-permute-start | bytes 1572872 | tf_op jit(solution)/shard_map/ppermute | solution.py:23
  7.1 1.1 %copy-start.2 = (bf16[768,512]{1,0:T(8,128)(2,1)S(1)}, bf16[768,512]{1,0:T(8,128)(2,1)}, u32[]{:S(2)}) copy-start(bf16[768,512]{1,0:T(8,128)(2,1)} %t.1) | copy-start | bytes 2359300
  16.0 17.5 %collective-permute-start.5 = (bf16[1024,256]{1,0:T(8,128)(2,1)S(1)}, bf16[1024,256]{1,0:T(8,128)(2,1)S(1)}, u32[]{:S(2)}, u32[]{:S(2)}) collective-permute-start(bf16[1024,256]{1,0:T(8,128)(2,1)S(1)} %get-tuple-element.55.rounded), channel_id=1, source_target_pairs={{0,4},{2,6},{4,8},{6,10},{8,12},{10,14},{12,16},{14,18},{16,20},{1... | collective-permute-start | bytes 1572872 | tf_op jit(solution)/shard_map/ppermute | solution.py:23
  21.6 22.2 %collective-permute-start.2 = (bf16[1024,256]{1,0:T(8,128)(2,1)S(1)}, bf16[1024,256]{1,0:T(8,128)(2,1)S(1)}, u32[]{:S(2)}, u32[]{:S(2)}) collective-permute-start(bf16[1024,256]{1,0:T(8,128)(2,1)S(1)} %get-tuple-element.46.rounded), channel_id=1, source_target_pairs={{0,4},{2,6},{4,8},{6,10},{8,12},{10,14},{12,16},{14,18},{16,20},{1... | collective-permute-start | bytes 1572872 | tf_op jit(solution)/shard_map/ppermute | solution.py:23
  35.1 11.4 %collective-permute-start.7 = (f32[8,64,256]{2,1,0:T(8,128)S(1)}, f32[8,64,256]{2,1,0:T(8,128)S(1)}, u32[]{:S(2)}, u32[]{:S(2)}) collective-permute-start(f32[8,64,256]{2,1,0:T(8,128)S(1)} %get-tuple-element.64), channel_id=1, source_target_pairs={{0,2},{2,0},{4,6},{6,4},{8,10},{10,8},{12,14},{14,12},{16,18},{18,... | collective-permute-start | bytes 1572872 | tf_op jit(solution)/shard_map/ppermute | solution.py:34
  45.3 2.8 %collective-permute-start.9 = (f32[8,64,256]{2,1,0:T(8,128)S(1)}, f32[8,64,256]{2,1,0:T(8,128)S(1)}, u32[]{:S(2)}, u32[]{:S(2)}) collective-permute-start(f32[8,64,256]{2,1,0:T(8,128)S(1)} %get-tuple-element.68), channel_id=1, source_target_pairs={{0,2},{2,0},{4,6},{6,4},{8,10},{10,8},{12,14},{14,12},{16,18},{18,... | collective-permute-start | bytes 1572872 | tf_op jit(solution)/shard_map/ppermute | solution.py:34
  45.4 19.8 %collective-permute-start.6 = (bf16[1024,256]{1,0:T(8,128)(2,1)S(1)}, bf16[1024,256]{1,0:T(8,128)(2,1)S(1)}, u32[]{:S(2)}, u32[]{:S(2)}) collective-permute-start(bf16[1024,256]{1,0:T(8,128)(2,1)S(1)} %get-tuple-element.59.rounded), channel_id=1, source_target_pairs={{0,8},{2,10},{4,12},{6,14},{8,16},{10,18},{12,20},{14,22},{16,24},... | collective-permute-start | bytes 1572872 | tf_op jit(solution)/shard_map/ppermute | solution.py:23
  45.5 27.9 %collective-permute-start.3 = (bf16[1024,256]{1,0:T(8,128)(2,1)S(1)}, bf16[1024,256]{1,0:T(8,128)(2,1)S(1)}, u32[]{:S(2)}, u32[]{:S(2)}) collective-permute-start(bf16[1024,256]{1,0:T(8,128)(2,1)S(1)} %get-tuple-element.50.rounded), channel_id=1, source_target_pairs={{0,8},{2,10},{4,12},{6,14},{8,16},{10,18},{12,20},{14,22},{16,24},... | collective-permute-start | bytes 1572872 | tf_op jit(solution)/shard_map/ppermute | solution.py:23
  46.6 5.0 %collective-permute-start.8 = (bf16[8,32,256]{2,1,0:T(8,128)(2,1)S(1)}, bf16[8,32,256]{2,1,0:T(8,128)(2,1)S(1)}, u32[]{:S(2)}, u32[]{:S(2)}) collective-permute-start(bf16[8,32,256]{2,1,0:T(8,128)(2,1)S(1)} %get-tuple-element.66), channel_id=1, source_target_pairs={{0,1},{1,0},{2,3},{3,2},{4,5},{5,4},{6,7},{7,6},{8,9},{9,8},{10,11... | collective-permute-start | bytes 393224 | tf_op jit(solution)/shard_map/ppermute | solution.py:34
  51.8 7.3 %collective-permute-start.10 = (bf16[4,32,512]{2,1,0:T(8,128)(2,1)S(1)}, bf16[4,32,512]{2,1,0:T(8,128)(2,1)S(1)}, u32[]{:S(2)}, u32[]{:S(2)}) collective-permute-start(bf16[4,32,512]{2,1,0:T(8,128)(2,1)S(1)} %get-tuple-element.70), channel_id=1, source_target_pairs={{0,4},{2,6},{4,0},{6,2},{8,12},{10,14},{12,8},{14,10},{16,20},{18,... | collective-permute-start | bytes 393224 | tf_op jit(solution)/shard_map/ppermute | solution.py:34
  52.5 4.3 %collective-permute-start.11 = (bf16[4,32,256]{2,1,0:T(8,128)(2,1)S(1)}, bf16[4,32,256]{2,1,0:T(8,128)(2,1)S(1)}, u32[]{:S(2)}, u32[]{:S(2)}) collective-permute-start(bf16[4,32,256]{2,1,0:T(8,128)(2,1)S(1)} %get-tuple-element.71), channel_id=1, source_target_pairs={{0,1},{1,0},{2,3},{3,2},{4,5},{5,4},{6,7},{7,6},{8,9},{9,8},{10,11... | collective-permute-start | bytes 196616 | tf_op jit(solution)/shard_map/ppermute | solution.py:34
  53.9 5.2 %collective-permute-start.12 = (bf16[4,32,256]{2,1,0:T(8,128)(2,1)S(1)}, bf16[4,32,256]{2,1,0:T(8,128)(2,1)S(1)}, u32[]{:S(2)}, u32[]{:S(2)}) collective-permute-start(bf16[4,32,256]{2,1,0:T(8,128)(2,1)S(1)} %get-tuple-element.72), channel_id=1, source_target_pairs={{0,5},{1,4},{2,7},{3,6},{4,1},{5,0},{6,3},{7,2},{8,13},{9,12},{10,... | collective-permute-start | bytes 196616 | tf_op jit(solution)/shard_map/ppermute | solution.py:317
  59.2 17.2 %collective-permute-start.13 = (bf16[32,512]{1,0:T(8,128)(2,1)S(1)}, bf16[32,512]{1,0:T(8,128)(2,1)S(1)}, u32[]{:S(2)}, u32[]{:S(2)}) collective-permute-start(bf16[32,512]{1,0:T(8,128)(2,1)S(1)} %get-tuple-element.74), channel_id=1, source_target_pairs={{0,16},{2,18},{8,24},{10,26},{16,0},{18,2},{24,8},{26,10},{1,17},{... | collective-permute-start | bytes 98312 | tf_op jit(solution)/shard_map/ppermute | solution.py:29
  64.2 12.2 %collective-permute-start.14 = (bf16[32,512]{1,0:T(8,128)(2,1)S(1)}, bf16[32,512]{1,0:T(8,128)(2,1)S(1)}, u32[]{:S(2)}, u32[]{:S(2)}) collective-permute-start(bf16[32,512]{1,0:T(8,128)(2,1)S(1)} %get-tuple-element.75), channel_id=1, source_target_pairs={{0,20},{2,22},{4,0},{6,2},{8,28},{10,30},{12,8},{14,10},{16,4},{18... | collective-permute-start | bytes 98312 | tf_op jit(solution)/shard_map/ppermute | solution.py:29
  64.4 12.0 %collective-permute-start.15 = (bf16[32,512]{1,0:T(8,128)(2,1)S(1)}, bf16[32,512]{1,0:T(8,128)(2,1)S(1)}, u32[]{:S(2)}, u32[]{:S(2)}) collective-permute-start(bf16[32,512]{1,0:T(8,128)(2,1)S(1)} %get-tuple-element.76), channel_id=1, source_target_pairs={{0,24},{2,26},{4,12},{6,14},{8,16},{10,18},{12,4},{14,6},{16,8},{1... | collective-permute-start | bytes 98312 | tf_op jit(solution)/shard_map/ppermute | solution.py:29
  65.2 11.2 %collective-permute-start.16 = (bf16[32,512]{1,0:T(8,128)(2,1)S(1)}, bf16[32,512]{1,0:T(8,128)(2,1)S(1)}, u32[]{:S(2)}, u32[]{:S(2)}) collective-permute-start(bf16[32,512]{1,0:T(8,128)(2,1)S(1)} %get-tuple-element.77), channel_id=1, source_target_pairs={{0,28},{2,30},{4,8},{6,10},{8,20},{10,22},{12,0},{14,2},{16,12},{1... | collective-permute-start | bytes 98312 | tf_op jit(solution)/shard_map/ppermute | solution.py:29

commit v14 on v12

--- a/solution.py
+++ b/solution.py
@@ -119,21 +119,16 @@
     pl.when(core == 1)(lambda: round_kernel(0, mix, base, on_chip.at[:, columns], rounded, master))
 
 
-def round_kernel(step, mix, base, arrived, rounded, master, *row_parts):
+def round_kernel(step, mix, base, arrived, rounded, master):
     _, peer = shares(mix, step)
     total = base[...] + peer * arrived[...].astype(jnp.float32)
     rounded[...] = total.astype(jnp.bfloat16)
     master[...] = total
-    row = 0
-    for part in row_parts:
-        part[...] = rounded[row:row + part.shape[0], :]
-        row += part.shape[0]
-
-
-def finish_kernel(row, mix, base, arrived, *refs):
+
+
+def finish_kernel(mix, base, arrived, *refs):
     _, peer = shares(mix, STEPS - 1)
-    rows = slice(row, row + arrived.shape[0])
-    refs[-1][...] = (base[rows, :] + peer * arrived[...].astype(jnp.float32)).astype(jnp.bfloat16)
+    refs[-1][...] = (base[...] + peer * arrived[...].astype(jnp.float32)).astype(jnp.bfloat16)
 
 
 def leg_kernel(axis, bit, kept, arrived, keep, give):
@@ -265,13 +260,10 @@
     parts, last = [], []
     for half in range(HALVES):
         base1, velocity1 = middles[half]
-        heights = [din] if half < HALVES - 1 else [din - din // 4, din // 4]
-        row_parts = [((height, width), jnp.bfloat16) for height in heights]
-        rounded2, master2, *sent = call(
-            functools.partial(round_kernel, 1), [mix, base1, arrived1[half]],
-            [half_bf16, half_f32] + (row_parts if len(heights) > 1 else []),
-        )
-        arrived2 = shifted((sent or [rounded2])[0], "gossip", 4)
+        rounded2, master2 = call(
+            functools.partial(round_kernel, 1), [mix, base1, arrived1[half]], [half_bf16, half_f32]
+        )
+        arrived2 = shifted(rounded2, "gossip", 4)
         outs, scratch = [half_f32] * 2, ()
         if split:
             pair = (n_gossip // 2, n_group * own_rows, width)
@@ -283,7 +275,7 @@
             outs,
             scratch,
         )
-        last.append((base2, arrived2))
+        last += [base2, arrived2]
         if not split:
             parts.append(part[0])
             continue
@@ -321,18 +313,14 @@
             gots.append(flipped(give, "gossip", 4 * other))
     else:
         mean_weights = scattered_sum(jnp.concatenate(parts, axis=1)) / replicas
-    arrived_tail = shifted(sent[1], "gossip", 4)
     result, replica_weights = ((din, dout), jnp.bfloat16), []
-    for part in range(HALVES + 1):
-        half = min(part, HALVES - 1)
-        base2, arrived2 = last[half]
-        row = din - din // 4 if part == HALVES else 0
-        arrived2 = arrived_tail if row else arrived2
-        height = arrived2.shape[0]
-        block = pl.BlockSpec((height, width), lambda i, at=(row // height, half): at)
+    for half in range(HALVES):
         replica_weights = call(
-            functools.partial(finish_kernel, row), [mix, base2, arrived2, *replica_weights], [result],
-            out_specs=[block], in_place=3 if part else None,
+            finish_kernel,
+            [mix, *last[2 * half:2 * half + 2], *replica_weights],
+            [result],
+            out_specs=[pl.BlockSpec((din, width), lambda i, half=half: (0, half))],
+            in_place=3 if half else None,
         )
     if split:
         (mean_weights,) = call(functools.partial(mean_kernel, replicas), [keep] + gots, [(shape, jnp.float32)])

time: 75.9 us -> 75.9 us (level)
  waiting for transfers between devices: 42.8 us -> 45.7 us
  starting transfers between devices: 19.7 us -> 17.4 us
    ppermute x7 -> x6, waiting for transfers between devices: 34.2 us -> 37.8 us  [shifted(): return lax.ppermute(value, axis, pairs)]
    ppermute x7 -> x6, starting transfers between devices: 6.37 us -> 4.79 us  [shifted(): return lax.ppermute(value, axis, pairs)]
    ppermute x1, waiting for transfers between devices: 3.62 us -> 2.39 us  [steps(): from_xy = lax.ppermute(give_xy, ('gossip', 'group'), pairs)]
    pallas_call x18 -> x17, Pallas kernels: 11.3 us -> 10.7 us  [call(): pl.pallas_call(kernel, grid=(1,) if out_specs else (), in_specs=in_specs,...]
  transfers between devices with their start and end apart: 17 -> 16, of which waited for: 11 -> 9; matrix products, arithmetic and copies ran while one was open for 0% -> 0% of each run, Pallas kernels for 14% -> 13%
where the time goes in v14:
time: 75.9 us; the launch traced here: 75.7 us
  waiting for transfers between devices  45.7 us (60%)
  starting transfers between devices  17.4 us (23%)
  Pallas kernels  10.7 us (14%)
  local copies, waits for them, and re-layouts  1.15 us (2%)
  between operations  0.81 us (1%)
    ppermute x6, waiting for transfers between devices, shifted(): return lax.ppermute(value, axis, pairs)  37.8 us
    pallas_call x17, Pallas kernels, call(): pl.pallas_call(kernel, grid=(1,) if out_specs else (), in_specs=in_specs,...  10.7 us
    ppermute x8, starting transfers between devices, flipped(): lax.ppermute(value, axis, [(source, source ^ bit) for source in range(cou...  8.5 us
    ppermute x8, waiting for transfers between devices, flipped(): lax.ppermute(value, axis, [(source, source ^ bit) for source in range(cou...  5.43 us
    ppermute x6, starting transfers between devices, shifted(): return lax.ppermute(value, axis, pairs)  4.79 us
    ppermute x1, starting transfers between devices, moved(): return lax.ppermute(value, 'gossip', pairs)  2.73 us
    ppermute x1, waiting for transfers between devices, steps(): from_xy = lax.ppermute(give_xy, ('gossip', 'group'), pairs)  2.39 us
  transfers between devices with their start and end apart: 16, of which 9 were waited for; matrix products, arithmetic and copies ran while one was open for 0% of the time, Pallas kernels for 13%

profile of v14, /device:TPU:0, one launch (start us, length us, event | category | flops | bytes accessed | tf_op | source)
XLA Modules:
  0.0 75.7 jit_solution(905205569857000351)
XLA Ops:
  0.6 0.0 copy-start
  0.7 2.7 %collective-permute-start.1 = (bf16[1024,512]{1,0:T(8,128)(2,1)}, bf16[1024,512]{1,0:T(8,128)(2,1)S(1)}, u32[]{:S(2)}, u32[]{:S(2)}) collective-permute-start(bf16[1024,512]{1,0:T(8,128)(2,1)} %bitcast.9), channel_id=1, source_target_pairs={{0,2},{4,6},{8,10},{12,14},{16,18},{20,22},{24,26},{28,30},{1,3},{... | collective-permute-start | bytes 3145736 | tf_op jit(solution)/shard_map/ppermute | solution.py:29
  3.4 0.1 shard_map.74
  3.5 0.4 collective-permute-start.4
  3.9 3.2 %collective-permute-start = (bf16[1024,256]{1,0:T(8,128)(2,1)S(1)}, bf16[1024,256]{1,0:T(8,128)(2,1)S(1)}, u32[]{:S(2)}, u32[]{:S(2)}) collective-permute-start(bf16[1024,256]{1,0:T(8,128)(2,1)S(1)} %shard_map.69), channel_id=1, source_target_pairs={{0,2},{2,4},{4,6},{6,8},{8,10},{10,12},{12,14},{14,16},{16,18},{18... | collective-permute-start | bytes 1572872 | tf_op jit(solution)/shard_map/ppermute | solution.py:23
  7.1 0.0 copy-start.2
  7.1 1.1 %copy-done.2 = bf16[768,512]{1,0:T(8,128)(2,1)S(1)} copy-done((bf16[768,512]{1,0:T(8,128)(2,1)S(1)}, bf16[768,512]{1,0:T(8,128)(2,1)}, u32[]{:S(2)}) %copy-start.2) | copy-done | bytes 786456
  8.2 1.9 %shard_map.68 = (f32[8,128]{1,0:T(8,128)S(1)}, bf16[256,1024]{1,0:T(8,128)(2,1)S(1)}, bf16[256,512]{1,0:T(8,128)(2,1)S(1)}, bf16[256,1024]{1,0:T(8,128)(2,1)S(1)...) custom-call(s32[1,3]{1,0:T(1,128)S(1)} %copy-done.4, ...), custom_call_target="tpu_custom_call" | custom-call | tf_op jit(solution)/shard_map/pallas_call | solution.py:185
  10.2 5.5 %collective-permute-done.4.from_chip = bf16[1024,256]{1,0:T(8,128)(2,1)S(1)} collective-permute-done((bf16[1024,256]{1,0:T(8,128)(2,1)S(1)}, bf16[1024,256]{1,0:T(8,128)(2,1)S(1)}, u32[]{:S(2)}, u32[]{:S(2)}) %collective-permute-start.4) | collective-permute-done | bytes 524320 | tf_op jit(solution)/shard_map/ppermute | solution.py:23
  15.7 0.0 collective-permute-done.1.on_chip
  15.7 0.3 shard_map.75
  16.0 0.1 collective-permute-start.5
  16.1 5.2 %collective-permute-done.from_chip = bf16[1024,256]{1,0:T(8,128)(2,1)S(1)} collective-permute-done((bf16[1024,256]{1,0:T(8,128)(2,1)S(1)}, bf16[1024,256]{1,0:T(8,128)(2,1)S(1)}, u32[]{:S(2)}, u32[]{:S(2)}) %collective-permute-start) | collective-permute-done | bytes 524320 | tf_op jit(solution)/shard_map/ppermute | solution.py:23
  21.3 0.3 shard_map.70
  21.6 0.1 collective-permute-start.2
  21.7 0.9 %shard_map.76 = (f32[1024,256]{1,0:T(8,128)S(1)}, f32[1024,256]{1,0:T(8,128)S(1)}) custom-call(f32[8,128]{1,0:T(8,128)S(1)} %get-tuple-element.39.mix, bf16[256,1024]{1,0:T(8,128)(2,1)S(1)} %get-tuple-element.42.x, bf16[256,512]{1,0:T(8,128)(2,1)S(1)} %get-tuple-element.43.t, bf16[1024,256]{1,0:T(8,128)(2,1)S(1)} %get-tuple-element.54.rounded, ...), custom_call_target="tpu_custom_call" | custom-call | tf_op jit(solution)/shard_map/pallas_call | solution.py:185
  22.6 10.9 %collective-permute-done.5.arrived = bf16[1024,256]{1,0:T(8,128)(2,1)S(1)} collective-permute-done((bf16[1024,256]{1,0:T(8,128)(2,1)S(1)}, bf16[1024,256]{1,0:T(8,128)(2,1)S(1)}, u32[]{:S(2)}, u32[]{:S(2)}) %collective-permute-start.5) | collective-permute-done | bytes 524320 | tf_op jit(solution)/shard_map/ppermute | solution.py:23
  33.6 0.3 shard_map.77
  33.9 1.2 %shard_map.78 = (f32[1024,256]{1,0:T(8,128)S(1)}, f32[8,64,256]{2,1,0:T(8,128)S(1)}, f32[8,64,256]{2,1,0:T(8,128)S(1)}) custom-call(f32[8,128]{1,0:T(8,128)S(1)} %get-tuple-element.39.mix, bf16[256,1024]{1,0:T(8,128)(2,1)S(1)} %get-tuple-element.40.x, bf16[256,512]{1,0:T(8,128)(2,1)S(1)} %get-tuple-element.41.t, ...), custom_call_target="tpu_custom_call" | custom-call | tf_op jit(solution)/shard_map/pallas_call | solution.py:185
  35.1 0.1 collective-permute-start.7
  35.2 0.9 %shard_map.71 = (f32[1024,256]{1,0:T(8,128)S(1)}, f32[1024,256]{1,0:T(8,128)S(1)}) custom-call(f32[8,128]{1,0:T(8,128)S(1)} %get-tuple-element.39.mix, bf16[256,1024]{1,0:T(8,128)(2,1)S(1)} %get-tuple-element.42.x, bf16[256,512]{1,0:T(8,128)(2,1)S(1)} %get-tuple-element.43.t, bf16[1024,256]{1,0:T(8,128)(2,1)S(1)} %get-tuple-element.45.rounded, ...), custom_call_target="tpu_custom_call" | custom-call | tf_op jit(solution)/shard_map/pallas_call | solution.py:185
  36.1 7.7 %collective-permute-done.2.arrived = bf16[1024,256]{1,0:T(8,128)(2,1)S(1)} collective-permute-done((bf16[1024,256]{1,0:T(8,128)(2,1)S(1)}, bf16[1024,256]{1,0:T(8,128)(2,1)S(1)}, u32[]{:S(2)}, u32[]{:S(2)}) %collective-permute-start.2) | collective-permute-done | bytes 524320 | tf_op jit(solution)/shard_map/ppermute | solution.py:23
  43.8 0.3 shard_map.72
  44.1 1.2 %shard_map.73 = (f32[1024,256]{1,0:T(8,128)S(1)}, f32[8,64,256]{2,1,0:T(8,128)S(1)}, f32[8,64,256]{2,1,0:T(8,128)S(1)}) custom-call(f32[8,128]{1,0:T(8,128)S(1)} %get-tuple-element.39.mix, bf16[256,1024]{1,0:T(8,128)(2,1)S(1)} %get-tuple-element.40.x, bf16[256,512]{1,0:T(8,128)(2,1)S(1)} %get-tuple-element.41.t, ...), custom_call_target="tpu_custom_call" | custom-call | tf_op jit(solution)/shard_map/pallas_call | solution.py:185
  45.3 0.1 collective-permute-start.9
  45.4 0.1 collective-permute-start.6
  45.5 1.1 %collective-permute-start.3 = (bf16[1024,256]{1,0:T(8,128)(2,1)S(1)}, bf16[1024,256]{1,0:T(8,128)(2,1)S(1)}, u32[]{:S(2)}, u32[]{:S(2)}) collective-permute-start(bf16[1024,256]{1,0:T(8,128)(2,1)S(1)} %get-tuple-element.49.rounded), channel_id=1, source_target_pairs={{0,8},{2,10},{4,12},{6,14},{8,16},{10,18},{12,20},{14,22},{16,24},... | collective-permute-start | bytes 1572872 | tf_op jit(solution)/shard_map/ppermute | solution.py:23
  46.5 0.1 shard_map.81
  46.6 1.6 %collective-permute-start.8 = (bf16[8,32,256]{2,1,0:T(8,128)(2,1)S(1)}, bf16[8,32,256]{2,1,0:T(8,128)(2,1)S(1)}, u32[]{:S(2)}, u32[]{:S(2)}) collective-permute-start(bf16[8,32,256]{2,1,0:T(8,128)(2,1)S(1)} %get-tuple-element.65), channel_id=1, source_target_pairs={{0,1},{1,0},{2,3},{3,2},{4,5},{5,4},{6,7},{7,6},{8,9},{9,8},{10,11... | collective-permute-start | bytes 393224 | tf_op jit(solution)/shard_map/ppermute | solution.py:34
  48.2 3.5 %collective-permute-done.8 = bf16[8,32,256]{2,1,0:T(8,128)(2,1)S(1)} collective-permute-done((bf16[8,32,256]{2,1,0:T(8,128)(2,1)S(1)}, bf16[8,32,256]{2,1,0:T(8,128)(2,1)S(1)}, u32[]{:S(2)}, u32[]{:S(2)}) %collective-permute-start.8) | collective-permute-done | bytes 131104 | tf_op jit(solution)/shard_map/ppermute | solution.py:34
  51.6 0.1 shard_map.82
  51.8 0.7 collective-permute-start.10
  52.4 1.5 %collective-permute-start.11 = (bf16[4,32,256]{2,1,0:T(8,128)(2,1)S(1)}, bf16[4,32,256]{2,1,0:T(8,128)(2,1)S(1)}, u32[]{:S(2)}, u32[]{:S(2)}) collective-permute-start(bf16[4,32,256]{2,1,0:T(8,128)(2,1)S(1)} %get-tuple-element.70), channel_id=1, source_target_pairs={{0,1},{1,0},{2,3},{3,2},{4,5},{5,4},{6,7},{7,6},{8,9},{9,8},{10,11... | collective-permute-start | bytes 196616 | tf_op jit(solution)/shard_map/ppermute | solution.py:34
  53.9 1.4 %collective-permute-start.12 = (bf16[4,32,256]{2,1,0:T(8,128)(2,1)S(1)}, bf16[4,32,256]{2,1,0:T(8,128)(2,1)S(1)}, u32[]{:S(2)}, u32[]{:S(2)}) collective-permute-start(bf16[4,32,256]{2,1,0:T(8,128)(2,1)S(1)} %get-tuple-element.71), channel_id=1, source_target_pairs={{0,5},{1,4},{2,7},{3,6},{4,1},{5,0},{6,3},{7,2},{8,13},{9,12},{10,... | collective-permute-start | bytes 196616 | tf_op jit(solution)/shard_map/ppermute | solution.py:307
  55.3 1.4 %collective-permute-done.11.from_x = bf16[4,32,256]{2,1,0:T(8,128)(2,1)S(1)} collective-permute-done((bf16[4,32,256]{2,1,0:T(8,128)(2,1)S(1)}, bf16[4,32,256]{2,1,0:T(8,128)(2,1)S(1)}, u32[]{:S(2)}, u32[]{:S(2)}) %collective-permute-start.11) | collective-permute-done | bytes 65568 | tf_op jit(solution)/shard_map/ppermute | solution.py:34
  56.7 2.4 %collective-permute-done.12.from_xy = bf16[4,32,256]{2,1,0:T(8,128)(2,1)S(1)} collective-permute-done((bf16[4,32,256]{2,1,0:T(8,128)(2,1)S(1)}, bf16[4,32,256]{2,1,0:T(8,128)(2,1)S(1)}, u32[]{:S(2)}, u32[]{:S(2)}) %collective-permute-start.12) | collective-permute-done | bytes 65568 | tf_op jit(solution)/shard_map/ppermute | solution.py:307
  59.1 0.0 collective-permute-done.10.from_y
  59.1 0.1 shard_map.83
  59.2 1.6 %collective-permute-start.13 = (bf16[32,512]{1,0:T(8,128)(2,1)S(1)}, bf16[32,512]{1,0:T(8,128)(2,1)S(1)}, u32[]{:S(2)}, u32[]{:S(2)}) collective-permute-start(bf16[32,512]{1,0:T(8,128)(2,1)S(1)} %get-tuple-element.73), channel_id=1, source_target_pairs={{0,8},{2,10},{4,12},{6,14},{8,0},{10,2},{12,4},{14,6},{16,24},{18,... | collective-permute-start | bytes 98312 | tf_op jit(solution)/shard_map/ppermute | solution.py:34
  60.8 1.8 %collective-permute-start.14 = (bf16[32,512]{1,0:T(8,128)(2,1)S(1)}, bf16[32,512]{1,0:T(8,128)(2,1)S(1)}, u32[]{:S(2)}, u32[]{:S(2)}) collective-permute-start(bf16[32,512]{1,0:T(8,128)(2,1)S(1)} %get-tuple-element.74), channel_id=1, source_target_pairs={{0,16},{2,18},{4,20},{6,22},{8,24},{10,26},{12,28},{14,30},{16,0},... | collective-permute-start | bytes 98312 | tf_op jit(solution)/shard_map/ppermute | solution.py:34
  62.6 1.2 %collective-permute-start.15 = (bf16[32,512]{1,0:T(8,128)(2,1)S(1)}, bf16[32,512]{1,0:T(8,128)(2,1)S(1)}, u32[]{:S(2)}, u32[]{:S(2)}) collective-permute-start(bf16[32,512]{1,0:T(8,128)(2,1)S(1)} %get-tuple-element.75), channel_id=1, source_target_pairs={{0,24},{2,26},{4,28},{6,30},{8,16},{10,18},{12,20},{14,22},{16,8},... | collective-permute-start | bytes 98312 | tf_op jit(solution)/shard_map/ppermute | solution.py:34
  63.8 1.1 %shard_map.79.refs_0_ = bf16[1024,512]{1,0:T(8,128)(2,1)} custom-call(f32[8,128]{1,0:T(8,128)S(1)} %get-tuple-element.39.mix, f32[1024,256]{1,0:T(8,128)S(1)} %get-tuple-element.61.base, bf16[1024,256]{1,0:T(8,128)(2,1)S(1)} %collective-permute-done.6.arrived), custom_call_target="tpu_custom_call" | custom-call | tf_op jit(solution)/shard_map/pallas_call | solution.py:185
  64.9 8.5 %collective-permute-done.3.arrived = bf16[1024,256]{1,0:T(8,128)(2,1)S(1)} collective-permute-done((bf16[1024,256]{1,0:T(8,128)(2,1)S(1)}, bf16[1024,256]{1,0:T(8,128)(2,1)S(1)}, u32[]{:S(2)}, u32[]{:S(2)}) %collective-permute-start.3) | collective-permute-done | bytes 524320 | tf_op jit(solution)/shard_map/ppermute | solution.py:23
  73.4 1.1 %shard_map.80 = bf16[1024,512]{1,0:T(8,128)(2,1)} custom-call(f32[8,128]{1,0:T(8,128)S(1)} %get-tuple-element.39.mix, f32[1024,256]{1,0:T(8,128)S(1)} %get-tuple-element.52.base, bf16[1024,256]{1,0:T(8,128)(2,1)S(1)} %collective-permute-done.3.arrived, bf16[1024,512]{1,0:T(8,128)(2,1)} %shard_map.79.refs_0_), custom_call_target="tpu_custom_call", output_to_operand_aliasing={{}: (3, {})} | custom-call | tf_op jit(solution)/shard_map/pallas_call | solution.py:185
  74.5 0.0 collective-permute-done.13.refs_0_
  74.5 0.5 collective-permute-done.14.refs_1_
  75.0 0.0 collective-permute-done.15.refs_2_
  75.0 0.6 shard_map.84
  (11 shorter events, 0.1 us)
Async XLA Ops:
  0.6 6.5 %copy-start = (bf16[1,1024,512]{2,1,0:T(8,128)(2,1)S(1)}, bf16[1,1024,512]{2,1,0:T(8,128)(2,1)}, u32[]{:S(2)}) copy-start(bf16[1,1024,512]{2,1,0:T(8,128)(2,1)} %param.5) | copy-start | bytes 3145732
  0.6 6.5 %copy-start.1 = (bf16[768,1024]{1,0:T(8,128)(2,1)S(1)}, bf16[768,1024]{1,0:T(8,128)(2,1)}, u32[]{:S(2)}) copy-start(bf16[768,1024]{1,0:T(8,128)(2,1)} %x.1) | copy-start | bytes 4718596
  0.7 6.4 %copy-start.3 = (s32[3,2]{0,1:T(2,128)S(1)}, s32[3,2]{0,1:T(2,128)}, u32[]{:S(2)}) copy-start(s32[3,2]{0,1:T(2,128)} %param.8) | copy-start | bytes 76
  0.7 6.4 %copy-start.4 = (s32[1,3]{1,0:T(1,128)S(1)}, s32[1,3]{1,0:T(1,128)}, u32[]{:S(2)}) copy-start(s32[1,3]{1,0:T(1,128)} %order.1) | copy-start | bytes 40
  0.7 15.0 %collective-permute-start.1 = (bf16[1024,512]{1,0:T(8,128)(2,1)}, bf16[1024,512]{1,0:T(8,128)(2,1)S(1)}, u32[]{:S(2)}, u32[]{:S(2)}) collective-permute-start(bf16[1024,512]{1,0:T(8,128)(2,1)} %bitcast.9), channel_id=1, source_target_pairs={{0,2},{4,6},{8,10},{12,14},{16,18},{20,22},{24,26},{28,30},{1,3},{... | collective-permute-start | bytes 3145736 | tf_op jit(solution)/shard_map/ppermute | solution.py:29
  3.5 12.2 %collective-permute-start.4 = (bf16[1024,256]{1,0:T(8,128)(2,1)S(1)}, bf16[1024,256]{1,0:T(8,128)(2,1)S(1)}, u32[]{:S(2)}, u32[]{:S(2)}) collective-permute-start(bf16[1024,256]{1,0:T(8,128)(2,1)S(1)} %shard_map.74), channel_id=1, source_target_pairs={{0,2},{2,4},{4,6},{6,8},{8,10},{10,12},{12,14},{14,16},{16,18},{18... | collective-permute-start | bytes 1572872 | tf_op jit(solution)/shard_map/ppermute | solution.py:23
  3.9 17.4 %collective-permute-start = (bf16[1024,256]{1,0:T(8,128)(2,1)S(1)}, bf16[1024,256]{1,0:T(8,128)(2,1)S(1)}, u32[]{:S(2)}, u32[]{:S(2)}) collective-permute-start(bf16[1024,256]{1,0:T(8,128)(2,1)S(1)} %shard_map.69), channel_id=1, source_target_pairs={{0,2},{2,4},{4,6},{6,8},{8,10},{10,12},{12,14},{14,16},{16,18},{18... | collective-permute-start | bytes 1572872 | tf_op jit(solution)/shard_map/ppermute | solution.py:23
  7.1 1.1 %copy-start.2 = (bf16[768,512]{1,0:T(8,128)(2,1)S(1)}, bf16[768,512]{1,0:T(8,128)(2,1)}, u32[]{:S(2)}) copy-start(bf16[768,512]{1,0:T(8,128)(2,1)} %t.1) | copy-start | bytes 2359300
  16.0 17.5 %collective-permute-start.5 = (bf16[1024,256]{1,0:T(8,128)(2,1)S(1)}, bf16[1024,256]{1,0:T(8,128)(2,1)S(1)}, u32[]{:S(2)}, u32[]{:S(2)}) collective-permute-start(bf16[1024,256]{1,0:T(8,128)(2,1)S(1)} %get-tuple-element.54.rounded), channel_id=1, source_target_pairs={{0,4},{2,6},{4,8},{6,10},{8,12},{10,14},{12,16},{14,18},{16,20},{1... | collective-permute-start | bytes 1572872 | tf_op jit(solution)/shard_map/ppermute | solution.py:23
  21.6 22.2 %collective-permute-start.2 = (bf16[1024,256]{1,0:T(8,128)(2,1)S(1)}, bf16[1024,256]{1,0:T(8,128)(2,1)S(1)}, u32[]{:S(2)}, u32[]{:S(2)}) collective-permute-start(bf16[1024,256]{1,0:T(8,128)(2,1)S(1)} %get-tuple-element.45.rounded), channel_id=1, source_target_pairs={{0,4},{2,6},{4,8},{6,10},{8,12},{10,14},{12,16},{14,18},{16,20},{1... | collective-permute-start | bytes 1572872 | tf_op jit(solution)/shard_map/ppermute | solution.py:23
  35.1 11.4 %collective-permute-start.7 = (f32[8,64,256]{2,1,0:T(8,128)S(1)}, f32[8,64,256]{2,1,0:T(8,128)S(1)}, u32[]{:S(2)}, u32[]{:S(2)}) collective-permute-start(f32[8,64,256]{2,1,0:T(8,128)S(1)} %get-tuple-element.63), channel_id=1, source_target_pairs={{0,2},{2,0},{4,6},{6,4},{8,10},{10,8},{12,14},{14,12},{16,18},{18,... | collective-permute-start | bytes 1572872 | tf_op jit(solution)/shard_map/ppermute | solution.py:34
  45.3 2.8 %collective-permute-start.9 = (f32[8,64,256]{2,1,0:T(8,128)S(1)}, f32[8,64,256]{2,1,0:T(8,128)S(1)}, u32[]{:S(2)}, u32[]{:S(2)}) collective-permute-start(f32[8,64,256]{2,1,0:T(8,128)S(1)} %get-tuple-element.67), channel_id=1, source_target_pairs={{0,2},{2,0},{4,6},{6,4},{8,10},{10,8},{12,14},{14,12},{16,18},{18,... | collective-permute-start | bytes 1572872 | tf_op jit(solution)/shard_map/ppermute | solution.py:34
  45.4 18.4 %collective-permute-start.6 = (bf16[1024,256]{1,0:T(8,128)(2,1)S(1)}, bf16[1024,256]{1,0:T(8,128)(2,1)S(1)}, u32[]{:S(2)}, u32[]{:S(2)}) collective-permute-start(bf16[1024,256]{1,0:T(8,128)(2,1)S(1)} %get-tuple-element.58.rounded), channel_id=1, source_target_pairs={{0,8},{2,10},{4,12},{6,14},{8,16},{10,18},{12,20},{14,22},{16,24},... | collective-permute-start | bytes 1572872 | tf_op jit(solution)/shard_map/ppermute | solution.py:23
  45.5 27.9 %collective-permute-start.3 = (bf16[1024,256]{1,0:T(8,128)(2,1)S(1)}, bf16[1024,256]{1,0:T(8,128)(2,1)S(1)}, u32[]{:S(2)}, u32[]{:S(2)}) collective-permute-start(bf16[1024,256]{1,0:T(8,128)(2,1)S(1)} %get-tuple-element.49.rounded), channel_id=1, source_target_pairs={{0,8},{2,10},{4,12},{6,14},{8,16},{10,18},{12,20},{14,22},{16,24},... | collective-permute-start | bytes 1572872 | tf_op jit(solution)/shard_map/ppermute | solution.py:23
  46.6 5.0 %collective-permute-start.8 = (bf16[8,32,256]{2,1,0:T(8,128)(2,1)S(1)}, bf16[8,32,256]{2,1,0:T(8,128)(2,1)S(1)}, u32[]{:S(2)}, u32[]{:S(2)}) collective-permute-start(bf16[8,32,256]{2,1,0:T(8,128)(2,1)S(1)} %get-tuple-element.65), channel_id=1, source_target_pairs={{0,1},{1,0},{2,3},{3,2},{4,5},{5,4},{6,7},{7,6},{8,9},{9,8},{10,11... | collective-permute-start | bytes 393224 | tf_op jit(solution)/shard_map/ppermute | solution.py:34
  51.8 7.3 %collective-permute-start.10 = (bf16[4,32,512]{2,1,0:T(8,128)(2,1)S(1)}, bf16[4,32,512]{2,1,0:T(8,128)(2,1)S(1)}, u32[]{:S(2)}, u32[]{:S(2)}) collective-permute-start(bf16[4,32,512]{2,1,0:T(8,128)(2,1)S(1)} %get-tuple-element.69), channel_id=1, source_target_pairs={{0,4},{2,6},{4,0},{6,2},{8,12},{10,14},{12,8},{14,10},{16,20},{18,... | collective-permute-start | bytes 393224 | tf_op jit(solution)/shard_map/ppermute | solution.py:34
  52.4 4.3 %collective-permute-start.11 = (bf16[4,32,256]{2,1,0:T(8,128)(2,1)S(1)}, bf16[4,32,256]{2,1,0:T(8,128)(2,1)S(1)}, u32[]{:S(2)}, u32[]{:S(2)}) collective-permute-start(bf16[4,32,256]{2,1,0:T(8,128)(2,1)S(1)} %get-tuple-element.70), channel_id=1, source_target_pairs={{0,1},{1,0},{2,3},{3,2},{4,5},{5,4},{6,7},{7,6},{8,9},{9,8},{10,11... | collective-permute-start | bytes 196616 | tf_op jit(solution)/shard_map/ppermute | solution.py:34
  53.9 5.2 %collective-permute-start.12 = (bf16[4,32,256]{2,1,0:T(8,128)(2,1)S(1)}, bf16[4,32,256]{2,1,0:T(8,128)(2,1)S(1)}, u32[]{:S(2)}, u32[]{:S(2)}) collective-permute-start(bf16[4,32,256]{2,1,0:T(8,128)(2,1)S(1)} %get-tuple-element.71), channel_id=1, source_target_pairs={{0,5},{1,4},{2,7},{3,6},{4,1},{5,0},{6,3},{7,2},{8,13},{9,12},{10,... | collective-permute-start | bytes 196616 | tf_op jit(solution)/shard_map/ppermute | solution.py:307
  59.2 15.3 %collective-permute-start.13 = (bf16[32,512]{1,0:T(8,128)(2,1)S(1)}, bf16[32,512]{1,0:T(8,128)(2,1)S(1)}, u32[]{:S(2)}, u32[]{:S(2)}) collective-permute-start(bf16[32,512]{1,0:T(8,128)(2,1)S(1)} %get-tuple-element.73), channel_id=1, source_target_pairs={{0,8},{2,10},{4,12},{6,14},{8,0},{10,2},{12,4},{14,6},{16,24},{18,... | collective-permute-start | bytes 98312 | tf_op jit(solution)/shard_map/ppermute | solution.py:34
  60.8 14.2 %collective-permute-start.14 = (bf16[32,512]{1,0:T(8,128)(2,1)S(1)}, bf16[32,512]{1,0:T(8,128)(2,1)S(1)}, u32[]{:S(2)}, u32[]{:S(2)}) collective-permute-start(bf16[32,512]{1,0:T(8,128)(2,1)S(1)} %get-tuple-element.74), channel_id=1, source_target_pairs={{0,16},{2,18},{4,20},{6,22},{8,24},{10,26},{12,28},{14,30},{16,0},... | collective-permute-start | bytes 98312 | tf_op jit(solution)/shard_map/ppermute | solution.py:34
  62.6 12.4 %collective-permute-start.15 = (bf16[32,512]{1,0:T(8,128)(2,1)S(1)}, bf16[32,512]{1,0:T(8,128)(2,1)S(1)}, u32[]{:S(2)}, u32[]{:S(2)}) collective-permute-start(bf16[32,512]{1,0:T(8,128)(2,1)S(1)} %get-tuple-element.75), channel_id=1, source_target_pairs={{0,24},{2,26},{4,28},{6,30},{8,16},{10,18},{12,20},{14,22},{16,8},... | collective-permute-start | bytes 98312 | tf_op jit(solution)/shard_map/ppermute | solution.py:34
